TPU v7x, 32 devices: a whole 2x2x4 slice. The times are simulated.
32 devices in a mesh: groups: 1, seq: 32 (over z, y, x, core).
Axes of the slice: x: 2, y: 2, z: 4, core: 2. Of those that a mesh axis runs over, the one named last changes fastest.
Arguments:
- queries: bfloat16 [8192, 1280], P(('groups', 'seq')), may hold values from -8 to 8
- key_rows: bfloat16 [8192, 1280], P(('groups', 'seq')), may hold values from -8 to 8
- value_rows: bfloat16 [8192, 1280], P(('groups', 'seq')), may hold values from -8 to 8
- step_rates: float32 [2, 8192], P(None, ('groups', 'seq')), may hold values from 0.02 to 0.2
- fast_weights: float32 [3, 1280, 640], P(None, 'seq'), may hold values from -0.25 to 0.25
- momentum: float32 [3, 1280, 640], P('groups', 'seq'), may hold values from -0.18 to 0.18
- out_gain: float32 [1280], replicated, may hold values from 0.5 to 1.5
Outputs:
- layer_out: bfloat16 [8192, 1280], P(('groups', 'seq'))
- new_weights: float32 [3, 1280, 640], P('groups', 'seq')
- new_momentum: float32 [3, 1280, 640], P('groups', 'seq')
All inputs are finite; a program needn't handle non-finite values.
Results may differ from a plain program's by a relative error of at most 0.0089.
Values may be sent and summed in bfloat16 or wider, within the bound.
No kernel may reach another device: no remote copies, remote signals or barrier semaphores. Data moves between devices by JAX's collectives and lax.ppermute only.
A program may use at most 128 MiB of HBM per device.

v0:
```python
import math

import jax
import jax.numpy as jnp
from jax import lax
from jax.experimental import pallas as pl
from jax.experimental.pallas import tpu as pltpu
from jax.sharding import PartitionSpec as P


ATT_DIM = 128
WINDOW = 1024
EPS = 1e-06
MASKED = -1e30
BF16 = jnp.bfloat16
F32 = jnp.float32


class Routes:
    def __init__(self, count):
        self.count = count
        half = count // 16
        self.bits = [1 << b for b in range(half.bit_length() - 1)]
        assert count % 16 == 0 and half == 1 << len(self.bits)
        home = [dev for dev in range(count) if self.is_home(dev)]
        away = [dev for dev in range(count) if not self.is_home(dev)]
        self.partner = [(dev, dev ^ 1) for dev in range(count)]
        self.x_swap = [(dev, dev ^ 2) for dev in range(count)]
        self.y_swap = [(dev, dev ^ 4) for dev in range(count)]
        self.pair_in = [(dev ^ 1, dev) for dev in home]
        self.pair_out = [(dev, dev ^ 1) for dev in home]
        shift = half * 8
        self.cross_out = [(dev, (dev + shift) % count) for dev in home]
        self.home_swap = [[(dev, dev ^ (8 * k)) for dev in home] for k in range(half)]
        self.away_swap = [[(dev, dev ^ (8 * k)) for dev in away] for k in range(half)]
        self.cross_back = [
            [(dev, ((dev ^ (8 * k)) + shift) % count) for dev in away] for k in range(half)
        ]
        self.z_up = [(dev, dev + 8) for dev in range(count - 8) if dev % 8 >= 4]
        self.back_x = [(dev, dev - 2) for dev in range(count) if dev % 4 >= 2]

    def is_home(self, dev):
        return (dev % 2) == (2 * dev // self.count)


def send(array, route):
    return lax.ppermute(array, "seq", route)


def gather_z(unit, routes, is_home):
    home_list = [unit]
    away_list = [send(unit, routes.cross_out)]
    for bit in routes.bits:
        home_list = home_list + [send(part, routes.home_swap[bit]) for part in home_list]
        away_list = away_list + [send(part, routes.away_swap[bit]) for part in away_list]
    return [jnp.where(is_home, home, away) for home, away in zip(home_list, away_list)]


def gather_plane(units, routes):
    pieces = []
    for idx, own in enumerate(units):
        first, second = (
            (routes.x_swap, routes.y_swap) if idx % 2 == 0 else (routes.y_swap, routes.x_swap)
        )
        near = send(own, first)
        side = send(own, second)
        pieces += [own, near, side, send(near, second)]
    return pieces


def reduce_z(sums, routes):
    total = sums[0]
    for k, part in enumerate(sums):
        sent = part.astype(BF16)
        total = total + send(sent, routes.cross_back[k]).astype(F32)
        if k > 0:
            total = total + send(sent, routes.home_swap[k]).astype(F32)
    return total


def nt_dot(left, right):
    return lax.dot_general(left, right, (((1,), (1,)), ((), ())), preferred_element_type=F32)


def nn_dot(left, right):
    return lax.dot_general(left, right, (((1,), (0,)), ((), ())), preferred_element_type=F32)


def vmem():
    return pl.BlockSpec(memory_space=pltpu.VMEM)


def key_kernel(grad_scale, k_own, v_own, k_near, v_near, rates, units, out, keys, ograd, pair, down):
    tokens = k_own.shape[1]
    parts, _, step, _ = units.shape
    rows = parts * step
    for idx, (k_ref, v_ref) in enumerate(((k_own, v_own), (k_near, v_near))):
        for side in range(2):
            at = (2 * idx + side) * tokens
            keys[at : at + tokens, :] = k_ref[side]
            rate = rates[at : at + tokens, :] * (-grad_scale)
            ograd[at : at + tokens, :] = (rate * v_ref[side].astype(F32)).astype(BF16)
    for idx in range(parts):
        pair[idx * step : (idx + 1) * step, :] = units[idx, 0]
        pair[rows + idx * step : rows + (idx + 1) * step, :] = units[idx, 1]
        down[idx * step : (idx + 1) * step, :] = units[idx, 2]
    both = nt_dot(pair[...], keys[...])
    gate, up = both[:rows], both[rows:]
    hidden_grad = nt_dot(down[...], ograd[...])
    sig = jax.nn.sigmoid(gate)
    silu = gate * sig
    hidden = (silu * up).astype(BF16)
    gate_grad = (hidden_grad * up * (sig * (1.0 + gate * (1.0 - sig)))).astype(BF16)
    up_grad = (hidden_grad * silu).astype(BF16)
    first = nn_dot(jnp.concatenate([gate_grad, up_grad], axis=0), keys[...])
    second = nn_dot(hidden, ograd[...])
    for idx in range(parts):
        at = idx * step
        out[idx, 0] = first[at : at + step].astype(out.dtype)
        out[idx, 1] = first[rows + at : rows + at + step].astype(out.dtype)
        out[idx, 2] = second[at : at + step].astype(out.dtype)


def key_side(grad_scale, k_own, v_own, k_near, v_near, rates, units, kind):
    _, tokens, width = k_own.shape
    parts, _, step, _ = units.shape
    rows = parts * step
    return pl.pallas_call(
        lambda *refs: key_kernel(grad_scale, *refs),
        out_shape=jax.ShapeDtypeStruct(units.shape, kind),
        in_specs=[vmem()] * 6,
        out_specs=vmem(),
        scratch_shapes=[
            pltpu.VMEM((4 * tokens, width), BF16),
            pltpu.VMEM((4 * tokens, width), BF16),
            pltpu.VMEM((2 * rows, width), BF16),
            pltpu.VMEM((rows, width), BF16),
        ],
        cost_estimate=pl.CostEstimate(
            flops=12 * 4 * tokens * rows * width,
            bytes_accessed=16 * tokens * width,
            transcendentals=0,
        ),
    )(k_own, v_own, k_near, v_near, rates, units)


def query_kernel(count, *refs):
    where, quer_in = refs[:2]
    pieces = refs[2 : 2 + count]
    gain, att, own, other = refs[2 + count : 6 + count]
    quer, weights, result = refs[6 + count :]
    tokens = quer_in.shape[1]
    rows = pieces[0].shape[1]
    mine = pl.multiple_of(where[0] * tokens, tokens)
    theirs = pl.multiple_of((1 - where[0]) * tokens, tokens)
    quer[pl.ds(mine, tokens), :] = quer_in[0]
    quer[pl.ds(theirs, tokens), :] = quer_in[1]
    for idx in range(count):
        weights[:, idx * rows : (idx + 1) * rows, :] = pieces[idx][...]
    gate = nt_dot(quer[...], weights[0])
    up = nt_dot(quer[...], weights[1])
    hidden = (gate * jax.nn.sigmoid(gate) * up).astype(BF16)
    out = nn_dot(hidden, weights[2])
    scale = lax.rsqrt(jnp.mean(out * out, axis=-1, keepdims=True) + EPS)
    result[...] = out * scale * gain[...] + att[...]
    own[...] = result[pl.ds(mine, tokens), :].astype(BF16)
    other[...] = result[pl.ds(theirs, tokens), :].astype(BF16)


def query_side(where, quer_in, pieces, gain, att):
    _, tokens, width = quer_in.shape
    count = len(pieces)
    rows = pieces[0].shape[1]
    total = 2 * tokens * count * rows * width
    return pl.pallas_call(
        lambda *refs: query_kernel(count, *refs),
        out_shape=[jax.ShapeDtypeStruct((tokens, width), BF16)] * 2,
        in_specs=[pl.BlockSpec(memory_space=pltpu.SMEM)] + [vmem()] * (3 + count),
        out_specs=[vmem()] * 2,
        scratch_shapes=[
            pltpu.VMEM((2 * tokens, width), BF16),
            pltpu.VMEM((3, count * rows, width), BF16),
            pltpu.VMEM((2 * tokens, width), F32),
        ],
        cost_estimate=pl.CostEstimate(
            flops=6 * total, bytes_accessed=6 * count * rows * width, transcendentals=0
        ),
        name="query_side",
    )(where, quer_in, *pieces, gain, att)


def att_kernel(where, quer_in, k_own, v_own, k_two, v_two, k_near, v_near, k_back, v_back, out,
               quer, keys, vals, bias):
    tokens = quer_in.shape[1]
    span = 2 * tokens
    tile = 128
    reach = WINDOW + tile
    core, odd, chip = where[0], where[1], where[2]
    mine = core * tokens
    theirs = (1 - core) * tokens

    def put(dest, base, pair):
        dest[pl.ds(pl.multiple_of(base + mine, tokens), tokens), :] = pair[0]
        dest[pl.ds(pl.multiple_of(base + theirs, tokens), tokens), :] = pair[1]

    put(quer, 0, quer_in)
    for dest, own, two, near, back in (
        (keys, k_own, k_two, k_near, k_back),
        (vals, v_own, v_two, v_near, v_back),
    ):
        put(dest, 2 * span, own)
        put(dest, 0, two)

        @pl.when(odd == 1)
        def _():
            put(dest, span, near)

        @pl.when(odd == 0)
        def _():
            put(dest, span, back)

    scale = 1.0 / math.sqrt(ATT_DIM)
    row = lax.broadcasted_iota(jnp.int32, (tile, reach), 0)
    col = lax.broadcasted_iota(jnp.int32, (tile, reach), 1)

    def one_tile(idx, carry):
        first = pl.multiple_of(idx * tile, tile)
        position = chip * span - WINDOW + first + col
        seen = (col > row) & (col <= row + WINDOW) & (position >= 0)
        bias[...] = jnp.where(seen, 0.0, MASKED)
        for head in range(quer.shape[1] // ATT_DIM):
            cols = slice(head * ATT_DIM, (head + 1) * ATT_DIM)
            scores = nt_dot(quer[pl.ds(first, tile), cols], keys[pl.ds(first, reach), cols])
            scores = scores * scale + bias[...]
            top = jnp.max(scores, axis=-1, keepdims=True)
            probs = jnp.exp(scores - top)
            norm = jnp.sum(probs, axis=-1, keepdims=True)
            att = nn_dot(probs.astype(BF16), vals[pl.ds(first, reach), cols]) / norm
            att = att * lax.rsqrt(jnp.mean(att * att, axis=-1, keepdims=True) + EPS)
            out[pl.ds(first, tile), cols] = att
        return carry

    lax.fori_loop(0, span // tile, one_tile, 0)


def attention(where, *blocks):
    _, tokens, width = blocks[0].shape
    span = 2 * tokens
    assert WINDOW == 2 * span
    return pl.pallas_call(
        att_kernel,
        out_shape=jax.ShapeDtypeStruct((span, width), F32),
        in_specs=[pl.BlockSpec(memory_space=pltpu.SMEM)] + [vmem()] * len(blocks),
        out_specs=vmem(),
        scratch_shapes=[
            pltpu.VMEM((span, width), BF16),
            pltpu.VMEM((3 * span, width), BF16),
            pltpu.VMEM((3 * span, width), BF16),
            pltpu.VMEM((128, WINDOW + 128), F32),
        ],
        cost_estimate=pl.CostEstimate(
            flops=4 * span * (WINDOW + 128) * width,
            bytes_accessed=40 * tokens * width,
            transcendentals=span * WINDOW * width // ATT_DIM,
        ),
        name="attention",
    )(where, *blocks)


def updated(weights, momentum, grads):
    new_momentum = 0.9 * momentum + grads
    moved = weights - new_momentum
    keep_norm = jnp.sqrt(jnp.mean(weights * weights, axis=-1, keepdims=True))
    new_weights = (
        moved * keep_norm * lax.rsqrt(jnp.mean(moved * moved, axis=-1, keepdims=True) + EPS)
    )
    return new_weights, new_momentum


def layer(queries, key_rows, value_rows, step_rates, fast_weights, momentum, out_gain):
    count = lax.axis_size("seq")
    routes = Routes(count)
    local_tokens = queries.shape[0]
    heads, width = step_rates.shape[0], fast_weights.shape[2]
    owned = fast_weights.shape[1]
    assert heads == 2
    here = lax.axis_index("seq")
    core = here % 2
    chip = here // 2
    is_home = core == (2 * here) // count
    where = jnp.stack([core, chip % 2, chip]).astype(jnp.int32)

    my_rate = lax.dynamic_slice_in_dim(step_rates, core, 1, 0)
    their_rate = lax.dynamic_slice_in_dim(step_rates, 1 - core, 1, 0)
    rates = jnp.concatenate([my_rate, send(their_rate, routes.partner)], axis=0)
    rates = jnp.concatenate([rates, send(rates, routes.x_swap)], axis=0)
    rates = rates.reshape(4 * local_tokens, 1)

    def by_core(array):
        kept = lax.dynamic_slice_in_dim(array, core * width, width, 1)
        sent = lax.dynamic_slice_in_dim(array, (1 - core) * width, width, 1)
        return jnp.stack([kept, send(sent, routes.partner)])

    k_own = by_core(key_rows)
    v_own = by_core(value_rows)
    k_own, v_own, rates = lax.optimization_barrier((k_own, v_own, rates))
    q_own = by_core(queries)

    pair_weights = jnp.concatenate([fast_weights, send(fast_weights, routes.pair_in)], axis=1)

    k_near = send(k_own, routes.x_swap)
    v_near = send(v_own, routes.x_swap)
    unit = pair_weights.astype(BF16)
    units = gather_z(unit, routes, is_home)
    own_units = jnp.stack(units)
    side_units = send(own_units, routes.y_swap)
    k_late, v_late, _ = lax.optimization_barrier((k_own, v_own, own_units))
    k_up = send(k_late, routes.z_up)
    v_up = send(v_late, routes.z_up)
    grad_scale = 1.0 / math.sqrt(local_tokens * count)
    tokens_in = (k_own, v_own, k_near, v_near, rates)
    side_grads = key_side(grad_scale, *tokens_in, side_units, BF16)
    side_in = send(side_grads, routes.y_swap)
    own_grads = key_side(grad_scale, *tokens_in, own_units, F32)
    sums = own_grads + side_in.astype(F32)
    sums, k_up, v_up = lax.optimization_barrier((sums, k_up, v_up))
    total = reduce_z([sums[k] for k in range(len(units))], routes)
    pair_momentum = jnp.concatenate([momentum, send(momentum, routes.pair_in)], axis=1)

    upper = chip // 2 % 2 == 1
    k_two = send(jnp.where(upper, k_up, k_own), routes.y_swap)
    v_two = send(jnp.where(upper, v_up, v_own), routes.y_swap)
    k_back = send(k_two, routes.back_x)
    v_back = send(v_two, routes.back_x)
    att = attention(where, q_own, k_own, v_own, k_two, v_two, k_near, v_near, k_back, v_back)

    pair_new, _ = updated(pair_weights, pair_momentum, total)
    applied = gather_plane(gather_z(pair_new.astype(BF16), routes, is_home), routes)
    partner_grads = send(total[:, owned:], routes.pair_out)
    grads = jnp.where(is_home, total[:, :owned], partner_grads)
    new_weights, new_momentum = updated(fast_weights, momentum, grads)
    gain = lax.dynamic_slice_in_dim(out_gain, core * width, width, 0).reshape(1, width)
    own, other = query_side(where, q_own, applied, gain, att)
    arrived = send(other, routes.partner)
    layer_out = jnp.where(
        core == 0,
        jnp.concatenate([own, arrived], axis=1),
        jnp.concatenate([arrived, own], axis=1),
    )
    return (layer_out, new_weights, new_momentum)


def solution(mesh):
    placed = (
        P(("groups", "seq"), None),
        P(("groups", "seq"), None),
        P(("groups", "seq"), None),
        P(None, ("groups", "seq")),
        P(None, "seq", None),
        P("groups", "seq", None),
        P(),
    )
    return jax.shard_map(
        layer,
        mesh=mesh,
        in_specs=placed,
        out_specs=(P(("groups", "seq"), None), P("groups", "seq", None), P("groups", "seq", None)),
        check_vma=False,
    )
```

profile of v0, /device:TPU:21, one launch (start us, length us, event | category | flops | bytes accessed | tf_op | source)
XLA Modules:
  0.0 191.3 jit_solution(3837848550214668116)
XLA Ops:
  0.6 1.4 collective-permute-start.1
  2.1 1.2 dynamic-slice_bitcast_fusion.1
  3.3 1.9 collective-permute-start.3
  5.4 0.5 collective-permute-start.5
  5.9 1.0 constant_dynamic-update-slice_fusion
  6.9 0.8 convert_element_type.25
  7.7 2.2 %collective-permute-start.9 = (bf16[3,80,640]{2,1,0:T(8,128)(2,1)}, bf16[3,80,640]{2,1,0:T(8,128)(2,1)S(1)}, u32[]{:S(2)}, u32[]{:S(2)}) collective-permute-start(bf16[3,80,640]{2,1,0:T(8,128)(2,1)} %convert_element_type.25), channel_id=1, source_target_pairs={{0,16},{2,18},{4,20},{6,22},{8,24},{10,26},{12,28},{14,30},{17,1},... | collective-permute-start | bytes 921608 | tf_op jit(solution)/shard_map/ppermute | solution.py:47
  9.9 1.3 collective-permute-start.6
  11.2 1.2 collective-permute-done.6
  12.4 3.2 %collective-permute-start.10 = (bf16[3,80,640]{2,1,0:T(8,128)(2,1)}, bf16[3,80,640]{2,1,0:T(8,128)(2,1)S(1)}, u32[]{:S(2)}, u32[]{:S(2)}) collective-permute-start(bf16[3,80,640]{2,1,0:T(8,128)(2,1)} %convert_element_type.25), channel_id=1, source_target_pairs={{0,8},{2,10},{4,12},{6,14},{8,0},{10,2},{12,4},{14,6},{17,25},{19,... | collective-permute-start | bytes 921608 | tf_op jit(solution)/shard_map/ppermute | solution.py:47
  15.7 1.5 collective-permute-done.9
  17.2 0.7 collective-permute-start.11
  18.0 1.3 collective-permute-start.7
  19.6 3.2 %collective-permute-done.10 = bf16[3,80,640]{2,1,0:T(8,128)(2,1)S(1)} collective-permute-done((bf16[3,80,640]{2,1,0:T(8,128)(2,1)}, bf16[3,80,640]{2,1,0:T(8,128)(2,1)S(1)}, u32[]{:S(2)}, u32[]{:S(2)}) %collective-permute-start.10) | collective-permute-done | bytes 307232 | tf_op jit(solution)/shard_map/ppermute | solution.py:47
  22.9 0.9 pad_maximum_fusion.3.refs_5_
  24.0 1.0 copy.10.refs_4_
  25.1 2.9 %collective-permute-done.7.refs_2_.k_near = bf16[2,256,640]{2,1,0:T(8,128)(2,1)S(1)} collective-permute-done((bf16[2,256,640]{2,1,0:T(8,128)(2,1)S(1)}, bf16[2,256,640]{2,1,0:T(8,128)(2,1)S(1)}, u32[]{:S(2)}, u32[]{:S(2)}) %collective-permute-start.7) | collective-permute-done | bytes 655392 | tf_op jit(solution)/shard_map/ppermute | solution.py:47
  27.9 14.1 %collective-permute-done.8.refs_3_.v_near = bf16[2,256,640]{2,1,0:T(8,128)(2,1)} collective-permute-done((bf16[2,256,640]{2,1,0:T(8,128)(2,1)S(1)}, bf16[2,256,640]{2,1,0:T(8,128)(2,1)}, u32[]{:S(2)}, u32[]{:S(2)}) %collective-permute-start.8) | collective-permute-done | bytes 655392 | tf_op jit(solution)/shard_map/ppermute | solution.py:47
  42.1 4.8 %shard_map.95 = bf16[2,3,80,640]{3,2,1,0:T(8,128)(2,1)} custom-call(bf16[2,256,640]{2,1,0:T(8,128)(2,1)} %copy-done, bf16[2,256,640]{2,1,0:T(8,128)(2,1)} %copy-done.2, bf16[2,256,640]{2,1,0:T(8,128)(2,1)} %copy-done.5, bf16[2,256,640]{2,1,0:T(8,128)(2,1)} %collective-permute-done.8.refs_3_.v_near, f32[1024,1]{1,0:T(8,128)} %copy.10.refs_4_, ...), custom_call_target="tpu_custom_call" | custom-call | flops 1258291200 | bytes 2621440 | tf_op jit(solution)/shard_map/pallas_call | solution.py:128
  46.9 1.9 collective-permute-start.14
  48.9 1.9 %collective-permute-start.15 = (bf16[2,256,640]{2,1,0:T(8,128)(2,1)}, bf16[2,256,640]{2,1,0:T(8,128)(2,1)}, u32[]{:S(2)}, u32[]{:S(2)}) collective-permute-start(bf16[2,256,640]{2,1,0:T(8,128)(2,1)} %copy-done.2), channel_id=1, source_target_pairs={{4,12},{5,13},{6,14},{7,15},{12,20},{13,21},{14,22},{15,23},{20,28... | collective-permute-start | bytes 1966088 | tf_op jit(solution)/shard_map/ppermute | solution.py:47
  50.8 1.3 collective-permute-start.2
  52.1 5.1 %shard_map.94 = f32[2,3,80,640]{3,2,1,0:T(8,128)} custom-call(bf16[2,256,640]{2,1,0:T(8,128)(2,1)} %copy-done, bf16[2,256,640]{2,1,0:T(8,128)(2,1)} %copy-done.2, bf16[2,256,640]{2,1,0:T(8,128)(2,1)} %copy-done.5, bf16[2,256,640]{2,1,0:T(8,128)(2,1)} %collective-permute-done.8.refs_3_.v_near, f32[1024,1]{1,0:T(8,128)} %copy.10.refs_4_, ...), custom_call_target="tpu_custom_call" | custom-call | flops 1258291200 | bytes 2621440 | tf_op jit(solution)/shard_map/pallas_call | solution.py:128
  57.2 1.4 convert_add_fusion
  58.7 15.5 %collective-permute-done.14 = bf16[2,256,640]{2,1,0:T(8,128)(2,1)} collective-permute-done((bf16[2,256,640]{2,1,0:T(8,128)(2,1)}, bf16[2,256,640]{2,1,0:T(8,128)(2,1)}, u32[]{:S(2)}, u32[]{:S(2)}) %collective-permute-start.14) | collective-permute-done | bytes 655392 | tf_op jit(solution)/shard_map/ppermute | solution.py:47
  74.1 14.0 %collective-permute-done.15 = bf16[2,256,640]{2,1,0:T(8,128)(2,1)} collective-permute-done((bf16[2,256,640]{2,1,0:T(8,128)(2,1)}, bf16[2,256,640]{2,1,0:T(8,128)(2,1)}, u32[]{:S(2)}, u32[]{:S(2)}) %collective-permute-start.15) | collective-permute-done | bytes 655392 | tf_op jit(solution)/shard_map/ppermute | solution.py:47
  88.2 0.9 bitcast_convert_fusion
  89.0 1.3 collective-permute-start.16
  90.3 1.3 collective-permute-start.17
  91.6 1.9 %collective-permute-start.18 = (bf16[3,80,640]{2,1,0:T(8,128)(2,1)}, bf16[3,80,640]{2,1,0:T(8,128)(2,1)}, u32[]{:S(2)}, u32[]{:S(2)}) collective-permute-start(bf16[3,80,640]{2,1,0:T(8,128)(2,1)} %get-tuple-element.30), channel_id=1, source_target_pairs={{0,8},{2,10},{4,12},{6,14},{8,0},{10,2},{12,4},{14,6},{17,25},{19,... | collective-permute-start | bytes 921608 | tf_op jit(solution)/shard_map/ppermute | solution.py:47
  93.6 1.2 broadcast_select_fusion
  94.9 2.9 %collective-permute-done.16 = bf16[3,80,640]{2,1,0:T(8,128)(2,1)S(1)} collective-permute-done((bf16[3,80,640]{2,1,0:T(8,128)(2,1)}, bf16[3,80,640]{2,1,0:T(8,128)(2,1)S(1)}, u32[]{:S(2)}, u32[]{:S(2)}) %collective-permute-start.16) | collective-permute-done | bytes 307232 | tf_op jit(solution)/shard_map/ppermute | solution.py:47
  97.8 8.3 %collective-permute-done.17 = bf16[3,80,640]{2,1,0:T(8,128)(2,1)} collective-permute-done((bf16[3,80,640]{2,1,0:T(8,128)(2,1)}, bf16[3,80,640]{2,1,0:T(8,128)(2,1)}, u32[]{:S(2)}, u32[]{:S(2)}) %collective-permute-start.17) | collective-permute-done | bytes 307232 | tf_op jit(solution)/shard_map/ppermute | solution.py:47
  106.2 1.8 multiply_reduce_fusion.1
  108.0 1.3 multiply_convert_fusion
  109.3 1.4 collective-permute-start.19
  110.8 1.2 broadcast_select_fusion.1
  112.0 3.1 %collective-permute-start.23 = (bf16[3,80,640]{2,1,0:T(8,128)(2,1)S(1)}, bf16[3,80,640]{2,1,0:T(8,128)(2,1)S(1)}, u32[]{:S(2)}, u32[]{:S(2)}) collective-permute-start(bf16[3,80,640]{2,1,0:T(8,128)(2,1)S(1)} %multiply_convert_fusion), channel_id=1, source_target_pairs={{0,8},{2,10},{4,12},{6,14},{8,0},{10,2},{12,4},{14,6},{17,25},{19,... | collective-permute-start | bytes 921608 | tf_op jit(solution)/shard_map/ppermute | solution.py:47
  115.1 2.7 %collective-permute-done.19 = bf16[3,80,640]{2,1,0:T(8,128)(2,1)S(1)} collective-permute-done((bf16[3,80,640]{2,1,0:T(8,128)(2,1)S(1)}, bf16[3,80,640]{2,1,0:T(8,128)(2,1)S(1)}, u32[]{:S(2)}, u32[]{:S(2)}) %collective-permute-start.19) | collective-permute-done | bytes 307232 | tf_op jit(solution)/shard_map/ppermute | solution.py:47
  117.8 0.7 collective-permute-start.24
  118.6 7.4 %collective-permute-start = (bf16[256,640]{1,0:T(8,128)(2,1)S(1)}, bf16[256,640]{1,0:T(8,128)(2,1)S(1)}, u32[]{:S(2)}, u32[]{:S(2)}) collective-permute-start(bf16[256,640]{1,0:T(8,128)(2,1)S(1)} %get-tuple-element.36), channel_id=1, source_target_pairs={{0,1},{1,0},{2,3},{3,2},{4,5},{5,4},{6,7},{7,6},{8,9},{9,8},{10,11... | collective-permute-start | bytes 983048 | tf_op jit(solution)/shard_map/ppermute | solution.py:47
  126.0 0.7 slice.19
  126.7 1.3 collective-permute-start.31
  128.0 0.8 broadcast_select_fusion.3.refs_2_
  128.8 1.9 %collective-permute-start.33 = (f32[3,40,640]{2,1,0:T(8,128)}, f32[3,40,640]{2,1,0:T(8,128)S(1)}, u32[]{:S(2)}, u32[]{:S(2)}) collective-permute-start(f32[3,40,640]{2,1,0:T(8,128)} %slice.19), channel_id=1, source_target_pairs={{0,1},{2,3},{4,5},{6,7},{8,9},{10,11},{12,13},{14,15},{17,16},{19,... | collective-permute-start | bytes 921608 | tf_op jit(solution)/shard_map/ppermute | solution.py:47
  130.7 3.3 %collective-permute-start.20 = (bf16[3,80,640]{2,1,0:T(8,128)(2,1)}, bf16[3,80,640]{2,1,0:T(8,128)(2,1)}, u32[]{:S(2)}, u32[]{:S(2)}) collective-permute-start(bf16[3,80,640]{2,1,0:T(8,128)(2,1)} %broadcast_select_fusion.3.refs_2_), channel_id=1, source_target_pairs={{0,2},{1,3},{2,0},{3,1},{4,6},{5,7},{6,4},{7,5},{8,10},{9,11},{10,... | collective-permute-start | bytes 921608 | tf_op jit(solution)/shard_map/ppermute | solution.py:47
  134.0 1.3 collective-permute-start.30
  135.3 0.8 broadcast_select_fusion.2.refs_6_
  136.2 0.6 reshape.42.refs_10_
  136.7 0.6 pad_add_fusion.where.refs_0_
  137.3 0.9 pad_maximum_fusion.quer_in.refs_1_
  138.2 1.5 collective-permute-start.21
  139.7 11.9 %collective-permute-done.20.refs_3_ = bf16[3,80,640]{2,1,0:T(8,128)(2,1)} collective-permute-done((bf16[3,80,640]{2,1,0:T(8,128)(2,1)}, bf16[3,80,640]{2,1,0:T(8,128)(2,1)}, u32[]{:S(2)}, u32[]{:S(2)}) %collective-permute-start.20) | collective-permute-done | bytes 307232 | tf_op jit(solution)/shard_map/ppermute | solution.py:47
  151.6 1.5 collective-permute-start.27
  153.1 1.1 multiply_reduce_fusion.3
  154.3 11.3 %collective-permute-done.30.k_back = bf16[2,256,640]{2,1,0:T(8,128)(2,1)} collective-permute-done((bf16[2,256,640]{2,1,0:T(8,128)(2,1)S(1)}, bf16[2,256,640]{2,1,0:T(8,128)(2,1)}, u32[]{:S(2)}, u32[]{:S(2)}) %collective-permute-start.30) | collective-permute-done | bytes 655392 | tf_op jit(solution)/shard_map/ppermute | solution.py:47
  165.6 13.9 %attention.1.refs_11_ = f32[512,640]{1,0:T(8,128)} custom-call(s32[3]{0:T(128)} %pad_add_fusion.where.refs_0_, bf16[2,256,640]{2,1,0:T(8,128)(2,1)} %pad_maximum_fusion.quer_in.refs_1_, bf16[2,256,640]{2,1,0:T(8,128)(2,1)} %copy-done, bf16[2,256,640]{2,1,0:T(8,128)(2,1)} %copy-done.2, bf16[2,256,640]{2,1,0:T(8,128)(2,1)} %copy-done.10, ...), custom_call_target="tpu_custom_call" | custom-call | flops 1509949440 | bytes 6553600 | tf_op jit(solution)/shard_map/attention/pallas_call | solution.py:250
  179.5 0.7 copy-done.16
  180.3 0.7 copy-done.18
  181.0 5.3 %query_side.1 = (bf16[256,640]{1,0:T(8,128)(2,1)}, bf16[256,640]{1,0:T(8,128)(2,1)}) custom-call(s32[3]{0:T(128)} %pad_add_fusion.where.refs_0_, bf16[2,256,640]{2,1,0:T(8,128)(2,1)} %pad_maximum_fusion.quer_in.refs_1_, bf16[3,80,640]{2,1,0:T(8,128)(2,1)} %broadcast_select_fusion.3.refs_2_, bf16[3,80,640]{2,1,0:T(8,128)(2,1)} %collective-permute-done.20.refs_3_, ...), custom_call_target="tpu_custom_call" | custom-call | flops 1258291200 | bytes 2457600 | tf_op jit(solution)/shard_map/query_side/pallas_call | solution.py:175
  186.4 1.3 collective-permute-start.32
  187.7 0.8 multiply_multiply_fusion
  188.6 0.6 collective-permute-done.32
  189.2 2.1 %maximum_select_fusion = bf16[256,1280]{1,0:T(8,128)(2,1)} fusion(bf16[256,640]{1,0:T(8,128)(2,1)S(1)} %collective-permute-done.32, bf16[256,640]{1,0:T(8,128)(2,1)} %get-tuple-element.21, pred[]{:T(512)S(6)} %eq.13), kind=kLoop, calls=%fused_computation.4 | loop fusion | flops 2949120 | bytes 1310721 | tf_op jit(solution)/shard_map/jit(_where)/select_n | solution.py:345
  (80 shorter events, 1.5 us)
Async XLA Ops:
  0.6 4.5 %copy-start.11 = (bf16[256,1280]{1,0:T(8,128)(2,1)S(1)}, bf16[256,1280]{1,0:T(8,128)(2,1)}, u32[]{:S(2)}) copy-start(bf16[256,1280]{1,0:T(8,128)(2,1)} %param.9) | copy-start | bytes 1966084
  0.6 5.3 %collective-permute-start.1 = (f32[3,40,640]{2,1,0:T(8,128)}, f32[3,40,640]{2,1,0:T(8,128)}, u32[]{:S(2)}, u32[]{:S(2)}) collective-permute-start(f32[3,40,640]{2,1,0:T(8,128)} %param.11), channel_id=1, source_target_pairs={{1,0},{3,2},{5,4},{7,6},{9,8},{11,10},{13,12},{15,14},{16,17},{18,... | collective-permute-start | bytes 921608 | tf_op jit(solution)/shard_map/ppermute | solution.py:47
  2.1 3.2 %copy-start.15 = (f32[2,256]{1,0:T(2,128)S(1)}, f32[2,256]{1,0:T(2,128)}, u32[]{:S(2)}) copy-start(f32[2,256]{1,0:T(2,128)} %param.10) | copy-start | bytes 6148
  2.1 3.8 %copy-start.4 = (f32[3,40,640]{2,1,0:T(8,128)S(1)}, f32[3,40,640]{2,1,0:T(8,128)}, u32[]{:S(2)}) copy-start(f32[3,40,640]{2,1,0:T(8,128)} %param.11) | copy-start | bytes 921604
  3.3 12.3 %collective-permute-start.3 = (bf16[256,640]{1,0:T(8,128)(2,1)S(1)}, bf16[256,640]{1,0:T(8,128)(2,1)S(1)}, u32[]{:S(2)}, u32[]{:S(2)}) collective-permute-start(bf16[256,640]{1,0:T(8,128)(2,1)S(1)} %get-tuple-element.34), channel_id=1, source_target_pairs={{0,1},{1,0},{2,3},{3,2},{4,5},{5,4},{6,7},{7,6},{8,9},{9,8},{10,11... | collective-permute-start | bytes 983048 | tf_op jit(solution)/shard_map/ppermute | solution.py:47
  5.3 12.7 %collective-permute-start.4 = (bf16[256,640]{1,0:T(8,128)(2,1)S(1)}, bf16[256,640]{1,0:T(8,128)(2,1)S(1)}, u32[]{:S(2)}, u32[]{:S(2)}) collective-permute-start(bf16[256,640]{1,0:T(8,128)(2,1)S(1)} %get-tuple-element.32), channel_id=1, source_target_pairs={{0,1},{1,0},{2,3},{3,2},{4,5},{5,4},{6,7},{7,6},{8,9},{9,8},{10,11... | collective-permute-start | bytes 983048 | tf_op jit(solution)/shard_map/ppermute | solution.py:47
  5.4 4.5 %collective-permute-start.5 = (f32[1,256]{1,0:T(1,128)S(1)}, f32[1,256]{1,0:T(1,128)S(1)}, u32[]{:S(2)}, u32[]{:S(2)}) collective-permute-start(f32[1,256]{1,0:T(1,128)S(1)} %get-tuple-element.38), channel_id=1, source_target_pairs={{0,1},{1,0},{2,3},{3,2},{4,5},{5,4},{6,7},{7,6},{8,9},{9,8},{10,11... | collective-permute-start | bytes 3080 | tf_op jit(solution)/shard_map/ppermute | solution.py:47
  7.7 9.5 %collective-permute-start.9 = (bf16[3,80,640]{2,1,0:T(8,128)(2,1)}, bf16[3,80,640]{2,1,0:T(8,128)(2,1)S(1)}, u32[]{:S(2)}, u32[]{:S(2)}) collective-permute-start(bf16[3,80,640]{2,1,0:T(8,128)(2,1)} %convert_element_type.25), channel_id=1, source_target_pairs={{0,16},{2,18},{4,20},{6,22},{8,24},{10,26},{12,28},{14,30},{17,1},... | collective-permute-start | bytes 921608 | tf_op jit(solution)/shard_map/ppermute | solution.py:47
  9.9 2.5 %collective-permute-start.6 = (f32[2,256]{1,0:T(2,128)S(1)}, f32[2,256]{1,0:T(2,128)S(1)}, u32[]{:S(2)}, u32[]{:S(2)}) collective-permute-start(f32[2,256]{1,0:T(2,128)S(1)} %pad_maximum_fusion.4), channel_id=1, source_target_pairs={{0,2},{1,3},{2,0},{3,1},{4,6},{5,7},{6,4},{7,5},{8,10},{9,11},{10,... | collective-permute-start | bytes 6152 | tf_op jit(solution)/shard_map/ppermute | solution.py:47
  12.4 10.4 %collective-permute-start.10 = (bf16[3,80,640]{2,1,0:T(8,128)(2,1)}, bf16[3,80,640]{2,1,0:T(8,128)(2,1)S(1)}, u32[]{:S(2)}, u32[]{:S(2)}) collective-permute-start(bf16[3,80,640]{2,1,0:T(8,128)(2,1)} %convert_element_type.25), channel_id=1, source_target_pairs={{0,8},{2,10},{4,12},{6,14},{8,0},{10,2},{12,4},{14,6},{17,25},{19,... | collective-permute-start | bytes 921608 | tf_op jit(solution)/shard_map/ppermute | solution.py:47
  15.7 26.4 %copy-start = (bf16[2,256,640]{2,1,0:T(8,128)(2,1)}, bf16[2,256,640]{2,1,0:T(8,128)(2,1)S(1)}, u32[]{:S(2)}) copy-start(bf16[2,256,640]{2,1,0:T(8,128)(2,1)S(1)} %pad_maximum_fusion.1.refs_0_.k_own) | copy-start | bytes 1966084
  17.2 5.6 %collective-permute-start.11 = (bf16[3,80,640]{2,1,0:T(8,128)(2,1)S(1)}, bf16[3,80,640]{2,1,0:T(8,128)(2,1)S(1)}, u32[]{:S(2)}, u32[]{:S(2)}) collective-permute-start(bf16[3,80,640]{2,1,0:T(8,128)(2,1)S(1)} %collective-permute-done.9), channel_id=1, source_target_pairs={{1,9},{3,11},{5,13},{7,15},{9,1},{11,3},{13,5},{15,7},{16,24},{18,... | collective-permute-start | bytes 921608 | tf_op jit(solution)/shard_map/ppermute | solution.py:47
  18.0 24.1 %copy-start.2 = (bf16[2,256,640]{2,1,0:T(8,128)(2,1)}, bf16[2,256,640]{2,1,0:T(8,128)(2,1)S(1)}, u32[]{:S(2)}) copy-start(bf16[2,256,640]{2,1,0:T(8,128)(2,1)S(1)} %pad_maximum_fusion.2.refs_1_.v_own) | copy-start | bytes 1966084
  18.0 9.9 %collective-permute-start.7 = (bf16[2,256,640]{2,1,0:T(8,128)(2,1)S(1)}, bf16[2,256,640]{2,1,0:T(8,128)(2,1)S(1)}, u32[]{:S(2)}, u32[]{:S(2)}) collective-permute-start(bf16[2,256,640]{2,1,0:T(8,128)(2,1)S(1)} %pad_maximum_fusion.1.refs_0_.k_own), channel_id=1, source_target_pairs={{0,2},{1,3},{2,0},{3,1},{4,6},{5,7},{6,4},{7,5},{8,10},{9,11},{10,... | collective-permute-start | bytes 1966088 | tf_op jit(solution)/shard_map/ppermute | solution.py:47
  19.3 22.8 %collective-permute-start.8 = (bf16[2,256,640]{2,1,0:T(8,128)(2,1)S(1)}, bf16[2,256,640]{2,1,0:T(8,128)(2,1)}, u32[]{:S(2)}, u32[]{:S(2)}) collective-permute-start(bf16[2,256,640]{2,1,0:T(8,128)(2,1)S(1)} %pad_maximum_fusion.2.refs_1_.v_own), channel_id=1, source_target_pairs={{0,2},{1,3},{2,0},{3,1},{4,6},{5,7},{6,4},{7,5},{8,10},{9,11},{10,... | collective-permute-start | bytes 1966088 | tf_op jit(solution)/shard_map/ppermute | solution.py:47
  23.8 18.3 %collective-permute-start.12 = (bf16[2,3,80,640]{3,2,1,0:T(8,128)(2,1)}, bf16[2,3,80,640]{3,2,1,0:T(8,128)(2,1)}, u32[]{:S(2)}, u32[]{:S(2)}) collective-permute-start(bf16[2,3,80,640]{3,2,1,0:T(8,128)(2,1)} %pad_maximum_fusion.3.refs_5_), channel_id=1, source_target_pairs={{0,4},{1,5},{2,6},{3,7},{4,0},{5,1},{6,2},{7,3},{8,12},{9,13},{10,... | collective-permute-start | bytes 1843208 | tf_op jit(solution)/shard_map/ppermute | solution.py:47
  27.9 14.2 %copy-start.5 = (bf16[2,256,640]{2,1,0:T(8,128)(2,1)}, bf16[2,256,640]{2,1,0:T(8,128)(2,1)S(1)}, u32[]{:S(2)}) copy-start(bf16[2,256,640]{2,1,0:T(8,128)(2,1)S(1)} %collective-permute-done.7.refs_2_.k_near) | copy-start | bytes 1966084
  46.9 10.3 %collective-permute-start.13 = (bf16[2,3,80,640]{3,2,1,0:T(8,128)(2,1)}, bf16[2,3,80,640]{3,2,1,0:T(8,128)(2,1)S(1)}, u32[]{:S(2)}, u32[]{:S(2)}) collective-permute-start(bf16[2,3,80,640]{3,2,1,0:T(8,128)(2,1)} %shard_map.95), channel_id=1, source_target_pairs={{0,4},{1,5},{2,6},{3,7},{4,0},{5,1},{6,2},{7,3},{8,12},{9,13},{10,... | collective-permute-start | bytes 1843208 | tf_op jit(solution)/shard_map/ppermute | solution.py:47
  46.9 27.2 %collective-permute-start.14 = (bf16[2,256,640]{2,1,0:T(8,128)(2,1)}, bf16[2,256,640]{2,1,0:T(8,128)(2,1)}, u32[]{:S(2)}, u32[]{:S(2)}) collective-permute-start(bf16[2,256,640]{2,1,0:T(8,128)(2,1)} %copy-done), channel_id=1, source_target_pairs={{4,12},{5,13},{6,14},{7,15},{12,20},{13,21},{14,22},{15,23},{20,28... | collective-permute-start | bytes 1966088 | tf_op jit(solution)/shard_map/ppermute | solution.py:47
  48.9 39.3 %collective-permute-start.15 = (bf16[2,256,640]{2,1,0:T(8,128)(2,1)}, bf16[2,256,640]{2,1,0:T(8,128)(2,1)}, u32[]{:S(2)}, u32[]{:S(2)}) collective-permute-start(bf16[2,256,640]{2,1,0:T(8,128)(2,1)} %copy-done.2), channel_id=1, source_target_pairs={{4,12},{5,13},{6,14},{7,15},{12,20},{13,21},{14,22},{15,23},{20,28... | collective-permute-start | bytes 1966088 | tf_op jit(solution)/shard_map/ppermute | solution.py:47
  50.8 44.1 %collective-permute-start.2 = (f32[3,40,640]{2,1,0:T(8,128)}, f32[3,40,640]{2,1,0:T(8,128)S(1)}, u32[]{:S(2)}, u32[]{:S(2)}) collective-permute-start(f32[3,40,640]{2,1,0:T(8,128)} %param.12), channel_id=1, source_target_pairs={{1,0},{3,2},{5,4},{7,6},{9,8},{11,10},{13,12},{15,14},{16,17},{18,... | collective-permute-start | bytes 921608 | tf_op jit(solution)/shard_map/ppermute | solution.py:47
  58.6 35.0 %copy-start.3 = (bf16[2,256,640]{2,1,0:T(8,128)(2,1)S(1)}, bf16[2,256,640]{2,1,0:T(8,128)(2,1)}, u32[]{:S(2)}) copy-start(bf16[2,256,640]{2,1,0:T(8,128)(2,1)} %copy-done.2) | copy-start | bytes 1966084
  89.0 8.8 %collective-permute-start.16 = (bf16[3,80,640]{2,1,0:T(8,128)(2,1)}, bf16[3,80,640]{2,1,0:T(8,128)(2,1)S(1)}, u32[]{:S(2)}, u32[]{:S(2)}) collective-permute-start(bf16[3,80,640]{2,1,0:T(8,128)(2,1)} %get-tuple-element.29), channel_id=1, source_target_pairs={{1,17},{3,19},{5,21},{7,23},{9,25},{11,27},{13,29},{15,31},{16,0},... | collective-permute-start | bytes 921608 | tf_op jit(solution)/shard_map/ppermute | solution.py:47
  90.3 15.8 %collective-permute-start.17 = (bf16[3,80,640]{2,1,0:T(8,128)(2,1)}, bf16[3,80,640]{2,1,0:T(8,128)(2,1)}, u32[]{:S(2)}, u32[]{:S(2)}) collective-permute-start(bf16[3,80,640]{2,1,0:T(8,128)(2,1)} %get-tuple-element.30), channel_id=1, source_target_pairs={{1,25},{3,27},{5,29},{7,31},{9,17},{11,19},{13,21},{15,23},{16,8},... | collective-permute-start | bytes 921608 | tf_op jit(solution)/shard_map/ppermute | solution.py:47
  91.6 14.5 %collective-permute-start.18 = (bf16[3,80,640]{2,1,0:T(8,128)(2,1)}, bf16[3,80,640]{2,1,0:T(8,128)(2,1)}, u32[]{:S(2)}, u32[]{:S(2)}) collective-permute-start(bf16[3,80,640]{2,1,0:T(8,128)(2,1)} %get-tuple-element.30), channel_id=1, source_target_pairs={{0,8},{2,10},{4,12},{6,14},{8,0},{10,2},{12,4},{14,6},{17,25},{19,... | collective-permute-start | bytes 921608 | tf_op jit(solution)/shard_map/ppermute | solution.py:47
  94.8 31.9 %collective-permute-start.29 = (bf16[2,256,640]{2,1,0:T(8,128)(2,1)S(1)}, bf16[2,256,640]{2,1,0:T(8,128)(2,1)S(1)}, u32[]{:S(2)}, u32[]{:S(2)}) collective-permute-start(bf16[2,256,640]{2,1,0:T(8,128)(2,1)S(1)} %broadcast_select_fusion), channel_id=1, source_target_pairs={{0,4},{1,5},{2,6},{3,7},{4,0},{5,1},{6,2},{7,3},{8,12},{9,13},{10,... | collective-permute-start | bytes 1966088 | tf_op jit(solution)/shard_map/ppermute | solution.py:47
  94.9 11.3 %copy-start.7 = (f32[3,40,640]{2,1,0:T(8,128)}, f32[3,40,640]{2,1,0:T(8,128)S(1)}, u32[]{:S(2)}) copy-start(f32[3,40,640]{2,1,0:T(8,128)S(1)} %collective-permute-done.2) | copy-start | bytes 921604
  97.8 8.3 %copy-start.13 = (bf16[3,80,640]{2,1,0:T(8,128)(2,1)}, bf16[3,80,640]{2,1,0:T(8,128)(2,1)S(1)}, u32[]{:S(2)}) copy-start(bf16[3,80,640]{2,1,0:T(8,128)(2,1)S(1)} %collective-permute-done.16) | copy-start | bytes 921604
  106.2 1.8 copy-start.8
  107.9 2.8 %copy-start.1 = (bf16[2,256,640]{2,1,0:T(8,128)(2,1)S(1)}, bf16[2,256,640]{2,1,0:T(8,128)(2,1)}, u32[]{:S(2)}) copy-start(bf16[2,256,640]{2,1,0:T(8,128)(2,1)} %copy-done) | copy-start | bytes 1966084
  109.3 9.2 %copy-start.12 = (bf16[256,1280]{1,0:T(8,128)(2,1)S(1)}, bf16[256,1280]{1,0:T(8,128)(2,1)}, u32[]{:S(2)}) copy-start(bf16[256,1280]{1,0:T(8,128)(2,1)} %param.7) | copy-start | bytes 1966084
  109.3 8.5 %collective-permute-start.19 = (bf16[3,80,640]{2,1,0:T(8,128)(2,1)S(1)}, bf16[3,80,640]{2,1,0:T(8,128)(2,1)S(1)}, u32[]{:S(2)}, u32[]{:S(2)}) collective-permute-start(bf16[3,80,640]{2,1,0:T(8,128)(2,1)S(1)} %multiply_convert_fusion), channel_id=1, source_target_pairs={{0,16},{2,18},{4,20},{6,22},{8,24},{10,26},{12,28},{14,30},{17,1},... | collective-permute-start | bytes 921608 | tf_op jit(solution)/shard_map/ppermute | solution.py:47
  111.9 18.8 %collective-permute-start.28 = (bf16[2,256,640]{2,1,0:T(8,128)(2,1)S(1)}, bf16[2,256,640]{2,1,0:T(8,128)(2,1)S(1)}, u32[]{:S(2)}, u32[]{:S(2)}) collective-permute-start(bf16[2,256,640]{2,1,0:T(8,128)(2,1)S(1)} %broadcast_select_fusion.1), channel_id=1, source_target_pairs={{0,4},{1,5},{2,6},{3,7},{4,0},{5,1},{6,2},{7,3},{8,12},{9,13},{10,... | collective-permute-start | bytes 1966088 | tf_op jit(solution)/shard_map/ppermute | solution.py:47
  112.0 16.8 %collective-permute-start.23 = (bf16[3,80,640]{2,1,0:T(8,128)(2,1)S(1)}, bf16[3,80,640]{2,1,0:T(8,128)(2,1)S(1)}, u32[]{:S(2)}, u32[]{:S(2)}) collective-permute-start(bf16[3,80,640]{2,1,0:T(8,128)(2,1)S(1)} %multiply_convert_fusion), channel_id=1, source_target_pairs={{0,8},{2,10},{4,12},{6,14},{8,0},{10,2},{12,4},{14,6},{17,25},{19,... | collective-permute-start | bytes 921608 | tf_op jit(solution)/shard_map/ppermute | solution.py:47
  117.8 16.2 %collective-permute-start.24 = (bf16[3,80,640]{2,1,0:T(8,128)(2,1)S(1)}, bf16[3,80,640]{2,1,0:T(8,128)(2,1)S(1)}, u32[]{:S(2)}, u32[]{:S(2)}) collective-permute-start(bf16[3,80,640]{2,1,0:T(8,128)(2,1)S(1)} %collective-permute-done.19), channel_id=1, source_target_pairs={{1,9},{3,11},{5,13},{7,15},{9,1},{11,3},{13,5},{15,7},{16,24},{18,... | collective-permute-start | bytes 921608 | tf_op jit(solution)/shard_map/ppermute | solution.py:47
  118.6 17.5 %copy-start.14 = (f32[1280]{0:T(1024)S(1)}, f32[1280]{0:T(1024)}, u32[]{:S(2)}) copy-start(f32[1280]{0:T(1024)} %param.13) | copy-start | bytes 15364
  118.6 17.5 %collective-permute-start = (bf16[256,640]{1,0:T(8,128)(2,1)S(1)}, bf16[256,640]{1,0:T(8,128)(2,1)S(1)}, u32[]{:S(2)}, u32[]{:S(2)}) collective-permute-start(bf16[256,640]{1,0:T(8,128)(2,1)S(1)} %get-tuple-element.36), channel_id=1, source_target_pairs={{0,1},{1,0},{2,3},{3,2},{4,5},{5,4},{6,7},{7,6},{8,9},{9,8},{10,11... | collective-permute-start | bytes 983048 | tf_op jit(solution)/shard_map/ppermute | solution.py:47
  126.7 11.5 %copy-start.9 = (bf16[2,256,640]{2,1,0:T(8,128)(2,1)}, bf16[2,256,640]{2,1,0:T(8,128)(2,1)S(1)}, u32[]{:S(2)}) copy-start(bf16[2,256,640]{2,1,0:T(8,128)(2,1)S(1)} %collective-permute-done.29.v_two) | copy-start | bytes 1966084
  126.7 24.9 %collective-permute-start.31 = (bf16[2,256,640]{2,1,0:T(8,128)(2,1)S(1)}, bf16[2,256,640]{2,1,0:T(8,128)(2,1)}, u32[]{:S(2)}, u32[]{:S(2)}) collective-permute-start(bf16[2,256,640]{2,1,0:T(8,128)(2,1)S(1)} %collective-permute-done.29.v_two), channel_id=1, source_target_pairs={{2,0},{3,1},{6,4},{7,5},{10,8},{11,9},{14,12},{15,13},{18,16},{19,... | collective-permute-start | bytes 1966088 | tf_op jit(solution)/shard_map/ppermute | solution.py:47
  128.8 9.4 %collective-permute-start.33 = (f32[3,40,640]{2,1,0:T(8,128)}, f32[3,40,640]{2,1,0:T(8,128)S(1)}, u32[]{:S(2)}, u32[]{:S(2)}) collective-permute-start(f32[3,40,640]{2,1,0:T(8,128)} %slice.19), channel_id=1, source_target_pairs={{0,1},{2,3},{4,5},{6,7},{8,9},{10,11},{12,13},{14,15},{17,16},{19,... | collective-permute-start | bytes 921608 | tf_op jit(solution)/shard_map/ppermute | solution.py:47
  130.7 23.5 %copy-start.10 = (bf16[2,256,640]{2,1,0:T(8,128)(2,1)}, bf16[2,256,640]{2,1,0:T(8,128)(2,1)S(1)}, u32[]{:S(2)}) copy-start(bf16[2,256,640]{2,1,0:T(8,128)(2,1)S(1)} %collective-permute-done.28.k_two) | copy-start | bytes 1966084
  130.7 20.8 %collective-permute-start.20 = (bf16[3,80,640]{2,1,0:T(8,128)(2,1)}, bf16[3,80,640]{2,1,0:T(8,128)(2,1)}, u32[]{:S(2)}, u32[]{:S(2)}) collective-permute-start(bf16[3,80,640]{2,1,0:T(8,128)(2,1)} %broadcast_select_fusion.3.refs_2_), channel_id=1, source_target_pairs={{0,2},{1,3},{2,0},{3,1},{4,6},{5,7},{6,4},{7,5},{8,10},{9,11},{10,... | collective-permute-start | bytes 921608 | tf_op jit(solution)/shard_map/ppermute | solution.py:47
  134.0 31.6 %collective-permute-start.30 = (bf16[2,256,640]{2,1,0:T(8,128)(2,1)S(1)}, bf16[2,256,640]{2,1,0:T(8,128)(2,1)}, u32[]{:S(2)}, u32[]{:S(2)}) collective-permute-start(bf16[2,256,640]{2,1,0:T(8,128)(2,1)S(1)} %collective-permute-done.28.k_two), channel_id=1, source_target_pairs={{2,0},{3,1},{6,4},{7,5},{10,8},{11,9},{14,12},{15,13},{18,16},{19,... | collective-permute-start | bytes 1966088 | tf_op jit(solution)/shard_map/ppermute | solution.py:47
  136.1 15.5 %collective-permute-start.25 = (bf16[3,80,640]{2,1,0:T(8,128)(2,1)}, bf16[3,80,640]{2,1,0:T(8,128)(2,1)}, u32[]{:S(2)}, u32[]{:S(2)}) collective-permute-start(bf16[3,80,640]{2,1,0:T(8,128)(2,1)} %broadcast_select_fusion.2.refs_6_), channel_id=1, source_target_pairs={{0,4},{1,5},{2,6},{3,7},{4,0},{5,1},{6,2},{7,3},{8,12},{9,13},{10,... | collective-permute-start | bytes 921608 | tf_op jit(solution)/shard_map/ppermute | solution.py:47
  138.2 41.2 %collective-permute-start.21 = (bf16[3,80,640]{2,1,0:T(8,128)(2,1)}, bf16[3,80,640]{2,1,0:T(8,128)(2,1)S(1)}, u32[]{:S(2)}, u32[]{:S(2)}) collective-permute-start(bf16[3,80,640]{2,1,0:T(8,128)(2,1)} %broadcast_select_fusion.3.refs_2_), channel_id=1, source_target_pairs={{0,4},{1,5},{2,6},{3,7},{4,0},{5,1},{6,2},{7,3},{8,12},{9,13},{10,... | collective-permute-start | bytes 921608 | tf_op jit(solution)/shard_map/ppermute | solution.py:47
  151.6 27.9 %collective-permute-start.26 = (bf16[3,80,640]{2,1,0:T(8,128)(2,1)}, bf16[3,80,640]{2,1,0:T(8,128)(2,1)S(1)}, u32[]{:S(2)}, u32[]{:S(2)}) collective-permute-start(bf16[3,80,640]{2,1,0:T(8,128)(2,1)} %broadcast_select_fusion.2.refs_6_), channel_id=1, source_target_pairs={{0,2},{1,3},{2,0},{3,1},{4,6},{5,7},{6,4},{7,5},{8,10},{9,11},{10,... | collective-permute-start | bytes 921608 | tf_op jit(solution)/shard_map/ppermute | solution.py:47
  151.6 27.9 %collective-permute-start.22 = (bf16[3,80,640]{2,1,0:T(8,128)(2,1)}, bf16[3,80,640]{2,1,0:T(8,128)(2,1)}, u32[]{:S(2)}, u32[]{:S(2)}) collective-permute-start(bf16[3,80,640]{2,1,0:T(8,128)(2,1)} %collective-permute-done.20.refs_3_), channel_id=1, source_target_pairs={{0,4},{1,5},{2,6},{3,7},{4,0},{5,1},{6,2},{7,3},{8,12},{9,13},{10,... | collective-permute-start | bytes 921608 | tf_op jit(solution)/shard_map/ppermute | solution.py:47
  151.6 27.9 %collective-permute-start.27 = (bf16[3,80,640]{2,1,0:T(8,128)(2,1)}, bf16[3,80,640]{2,1,0:T(8,128)(2,1)S(1)}, u32[]{:S(2)}, u32[]{:S(2)}) collective-permute-start(bf16[3,80,640]{2,1,0:T(8,128)(2,1)} %collective-permute-done.25.refs_7_), channel_id=1, source_target_pairs={{0,2},{1,3},{2,0},{3,1},{4,6},{5,7},{6,4},{7,5},{8,10},{9,11},{10,... | collective-permute-start | bytes 921608 | tf_op jit(solution)/shard_map/ppermute | solution.py:47
  154.3 33.5 %copy-start.6 = (f32[3,40,640]{2,1,0:T(8,128)}, f32[3,40,640]{2,1,0:T(8,128)S(1)}, u32[]{:S(2)}) copy-start(f32[3,40,640]{2,1,0:T(8,128)S(1)} %get-tuple-element.27) | copy-start | bytes 921604
  179.5 0.7 copy-start.16
  179.5 0.8 copy-start.17
  180.3 0.7 copy-start.18
  186.4 2.8 %collective-permute-start.32 = (bf16[256,640]{1,0:T(8,128)(2,1)}, bf16[256,640]{1,0:T(8,128)(2,1)S(1)}, u32[]{:S(2)}, u32[]{:S(2)}) collective-permute-start(bf16[256,640]{1,0:T(8,128)(2,1)} %get-tuple-element.22), channel_id=1, source_target_pairs={{0,1},{1,0},{2,3},{3,2},{4,5},{5,4},{6,7},{7,6},{8,9},{9,8},{10,11... | collective-permute-start | bytes 983048 | tf_op jit(solution)/shard_map/ppermute | solution.py:47
where the time goes:
time: 192 us; the launch traced here: 191 us
  waiting for transfers between devices  90.3 us (47%)
  starting transfers between devices  47.4 us (25%)
  Pallas kernels  29.1 us (15%)
  other arithmetic  15.9 us (8%)
  local copies, waits for them, and re-layouts  7.32 us (4%)
    ppermute x34, waiting for transfers between devices, send(): return lax.ppermute(array, 'seq', route)  90.3 us
    ppermute x34, starting transfers between devices, send(): return lax.ppermute(array, 'seq', route)  47.4 us
    pallas_call x1, Pallas kernels, attention(): pl.pallas_call(att_kernel, out_shape=jax.ShapeDtypeStruct((span, width),...  13.9 us
    pallas_call x2, Pallas kernels, key_side(): pl.pallas_call(lambda *refs: key_kernel(grad_scale, *refs), out_shape=jax...  9.95 us
    pallas_call x1, Pallas kernels, query_side(): pl.pallas_call(lambda *refs: query_kernel(count, *refs), out_shape=[jax.S...  5.34 us
  transfers between devices with their start and end apart: 34, of which 13 were waited for; matrix products, arithmetic and copies ran while one was open for 10% of the time, Pallas kernels for 10%

commit v1 on v0

--- a/solution.py
+++ b/solution.py
@@ -33,10 +33,8 @@
         self.cross_out = [(dev, (dev + shift) % count) for dev in home]
         self.home_swap = [[(dev, dev ^ (8 * k)) for dev in home] for k in range(half)]
         self.away_swap = [[(dev, dev ^ (8 * k)) for dev in away] for k in range(half)]
-        self.cross_back = [
-            [(dev, ((dev ^ (8 * k)) + shift) % count) for dev in away] for k in range(half)
-        ]
-        self.z_up = [(dev, dev + 8) for dev in range(count - 8) if dev % 8 >= 4]
+        self.cross_back = [(dev, (dev + shift) % count) for dev in away]
+        self.z_up = [(dev, dev + 8) for dev in range(count - 8) if dev % 8 < 4]
         self.back_x = [(dev, dev - 2) for dev in range(count) if dev % 4 >= 2]
 
     def is_home(self, dev):
@@ -69,13 +67,20 @@
 
 
 def reduce_z(sums, routes):
-    total = sums[0]
-    for k, part in enumerate(sums):
-        sent = part.astype(BF16)
-        total = total + send(sent, routes.cross_back[k]).astype(F32)
-        if k > 0:
-            total = total + send(sent, routes.home_swap[k]).astype(F32)
-    return total
+    away, home = sums, sums
+    for bit in reversed(routes.bits):
+        half = len(away) // 2
+        sent = [part.astype(BF16) for part in away[half:]]
+        arrived = [send(part, routes.away_swap[bit]) for part in sent]
+        away = [low + part.astype(F32) for low, part in zip(away[:half], arrived)]
+    crossed = away[0].astype(BF16)
+    home, crossed = lax.optimization_barrier((home, crossed))
+    crossed = send(crossed, routes.cross_back)
+    for bit in reversed(routes.bits):
+        half = len(home) // 2
+        arrived = [send(part.astype(BF16), routes.home_swap[bit]) for part in home[half:]]
+        home = [low + part.astype(F32) for low, part in zip(home[:half], arrived)]
+    return home[0] + crossed.astype(F32)
 
 
 def nt_dot(left, right):
@@ -90,9 +95,13 @@
     return pl.BlockSpec(memory_space=pltpu.VMEM)
 
 
-def key_kernel(grad_scale, k_own, v_own, k_near, v_near, rates, units, out, keys, ograd, pair, down):
+def key_kernel(grad_scale, *refs):
+    k_own, v_own, k_near, v_near, rates = refs[:5]
+    units = refs[5:-5]
+    out, keys, ograd, pair, down = refs[-5:]
     tokens = k_own.shape[1]
-    parts, _, step, _ = units.shape
+    parts = len(units)
+    step = units[0].shape[1]
     rows = parts * step
     for idx, (k_ref, v_ref) in enumerate(((k_own, v_own), (k_near, v_near))):
         for side in range(2):
@@ -101,9 +110,9 @@
             rate = rates[at : at + tokens, :] * (-grad_scale)
             ograd[at : at + tokens, :] = (rate * v_ref[side].astype(F32)).astype(BF16)
     for idx in range(parts):
-        pair[idx * step : (idx + 1) * step, :] = units[idx, 0]
-        pair[rows + idx * step : rows + (idx + 1) * step, :] = units[idx, 1]
-        down[idx * step : (idx + 1) * step, :] = units[idx, 2]
+        pair[idx * step : (idx + 1) * step, :] = units[idx][0]
+        pair[rows + idx * step : rows + (idx + 1) * step, :] = units[idx][1]
+        down[idx * step : (idx + 1) * step, :] = units[idx][2]
     both = nt_dot(pair[...], keys[...])
     gate, up = both[:rows], both[rows:]
     hidden_grad = nt_dot(down[...], ograd[...])
@@ -123,12 +132,13 @@
 
 def key_side(grad_scale, k_own, v_own, k_near, v_near, rates, units, kind):
     _, tokens, width = k_own.shape
-    parts, _, step, _ = units.shape
+    parts = len(units)
+    step = units[0].shape[1]
     rows = parts * step
     return pl.pallas_call(
         lambda *refs: key_kernel(grad_scale, *refs),
-        out_shape=jax.ShapeDtypeStruct(units.shape, kind),
-        in_specs=[vmem()] * 6,
+        out_shape=jax.ShapeDtypeStruct((parts, 3, step, width), kind),
+        in_specs=[vmem()] * (5 + parts),
         out_specs=vmem(),
         scratch_shapes=[
             pltpu.VMEM((4 * tokens, width), BF16),
@@ -141,14 +151,14 @@
             bytes_accessed=16 * tokens * width,
             transcendentals=0,
         ),
-    )(k_own, v_own, k_near, v_near, rates, units)
+    )(k_own, v_own, k_near, v_near, rates, *units)
 
 
 def query_kernel(count, *refs):
     where, quer_in = refs[:2]
     pieces = refs[2 : 2 + count]
-    gain, att, own, other = refs[2 + count : 6 + count]
-    quer, weights, result = refs[6 + count :]
+    gain, att_a, att_b, own, other = refs[2 + count : 7 + count]
+    quer, weights, result = refs[7 + count :]
     tokens = quer_in.shape[1]
     rows = pieces[0].shape[1]
     mine = pl.multiple_of(where[0] * tokens, tokens)
@@ -162,12 +172,15 @@
     hidden = (gate * jax.nn.sigmoid(gate) * up).astype(BF16)
     out = nn_dot(hidden, weights[2])
     scale = lax.rsqrt(jnp.mean(out * out, axis=-1, keepdims=True) + EPS)
-    result[...] = out * scale * gain[...] + att[...]
+    normed = out * scale * gain[...]
+    split = att_a.shape[1]
+    result[:, :split] = normed[:, :split] + att_a[...]
+    result[:, split:] = normed[:, split:] + att_b[...]
     own[...] = result[pl.ds(mine, tokens), :].astype(BF16)
     other[...] = result[pl.ds(theirs, tokens), :].astype(BF16)
 
 
-def query_side(where, quer_in, pieces, gain, att):
+def query_side(where, quer_in, pieces, gain, atts):
     _, tokens, width = quer_in.shape
     count = len(pieces)
     rows = pieces[0].shape[1]
@@ -175,7 +188,7 @@
     return pl.pallas_call(
         lambda *refs: query_kernel(count, *refs),
         out_shape=[jax.ShapeDtypeStruct((tokens, width), BF16)] * 2,
-        in_specs=[pl.BlockSpec(memory_space=pltpu.SMEM)] + [vmem()] * (3 + count),
+        in_specs=[pl.BlockSpec(memory_space=pltpu.SMEM)] + [vmem()] * (4 + count),
         out_specs=[vmem()] * 2,
         scratch_shapes=[
             pltpu.VMEM((2 * tokens, width), BF16),
@@ -186,85 +199,94 @@
             flops=6 * total, bytes_accessed=6 * count * rows * width, transcendentals=0
         ),
         name="query_side",
-    )(where, quer_in, *pieces, gain, att)
-
-
-def att_kernel(where, quer_in, k_own, v_own, k_two, v_two, k_near, v_near, k_back, v_back, out,
+    )(where, quer_in, *pieces, gain, *atts)
+
+
+def att_kernel(low, where, quer_in, k_own, v_own, k_near, v_near, two, back, out,
                quer, keys, vals, bias):
     tokens = quer_in.shape[1]
     span = 2 * tokens
-    tile = 128
-    reach = WINDOW + tile
+    reach = WINDOW + span
+    wide = out.shape[1]
+    cols = slice(low, low + wide)
     core, odd, chip = where[0], where[1], where[2]
     mine = core * tokens
     theirs = (1 - core) * tokens
 
-    def put(dest, base, pair):
-        dest[pl.ds(pl.multiple_of(base + mine, tokens), tokens), :] = pair[0]
-        dest[pl.ds(pl.multiple_of(base + theirs, tokens), tokens), :] = pair[1]
-
-    put(quer, 0, quer_in)
-    for dest, own, two, near, back in (
-        (keys, k_own, k_two, k_near, k_back),
-        (vals, v_own, v_two, v_near, v_back),
-    ):
-        put(dest, 2 * span, own)
-        put(dest, 0, two)
+    def put(dest, base, first, second):
+        dest[pl.ds(pl.multiple_of(base + mine, tokens), tokens), :] = first
+        dest[pl.ds(pl.multiple_of(base + theirs, tokens), tokens), :] = second
+
+    put(quer, 0, quer_in[0, :, cols], quer_in[1, :, cols])
+    for idx, (dest, own, near) in enumerate(((keys, k_own, k_near), (vals, v_own, v_near))):
+        put(dest, 2 * span, own[0, :, cols], own[1, :, cols])
+        put(dest, 0, two[2 * idx], two[2 * idx + 1])
 
         @pl.when(odd == 1)
         def _():
-            put(dest, span, near)
+            put(dest, span, near[0, :, cols], near[1, :, cols])
 
         @pl.when(odd == 0)
         def _():
-            put(dest, span, back)
+            put(dest, span, back[2 * idx], back[2 * idx + 1])
 
     scale = 1.0 / math.sqrt(ATT_DIM)
-    row = lax.broadcasted_iota(jnp.int32, (tile, reach), 0)
-    col = lax.broadcasted_iota(jnp.int32, (tile, reach), 1)
-
-    def one_tile(idx, carry):
-        first = pl.multiple_of(idx * tile, tile)
-        position = chip * span - WINDOW + first + col
-        seen = (col > row) & (col <= row + WINDOW) & (position >= 0)
-        bias[...] = jnp.where(seen, 0.0, MASKED)
-        for head in range(quer.shape[1] // ATT_DIM):
-            cols = slice(head * ATT_DIM, (head + 1) * ATT_DIM)
-            scores = nt_dot(quer[pl.ds(first, tile), cols], keys[pl.ds(first, reach), cols])
-            scores = scores * scale + bias[...]
-            top = jnp.max(scores, axis=-1, keepdims=True)
-            probs = jnp.exp(scores - top)
-            norm = jnp.sum(probs, axis=-1, keepdims=True)
-            att = nn_dot(probs.astype(BF16), vals[pl.ds(first, reach), cols]) / norm
-            att = att * lax.rsqrt(jnp.mean(att * att, axis=-1, keepdims=True) + EPS)
-            out[pl.ds(first, tile), cols] = att
-        return carry
-
-    lax.fori_loop(0, span // tile, one_tile, 0)
-
-
-def attention(where, *blocks):
-    _, tokens, width = blocks[0].shape
+    row = lax.broadcasted_iota(jnp.int32, (span, reach), 0)
+    col = lax.broadcasted_iota(jnp.int32, (span, reach), 1)
+    seen = (col > row) & (col <= row + WINDOW) & (chip * span - WINDOW + col >= 0)
+    bias[...] = jnp.where(seen, 0.0, MASKED)
+    for head in range(wide // ATT_DIM):
+        at = slice(head * ATT_DIM, (head + 1) * ATT_DIM)
+        scores = nt_dot(quer[:, at], keys[:, at]) + bias[...]
+        top = jnp.max(scores, axis=-1, keepdims=True)
+        probs = jnp.exp((scores - top) * scale)
+        norm = jnp.sum(probs, axis=-1, keepdims=True)
+        att = nn_dot(probs.astype(BF16), vals[:, at]) / norm
+        out[:, at] = att * lax.rsqrt(jnp.mean(att * att, axis=-1, keepdims=True) + EPS)
+
+
+def attention(where, quer_in, k_own, v_own, k_near, v_near, two, back, low):
+    _, tokens, _ = quer_in.shape
+    wide = two.shape[2]
     span = 2 * tokens
+    reach = WINDOW + span
     assert WINDOW == 2 * span
     return pl.pallas_call(
-        att_kernel,
-        out_shape=jax.ShapeDtypeStruct((span, width), F32),
-        in_specs=[pl.BlockSpec(memory_space=pltpu.SMEM)] + [vmem()] * len(blocks),
+        lambda *refs: att_kernel(low, *refs),
+        out_shape=jax.ShapeDtypeStruct((span, wide), F32),
+        in_specs=[pl.BlockSpec(memory_space=pltpu.SMEM)] + [vmem()] * 7,
         out_specs=vmem(),
         scratch_shapes=[
-            pltpu.VMEM((span, width), BF16),
-            pltpu.VMEM((3 * span, width), BF16),
-            pltpu.VMEM((3 * span, width), BF16),
-            pltpu.VMEM((128, WINDOW + 128), F32),
+            pltpu.VMEM((span, wide), BF16),
+            pltpu.VMEM((reach, wide), BF16),
+            pltpu.VMEM((reach, wide), BF16),
+            pltpu.VMEM((span, reach), F32),
         ],
         cost_estimate=pl.CostEstimate(
-            flops=4 * span * (WINDOW + 128) * width,
-            bytes_accessed=40 * tokens * width,
-            transcendentals=span * WINDOW * width // ATT_DIM,
+            flops=4 * span * reach * wide,
+            bytes_accessed=40 * tokens * wide,
+            transcendentals=span * reach * wide // ATT_DIM,
         ),
-        name="attention",
-    )(where, *blocks)
+    )(where, quer_in, k_own, v_own, k_near, v_near, two, back)
+
+
+def join_kernel(where, own, arrived, out):
+    width = own.shape[1]
+    mine = pl.multiple_of(where[0] * width, ATT_DIM)
+    theirs = pl.multiple_of((1 - where[0]) * width, ATT_DIM)
+    out[:, pl.ds(mine, width)] = own[...]
+    out[:, pl.ds(theirs, width)] = arrived[...]
+
+
+def join(where, own, arrived):
+    tokens, width = own.shape
+    return pl.pallas_call(
+        join_kernel,
+        out_shape=jax.ShapeDtypeStruct((tokens, 2 * width), own.dtype),
+        in_specs=[pl.BlockSpec(memory_space=pltpu.SMEM), vmem(), vmem()],
+        out_specs=vmem(),
+        name="join",
+    )(where, own, arrived)
 
 
 def updated(weights, momentum, grads):
@@ -310,29 +332,35 @@
 
     k_near = send(k_own, routes.x_swap)
     v_near = send(v_own, routes.x_swap)
+    cut = 3 * ATT_DIM
+    early = jnp.concatenate([k_own[:, :, :cut], v_own[:, :, :cut]], axis=0)
+    late = jnp.concatenate([k_own[:, :, cut:], v_own[:, :, cut:]], axis=0)
     unit = pair_weights.astype(BF16)
     units = gather_z(unit, routes, is_home)
-    own_units = jnp.stack(units)
-    side_units = send(own_units, routes.y_swap)
-    k_late, v_late, _ = lax.optimization_barrier((k_own, v_own, own_units))
-    k_up = send(k_late, routes.z_up)
-    v_up = send(v_late, routes.z_up)
+    side_units = [send(part, routes.y_swap) for part in units]
     grad_scale = 1.0 / math.sqrt(local_tokens * count)
     tokens_in = (k_own, v_own, k_near, v_near, rates)
+
+    upper = chip // 2 % 2 == 1
+    early_y = send(early, routes.y_swap)
+    early_z = send(early_y, routes.z_up)
+    early_two = jnp.where(upper, early_y, early_z)
+    early_back = send(early_two, routes.back_x)
+    late, _ = lax.optimization_barrier((late, side_units))
+    late_y = send(late, routes.y_swap)
+    late_z = send(late_y, routes.z_up)
+    late_two = jnp.where(upper, late_y, late_z)
+    late_back = send(late_two, routes.back_x)
+
     side_grads = key_side(grad_scale, *tokens_in, side_units, BF16)
     side_in = send(side_grads, routes.y_swap)
-    own_grads = key_side(grad_scale, *tokens_in, own_units, F32)
+    own_grads = key_side(grad_scale, *tokens_in, units, F32)
     sums = own_grads + side_in.astype(F32)
-    sums, k_up, v_up = lax.optimization_barrier((sums, k_up, v_up))
     total = reduce_z([sums[k] for k in range(len(units))], routes)
     pair_momentum = jnp.concatenate([momentum, send(momentum, routes.pair_in)], axis=1)
-
-    upper = chip // 2 % 2 == 1
-    k_two = send(jnp.where(upper, k_up, k_own), routes.y_swap)
-    v_two = send(jnp.where(upper, v_up, v_own), routes.y_swap)
-    k_back = send(k_two, routes.back_x)
-    v_back = send(v_two, routes.back_x)
-    att = attention(where, q_own, k_own, v_own, k_two, v_two, k_near, v_near, k_back, v_back)
+    att_in = (where, q_own, k_own, v_own, k_near, v_near)
+    early_att = attention(*att_in, early_two, early_back, 0)
+    late_att = attention(*att_in, late_two, late_back, cut)
 
     pair_new, _ = updated(pair_weights, pair_momentum, total)
     applied = gather_plane(gather_z(pair_new.astype(BF16), routes, is_home), routes)
@@ -340,13 +368,9 @@
     grads = jnp.where(is_home, total[:, :owned], partner_grads)
     new_weights, new_momentum = updated(fast_weights, momentum, grads)
     gain = lax.dynamic_slice_in_dim(out_gain, core * width, width, 0).reshape(1, width)
-    own, other = query_side(where, q_own, applied, gain, att)
+    own, other = query_side(where, q_own, applied, gain, (early_att, late_att))
     arrived = send(other, routes.partner)
-    layer_out = jnp.where(
-        core == 0,
-        jnp.concatenate([own, arrived], axis=1),
-        jnp.concatenate([arrived, own], axis=1),
-    )
+    layer_out = join(where, own, arrived)
     return (layer_out, new_weights, new_momentum)
 
 

time: 192 us -> 182 us (0.948)
  the two profiles are of different devices: /device:TPU:21 before, /device:TPU:25 now
where the time goes in v1:
time: 182 us
  starting transfers between devices  75.5 us (41%)
  waiting for transfers between devices  51.3 us (28%)
  Pallas kernels  32 us (18%)
  other arithmetic  12.4 us (7%)
  local copies, waits for them, and re-layouts  9.2 us (5%)
    ppermute x35, starting transfers between devices, send(): return lax.ppermute(array, 'seq', route)  75.5 us
    ppermute x35, waiting for transfers between devices, send(): return lax.ppermute(array, 'seq', route)  51.3 us
    pallas_call x2, Pallas kernels, attention(): pl.pallas_call(lambda *refs: att_kernel(low, *refs), out_shape=jax.ShapeD...  14.8 us
    pallas_call x2, Pallas kernels, key_side(): pl.pallas_call(lambda *refs: key_kernel(grad_scale, *refs), out_shape=jax...  9.87 us
    pallas_call x1, Pallas kernels, query_side(): pl.pallas_call(lambda *refs: query_kernel(count, *refs), out_shape=[jax.S...  5.3 us
  transfers between devices with their start and end apart: 35, of which 11 were waited for; matrix products, arithmetic and copies ran while one was open for 10% of the time, Pallas kernels for 11%

profile of v1, /device:TPU:25, one launch (start us, length us, event | category | flops | bytes accessed | tf_op | source)
XLA Modules:
  0.0 181.5 jit_solution(11987789438971651332)
XLA Ops:
  0.7 1.2 dynamic-slice_bitcast_fusion.1
  1.9 0.7 collective-permute-start.3
  2.6 1.3 collective-permute-start.1
  4.0 1.2 collective-permute-start.4
  5.4 0.8 collective-permute-done.1
  6.1 0.8 convert_element_type.27
  6.9 2.3 %collective-permute-start.9 = (bf16[3,80,640]{2,1,0:T(8,128)(2,1)}, bf16[3,80,640]{2,1,0:T(8,128)(2,1)}, u32[]{:S(2)}, u32[]{:S(2)}) collective-permute-start(bf16[3,80,640]{2,1,0:T(8,128)(2,1)} %convert_element_type.27), channel_id=1, source_target_pairs={{0,16},{2,18},{4,20},{6,22},{8,24},{10,26},{12,28},{14,30},{17,1},... | collective-permute-start | bytes 921608 | tf_op jit(solution)/shard_map/ppermute | solution.py:45
  9.2 1.3 collective-permute-start.6
  10.5 1.2 collective-permute-done.6
  11.8 1.9 %collective-permute-start.10 = (bf16[3,80,640]{2,1,0:T(8,128)(2,1)}, bf16[3,80,640]{2,1,0:T(8,128)(2,1)S(1)}, u32[]{:S(2)}, u32[]{:S(2)}) collective-permute-start(bf16[3,80,640]{2,1,0:T(8,128)(2,1)} %convert_element_type.27), channel_id=1, source_target_pairs={{0,8},{2,10},{4,12},{6,14},{8,0},{10,2},{12,4},{14,6},{17,25},{19,... | collective-permute-start | bytes 921608 | tf_op jit(solution)/shard_map/ppermute | solution.py:45
  13.8 0.7 collective-permute-start.11
  14.6 1.4 collective-permute-start.7
  16.2 0.8 broadcast_select_fusion.5.refs_5_
  16.9 1.4 collective-permute-start.12
  18.3 4.3 %collective-permute-done.10 = bf16[3,80,640]{2,1,0:T(8,128)(2,1)S(1)} collective-permute-done((bf16[3,80,640]{2,1,0:T(8,128)(2,1)}, bf16[3,80,640]{2,1,0:T(8,128)(2,1)S(1)}, u32[]{:S(2)}, u32[]{:S(2)}) %collective-permute-start.10) | collective-permute-done | bytes 307232 | tf_op jit(solution)/shard_map/ppermute | solution.py:45
  22.7 0.8 broadcast_select_fusion.4.refs_6_
  23.4 1.2 collective-permute-start.13
  24.7 1.0 copy.10.refs_4_
  25.7 11.7 %collective-permute-done.8.refs_3_.refs_5_ = bf16[2,256,640]{2,1,0:T(8,128)(2,1)S(1)} collective-permute-done((bf16[2,256,640]{2,1,0:T(8,128)(2,1)S(1)}, bf16[2,256,640]{2,1,0:T(8,128)(2,1)S(1)}, u32[]{:S(2)}, u32[]{:S(2)}) %collective-permute-start.8) | collective-permute-done | bytes 655392 | tf_op jit(solution)/shard_map/ppermute | solution.py:45
  37.4 0.8 copy-done.5
  38.2 4.8 %shard_map.95 = bf16[2,3,80,640]{3,2,1,0:T(8,128)(2,1)} custom-call(bf16[2,256,640]{2,1,0:T(8,128)(2,1)} %copy-done, bf16[2,256,640]{2,1,0:T(8,128)(2,1)} %copy-done.2, bf16[2,256,640]{2,1,0:T(8,128)(2,1)} %copy-done.4, bf16[2,256,640]{2,1,0:T(8,128)(2,1)} %copy-done.5, f32[1024,1]{1,0:T(8,128)} %copy.10.refs_4_, ...), custom_call_target="tpu_custom_call" | custom-call | flops 1258291200 | bytes 2621440 | tf_op jit(solution)/shard_map/pallas_call | solution.py:138
  43.0 1.5 collective-permute-start.14
  44.5 1.3 collective-permute-start.2
  45.8 1.0 slice.28
  46.8 1.0 slice.29
  47.9 1.0 pad_maximum_fusion
  49.0 5.1 %shard_map.94 = f32[2,3,80,640]{3,2,1,0:T(8,128)} custom-call(bf16[2,256,640]{2,1,0:T(8,128)(2,1)} %copy-done, bf16[2,256,640]{2,1,0:T(8,128)(2,1)} %copy-done.2, bf16[2,256,640]{2,1,0:T(8,128)(2,1)} %copy-done.4, bf16[2,256,640]{2,1,0:T(8,128)(2,1)} %copy-done.5, f32[1024,1]{1,0:T(8,128)} %copy.10.refs_4_, ...), custom_call_target="tpu_custom_call" | custom-call | flops 1258291200 | bytes 2621440 | tf_op jit(solution)/shard_map/pallas_call | solution.py:138
  54.1 1.5 convert_add_fusion
  55.7 0.7 collective-permute-start.15
  56.4 1.4 collective-permute-start.30
  57.9 4.4 %collective-permute-start.16 = (bf16[3,80,640]{2,1,0:T(8,128)(2,1)S(1)}, bf16[3,80,640]{2,1,0:T(8,128)(2,1)S(1)}, u32[]{:S(2)}, u32[]{:S(2)}) collective-permute-start(bf16[3,80,640]{2,1,0:T(8,128)(2,1)S(1)} %fusion.3), channel_id=1, source_target_pairs={{0,8},{2,10},{4,12},{6,14},{8,0},{10,2},{12,4},{14,6},{17,25},{19,... | collective-permute-start | bytes 921608 | tf_op jit(solution)/shard_map/ppermute | solution.py:45
  62.3 1.3 collective-permute-start.17
  63.6 3.6 %collective-permute-done.27 = bf16[4,256,384]{2,1,0:T(8,128)(2,1)S(1)} collective-permute-done((bf16[4,256,384]{2,1,0:T(8,128)(2,1)}, bf16[4,256,384]{2,1,0:T(8,128)(2,1)S(1)}, u32[]{:S(2)}, u32[]{:S(2)}) %collective-permute-start.27) | collective-permute-done | bytes 786464 | tf_op jit(solution)/shard_map/ppermute | solution.py:45
  67.2 1.3 collective-permute-start.28
  68.5 9.8 %collective-permute-done.30 = bf16[4,256,256]{2,1,0:T(8,128)(2,1)} collective-permute-done((bf16[4,256,256]{2,1,0:T(8,128)(2,1)S(1)}, bf16[4,256,256]{2,1,0:T(8,128)(2,1)}, u32[]{:S(2)}, u32[]{:S(2)}) %collective-permute-start.30) | collective-permute-done | bytes 524320 | tf_op jit(solution)/shard_map/ppermute | solution.py:45
  78.3 1.3 collective-permute-start.31
  79.6 11.8 %collective-permute-done.17 = bf16[3,80,640]{2,1,0:T(8,128)(2,1)S(1)} collective-permute-done((bf16[3,80,640]{2,1,0:T(8,128)(2,1)S(1)}, bf16[3,80,640]{2,1,0:T(8,128)(2,1)S(1)}, u32[]{:S(2)}, u32[]{:S(2)}) %collective-permute-start.17) | collective-permute-done | bytes 307232 | tf_op jit(solution)/shard_map/ppermute | solution.py:45
  92.0 13.7 %collective-permute-start.18 = (bf16[3,80,640]{2,1,0:T(8,128)(2,1)S(1)}, bf16[3,80,640]{2,1,0:T(8,128)(2,1)}, u32[]{:S(2)}, u32[]{:S(2)}) collective-permute-start(bf16[3,80,640]{2,1,0:T(8,128)(2,1)S(1)} %multiply_convert_fusion), channel_id=1, source_target_pairs={{0,16},{2,18},{4,20},{6,22},{8,24},{10,26},{12,28},{14,30},{17,1},... | collective-permute-start | bytes 921608 | tf_op jit(solution)/shard_map/ppermute | solution.py:45
  105.7 0.8 dynamic-slice_bitcast_fusion.2
  106.5 1.2 broadcast_select_fusion.refs_6_
  107.7 1.3 collective-permute-start.29
  109.0 4.1 %collective-permute-start.22 = (bf16[3,80,640]{2,1,0:T(8,128)(2,1)S(1)}, bf16[3,80,640]{2,1,0:T(8,128)(2,1)S(1)}, u32[]{:S(2)}, u32[]{:S(2)}) collective-permute-start(bf16[3,80,640]{2,1,0:T(8,128)(2,1)S(1)} %multiply_convert_fusion), channel_id=1, source_target_pairs={{0,8},{2,10},{4,12},{6,14},{8,0},{10,2},{12,4},{14,6},{17,25},{19,... | collective-permute-start | bytes 921608 | tf_op jit(solution)/shard_map/ppermute | solution.py:45
  113.2 0.7 collective-permute-start.23
  113.9 1.1 broadcast_select_fusion.1.refs_6_
  115.0 1.4 collective-permute-start.32
  116.5 0.7 slice.35
  117.2 0.8 broadcast_select_fusion.3.refs_2_
  118.0 20.8 %collective-permute-start.34 = (f32[3,40,640]{2,1,0:T(8,128)}, f32[3,40,640]{2,1,0:T(8,128)}, u32[]{:S(2)}, u32[]{:S(2)}) collective-permute-start(f32[3,40,640]{2,1,0:T(8,128)} %slice.35), channel_id=1, source_target_pairs={{0,1},{2,3},{4,5},{6,7},{8,9},{10,11},{12,13},{14,15},{17,16},{19,... | collective-permute-start | bytes 921608 | tf_op jit(solution)/shard_map/ppermute | solution.py:45
  138.8 3.2 %collective-permute-start.19 = (bf16[3,80,640]{2,1,0:T(8,128)(2,1)}, bf16[3,80,640]{2,1,0:T(8,128)(2,1)}, u32[]{:S(2)}, u32[]{:S(2)}) collective-permute-start(bf16[3,80,640]{2,1,0:T(8,128)(2,1)} %broadcast_select_fusion.3.refs_2_), channel_id=1, source_target_pairs={{0,2},{1,3},{2,0},{3,1},{4,6},{5,7},{6,4},{7,5},{8,10},{9,11},{10,... | collective-permute-start | bytes 921608 | tf_op jit(solution)/shard_map/ppermute | solution.py:45
  142.1 0.6 pad_add_fusion.refs_0_.where
  143.3 1.9 %pad_maximum_fusion.1.refs_1_ = bf16[2,256,640]{2,1,0:T(8,128)(2,1)} fusion(bf16[1,256,640]{2,1,0:T(8,128)(2,1)} %bitcast.4, bf16[1,256,640]{2,1,0:T(8,128)(2,1)S(1)} %get-tuple-element.33), kind=kLoop, calls=%fused_computation.3 | loop fusion | flops 327680 | bytes 1310720 | tf_op jit(solution)/shard_map/stack | solution.py:324
  145.2 0.9 copy-done.11
  146.1 8.1 %shard_map.96.refs_11_ = f32[512,384]{1,0:T(8,128)} custom-call(s32[3]{0:T(128)} %pad_add_fusion.refs_0_.where, bf16[2,256,640]{2,1,0:T(8,128)(2,1)} %pad_maximum_fusion.1.refs_1_, bf16[2,256,640]{2,1,0:T(8,128)(2,1)} %copy-done, bf16[2,256,640]{2,1,0:T(8,128)(2,1)} %copy-done.2, bf16[2,256,640]{2,1,0:T(8,128)(2,1)} %copy-done.4, ...), custom_call_target="tpu_custom_call" | custom-call | flops 1207959552 | bytes 3932160 | tf_op jit(solution)/shard_map/pallas_call | solution.py:254
  154.2 1.4 collective-permute-start.20
  155.8 1.4 collective-permute-start.26
  157.4 6.7 %shard_map.97.refs_12_ = f32[512,256]{1,0:T(8,128)} custom-call(s32[3]{0:T(128)} %pad_add_fusion.refs_0_.where, bf16[2,256,640]{2,1,0:T(8,128)(2,1)} %pad_maximum_fusion.1.refs_1_, bf16[2,256,640]{2,1,0:T(8,128)(2,1)} %copy-done, bf16[2,256,640]{2,1,0:T(8,128)(2,1)} %copy-done.2, bf16[2,256,640]{2,1,0:T(8,128)(2,1)} %copy-done.4, ...), custom_call_target="tpu_custom_call" | custom-call | flops 805306368 | bytes 2621440 | tf_op jit(solution)/shard_map/pallas_call | solution.py:254
  164.2 0.8 collective-permute-done.25.refs_8_
  164.9 4.9 %collective-permute-done.21.refs_5_ = bf16[3,80,640]{2,1,0:T(8,128)(2,1)S(1)} collective-permute-done((bf16[3,80,640]{2,1,0:T(8,128)(2,1)}, bf16[3,80,640]{2,1,0:T(8,128)(2,1)S(1)}, u32[]{:S(2)}, u32[]{:S(2)}) %collective-permute-start.21) | collective-permute-done | bytes 307232 | tf_op jit(solution)/shard_map/ppermute | solution.py:45
  169.9 1.8 collective-permute-done.26.refs_9_
  171.6 5.3 %query_side.1 = (bf16[256,640]{1,0:T(8,128)(2,1)}, bf16[256,640]{1,0:T(8,128)(2,1)}) custom-call(s32[3]{0:T(128)} %pad_add_fusion.refs_0_.where, bf16[2,256,640]{2,1,0:T(8,128)(2,1)} %pad_maximum_fusion.1.refs_1_, bf16[3,80,640]{2,1,0:T(8,128)(2,1)} %broadcast_select_fusion.3.refs_2_, bf16[3,80,640]{2,1,0:T(8,128)(2,1)} %collective-permute-done.19.refs_3_, ...), custom_call_target="tpu_custom_call" | custom-call | flops 1258291200 | bytes 2457600 | tf_op jit(solution)/shard_map/query_side/pallas_call | solution.py:188
  177.4 0.8 multiply_multiply_fusion
  178.2 0.6 collective-permute-done.33.arrived
  178.8 0.7 copy-done.14
  179.6 2.0 %join.1 = bf16[256,1280]{1,0:T(8,128)(2,1)} custom-call(s32[3]{0:T(128)} %pad_add_fusion.refs_0_.where, bf16[256,640]{1,0:T(8,128)(2,1)} %get-tuple-element.19.own, bf16[256,640]{1,0:T(8,128)(2,1)} %copy-done.14), custom_call_target="tpu_custom_call" | custom-call | tf_op jit(solution)/shard_map/join/pallas_call | solution.py:283
  (94 shorter events, 3.3 us)
Async XLA Ops:
  0.6 2.0 %copy-start.7 = (f32[3,40,640]{2,1,0:T(8,128)S(1)}, f32[3,40,640]{2,1,0:T(8,128)}, u32[]{:S(2)}) copy-start(f32[3,40,640]{2,1,0:T(8,128)} %param.11) | copy-start | bytes 921604
  0.6 3.3 %copy-start.12 = (bf16[256,1280]{1,0:T(8,128)(2,1)S(1)}, bf16[256,1280]{1,0:T(8,128)(2,1)}, u32[]{:S(2)}) copy-start(bf16[256,1280]{1,0:T(8,128)(2,1)} %param.9) | copy-start | bytes 1966084
  0.7 4.5 %copy-start.17 = (f32[2,256]{1,0:T(2,128)S(1)}, f32[2,256]{1,0:T(2,128)}, u32[]{:S(2)}) copy-start(f32[2,256]{1,0:T(2,128)} %param.10) | copy-start | bytes 6148
  1.9 11.8 %collective-permute-start.3 = (bf16[256,640]{1,0:T(8,128)(2,1)S(1)}, bf16[256,640]{1,0:T(8,128)(2,1)S(1)}, u32[]{:S(2)}, u32[]{:S(2)}) collective-permute-start(bf16[256,640]{1,0:T(8,128)(2,1)S(1)} %get-tuple-element.32), channel_id=1, source_target_pairs={{0,1},{1,0},{2,3},{3,2},{4,5},{5,4},{6,7},{7,6},{8,9},{9,8},{10,11... | collective-permute-start | bytes 983048 | tf_op jit(solution)/shard_map/ppermute | solution.py:45
  2.6 3.5 %collective-permute-start.1 = (f32[3,40,640]{2,1,0:T(8,128)S(1)}, f32[3,40,640]{2,1,0:T(8,128)S(1)}, u32[]{:S(2)}, u32[]{:S(2)}) collective-permute-start(f32[3,40,640]{2,1,0:T(8,128)S(1)} %copy-done.7), channel_id=1, source_target_pairs={{1,0},{3,2},{5,4},{7,6},{9,8},{11,10},{13,12},{15,14},{16,17},{18,... | collective-permute-start | bytes 921608 | tf_op jit(solution)/shard_map/ppermute | solution.py:45
  4.0 10.5 %collective-permute-start.4 = (bf16[256,640]{1,0:T(8,128)(2,1)S(1)}, bf16[256,640]{1,0:T(8,128)(2,1)S(1)}, u32[]{:S(2)}, u32[]{:S(2)}) collective-permute-start(bf16[256,640]{1,0:T(8,128)(2,1)S(1)} %get-tuple-element.30), channel_id=1, source_target_pairs={{0,1},{1,0},{2,3},{3,2},{4,5},{5,4},{6,7},{7,6},{8,9},{9,8},{10,11... | collective-permute-start | bytes 983048 | tf_op jit(solution)/shard_map/ppermute | solution.py:45
  5.2 4.0 %collective-permute-start.5 = (f32[1,256]{1,0:T(1,128)S(1)}, f32[1,256]{1,0:T(1,128)S(1)}, u32[]{:S(2)}, u32[]{:S(2)}) collective-permute-start(f32[1,256]{1,0:T(1,128)S(1)} %get-tuple-element.36), channel_id=1, source_target_pairs={{0,1},{1,0},{2,3},{3,2},{4,5},{5,4},{6,7},{7,6},{8,9},{9,8},{10,11... | collective-permute-start | bytes 3080 | tf_op jit(solution)/shard_map/ppermute | solution.py:45
  6.9 6.9 %collective-permute-start.9 = (bf16[3,80,640]{2,1,0:T(8,128)(2,1)}, bf16[3,80,640]{2,1,0:T(8,128)(2,1)}, u32[]{:S(2)}, u32[]{:S(2)}) collective-permute-start(bf16[3,80,640]{2,1,0:T(8,128)(2,1)} %convert_element_type.27), channel_id=1, source_target_pairs={{0,16},{2,18},{4,20},{6,22},{8,24},{10,26},{12,28},{14,30},{17,1},... | collective-permute-start | bytes 921608 | tf_op jit(solution)/shard_map/ppermute | solution.py:45
  9.2 2.5 %collective-permute-start.6 = (f32[2,256]{1,0:T(2,128)S(1)}, f32[2,256]{1,0:T(2,128)S(1)}, u32[]{:S(2)}, u32[]{:S(2)}) collective-permute-start(f32[2,256]{1,0:T(2,128)S(1)} %pad_maximum_fusion.5), channel_id=1, source_target_pairs={{0,2},{1,3},{2,0},{3,1},{4,6},{5,7},{6,4},{7,5},{8,10},{9,11},{10,... | collective-permute-start | bytes 6152 | tf_op jit(solution)/shard_map/ppermute | solution.py:45
  11.8 10.9 %collective-permute-start.10 = (bf16[3,80,640]{2,1,0:T(8,128)(2,1)}, bf16[3,80,640]{2,1,0:T(8,128)(2,1)S(1)}, u32[]{:S(2)}, u32[]{:S(2)}) collective-permute-start(bf16[3,80,640]{2,1,0:T(8,128)(2,1)} %convert_element_type.27), channel_id=1, source_target_pairs={{0,8},{2,10},{4,12},{6,14},{8,0},{10,2},{12,4},{14,6},{17,25},{19,... | collective-permute-start | bytes 921608 | tf_op jit(solution)/shard_map/ppermute | solution.py:45
  13.8 23.6 %copy-start = (bf16[2,256,640]{2,1,0:T(8,128)(2,1)}, bf16[2,256,640]{2,1,0:T(8,128)(2,1)S(1)}, u32[]{:S(2)}) copy-start(bf16[2,256,640]{2,1,0:T(8,128)(2,1)S(1)} %pad_maximum_fusion.2.refs_0_.refs_2_) | copy-start | bytes 1966084
  13.8 8.8 %collective-permute-start.11 = (bf16[3,80,640]{2,1,0:T(8,128)(2,1)}, bf16[3,80,640]{2,1,0:T(8,128)(2,1)S(1)}, u32[]{:S(2)}, u32[]{:S(2)}) collective-permute-start(bf16[3,80,640]{2,1,0:T(8,128)(2,1)} %collective-permute-done.9), channel_id=1, source_target_pairs={{1,9},{3,11},{5,13},{7,15},{9,1},{11,3},{13,5},{15,7},{16,24},{18,... | collective-permute-start | bytes 921608 | tf_op jit(solution)/shard_map/ppermute | solution.py:45
  14.6 22.8 %copy-start.2 = (bf16[2,256,640]{2,1,0:T(8,128)(2,1)}, bf16[2,256,640]{2,1,0:T(8,128)(2,1)S(1)}, u32[]{:S(2)}) copy-start(bf16[2,256,640]{2,1,0:T(8,128)(2,1)S(1)} %pad_maximum_fusion.3.refs_1_.refs_3_) | copy-start | bytes 1966084
  14.6 11.1 %collective-permute-start.7 = (bf16[2,256,640]{2,1,0:T(8,128)(2,1)S(1)}, bf16[2,256,640]{2,1,0:T(8,128)(2,1)S(1)}, u32[]{:S(2)}, u32[]{:S(2)}) collective-permute-start(bf16[2,256,640]{2,1,0:T(8,128)(2,1)S(1)} %pad_maximum_fusion.2.refs_0_.refs_2_), channel_id=1, source_target_pairs={{0,2},{1,3},{2,0},{3,1},{4,6},{5,7},{6,4},{7,5},{8,10},{9,11},{10,... | collective-permute-start | bytes 1966088 | tf_op jit(solution)/shard_map/ppermute | solution.py:45
  16.0 21.3 %collective-permute-start.8 = (bf16[2,256,640]{2,1,0:T(8,128)(2,1)S(1)}, bf16[2,256,640]{2,1,0:T(8,128)(2,1)S(1)}, u32[]{:S(2)}, u32[]{:S(2)}) collective-permute-start(bf16[2,256,640]{2,1,0:T(8,128)(2,1)S(1)} %pad_maximum_fusion.3.refs_1_.refs_3_), channel_id=1, source_target_pairs={{0,2},{1,3},{2,0},{3,1},{4,6},{5,7},{6,4},{7,5},{8,10},{9,11},{10,... | collective-permute-start | bytes 1966088 | tf_op jit(solution)/shard_map/ppermute | solution.py:45
  16.9 8.8 %collective-permute-start.12 = (bf16[3,80,640]{2,1,0:T(8,128)(2,1)}, bf16[3,80,640]{2,1,0:T(8,128)(2,1)}, u32[]{:S(2)}, u32[]{:S(2)}) collective-permute-start(bf16[3,80,640]{2,1,0:T(8,128)(2,1)} %broadcast_select_fusion.5.refs_5_), channel_id=1, source_target_pairs={{0,4},{1,5},{2,6},{3,7},{4,0},{5,1},{6,2},{7,3},{8,12},{9,13},{10,... | collective-permute-start | bytes 921608 | tf_op jit(solution)/shard_map/ppermute | solution.py:45
  23.4 13.9 %collective-permute-start.13 = (bf16[3,80,640]{2,1,0:T(8,128)(2,1)}, bf16[3,80,640]{2,1,0:T(8,128)(2,1)}, u32[]{:S(2)}, u32[]{:S(2)}) collective-permute-start(bf16[3,80,640]{2,1,0:T(8,128)(2,1)} %broadcast_select_fusion.4.refs_6_), channel_id=1, source_target_pairs={{0,4},{1,5},{2,6},{3,7},{4,0},{5,1},{6,2},{7,3},{8,12},{9,13},{10,... | collective-permute-start | bytes 921608 | tf_op jit(solution)/shard_map/ppermute | solution.py:45
  25.7 11.7 %copy-start.4 = (bf16[2,256,640]{2,1,0:T(8,128)(2,1)}, bf16[2,256,640]{2,1,0:T(8,128)(2,1)S(1)}, u32[]{:S(2)}) copy-start(bf16[2,256,640]{2,1,0:T(8,128)(2,1)S(1)} %collective-permute-done.7.refs_2_.refs_4_) | copy-start | bytes 1966084
  37.4 0.8 copy-start.5
  43.0 4.8 %copy-start.1 = (bf16[2,256,640]{2,1,0:T(8,128)(2,1)S(1)}, bf16[2,256,640]{2,1,0:T(8,128)(2,1)}, u32[]{:S(2)}) copy-start(bf16[2,256,640]{2,1,0:T(8,128)(2,1)} %copy-done) | copy-start | bytes 1966084
  43.0 4.8 %copy-start.3 = (bf16[2,256,640]{2,1,0:T(8,128)(2,1)S(1)}, bf16[2,256,640]{2,1,0:T(8,128)(2,1)}, u32[]{:S(2)}) copy-start(bf16[2,256,640]{2,1,0:T(8,128)(2,1)} %copy-done.2) | copy-start | bytes 1966084
  43.0 11.1 %collective-permute-start.14 = (bf16[2,3,80,640]{3,2,1,0:T(8,128)(2,1)}, bf16[2,3,80,640]{3,2,1,0:T(8,128)(2,1)}, u32[]{:S(2)}, u32[]{:S(2)}) collective-permute-start(bf16[2,3,80,640]{3,2,1,0:T(8,128)(2,1)} %shard_map.95), channel_id=1, source_target_pairs={{0,4},{1,5},{2,6},{3,7},{4,0},{5,1},{6,2},{7,3},{8,12},{9,13},{10,... | collective-permute-start | bytes 1843208 | tf_op jit(solution)/shard_map/ppermute | solution.py:45
  44.5 35.1 %collective-permute-start.2 = (f32[3,40,640]{2,1,0:T(8,128)}, f32[3,40,640]{2,1,0:T(8,128)S(1)}, u32[]{:S(2)}, u32[]{:S(2)}) collective-permute-start(f32[3,40,640]{2,1,0:T(8,128)} %param.12), channel_id=1, source_target_pairs={{1,0},{3,2},{5,4},{7,6},{9,8},{11,10},{13,12},{15,14},{16,17},{18,... | collective-permute-start | bytes 921608 | tf_op jit(solution)/shard_map/ppermute | solution.py:45
  48.9 18.3 %collective-permute-start.27 = (bf16[4,256,384]{2,1,0:T(8,128)(2,1)}, bf16[4,256,384]{2,1,0:T(8,128)(2,1)S(1)}, u32[]{:S(2)}, u32[]{:S(2)}) collective-permute-start(bf16[4,256,384]{2,1,0:T(8,128)(2,1)} %pad_maximum_fusion), channel_id=1, source_target_pairs={{0,4},{1,5},{2,6},{3,7},{4,0},{5,1},{6,2},{7,3},{8,12},{9,13},{10,... | collective-permute-start | bytes 2359304 | tf_op jit(solution)/shard_map/ppermute | solution.py:45
  55.7 2.2 %collective-permute-start.15 = (bf16[3,80,640]{2,1,0:T(8,128)(2,1)S(1)}, bf16[3,80,640]{2,1,0:T(8,128)(2,1)S(1)}, u32[]{:S(2)}, u32[]{:S(2)}) collective-permute-start(bf16[3,80,640]{2,1,0:T(8,128)(2,1)S(1)} %fusion.3), channel_id=1, source_target_pairs={{1,9},{3,11},{5,13},{7,15},{9,1},{11,3},{13,5},{15,7},{16,24},{18,... | collective-permute-start | bytes 921608 | tf_op jit(solution)/shard_map/ppermute | solution.py:45
  56.4 35.0 %copy-start.8 = (f32[3,40,640]{2,1,0:T(8,128)S(1)}, f32[3,40,640]{2,1,0:T(8,128)}, u32[]{:S(2)}) copy-start(f32[3,40,640]{2,1,0:T(8,128)} %param.12) | copy-start | bytes 921604
  56.4 21.9 %collective-permute-start.30 = (bf16[4,256,256]{2,1,0:T(8,128)(2,1)S(1)}, bf16[4,256,256]{2,1,0:T(8,128)(2,1)}, u32[]{:S(2)}, u32[]{:S(2)}) collective-permute-start(bf16[4,256,256]{2,1,0:T(8,128)(2,1)S(1)} %pad_maximum_fusion.4), channel_id=1, source_target_pairs={{0,4},{1,5},{2,6},{3,7},{4,0},{5,1},{6,2},{7,3},{8,12},{9,13},{10,... | collective-permute-start | bytes 1572872 | tf_op jit(solution)/shard_map/ppermute | solution.py:45
  57.9 21.7 %collective-permute-start.16 = (bf16[3,80,640]{2,1,0:T(8,128)(2,1)S(1)}, bf16[3,80,640]{2,1,0:T(8,128)(2,1)S(1)}, u32[]{:S(2)}, u32[]{:S(2)}) collective-permute-start(bf16[3,80,640]{2,1,0:T(8,128)(2,1)S(1)} %fusion.3), channel_id=1, source_target_pairs={{0,8},{2,10},{4,12},{6,14},{8,0},{10,2},{12,4},{14,6},{17,25},{19,... | collective-permute-start | bytes 921608 | tf_op jit(solution)/shard_map/ppermute | solution.py:45
  62.3 29.1 %collective-permute-start.17 = (bf16[3,80,640]{2,1,0:T(8,128)(2,1)S(1)}, bf16[3,80,640]{2,1,0:T(8,128)(2,1)S(1)}, u32[]{:S(2)}, u32[]{:S(2)}) collective-permute-start(bf16[3,80,640]{2,1,0:T(8,128)(2,1)S(1)} %add_convert_fusion), channel_id=1, source_target_pairs={{1,17},{3,19},{5,21},{7,23},{9,25},{11,27},{13,29},{15,31},{16,0},... | collective-permute-start | bytes 921608 | tf_op jit(solution)/shard_map/ppermute | solution.py:45
  67.2 39.3 %collective-permute-start.28 = (bf16[4,256,384]{2,1,0:T(8,128)(2,1)S(1)}, bf16[4,256,384]{2,1,0:T(8,128)(2,1)}, u32[]{:S(2)}, u32[]{:S(2)}) collective-permute-start(bf16[4,256,384]{2,1,0:T(8,128)(2,1)S(1)} %collective-permute-done.27), channel_id=1, source_target_pairs={{0,8},{1,9},{2,10},{3,11},{8,16},{9,17},{10,18},{11,19},{16,24},{1... | collective-permute-start | bytes 2359304 | tf_op jit(solution)/shard_map/ppermute | solution.py:45
  78.3 35.6 %collective-permute-start.31 = (bf16[4,256,256]{2,1,0:T(8,128)(2,1)}, bf16[4,256,256]{2,1,0:T(8,128)(2,1)}, u32[]{:S(2)}, u32[]{:S(2)}) collective-permute-start(bf16[4,256,256]{2,1,0:T(8,128)(2,1)} %collective-permute-done.30), channel_id=1, source_target_pairs={{0,8},{1,9},{2,10},{3,11},{8,16},{9,17},{10,18},{11,19},{16,24},{1... | collective-permute-start | bytes 1572872 | tf_op jit(solution)/shard_map/ppermute | solution.py:45
  91.7 14.0 %copy-start.13 = (bf16[256,1280]{1,0:T(8,128)(2,1)S(1)}, bf16[256,1280]{1,0:T(8,128)(2,1)}, u32[]{:S(2)}) copy-start(bf16[256,1280]{1,0:T(8,128)(2,1)} %param.7) | copy-start | bytes 1966084
  92.0 21.2 %collective-permute-start.18 = (bf16[3,80,640]{2,1,0:T(8,128)(2,1)S(1)}, bf16[3,80,640]{2,1,0:T(8,128)(2,1)}, u32[]{:S(2)}, u32[]{:S(2)}) collective-permute-start(bf16[3,80,640]{2,1,0:T(8,128)(2,1)S(1)} %multiply_convert_fusion), channel_id=1, source_target_pairs={{0,16},{2,18},{4,20},{6,22},{8,24},{10,26},{12,28},{14,30},{17,1},... | collective-permute-start | bytes 921608 | tf_op jit(solution)/shard_map/ppermute | solution.py:45
  106.5 35.5 %collective-permute-start = (bf16[256,640]{1,0:T(8,128)(2,1)}, bf16[256,640]{1,0:T(8,128)(2,1)}, u32[]{:S(2)}, u32[]{:S(2)}) collective-permute-start(bf16[256,640]{1,0:T(8,128)(2,1)} %get-tuple-element.34), channel_id=1, source_target_pairs={{0,1},{1,0},{2,3},{3,2},{4,5},{5,4},{6,7},{7,6},{8,9},{9,8},{10,11... | collective-permute-start | bytes 983048 | tf_op jit(solution)/shard_map/ppermute | solution.py:45
  107.7 10.2 %copy-start.6 = (bf16[4,256,384]{2,1,0:T(8,128)(2,1)}, bf16[4,256,384]{2,1,0:T(8,128)(2,1)S(1)}, u32[]{:S(2)}) copy-start(bf16[4,256,384]{2,1,0:T(8,128)(2,1)S(1)} %broadcast_select_fusion.refs_6_) | copy-start | bytes 2359300
  107.7 37.5 %collective-permute-start.29 = (bf16[4,256,384]{2,1,0:T(8,128)(2,1)S(1)}, bf16[4,256,384]{2,1,0:T(8,128)(2,1)S(1)}, u32[]{:S(2)}, u32[]{:S(2)}) collective-permute-start(bf16[4,256,384]{2,1,0:T(8,128)(2,1)S(1)} %broadcast_select_fusion.refs_6_), channel_id=1, source_target_pairs={{2,0},{3,1},{6,4},{7,5},{10,8},{11,9},{14,12},{15,13},{18,16},{19,... | collective-permute-start | bytes 2359304 | tf_op jit(solution)/shard_map/ppermute | solution.py:45
  109.0 8.9 %collective-permute-start.22 = (bf16[3,80,640]{2,1,0:T(8,128)(2,1)S(1)}, bf16[3,80,640]{2,1,0:T(8,128)(2,1)S(1)}, u32[]{:S(2)}, u32[]{:S(2)}) collective-permute-start(bf16[3,80,640]{2,1,0:T(8,128)(2,1)S(1)} %multiply_convert_fusion), channel_id=1, source_target_pairs={{0,8},{2,10},{4,12},{6,14},{8,0},{10,2},{12,4},{14,6},{17,25},{19,... | collective-permute-start | bytes 921608 | tf_op jit(solution)/shard_map/ppermute | solution.py:45
  113.2 25.5 %collective-permute-start.23 = (bf16[3,80,640]{2,1,0:T(8,128)(2,1)}, bf16[3,80,640]{2,1,0:T(8,128)(2,1)S(1)}, u32[]{:S(2)}, u32[]{:S(2)}) collective-permute-start(bf16[3,80,640]{2,1,0:T(8,128)(2,1)} %collective-permute-done.18), channel_id=1, source_target_pairs={{1,9},{3,11},{5,13},{7,15},{9,1},{11,3},{13,5},{15,7},{16,24},{18,... | collective-permute-start | bytes 921608 | tf_op jit(solution)/shard_map/ppermute | solution.py:45
  115.0 26.9 %copy-start.9 = (bf16[4,256,256]{2,1,0:T(8,128)(2,1)}, bf16[4,256,256]{2,1,0:T(8,128)(2,1)S(1)}, u32[]{:S(2)}) copy-start(bf16[4,256,256]{2,1,0:T(8,128)(2,1)S(1)} %broadcast_select_fusion.1.refs_6_) | copy-start | bytes 1572868
  115.0 27.6 %copy-start.16 = (f32[1280]{0:T(1024)S(1)}, f32[1280]{0:T(1024)}, u32[]{:S(2)}) copy-start(f32[1280]{0:T(1024)} %param.13) | copy-start | bytes 15364
  115.0 42.4 %collective-permute-start.32 = (bf16[4,256,256]{2,1,0:T(8,128)(2,1)S(1)}, bf16[4,256,256]{2,1,0:T(8,128)(2,1)}, u32[]{:S(2)}, u32[]{:S(2)}) collective-permute-start(bf16[4,256,256]{2,1,0:T(8,128)(2,1)S(1)} %broadcast_select_fusion.1.refs_6_), channel_id=1, source_target_pairs={{2,0},{3,1},{6,4},{7,5},{10,8},{11,9},{14,12},{15,13},{18,16},{19,... | collective-permute-start | bytes 1572872 | tf_op jit(solution)/shard_map/ppermute | solution.py:45
  118.0 37.7 %collective-permute-start.34 = (f32[3,40,640]{2,1,0:T(8,128)}, f32[3,40,640]{2,1,0:T(8,128)}, u32[]{:S(2)}, u32[]{:S(2)}) collective-permute-start(f32[3,40,640]{2,1,0:T(8,128)} %slice.35), channel_id=1, source_target_pairs={{0,1},{2,3},{4,5},{6,7},{8,9},{10,11},{12,13},{14,15},{17,16},{19,... | collective-permute-start | bytes 921608 | tf_op jit(solution)/shard_map/ppermute | solution.py:45
  138.8 16.9 %collective-permute-start.19 = (bf16[3,80,640]{2,1,0:T(8,128)(2,1)}, bf16[3,80,640]{2,1,0:T(8,128)(2,1)}, u32[]{:S(2)}, u32[]{:S(2)}) collective-permute-start(bf16[3,80,640]{2,1,0:T(8,128)(2,1)} %broadcast_select_fusion.3.refs_2_), channel_id=1, source_target_pairs={{0,2},{1,3},{2,0},{3,1},{4,6},{5,7},{6,4},{7,5},{8,10},{9,11},{10,... | collective-permute-start | bytes 921608 | tf_op jit(solution)/shard_map/ppermute | solution.py:45
  142.0 13.7 %copy-start.15 = (bf16[3,80,640]{2,1,0:T(8,128)(2,1)}, bf16[3,80,640]{2,1,0:T(8,128)(2,1)S(1)}, u32[]{:S(2)}) copy-start(bf16[3,80,640]{2,1,0:T(8,128)(2,1)S(1)} %broadcast_select_fusion.2.refs_6_) | copy-start | bytes 921604
  142.0 13.8 %collective-permute-start.24 = (bf16[3,80,640]{2,1,0:T(8,128)(2,1)S(1)}, bf16[3,80,640]{2,1,0:T(8,128)(2,1)}, u32[]{:S(2)}, u32[]{:S(2)}) collective-permute-start(bf16[3,80,640]{2,1,0:T(8,128)(2,1)S(1)} %broadcast_select_fusion.2.refs_6_), channel_id=1, source_target_pairs={{0,4},{1,5},{2,6},{3,7},{4,0},{5,1},{6,2},{7,3},{8,12},{9,13},{10,... | collective-permute-start | bytes 921608 | tf_op jit(solution)/shard_map/ppermute | solution.py:45
  145.2 0.9 copy-start.11
  154.2 10.0 %collective-permute-start.20 = (bf16[3,80,640]{2,1,0:T(8,128)(2,1)}, bf16[3,80,640]{2,1,0:T(8,128)(2,1)S(1)}, u32[]{:S(2)}, u32[]{:S(2)}) collective-permute-start(bf16[3,80,640]{2,1,0:T(8,128)(2,1)} %broadcast_select_fusion.3.refs_2_), channel_id=1, source_target_pairs={{0,4},{1,5},{2,6},{3,7},{4,0},{5,1},{6,2},{7,3},{8,12},{9,13},{10,... | collective-permute-start | bytes 921608 | tf_op jit(solution)/shard_map/ppermute | solution.py:45
  155.7 9.3 %collective-permute-start.25 = (bf16[3,80,640]{2,1,0:T(8,128)(2,1)S(1)}, bf16[3,80,640]{2,1,0:T(8,128)(2,1)S(1)}, u32[]{:S(2)}, u32[]{:S(2)}) collective-permute-start(bf16[3,80,640]{2,1,0:T(8,128)(2,1)S(1)} %broadcast_select_fusion.2.refs_6_), channel_id=1, source_target_pairs={{0,2},{1,3},{2,0},{3,1},{4,6},{5,7},{6,4},{7,5},{8,10},{9,11},{10,... | collective-permute-start | bytes 921608 | tf_op jit(solution)/shard_map/ppermute | solution.py:45
  155.7 14.2 %collective-permute-start.21 = (bf16[3,80,640]{2,1,0:T(8,128)(2,1)}, bf16[3,80,640]{2,1,0:T(8,128)(2,1)S(1)}, u32[]{:S(2)}, u32[]{:S(2)}) collective-permute-start(bf16[3,80,640]{2,1,0:T(8,128)(2,1)} %collective-permute-done.19.refs_3_), channel_id=1, source_target_pairs={{0,4},{1,5},{2,6},{3,7},{4,0},{5,1},{6,2},{7,3},{8,12},{9,13},{10,... | collective-permute-start | bytes 921608 | tf_op jit(solution)/shard_map/ppermute | solution.py:45
  155.8 15.8 %collective-permute-start.26 = (bf16[3,80,640]{2,1,0:T(8,128)(2,1)}, bf16[3,80,640]{2,1,0:T(8,128)(2,1)}, u32[]{:S(2)}, u32[]{:S(2)}) collective-permute-start(bf16[3,80,640]{2,1,0:T(8,128)(2,1)} %collective-permute-done.24.refs_7_), channel_id=1, source_target_pairs={{0,2},{1,3},{2,0},{3,1},{4,6},{5,7},{6,4},{7,5},{8,10},{9,11},{10,... | collective-permute-start | bytes 921608 | tf_op jit(solution)/shard_map/ppermute | solution.py:45
  157.4 20.0 %copy-start.10 = (f32[3,40,640]{2,1,0:T(8,128)}, f32[3,40,640]{2,1,0:T(8,128)S(1)}, u32[]{:S(2)}) copy-start(f32[3,40,640]{2,1,0:T(8,128)S(1)} %get-tuple-element.25) | copy-start | bytes 921604
  164.2 7.5 %copy-start.18 = (bf16[3,80,640]{2,1,0:T(8,128)(2,1)}, bf16[3,80,640]{2,1,0:T(8,128)(2,1)S(1)}, u32[]{:S(2)}) copy-start(bf16[3,80,640]{2,1,0:T(8,128)(2,1)S(1)} %collective-permute-done.20.refs_4_) | copy-start | bytes 921604
  164.9 6.7 %copy-start.19 = (bf16[3,80,640]{2,1,0:T(8,128)(2,1)}, bf16[3,80,640]{2,1,0:T(8,128)(2,1)S(1)}, u32[]{:S(2)}) copy-start(bf16[3,80,640]{2,1,0:T(8,128)(2,1)S(1)} %collective-permute-done.25.refs_8_) | copy-start | bytes 921604
  169.9 1.8 copy-start.20
  176.9 1.9 %collective-permute-start.33 = (bf16[256,640]{1,0:T(8,128)(2,1)}, bf16[256,640]{1,0:T(8,128)(2,1)S(1)}, u32[]{:S(2)}, u32[]{:S(2)}) collective-permute-start(bf16[256,640]{1,0:T(8,128)(2,1)} %get-tuple-element.20), channel_id=1, source_target_pairs={{0,1},{1,0},{2,3},{3,2},{4,5},{5,4},{6,7},{7,6},{8,9},{9,8},{10,11... | collective-permute-start | bytes 983048 | tf_op jit(solution)/shard_map/ppermute | solution.py:45
  178.8 0.7 copy-start.14

commit v2 on v1

--- a/solution.py
+++ b/solution.py
@@ -33,6 +33,7 @@
         self.cross_out = [(dev, (dev + shift) % count) for dev in home]
         self.home_swap = [[(dev, dev ^ (8 * k)) for dev in home] for k in range(half)]
         self.away_swap = [[(dev, dev ^ (8 * k)) for dev in away] for k in range(half)]
+        self.z_swap = [[(dev, dev ^ (8 * k)) for dev in range(count)] for k in range(half)]
         self.cross_back = [(dev, (dev + shift) % count) for dev in away]
         self.z_up = [(dev, dev + 8) for dev in range(count - 8) if dev % 8 < 4]
         self.back_x = [(dev, dev - 2) for dev in range(count) if dev % 4 >= 2]
@@ -66,21 +67,46 @@
     return pieces
 
 
-def reduce_z(sums, routes):
-    away, home = sums, sums
-    for bit in reversed(routes.bits):
-        half = len(away) // 2
-        sent = [part.astype(BF16) for part in away[half:]]
-        arrived = [send(part, routes.away_swap[bit]) for part in sent]
-        away = [low + part.astype(F32) for low, part in zip(away[:half], arrived)]
-    crossed = away[0].astype(BF16)
-    home, crossed = lax.optimization_barrier((home, crossed))
-    crossed = send(crossed, routes.cross_back)
-    for bit in reversed(routes.bits):
-        half = len(home) // 2
-        arrived = [send(part.astype(BF16), routes.home_swap[bit]) for part in home[half:]]
-        home = [low + part.astype(F32) for low, part in zip(home[:half], arrived)]
-    return home[0] + crossed.astype(F32)
+def fold_kernel(keep_from, send_from, low, arrived, keep, sent):
+    count = keep.shape[0]
+    total = low[...] + arrived[...].astype(F32)
+    keep[...] = total[keep_from : keep_from + count]
+    sent[...] = total[send_from : send_from + count].astype(BF16)
+
+
+def fold(low, arrived):
+    count = low.shape[0]
+    half = max(count // 2, 1)
+    shape = (half,) + low.shape[1:]
+    return pl.pallas_call(
+        lambda *refs: fold_kernel(0, count - half, *refs),
+        out_shape=[jax.ShapeDtypeStruct(shape, F32), jax.ShapeDtypeStruct(shape, BF16)],
+        in_specs=[vmem(), vmem()],
+        out_specs=[vmem(), vmem()],
+        cost_estimate=pl.CostEstimate(flops=low.size, bytes_accessed=12 * low.size, transcendentals=0),
+    )(low, arrived)
+
+
+def update_kernel(part, crossed, weights, momentum, total, applied):
+    grads = part[0] + crossed[0].astype(F32)
+    total[...] = grads
+    applied[...] = updated(weights[...], momentum[...], grads)[0].astype(BF16)
+
+
+def update_pair(part, crossed, weights, momentum):
+    return pl.pallas_call(
+        update_kernel,
+        out_shape=[
+            jax.ShapeDtypeStruct(weights.shape, F32),
+            jax.ShapeDtypeStruct(weights.shape, BF16),
+        ],
+        in_specs=[vmem()] * 4,
+        out_specs=[vmem()] * 2,
+        cost_estimate=pl.CostEstimate(
+            flops=10 * weights.size, bytes_accessed=20 * weights.size, transcendentals=0
+        ),
+        name="update",
+    )(part, crossed, weights, momentum)
 
 
 def nt_dot(left, right):
@@ -103,11 +129,12 @@
     parts = len(units)
     step = units[0].shape[1]
     rows = parts * step
+    by_token = jnp.transpose(rates[...] * (-grad_scale))
     for idx, (k_ref, v_ref) in enumerate(((k_own, v_own), (k_near, v_near))):
         for side in range(2):
             at = (2 * idx + side) * tokens
             keys[at : at + tokens, :] = k_ref[side]
-            rate = rates[at : at + tokens, :] * (-grad_scale)
+            rate = by_token[:, 2 * idx + side : 2 * idx + side + 1]
             ograd[at : at + tokens, :] = (rate * v_ref[side].astype(F32)).astype(BF16)
     for idx in range(parts):
         pair[idx * step : (idx + 1) * step, :] = units[idx][0]
@@ -154,52 +181,84 @@
     )(k_own, v_own, k_near, v_near, rates, *units)
 
 
-def query_kernel(count, *refs):
-    where, quer_in = refs[:2]
-    pieces = refs[2 : 2 + count]
-    gain, att_a, att_b, own, other = refs[2 + count : 7 + count]
-    quer, weights, result = refs[7 + count :]
-    tokens = quer_in.shape[1]
+def load_rows(pieces, weights):
     rows = pieces[0].shape[1]
-    mine = pl.multiple_of(where[0] * tokens, tokens)
-    theirs = pl.multiple_of((1 - where[0]) * tokens, tokens)
-    quer[pl.ds(mine, tokens), :] = quer_in[0]
-    quer[pl.ds(theirs, tokens), :] = quer_in[1]
-    for idx in range(count):
-        weights[:, idx * rows : (idx + 1) * rows, :] = pieces[idx][...]
-    gate = nt_dot(quer[...], weights[0])
-    up = nt_dot(quer[...], weights[1])
+    for idx, piece in enumerate(pieces):
+        weights[:, idx * rows : (idx + 1) * rows, :] = piece[...]
+
+
+def fast_product(quer_in, weights):
+    quer = jnp.concatenate([quer_in[0], quer_in[1]], axis=0)
+    gate = nt_dot(quer, weights[0])
+    up = nt_dot(quer, weights[1])
     hidden = (gate * jax.nn.sigmoid(gate) * up).astype(BF16)
-    out = nn_dot(hidden, weights[2])
-    scale = lax.rsqrt(jnp.mean(out * out, axis=-1, keepdims=True) + EPS)
-    normed = out * scale * gain[...]
-    split = att_a.shape[1]
-    result[:, :split] = normed[:, :split] + att_a[...]
-    result[:, split:] = normed[:, split:] + att_b[...]
-    own[...] = result[pl.ds(mine, tokens), :].astype(BF16)
-    other[...] = result[pl.ds(theirs, tokens), :].astype(BF16)
-
-
-def query_side(where, quer_in, pieces, gain, atts):
+    return nn_dot(hidden, weights[2])
+
+
+def query_first_kernel(count, *refs):
+    quer_in = refs[0]
+    out, weights = refs[1 + count :]
+    load_rows(refs[1 : 1 + count], weights)
+    out[...] = fast_product(quer_in, weights)
+
+
+def query_first(quer_in, pieces):
     _, tokens, width = quer_in.shape
     count = len(pieces)
     rows = pieces[0].shape[1]
-    total = 2 * tokens * count * rows * width
-    return pl.pallas_call(
-        lambda *refs: query_kernel(count, *refs),
-        out_shape=[jax.ShapeDtypeStruct((tokens, width), BF16)] * 2,
-        in_specs=[pl.BlockSpec(memory_space=pltpu.SMEM)] + [vmem()] * (4 + count),
+    return pl.pallas_call(
+        lambda *refs: query_first_kernel(count, *refs),
+        out_shape=jax.ShapeDtypeStruct((2 * tokens, width), F32),
+        in_specs=[vmem()] * (1 + count),
+        out_specs=vmem(),
+        scratch_shapes=[pltpu.VMEM((3, count * rows, width), BF16)],
+        cost_estimate=pl.CostEstimate(
+            flops=12 * tokens * count * rows * width,
+            bytes_accessed=6 * count * rows * width,
+            transcendentals=0,
+        ),
+        name="query_first",
+    )(quer_in, *pieces)
+
+
+def query_last_kernel(count, *refs):
+    where, quer_in = refs[:2]
+    sums, gain, att_a, att_b, own, other, weights = refs[2 + count :]
+    tokens, width = other.shape
+    load_rows(refs[2 : 2 + count], weights)
+    fast = sums[...] + fast_product(quer_in, weights)
+    scale = lax.rsqrt(jnp.mean(fast * fast, axis=-1, keepdims=True) + EPS)
+    normed = fast * scale * gain[...]
+    here = pl.multiple_of(where[0] * width, ATT_DIM)
+    at = [pl.multiple_of(core * tokens, tokens) for core in (where[0], 1 - where[0])]
+    att = [
+        jnp.concatenate([ref[pl.ds(base, tokens), :] for ref in (att_a, att_b)], axis=1)
+        for base in at
+    ]
+    own[:, pl.ds(here, width)] = (normed[:tokens] + att[0]).astype(BF16)
+    other[...] = (normed[tokens:] + att[1]).astype(BF16)
+
+
+def query_last(where, quer_in, pieces, sums, gain, atts):
+    _, tokens, width = quer_in.shape
+    count = len(pieces)
+    rows = pieces[0].shape[1]
+    return pl.pallas_call(
+        lambda *refs: query_last_kernel(count, *refs),
+        out_shape=[
+            jax.ShapeDtypeStruct((tokens, 2 * width), BF16),
+            jax.ShapeDtypeStruct((tokens, width), BF16),
+        ],
+        in_specs=[pl.BlockSpec(memory_space=pltpu.SMEM)] + [vmem()] * (5 + count),
         out_specs=[vmem()] * 2,
-        scratch_shapes=[
-            pltpu.VMEM((2 * tokens, width), BF16),
-            pltpu.VMEM((3, count * rows, width), BF16),
-            pltpu.VMEM((2 * tokens, width), F32),
-        ],
+        scratch_shapes=[pltpu.VMEM((3, count * rows, width), BF16)],
         cost_estimate=pl.CostEstimate(
-            flops=6 * total, bytes_accessed=6 * count * rows * width, transcendentals=0
+            flops=12 * tokens * count * rows * width,
+            bytes_accessed=6 * count * rows * width,
+            transcendentals=0,
         ),
-        name="query_side",
-    )(where, quer_in, *pieces, gain, *atts)
+        name="query_last",
+    )(where, quer_in, *pieces, sums, gain, *atts)
 
 
 def att_kernel(low, where, quer_in, k_own, v_own, k_near, v_near, two, back, out,
@@ -270,25 +329,6 @@
     )(where, quer_in, k_own, v_own, k_near, v_near, two, back)
 
 
-def join_kernel(where, own, arrived, out):
-    width = own.shape[1]
-    mine = pl.multiple_of(where[0] * width, ATT_DIM)
-    theirs = pl.multiple_of((1 - where[0]) * width, ATT_DIM)
-    out[:, pl.ds(mine, width)] = own[...]
-    out[:, pl.ds(theirs, width)] = arrived[...]
-
-
-def join(where, own, arrived):
-    tokens, width = own.shape
-    return pl.pallas_call(
-        join_kernel,
-        out_shape=jax.ShapeDtypeStruct((tokens, 2 * width), own.dtype),
-        in_specs=[pl.BlockSpec(memory_space=pltpu.SMEM), vmem(), vmem()],
-        out_specs=vmem(),
-        name="join",
-    )(where, own, arrived)
-
-
 def updated(weights, momentum, grads):
     new_momentum = 0.9 * momentum + grads
     moved = weights - new_momentum
@@ -316,7 +356,6 @@
     their_rate = lax.dynamic_slice_in_dim(step_rates, 1 - core, 1, 0)
     rates = jnp.concatenate([my_rate, send(their_rate, routes.partner)], axis=0)
     rates = jnp.concatenate([rates, send(rates, routes.x_swap)], axis=0)
-    rates = rates.reshape(4 * local_tokens, 1)
 
     def by_core(array):
         kept = lax.dynamic_slice_in_dim(array, core * width, width, 1)
@@ -325,7 +364,6 @@
 
     k_own = by_core(key_rows)
     v_own = by_core(value_rows)
-    k_own, v_own, rates = lax.optimization_barrier((k_own, v_own, rates))
     q_own = by_core(queries)
 
     pair_weights = jnp.concatenate([fast_weights, send(fast_weights, routes.pair_in)], axis=1)
@@ -355,22 +393,28 @@
     side_grads = key_side(grad_scale, *tokens_in, side_units, BF16)
     side_in = send(side_grads, routes.y_swap)
     own_grads = key_side(grad_scale, *tokens_in, units, F32)
-    sums = own_grads + side_in.astype(F32)
-    total = reduce_z([sums[k] for k in range(len(units))], routes)
-    pair_momentum = jnp.concatenate([momentum, send(momentum, routes.pair_in)], axis=1)
+    part, sent = fold(own_grads, side_in)
+    for bit in reversed(routes.bits):
+        part, sent = fold(part, send(sent, routes.z_swap[bit]))
+    crossed = send(sent, routes.cross_back)
+    their_momentum = send(momentum, routes.pair_in)
+    pair_momentum = jnp.concatenate([momentum, their_momentum], axis=1)
     att_in = (where, q_own, k_own, v_own, k_near, v_near)
     early_att = attention(*att_in, early_two, early_back, 0)
     late_att = attention(*att_in, late_two, late_back, cut)
 
-    pair_new, _ = updated(pair_weights, pair_momentum, total)
-    applied = gather_plane(gather_z(pair_new.astype(BF16), routes, is_home), routes)
+    total, pair_new = update_pair(part, crossed, pair_weights, pair_momentum)
+    applied = gather_plane(gather_z(pair_new, routes, is_home), routes)
     partner_grads = send(total[:, owned:], routes.pair_out)
     grads = jnp.where(is_home, total[:, :owned], partner_grads)
     new_weights, new_momentum = updated(fast_weights, momentum, grads)
     gain = lax.dynamic_slice_in_dim(out_gain, core * width, width, 0).reshape(1, width)
-    own, other = query_side(where, q_own, applied, gain, (early_att, late_att))
+    soon = [piece for idx, piece in enumerate(applied) if idx % 4 != 3]
+    last = applied[3::4]
+    sums = query_first(q_own, soon)
+    own, other = query_last(where, q_own, last, sums, gain, (early_att, late_att))
     arrived = send(other, routes.partner)
-    layer_out = join(where, own, arrived)
+    layer_out = lax.dynamic_update_slice_in_dim(own, arrived, (1 - core) * width, 1)
     return (layer_out, new_weights, new_momentum)
 
 

time: 182 us -> 171 us (0.940)
  the two profiles are of different devices: /device:TPU:25 before, /device:TPU:1 now
where the time goes in v2:
time: 171 us; the launch traced here: 169 us
  starting transfers between devices  62 us (36%)
  waiting for transfers between devices  50.5 us (30%)
  Pallas kernels  39.8 us (23%)
  local copies, waits for them, and re-layouts  8.21 us (5%)
  other arithmetic  7.79 us (5%)
    ppermute x34, starting transfers between devices, send(): return lax.ppermute(array, 'seq', route)  62 us
    ppermute x34, waiting for transfers between devices, send(): return lax.ppermute(array, 'seq', route)  50.5 us
    pallas_call x2, Pallas kernels, attention(): pl.pallas_call(lambda *refs: att_kernel(low, *refs), out_shape=jax.ShapeD...  14.8 us
    pallas_call x2, Pallas kernels, key_side(): pl.pallas_call(lambda *refs: key_kernel(grad_scale, *refs), out_shape=jax...  9.61 us
    unnamed x51, local copies, waits for them, and re-layouts  4.65 us
    pallas_call x2, Pallas kernels, fold(): pl.pallas_call(lambda *refs: fold_kernel(0, count - half, *refs), out_sha...  4.56 us
    pallas_call x1, Pallas kernels, query_first(): pl.pallas_call(lambda *refs: query_first_kernel(count, *refs), out_shape=...  4.17 us
    pallas_call x1, Pallas kernels, query_last(): pl.pallas_call(lambda *refs: query_last_kernel(count, *refs), out_shape=[...  4.01 us
  transfers between devices with their start and end apart: 34, of which 10 were waited for; matrix products, arithmetic and copies ran while one was open for 6% of the time, Pallas kernels for 21%

profile of v2, /device:TPU:1, one launch (start us, length us, event | category | flops | bytes accessed | tf_op | source)
XLA Modules:
  0.0 169.5 jit_solution(9164695151947714201)
XLA Ops:
  0.6 2.1 %collective-permute-start.7 = (f32[3,40,640]{2,1,0:T(8,128)}, f32[3,40,640]{2,1,0:T(8,128)S(1)}, u32[]{:S(2)}, u32[]{:S(2)}) collective-permute-start(f32[3,40,640]{2,1,0:T(8,128)} %param.11), channel_id=1, source_target_pairs={{1,0},{3,2},{5,4},{7,6},{9,8},{11,10},{13,12},{15,14},{16,17},{18,... | collective-permute-start | bytes 921608 | tf_op jit(solution)/shard_map/ppermute | solution.py:46
  2.8 1.2 dynamic-slice_bitcast_fusion.1
  4.1 0.5 collective-permute-start.2
  4.9 1.3 collective-permute-start.8
  6.2 2.8 %collective-permute-start.6 = (f32[2,256]{1,0:T(2,128)S(1)}, f32[2,256]{1,0:T(2,128)S(1)}, u32[]{:S(2)}, u32[]{:S(2)}) collective-permute-start(f32[2,256]{1,0:T(2,128)S(1)} %pad_maximum_fusion.7), channel_id=1, source_target_pairs={{0,2},{1,3},{2,0},{3,1},{4,6},{5,7},{6,4},{7,5},{8,10},{9,11},{10,... | collective-permute-start | bytes 6152 | tf_op jit(solution)/shard_map/ppermute | solution.py:46
  9.0 0.7 collective-permute-start.9
  9.9 7.5 %collective-permute-done.8 = bf16[3,80,640]{2,1,0:T(8,128)(2,1)S(1)} collective-permute-done((bf16[3,80,640]{2,1,0:T(8,128)(2,1)S(1)}, bf16[3,80,640]{2,1,0:T(8,128)(2,1)S(1)}, u32[]{:S(2)}, u32[]{:S(2)}) %collective-permute-start.8) | collective-permute-done | bytes 307232 | tf_op jit(solution)/shard_map/ppermute | solution.py:46
  17.3 1.9 %collective-permute-start.10 = (bf16[3,80,640]{2,1,0:T(8,128)(2,1)S(1)}, bf16[3,80,640]{2,1,0:T(8,128)(2,1)S(1)}, u32[]{:S(2)}, u32[]{:S(2)}) collective-permute-start(bf16[3,80,640]{2,1,0:T(8,128)(2,1)S(1)} %collective-permute-done.8), channel_id=1, source_target_pairs={{1,9},{3,11},{5,13},{7,15},{9,1},{11,3},{13,5},{15,7},{16,24},{18,... | collective-permute-start | bytes 921608 | tf_op jit(solution)/shard_map/ppermute | solution.py:46
  19.3 2.2 %collective-permute-start.3 = (bf16[2,256,640]{2,1,0:T(8,128)(2,1)S(1)}, bf16[2,256,640]{2,1,0:T(8,128)(2,1)S(1)}, u32[]{:S(2)}, u32[]{:S(2)}) collective-permute-start(bf16[2,256,640]{2,1,0:T(8,128)(2,1)S(1)} %pad_maximum_fusion.refs_0_.refs_2_), channel_id=1, source_target_pairs={{0,2},{1,3},{2,0},{3,1},{4,6},{5,7},{6,4},{7,5},{8,10},{9,11},{10,... | collective-permute-start | bytes 1966088 | tf_op jit(solution)/shard_map/ppermute | solution.py:46
  21.7 1.5 collective-permute-start.11
  23.2 2.0 %collective-permute-done.10 = bf16[3,80,640]{2,1,0:T(8,128)(2,1)S(1)} collective-permute-done((bf16[3,80,640]{2,1,0:T(8,128)(2,1)S(1)}, bf16[3,80,640]{2,1,0:T(8,128)(2,1)S(1)}, u32[]{:S(2)}, u32[]{:S(2)}) %collective-permute-start.10) | collective-permute-done | bytes 307232 | tf_op jit(solution)/shard_map/ppermute | solution.py:46
  25.3 2.2 %collective-permute-start.12 = (bf16[3,80,640]{2,1,0:T(8,128)(2,1)S(1)}, bf16[3,80,640]{2,1,0:T(8,128)(2,1)S(1)}, u32[]{:S(2)}, u32[]{:S(2)}) collective-permute-start(bf16[3,80,640]{2,1,0:T(8,128)(2,1)S(1)} %broadcast_select_fusion.4.refs_6_), channel_id=1, source_target_pairs={{0,4},{1,5},{2,6},{3,7},{4,0},{5,1},{6,2},{7,3},{8,12},{9,13},{10,... | collective-permute-start | bytes 921608 | tf_op jit(solution)/shard_map/ppermute | solution.py:46
  27.6 1.0 pad_maximum_fusion.2
  28.7 0.6 pad_maximum_fusion.6.refs_4_
  29.3 1.5 collective-permute-done.11.refs_5_
  30.7 6.1 %collective-permute-done.3.refs_2_.refs_4_ = bf16[2,256,640]{2,1,0:T(8,128)(2,1)S(1)} collective-permute-done((bf16[2,256,640]{2,1,0:T(8,128)(2,1)S(1)}, bf16[2,256,640]{2,1,0:T(8,128)(2,1)S(1)}, u32[]{:S(2)}, u32[]{:S(2)}) %collective-permute-start.3) | collective-permute-done | bytes 655392 | tf_op jit(solution)/shard_map/ppermute | solution.py:46
  36.8 11.4 %collective-permute-done.4.refs_3_.refs_5_ = bf16[2,256,640]{2,1,0:T(8,128)(2,1)S(1)} collective-permute-done((bf16[2,256,640]{2,1,0:T(8,128)(2,1)S(1)}, bf16[2,256,640]{2,1,0:T(8,128)(2,1)S(1)}, u32[]{:S(2)}, u32[]{:S(2)}) %collective-permute-start.4) | collective-permute-done | bytes 655392 | tf_op jit(solution)/shard_map/ppermute | solution.py:46
  48.2 0.8 copy-done.6
  49.1 0.7 copy-done.24
  49.8 4.7 %shard_map.95 = bf16[2,3,80,640]{3,2,1,0:T(8,128)(2,1)} custom-call(bf16[2,256,640]{2,1,0:T(8,128)(2,1)} %copy-done.1, bf16[2,256,640]{2,1,0:T(8,128)(2,1)} %copy-done.2, bf16[2,256,640]{2,1,0:T(8,128)(2,1)} %copy-done.5, bf16[2,256,640]{2,1,0:T(8,128)(2,1)} %copy-done.6, f32[4,256]{1,0:T(4,128)} %pad_maximum_fusion.6.refs_4_, ...), custom_call_target="tpu_custom_call" | custom-call | flops 1258291200 | bytes 2621440 | tf_op jit(solution)/shard_map/pallas_call | solution.py:165
  54.5 1.2 collective-permute-start.13
  55.8 5.5 %collective-permute-start.27 = (bf16[4,256,384]{2,1,0:T(8,128)(2,1)}, bf16[4,256,384]{2,1,0:T(8,128)(2,1)S(1)}, u32[]{:S(2)}, u32[]{:S(2)}) collective-permute-start(bf16[4,256,384]{2,1,0:T(8,128)(2,1)} %collective-permute-done.26), channel_id=1, source_target_pairs={{0,8},{1,9},{2,10},{3,11},{8,16},{9,17},{10,18},{11,19},{16,24},{1... | collective-permute-start | bytes 2359304 | tf_op jit(solution)/shard_map/ppermute | solution.py:46
  61.4 4.9 %shard_map.94.refs_0_ = f32[2,3,80,640]{3,2,1,0:T(8,128)} custom-call(bf16[2,256,640]{2,1,0:T(8,128)(2,1)} %copy-done.1, bf16[2,256,640]{2,1,0:T(8,128)(2,1)} %copy-done.2, bf16[2,256,640]{2,1,0:T(8,128)(2,1)} %copy-done.5, bf16[2,256,640]{2,1,0:T(8,128)(2,1)} %copy-done.6, f32[4,256]{1,0:T(4,128)} %pad_maximum_fusion.6.refs_4_, ...), custom_call_target="tpu_custom_call" | custom-call | flops 1258291200 | bytes 2621440 | tf_op jit(solution)/shard_map/pallas_call | solution.py:165
  66.4 4.2 %collective-permute-done.13.refs_1_ = bf16[2,3,80,640]{3,2,1,0:T(8,128)(2,1)S(1)} collective-permute-done((bf16[2,3,80,640]{3,2,1,0:T(8,128)(2,1)}, bf16[2,3,80,640]{3,2,1,0:T(8,128)(2,1)S(1)}, u32[]{:S(2)}, u32[]{:S(2)}) %collective-permute-start.13) | collective-permute-done | bytes 614432 | tf_op jit(solution)/shard_map/ppermute | solution.py:46
  70.6 0.8 copy-done.14
  71.4 2.4 %shard_map.96 = (f32[1,3,80,640]{3,2,1,0:T(8,128)}, bf16[1,3,80,640]{3,2,1,0:T(8,128)(2,1)}) custom-call(f32[2,3,80,640]{3,2,1,0:T(8,128)} %shard_map.94.refs_0_, bf16[2,3,80,640]{3,2,1,0:T(8,128)(2,1)} %copy-done.14), custom_call_target="tpu_custom_call" | custom-call | flops 307200 | bytes 3686400 | tf_op jit(solution)/shard_map/pallas_call | solution.py:81
  73.8 3.5 %collective-permute-start.14 = (bf16[1,3,80,640]{3,2,1,0:T(8,128)(2,1)}, bf16[1,3,80,640]{3,2,1,0:T(8,128)(2,1)S(1)}, u32[]{:S(2)}, u32[]{:S(2)}) collective-permute-start(bf16[1,3,80,640]{3,2,1,0:T(8,128)(2,1)} %get-tuple-element.13), channel_id=1, source_target_pairs={{0,8},{1,9},{2,10},{3,11},{4,12},{5,13},{6,14},{7,15},{8,0},{9,1},... | collective-permute-start | bytes 921608 | tf_op jit(solution)/shard_map/ppermute | solution.py:46
  77.3 2.8 %collective-permute-start.16 = (f32[3,40,640]{2,1,0:T(8,128)S(1)}, f32[3,40,640]{2,1,0:T(8,128)S(1)}, u32[]{:S(2)}, u32[]{:S(2)}) collective-permute-start(f32[3,40,640]{2,1,0:T(8,128)S(1)} %copy-done.9), channel_id=1, source_target_pairs={{1,0},{3,2},{5,4},{7,6},{9,8},{11,10},{13,12},{15,14},{16,17},{18,... | collective-permute-start | bytes 921608 | tf_op jit(solution)/shard_map/ppermute | solution.py:46
  80.1 5.3 %collective-permute-done.14.refs_1_ = bf16[1,3,80,640]{3,2,1,0:T(8,128)(2,1)S(1)} collective-permute-done((bf16[1,3,80,640]{3,2,1,0:T(8,128)(2,1)}, bf16[1,3,80,640]{3,2,1,0:T(8,128)(2,1)S(1)}, u32[]{:S(2)}, u32[]{:S(2)}) %collective-permute-start.14) | collective-permute-done | bytes 307232 | tf_op jit(solution)/shard_map/ppermute | solution.py:46
  85.4 0.7 copy-done.17
  86.1 2.1 %shard_map.97 = (f32[1,3,80,640]{3,2,1,0:T(8,128)}, bf16[1,3,80,640]{3,2,1,0:T(8,128)(2,1)}) custom-call(f32[1,3,80,640]{3,2,1,0:T(8,128)} %get-tuple-element.12.refs_0_, bf16[1,3,80,640]{3,2,1,0:T(8,128)(2,1)} %copy-done.17), custom_call_target="tpu_custom_call" | custom-call | flops 153600 | bytes 1843200 | tf_op jit(solution)/shard_map/pallas_call | solution.py:81
  88.2 1.3 collective-permute-start.15
  89.5 4.0 %collective-permute-start.30 = (bf16[4,256,256]{2,1,0:T(8,128)(2,1)S(1)}, bf16[4,256,256]{2,1,0:T(8,128)(2,1)S(1)}, u32[]{:S(2)}, u32[]{:S(2)}) collective-permute-start(bf16[4,256,256]{2,1,0:T(8,128)(2,1)S(1)} %collective-permute-done.29), channel_id=1, source_target_pairs={{0,8},{1,9},{2,10},{3,11},{8,16},{9,17},{10,18},{11,19},{16,24},{1... | collective-permute-start | bytes 1572872 | tf_op jit(solution)/shard_map/ppermute | solution.py:46
  93.6 0.9 pad_maximum_fusion.4.momentum
  94.5 0.7 copy-done.20
  95.2 2.6 %update.1 = (f32[3,80,640]{2,1,0:T(8,128)}, bf16[3,80,640]{2,1,0:T(8,128)(2,1)}) custom-call(f32[1,3,80,640]{3,2,1,0:T(8,128)} %get-tuple-element.14.part, bf16[1,3,80,640]{3,2,1,0:T(8,128)(2,1)} %copy-done.20, f32[3,80,640]{2,1,0:T(8,128)} %copy-done, f32[3,80,640]{2,1,0:T(8,128)} %pad_maximum_fusion.4.momentum), custom_call_target="tpu_custom_call" | custom-call | flops 1536000 | bytes 3072000 | tf_op jit(solution)/shard_map/update/pallas_call | solution.py:97
  97.8 1.3 collective-permute-start.17
  99.1 0.8 dynamic-slice_bitcast_fusion.2
  100.0 8.4 %collective-permute-start = (bf16[256,640]{1,0:T(8,128)(2,1)}, bf16[256,640]{1,0:T(8,128)(2,1)}, u32[]{:S(2)}, u32[]{:S(2)}) collective-permute-start(bf16[256,640]{1,0:T(8,128)(2,1)} %get-tuple-element.29), channel_id=1, source_target_pairs={{0,1},{1,0},{2,3},{3,2},{4,5},{5,4},{6,7},{7,6},{8,9},{9,8},{10,11... | collective-permute-start | bytes 983048 | tf_op jit(solution)/shard_map/ppermute | solution.py:46
  108.5 1.4 collective-permute-start.28
  109.9 0.7 collective-permute-start.20
  110.6 2.9 %collective-permute-start.21 = (bf16[3,80,640]{2,1,0:T(8,128)(2,1)}, bf16[3,80,640]{2,1,0:T(8,128)(2,1)S(1)}, u32[]{:S(2)}, u32[]{:S(2)}) collective-permute-start(bf16[3,80,640]{2,1,0:T(8,128)(2,1)} %collective-permute-done.17), channel_id=1, source_target_pairs={{1,9},{3,11},{5,13},{7,15},{9,1},{11,3},{13,5},{15,7},{16,24},{18,... | collective-permute-start | bytes 921608 | tf_op jit(solution)/shard_map/ppermute | solution.py:46
  113.7 1.4 collective-permute-start.31
  115.2 1.0 broadcast_select_fusion.3.refs_1_
  116.2 1.3 collective-permute-start.33
  117.5 4.4 %collective-permute-done.21 = bf16[3,80,640]{2,1,0:T(8,128)(2,1)S(1)} collective-permute-done((bf16[3,80,640]{2,1,0:T(8,128)(2,1)}, bf16[3,80,640]{2,1,0:T(8,128)(2,1)S(1)}, u32[]{:S(2)}, u32[]{:S(2)}) %collective-permute-start.21) | collective-permute-done | bytes 307232 | tf_op jit(solution)/shard_map/ppermute | solution.py:46
  121.9 3.0 %collective-permute-start.18 = (bf16[3,80,640]{2,1,0:T(8,128)(2,1)S(1)}, bf16[3,80,640]{2,1,0:T(8,128)(2,1)}, u32[]{:S(2)}, u32[]{:S(2)}) collective-permute-start(bf16[3,80,640]{2,1,0:T(8,128)(2,1)S(1)} %broadcast_select_fusion.3.refs_1_), channel_id=1, source_target_pairs={{0,2},{1,3},{2,0},{3,1},{4,6},{5,7},{6,4},{7,5},{8,10},{9,11},{10,... | collective-permute-start | bytes 921608 | tf_op jit(solution)/shard_map/ppermute | solution.py:46
  125.0 2.3 %collective-permute-start.22 = (bf16[3,80,640]{2,1,0:T(8,128)(2,1)S(1)}, bf16[3,80,640]{2,1,0:T(8,128)(2,1)}, u32[]{:S(2)}, u32[]{:S(2)}) collective-permute-start(bf16[3,80,640]{2,1,0:T(8,128)(2,1)S(1)} %broadcast_select_fusion.2.refs_4_), channel_id=1, source_target_pairs={{0,4},{1,5},{2,6},{3,7},{4,0},{5,1},{6,2},{7,3},{8,12},{9,13},{10,... | collective-permute-start | bytes 921608 | tf_op jit(solution)/shard_map/ppermute | solution.py:46
  127.3 0.7 pad_add_fusion.refs_0_
  128.1 0.6 reshape.23.refs_5_
  128.6 1.9 %pad_maximum_fusion.3.refs_0_.refs_1_ = bf16[2,256,640]{2,1,0:T(8,128)(2,1)} fusion(bf16[1,256,640]{2,1,0:T(8,128)(2,1)} %bitcast.4, bf16[1,256,640]{2,1,0:T(8,128)(2,1)S(1)} %get-tuple-element.28), kind=kLoop, calls=%fused_computation.12 | loop fusion | flops 327680 | bytes 1310720 | tf_op jit(solution)/shard_map/stack | solution.py:363
  130.5 8.1 %shard_map.98.refs_6_ = f32[512,384]{1,0:T(8,128)} custom-call(s32[3]{0:T(128)} %pad_add_fusion.refs_0_, bf16[2,256,640]{2,1,0:T(8,128)(2,1)} %pad_maximum_fusion.3.refs_0_.refs_1_, bf16[2,256,640]{2,1,0:T(8,128)(2,1)} %copy-done.1, bf16[2,256,640]{2,1,0:T(8,128)(2,1)} %copy-done.2, bf16[2,256,640]{2,1,0:T(8,128)(2,1)} %copy-done.5, ...), custom_call_target="tpu_custom_call" | custom-call | flops 1207959552 | bytes 3932160 | tf_op jit(solution)/shard_map/pallas_call | solution.py:313
  138.6 1.4 collective-permute-start.24
  140.1 7.5 %collective-permute-done.18.refs_2_ = bf16[3,80,640]{2,1,0:T(8,128)(2,1)} collective-permute-done((bf16[3,80,640]{2,1,0:T(8,128)(2,1)S(1)}, bf16[3,80,640]{2,1,0:T(8,128)(2,1)}, u32[]{:S(2)}, u32[]{:S(2)}) %collective-permute-start.18) | collective-permute-done | bytes 307232 | tf_op jit(solution)/shard_map/ppermute | solution.py:46
  147.6 2.2 %collective-permute-start.19 = (bf16[3,80,640]{2,1,0:T(8,128)(2,1)}, bf16[3,80,640]{2,1,0:T(8,128)(2,1)S(1)}, u32[]{:S(2)}, u32[]{:S(2)}) collective-permute-start(bf16[3,80,640]{2,1,0:T(8,128)(2,1)} %collective-permute-done.18.refs_2_), channel_id=1, source_target_pairs={{0,4},{1,5},{2,6},{3,7},{4,0},{5,1},{6,2},{7,3},{8,12},{9,13},{10,... | collective-permute-start | bytes 921608 | tf_op jit(solution)/shard_map/ppermute | solution.py:46
  149.8 0.2 multiply_reduce_fusion.1
  150.0 6.8 %shard_map.99.refs_7_ = f32[512,256]{1,0:T(8,128)} custom-call(s32[3]{0:T(128)} %pad_add_fusion.refs_0_, bf16[2,256,640]{2,1,0:T(8,128)(2,1)} %pad_maximum_fusion.3.refs_0_.refs_1_, bf16[2,256,640]{2,1,0:T(8,128)(2,1)} %copy-done.1, bf16[2,256,640]{2,1,0:T(8,128)(2,1)} %copy-done.2, bf16[2,256,640]{2,1,0:T(8,128)(2,1)} %copy-done.5, ...), custom_call_target="tpu_custom_call" | custom-call | flops 805306368 | bytes 2621440 | tf_op jit(solution)/shard_map/pallas_call | solution.py:313
  156.8 4.2 %query_first.1.refs_4_ = f32[512,640]{1,0:T(8,128)} custom-call(bf16[2,256,640]{2,1,0:T(8,128)(2,1)} %pad_maximum_fusion.3.refs_0_.refs_1_, bf16[3,80,640]{2,1,0:T(8,128)(2,1)} %copy-done.10, bf16[3,80,640]{2,1,0:T(8,128)(2,1)} %collective-permute-done.18.refs_2_, bf16[3,80,640]{2,1,0:T(8,128)(2,1)} %collective-permute-done.24.refs_3_, ...), custom_call_target="tpu_custom_call" | custom-call | flops 943718400 | bytes 1843200 | tf_op jit(solution)/shard_map/query_first/pallas_call | solution.py:209
  160.9 0.7 copy-done.19
  161.7 4.0 %query_last.1 = (bf16[256,1280]{1,0:T(8,128)(2,1)}, bf16[256,640]{1,0:T(8,128)(2,1)}) custom-call(s32[3]{0:T(128)} %pad_add_fusion.refs_0_, bf16[2,256,640]{2,1,0:T(8,128)(2,1)} %pad_maximum_fusion.3.refs_0_.refs_1_, bf16[3,80,640]{2,1,0:T(8,128)(2,1)} %copy-done.19, bf16[3,80,640]{2,1,0:T(8,128)(2,1)} %collective-permute-done.23.refs_3_, ...), custom_call_target="tpu_custom_call" | custom-call | flops 314572800 | bytes 614400 | tf_op jit(solution)/shard_map/query_last/pallas_call | solution.py:246
  165.7 1.6 collective-permute-start.32
  167.3 0.8 multiply_multiply_fusion
  168.1 0.6 collective-permute-done.32
  168.7 0.8 constant_dynamic-update-slice_fusion.2
  (96 shorter events, 1.6 us)
Async XLA Ops:
  0.6 3.4 %copy-start.12 = (bf16[256,1280]{1,0:T(8,128)(2,1)S(1)}, bf16[256,1280]{1,0:T(8,128)(2,1)}, u32[]{:S(2)}) copy-start(bf16[256,1280]{1,0:T(8,128)(2,1)} %param.9) | copy-start | bytes 1966084
  0.6 4.2 %collective-permute-start.7 = (f32[3,40,640]{2,1,0:T(8,128)}, f32[3,40,640]{2,1,0:T(8,128)S(1)}, u32[]{:S(2)}, u32[]{:S(2)}) collective-permute-start(f32[3,40,640]{2,1,0:T(8,128)} %param.11), channel_id=1, source_target_pairs={{1,0},{3,2},{5,4},{7,6},{9,8},{11,10},{13,12},{15,14},{16,17},{18,... | collective-permute-start | bytes 921608 | tf_op jit(solution)/shard_map/ppermute | solution.py:46
  2.7 1.9 %copy-start.22 = (f32[2,256]{1,0:T(2,128)S(1)}, f32[2,256]{1,0:T(2,128)}, u32[]{:S(2)}) copy-start(f32[2,256]{1,0:T(2,128)} %param.10) | copy-start | bytes 6148
  2.8 2.0 %copy-start.4 = (f32[3,40,640]{2,1,0:T(8,128)S(1)}, f32[3,40,640]{2,1,0:T(8,128)}, u32[]{:S(2)}) copy-start(f32[3,40,640]{2,1,0:T(8,128)} %param.11) | copy-start | bytes 921604
  3.9 5.7 %collective-permute-start.1 = (bf16[256,640]{1,0:T(8,128)(2,1)S(1)}, bf16[256,640]{1,0:T(8,128)(2,1)S(1)}, u32[]{:S(2)}, u32[]{:S(2)}) collective-permute-start(bf16[256,640]{1,0:T(8,128)(2,1)S(1)} %get-tuple-element.27), channel_id=1, source_target_pairs={{0,1},{1,0},{2,3},{3,2},{4,5},{5,4},{6,7},{7,6},{8,9},{9,8},{10,11... | collective-permute-start | bytes 983048 | tf_op jit(solution)/shard_map/ppermute | solution.py:46
  4.1 5.6 %collective-permute-start.2 = (bf16[256,640]{1,0:T(8,128)(2,1)S(1)}, bf16[256,640]{1,0:T(8,128)(2,1)S(1)}, u32[]{:S(2)}, u32[]{:S(2)}) collective-permute-start(bf16[256,640]{1,0:T(8,128)(2,1)S(1)} %get-tuple-element.25), channel_id=1, source_target_pairs={{0,1},{1,0},{2,3},{3,2},{4,5},{5,4},{6,7},{7,6},{8,9},{9,8},{10,11... | collective-permute-start | bytes 983048 | tf_op jit(solution)/shard_map/ppermute | solution.py:46
  4.7 1.6 collective-permute-start.5
  4.9 16.8 %copy-start = (f32[3,80,640]{2,1,0:T(8,128)}, f32[3,80,640]{2,1,0:T(8,128)S(1)}, u32[]{:S(2)}) copy-start(f32[3,80,640]{2,1,0:T(8,128)S(1)} %constant_dynamic-update-slice_fusion.weights) | copy-start | bytes 1843204
  4.9 12.4 %collective-permute-start.8 = (bf16[3,80,640]{2,1,0:T(8,128)(2,1)S(1)}, bf16[3,80,640]{2,1,0:T(8,128)(2,1)S(1)}, u32[]{:S(2)}, u32[]{:S(2)}) collective-permute-start(bf16[3,80,640]{2,1,0:T(8,128)(2,1)S(1)} %convert_element_type.3), channel_id=1, source_target_pairs={{0,16},{2,18},{4,20},{6,22},{8,24},{10,26},{12,28},{14,30},{17,1},... | collective-permute-start | bytes 921608 | tf_op jit(solution)/shard_map/ppermute | solution.py:46
  6.2 22.3 %collective-permute-start.6 = (f32[2,256]{1,0:T(2,128)S(1)}, f32[2,256]{1,0:T(2,128)S(1)}, u32[]{:S(2)}, u32[]{:S(2)}) collective-permute-start(f32[2,256]{1,0:T(2,128)S(1)} %pad_maximum_fusion.7), channel_id=1, source_target_pairs={{0,2},{1,3},{2,0},{3,1},{4,6},{5,7},{6,4},{7,5},{8,10},{9,11},{10,... | collective-permute-start | bytes 6152 | tf_op jit(solution)/shard_map/ppermute | solution.py:46
  9.0 12.7 %collective-permute-start.9 = (bf16[3,80,640]{2,1,0:T(8,128)(2,1)S(1)}, bf16[3,80,640]{2,1,0:T(8,128)(2,1)S(1)}, u32[]{:S(2)}, u32[]{:S(2)}) collective-permute-start(bf16[3,80,640]{2,1,0:T(8,128)(2,1)S(1)} %convert_element_type.3), channel_id=1, source_target_pairs={{0,8},{2,10},{4,12},{6,14},{8,0},{10,2},{12,4},{14,6},{17,25},{19,... | collective-permute-start | bytes 921608 | tf_op jit(solution)/shard_map/ppermute | solution.py:46
  9.8 11.9 %copy-start.1 = (bf16[2,256,640]{2,1,0:T(8,128)(2,1)}, bf16[2,256,640]{2,1,0:T(8,128)(2,1)S(1)}, u32[]{:S(2)}) copy-start(bf16[2,256,640]{2,1,0:T(8,128)(2,1)S(1)} %pad_maximum_fusion.refs_0_.refs_2_) | copy-start | bytes 1966084
  9.9 15.4 %copy-start.2 = (bf16[2,256,640]{2,1,0:T(8,128)(2,1)}, bf16[2,256,640]{2,1,0:T(8,128)(2,1)S(1)}, u32[]{:S(2)}) copy-start(bf16[2,256,640]{2,1,0:T(8,128)(2,1)S(1)} %pad_maximum_fusion.1.refs_1_.refs_3_) | copy-start | bytes 1966084
  17.3 7.9 %collective-permute-start.10 = (bf16[3,80,640]{2,1,0:T(8,128)(2,1)S(1)}, bf16[3,80,640]{2,1,0:T(8,128)(2,1)S(1)}, u32[]{:S(2)}, u32[]{:S(2)}) collective-permute-start(bf16[3,80,640]{2,1,0:T(8,128)(2,1)S(1)} %collective-permute-done.8), channel_id=1, source_target_pairs={{1,9},{3,11},{5,13},{7,15},{9,1},{11,3},{13,5},{15,7},{16,24},{18,... | collective-permute-start | bytes 921608 | tf_op jit(solution)/shard_map/ppermute | solution.py:46
  19.3 17.5 %collective-permute-start.3 = (bf16[2,256,640]{2,1,0:T(8,128)(2,1)S(1)}, bf16[2,256,640]{2,1,0:T(8,128)(2,1)S(1)}, u32[]{:S(2)}, u32[]{:S(2)}) collective-permute-start(bf16[2,256,640]{2,1,0:T(8,128)(2,1)S(1)} %pad_maximum_fusion.refs_0_.refs_2_), channel_id=1, source_target_pairs={{0,2},{1,3},{2,0},{3,1},{4,6},{5,7},{6,4},{7,5},{8,10},{9,11},{10,... | collective-permute-start | bytes 1966088 | tf_op jit(solution)/shard_map/ppermute | solution.py:46
  21.5 26.7 %collective-permute-start.4 = (bf16[2,256,640]{2,1,0:T(8,128)(2,1)S(1)}, bf16[2,256,640]{2,1,0:T(8,128)(2,1)S(1)}, u32[]{:S(2)}, u32[]{:S(2)}) collective-permute-start(bf16[2,256,640]{2,1,0:T(8,128)(2,1)S(1)} %pad_maximum_fusion.1.refs_1_.refs_3_), channel_id=1, source_target_pairs={{0,2},{1,3},{2,0},{3,1},{4,6},{5,7},{6,4},{7,5},{8,10},{9,11},{10,... | collective-permute-start | bytes 1966088 | tf_op jit(solution)/shard_map/ppermute | solution.py:46
  21.7 6.9 %copy-start.18 = (bf16[3,80,640]{2,1,0:T(8,128)(2,1)}, bf16[3,80,640]{2,1,0:T(8,128)(2,1)S(1)}, u32[]{:S(2)}) copy-start(bf16[3,80,640]{2,1,0:T(8,128)(2,1)S(1)} %broadcast_select_fusion.5.refs_5_) | copy-start | bytes 921604
  21.7 9.0 %collective-permute-start.11 = (bf16[3,80,640]{2,1,0:T(8,128)(2,1)S(1)}, bf16[3,80,640]{2,1,0:T(8,128)(2,1)S(1)}, u32[]{:S(2)}, u32[]{:S(2)}) collective-permute-start(bf16[3,80,640]{2,1,0:T(8,128)(2,1)S(1)} %broadcast_select_fusion.5.refs_5_), channel_id=1, source_target_pairs={{0,4},{1,5},{2,6},{3,7},{4,0},{5,1},{6,2},{7,3},{8,12},{9,13},{10,... | collective-permute-start | bytes 921608 | tf_op jit(solution)/shard_map/ppermute | solution.py:46
  25.3 3.3 %copy-start.16 = (bf16[3,80,640]{2,1,0:T(8,128)(2,1)}, bf16[3,80,640]{2,1,0:T(8,128)(2,1)S(1)}, u32[]{:S(2)}) copy-start(bf16[3,80,640]{2,1,0:T(8,128)(2,1)S(1)} %broadcast_select_fusion.4.refs_6_) | copy-start | bytes 921604
  25.3 23.8 %collective-permute-start.12 = (bf16[3,80,640]{2,1,0:T(8,128)(2,1)S(1)}, bf16[3,80,640]{2,1,0:T(8,128)(2,1)S(1)}, u32[]{:S(2)}, u32[]{:S(2)}) collective-permute-start(bf16[3,80,640]{2,1,0:T(8,128)(2,1)S(1)} %broadcast_select_fusion.4.refs_6_), channel_id=1, source_target_pairs={{0,4},{1,5},{2,6},{3,7},{4,0},{5,1},{6,2},{7,3},{8,12},{9,13},{10,... | collective-permute-start | bytes 921608 | tf_op jit(solution)/shard_map/ppermute | solution.py:46
  28.6 27.2 %collective-permute-start.26 = (bf16[4,256,384]{2,1,0:T(8,128)(2,1)}, bf16[4,256,384]{2,1,0:T(8,128)(2,1)}, u32[]{:S(2)}, u32[]{:S(2)}) collective-permute-start(bf16[4,256,384]{2,1,0:T(8,128)(2,1)} %pad_maximum_fusion.2), channel_id=1, source_target_pairs={{0,4},{1,5},{2,6},{3,7},{4,0},{5,1},{6,2},{7,3},{8,12},{9,13},{10,... | collective-permute-start | bytes 2359304 | tf_op jit(solution)/shard_map/ppermute | solution.py:46
  30.7 18.3 %copy-start.23 = (bf16[3,80,640]{2,1,0:T(8,128)(2,1)}, bf16[3,80,640]{2,1,0:T(8,128)(2,1)S(1)}, u32[]{:S(2)}) copy-start(bf16[3,80,640]{2,1,0:T(8,128)(2,1)S(1)} %collective-permute-done.11.refs_5_) | copy-start | bytes 921604
  36.8 11.4 %copy-start.5 = (bf16[2,256,640]{2,1,0:T(8,128)(2,1)}, bf16[2,256,640]{2,1,0:T(8,128)(2,1)S(1)}, u32[]{:S(2)}) copy-start(bf16[2,256,640]{2,1,0:T(8,128)(2,1)S(1)} %collective-permute-done.3.refs_2_.refs_4_) | copy-start | bytes 1966084
  48.2 0.8 copy-start.6
  49.0 0.7 copy-start.24
  54.5 16.1 %collective-permute-start.13 = (bf16[2,3,80,640]{3,2,1,0:T(8,128)(2,1)}, bf16[2,3,80,640]{3,2,1,0:T(8,128)(2,1)S(1)}, u32[]{:S(2)}, u32[]{:S(2)}) collective-permute-start(bf16[2,3,80,640]{3,2,1,0:T(8,128)(2,1)} %shard_map.95), channel_id=1, source_target_pairs={{0,4},{1,5},{2,6},{3,7},{4,0},{5,1},{6,2},{7,3},{8,12},{9,13},{10,... | collective-permute-start | bytes 1843208 | tf_op jit(solution)/shard_map/ppermute | solution.py:46
  55.8 52.5 %collective-permute-start.27 = (bf16[4,256,384]{2,1,0:T(8,128)(2,1)}, bf16[4,256,384]{2,1,0:T(8,128)(2,1)S(1)}, u32[]{:S(2)}, u32[]{:S(2)}) collective-permute-start(bf16[4,256,384]{2,1,0:T(8,128)(2,1)} %collective-permute-done.26), channel_id=1, source_target_pairs={{0,8},{1,9},{2,10},{3,11},{8,16},{9,17},{10,18},{11,19},{16,24},{1... | collective-permute-start | bytes 2359304 | tf_op jit(solution)/shard_map/ppermute | solution.py:46
  61.4 28.2 %collective-permute-start.29 = (bf16[4,256,256]{2,1,0:T(8,128)(2,1)S(1)}, bf16[4,256,256]{2,1,0:T(8,128)(2,1)S(1)}, u32[]{:S(2)}, u32[]{:S(2)}) collective-permute-start(bf16[4,256,256]{2,1,0:T(8,128)(2,1)S(1)} %pad_maximum_fusion.5), channel_id=1, source_target_pairs={{0,4},{1,5},{2,6},{3,7},{4,0},{5,1},{6,2},{7,3},{8,12},{9,13},{10,... | collective-permute-start | bytes 1572872 | tf_op jit(solution)/shard_map/ppermute | solution.py:46
  66.3 10.9 %copy-start.9 = (f32[3,40,640]{2,1,0:T(8,128)S(1)}, f32[3,40,640]{2,1,0:T(8,128)}, u32[]{:S(2)}) copy-start(f32[3,40,640]{2,1,0:T(8,128)} %param.12) | copy-start | bytes 921604
  70.6 0.9 copy-start.14
  73.8 11.5 %collective-permute-start.14 = (bf16[1,3,80,640]{3,2,1,0:T(8,128)(2,1)}, bf16[1,3,80,640]{3,2,1,0:T(8,128)(2,1)S(1)}, u32[]{:S(2)}, u32[]{:S(2)}) collective-permute-start(bf16[1,3,80,640]{3,2,1,0:T(8,128)(2,1)} %get-tuple-element.13), channel_id=1, source_target_pairs={{0,8},{1,9},{2,10},{3,11},{4,12},{5,13},{6,14},{7,15},{8,0},{9,1},... | collective-permute-start | bytes 921608 | tf_op jit(solution)/shard_map/ppermute | solution.py:46
  77.3 16.3 %collective-permute-start.16 = (f32[3,40,640]{2,1,0:T(8,128)S(1)}, f32[3,40,640]{2,1,0:T(8,128)S(1)}, u32[]{:S(2)}, u32[]{:S(2)}) collective-permute-start(f32[3,40,640]{2,1,0:T(8,128)S(1)} %copy-done.9), channel_id=1, source_target_pairs={{1,0},{3,2},{5,4},{7,6},{9,8},{11,10},{13,12},{15,14},{16,17},{18,... | collective-permute-start | bytes 921608 | tf_op jit(solution)/shard_map/ppermute | solution.py:46
  85.4 0.7 copy-start.17
  88.2 6.3 %collective-permute-start.15 = (bf16[1,3,80,640]{3,2,1,0:T(8,128)(2,1)}, bf16[1,3,80,640]{3,2,1,0:T(8,128)(2,1)S(1)}, u32[]{:S(2)}, u32[]{:S(2)}) collective-permute-start(bf16[1,3,80,640]{3,2,1,0:T(8,128)(2,1)} %get-tuple-element.15), channel_id=1, source_target_pairs={{1,17},{3,19},{5,21},{7,23},{9,25},{11,27},{13,29},{15,31},{16,0},... | collective-permute-start | bytes 921608 | tf_op jit(solution)/shard_map/ppermute | solution.py:46
  89.5 24.1 %collective-permute-start.30 = (bf16[4,256,256]{2,1,0:T(8,128)(2,1)S(1)}, bf16[4,256,256]{2,1,0:T(8,128)(2,1)S(1)}, u32[]{:S(2)}, u32[]{:S(2)}) collective-permute-start(bf16[4,256,256]{2,1,0:T(8,128)(2,1)S(1)} %collective-permute-done.29), channel_id=1, source_target_pairs={{0,8},{1,9},{2,10},{3,11},{8,16},{9,17},{10,18},{11,19},{16,24},{1... | collective-permute-start | bytes 1572872 | tf_op jit(solution)/shard_map/ppermute | solution.py:46
  94.5 4.6 %copy-start.13 = (bf16[256,1280]{1,0:T(8,128)(2,1)S(1)}, bf16[256,1280]{1,0:T(8,128)(2,1)}, u32[]{:S(2)}) copy-start(bf16[256,1280]{1,0:T(8,128)(2,1)} %param.7) | copy-start | bytes 1966084
  94.5 0.7 copy-start.20
  97.8 12.8 %collective-permute-start.17 = (bf16[3,80,640]{2,1,0:T(8,128)(2,1)}, bf16[3,80,640]{2,1,0:T(8,128)(2,1)}, u32[]{:S(2)}, u32[]{:S(2)}) collective-permute-start(bf16[3,80,640]{2,1,0:T(8,128)(2,1)} %get-tuple-element.16), channel_id=1, source_target_pairs={{0,16},{2,18},{4,20},{6,22},{8,24},{10,26},{12,28},{14,30},{17,1},... | collective-permute-start | bytes 921608 | tf_op jit(solution)/shard_map/ppermute | solution.py:46
  100.0 25.0 %collective-permute-start = (bf16[256,640]{1,0:T(8,128)(2,1)}, bf16[256,640]{1,0:T(8,128)(2,1)}, u32[]{:S(2)}, u32[]{:S(2)}) collective-permute-start(bf16[256,640]{1,0:T(8,128)(2,1)} %get-tuple-element.29), channel_id=1, source_target_pairs={{0,1},{1,0},{2,3},{3,2},{4,5},{5,4},{6,7},{7,6},{8,9},{9,8},{10,11... | collective-permute-start | bytes 983048 | tf_op jit(solution)/shard_map/ppermute | solution.py:46
  108.5 7.7 %copy-start.3 = (bf16[4,256,384]{2,1,0:T(8,128)(2,1)}, bf16[4,256,384]{2,1,0:T(8,128)(2,1)S(1)}, u32[]{:S(2)}) copy-start(bf16[4,256,384]{2,1,0:T(8,128)(2,1)S(1)} %broadcast_select_fusion.refs_6_) | copy-start | bytes 2359300
  108.5 6.6 %copy-start.15 = (f32[3,80,640]{2,1,0:T(8,128)S(1)}, f32[3,80,640]{2,1,0:T(8,128)}, u32[]{:S(2)}) copy-start(f32[3,80,640]{2,1,0:T(8,128)} %get-tuple-element.20) | copy-start | bytes 1843204
  108.5 22.0 %collective-permute-start.28 = (bf16[4,256,384]{2,1,0:T(8,128)(2,1)S(1)}, bf16[4,256,384]{2,1,0:T(8,128)(2,1)}, u32[]{:S(2)}, u32[]{:S(2)}) collective-permute-start(bf16[4,256,384]{2,1,0:T(8,128)(2,1)S(1)} %broadcast_select_fusion.refs_6_), channel_id=1, source_target_pairs={{2,0},{3,1},{6,4},{7,5},{10,8},{11,9},{14,12},{15,13},{18,16},{19,... | collective-permute-start | bytes 2359304 | tf_op jit(solution)/shard_map/ppermute | solution.py:46
  109.9 6.3 %collective-permute-start.20 = (bf16[3,80,640]{2,1,0:T(8,128)(2,1)}, bf16[3,80,640]{2,1,0:T(8,128)(2,1)S(1)}, u32[]{:S(2)}, u32[]{:S(2)}) collective-permute-start(bf16[3,80,640]{2,1,0:T(8,128)(2,1)} %get-tuple-element.16), channel_id=1, source_target_pairs={{0,8},{2,10},{4,12},{6,14},{8,0},{10,2},{12,4},{14,6},{17,25},{19,... | collective-permute-start | bytes 921608 | tf_op jit(solution)/shard_map/ppermute | solution.py:46
  110.6 11.3 %collective-permute-start.21 = (bf16[3,80,640]{2,1,0:T(8,128)(2,1)}, bf16[3,80,640]{2,1,0:T(8,128)(2,1)S(1)}, u32[]{:S(2)}, u32[]{:S(2)}) collective-permute-start(bf16[3,80,640]{2,1,0:T(8,128)(2,1)} %collective-permute-done.17), channel_id=1, source_target_pairs={{1,9},{3,11},{5,13},{7,15},{9,1},{11,3},{13,5},{15,7},{16,24},{18,... | collective-permute-start | bytes 921608 | tf_op jit(solution)/shard_map/ppermute | solution.py:46
  113.7 16.9 %copy-start.7 = (bf16[4,256,256]{2,1,0:T(8,128)(2,1)}, bf16[4,256,256]{2,1,0:T(8,128)(2,1)S(1)}, u32[]{:S(2)}) copy-start(bf16[4,256,256]{2,1,0:T(8,128)(2,1)S(1)} %broadcast_select_fusion.1.refs_6_) | copy-start | bytes 1572868
  113.7 14.3 %copy-start.21 = (f32[1280]{0:T(1024)S(1)}, f32[1280]{0:T(1024)}, u32[]{:S(2)}) copy-start(f32[1280]{0:T(1024)} %param.13) | copy-start | bytes 15364
  113.7 36.3 %collective-permute-start.31 = (bf16[4,256,256]{2,1,0:T(8,128)(2,1)S(1)}, bf16[4,256,256]{2,1,0:T(8,128)(2,1)}, u32[]{:S(2)}, u32[]{:S(2)}) collective-permute-start(bf16[4,256,256]{2,1,0:T(8,128)(2,1)S(1)} %broadcast_select_fusion.1.refs_6_), channel_id=1, source_target_pairs={{2,0},{3,1},{6,4},{7,5},{10,8},{11,9},{14,12},{15,13},{18,16},{19,... | collective-permute-start | bytes 1572872 | tf_op jit(solution)/shard_map/ppermute | solution.py:46
  116.2 22.4 %copy-start.10 = (bf16[3,80,640]{2,1,0:T(8,128)(2,1)}, bf16[3,80,640]{2,1,0:T(8,128)(2,1)S(1)}, u32[]{:S(2)}) copy-start(bf16[3,80,640]{2,1,0:T(8,128)(2,1)S(1)} %broadcast_select_fusion.3.refs_1_) | copy-start | bytes 921604
  116.2 23.8 %collective-permute-start.33 = (f32[3,40,640]{2,1,0:T(8,128)S(1)}, f32[3,40,640]{2,1,0:T(8,128)S(1)}, u32[]{:S(2)}, u32[]{:S(2)}) collective-permute-start(f32[3,40,640]{2,1,0:T(8,128)S(1)} %slice.23), channel_id=1, source_target_pairs={{0,1},{2,3},{4,5},{6,7},{8,9},{10,11},{12,13},{14,15},{17,16},{19,... | collective-permute-start | bytes 921608 | tf_op jit(solution)/shard_map/ppermute | solution.py:46
  121.9 25.6 %collective-permute-start.18 = (bf16[3,80,640]{2,1,0:T(8,128)(2,1)S(1)}, bf16[3,80,640]{2,1,0:T(8,128)(2,1)}, u32[]{:S(2)}, u32[]{:S(2)}) collective-permute-start(bf16[3,80,640]{2,1,0:T(8,128)(2,1)S(1)} %broadcast_select_fusion.3.refs_1_), channel_id=1, source_target_pairs={{0,2},{1,3},{2,0},{3,1},{4,6},{5,7},{6,4},{7,5},{8,10},{9,11},{10,... | collective-permute-start | bytes 921608 | tf_op jit(solution)/shard_map/ppermute | solution.py:46
  125.0 15.1 %copy-start.11 = (bf16[3,80,640]{2,1,0:T(8,128)(2,1)}, bf16[3,80,640]{2,1,0:T(8,128)(2,1)S(1)}, u32[]{:S(2)}) copy-start(bf16[3,80,640]{2,1,0:T(8,128)(2,1)S(1)} %broadcast_select_fusion.2.refs_4_) | copy-start | bytes 921604
  125.0 24.8 %collective-permute-start.22 = (bf16[3,80,640]{2,1,0:T(8,128)(2,1)S(1)}, bf16[3,80,640]{2,1,0:T(8,128)(2,1)}, u32[]{:S(2)}, u32[]{:S(2)}) collective-permute-start(bf16[3,80,640]{2,1,0:T(8,128)(2,1)S(1)} %broadcast_select_fusion.2.refs_4_), channel_id=1, source_target_pairs={{0,4},{1,5},{2,6},{3,7},{4,0},{5,1},{6,2},{7,3},{8,12},{9,13},{10,... | collective-permute-start | bytes 921608 | tf_op jit(solution)/shard_map/ppermute | solution.py:46
  138.6 18.2 %collective-permute-start.24 = (bf16[3,80,640]{2,1,0:T(8,128)(2,1)S(1)}, bf16[3,80,640]{2,1,0:T(8,128)(2,1)}, u32[]{:S(2)}, u32[]{:S(2)}) collective-permute-start(bf16[3,80,640]{2,1,0:T(8,128)(2,1)S(1)} %broadcast_select_fusion.3.refs_1_), channel_id=1, source_target_pairs={{0,4},{1,5},{2,6},{3,7},{4,0},{5,1},{6,2},{7,3},{8,12},{9,13},{10,... | collective-permute-start | bytes 921608 | tf_op jit(solution)/shard_map/ppermute | solution.py:46
  140.0 16.7 %collective-permute-start.25 = (bf16[3,80,640]{2,1,0:T(8,128)(2,1)S(1)}, bf16[3,80,640]{2,1,0:T(8,128)(2,1)}, u32[]{:S(2)}, u32[]{:S(2)}) collective-permute-start(bf16[3,80,640]{2,1,0:T(8,128)(2,1)S(1)} %broadcast_select_fusion.2.refs_4_), channel_id=1, source_target_pairs={{0,2},{1,3},{2,0},{3,1},{4,6},{5,7},{6,4},{7,5},{8,10},{9,11},{10,... | collective-permute-start | bytes 921608 | tf_op jit(solution)/shard_map/ppermute | solution.py:46
  147.6 13.4 %collective-permute-start.19 = (bf16[3,80,640]{2,1,0:T(8,128)(2,1)}, bf16[3,80,640]{2,1,0:T(8,128)(2,1)S(1)}, u32[]{:S(2)}, u32[]{:S(2)}) collective-permute-start(bf16[3,80,640]{2,1,0:T(8,128)(2,1)} %collective-permute-done.18.refs_2_), channel_id=1, source_target_pairs={{0,4},{1,5},{2,6},{3,7},{4,0},{5,1},{6,2},{7,3},{8,12},{9,13},{10,... | collective-permute-start | bytes 921608 | tf_op jit(solution)/shard_map/ppermute | solution.py:46
  149.8 11.1 %collective-permute-start.23 = (bf16[3,80,640]{2,1,0:T(8,128)(2,1)}, bf16[3,80,640]{2,1,0:T(8,128)(2,1)}, u32[]{:S(2)}, u32[]{:S(2)}) collective-permute-start(bf16[3,80,640]{2,1,0:T(8,128)(2,1)} %collective-permute-done.22.refs_5_), channel_id=1, source_target_pairs={{0,2},{1,3},{2,0},{3,1},{4,6},{5,7},{6,4},{7,5},{8,10},{9,11},{10,... | collective-permute-start | bytes 921608 | tf_op jit(solution)/shard_map/ppermute | solution.py:46
  150.0 17.3 %copy-start.8 = (f32[3,40,640]{2,1,0:T(8,128)}, f32[3,40,640]{2,1,0:T(8,128)S(1)}, u32[]{:S(2)}) copy-start(f32[3,40,640]{2,1,0:T(8,128)S(1)} %get-tuple-element.23) | copy-start | bytes 921604
  160.9 0.7 copy-start.19
  165.7 3.1 %collective-permute-start.32 = (bf16[256,640]{1,0:T(8,128)(2,1)}, bf16[256,640]{1,0:T(8,128)(2,1)S(1)}, u32[]{:S(2)}, u32[]{:S(2)}) collective-permute-start(bf16[256,640]{1,0:T(8,128)(2,1)} %get-tuple-element.19), channel_id=1, source_target_pairs={{0,1},{1,0},{2,3},{3,2},{4,5},{5,4},{6,7},{7,6},{8,9},{9,8},{10,11... | collective-permute-start | bytes 983048 | tf_op jit(solution)/shard_map/ppermute | solution.py:46

commit v3 on v2

--- a/solution.py
+++ b/solution.py
@@ -35,7 +35,8 @@
         self.away_swap = [[(dev, dev ^ (8 * k)) for dev in away] for k in range(half)]
         self.z_swap = [[(dev, dev ^ (8 * k)) for dev in range(count)] for k in range(half)]
         self.cross_back = [(dev, (dev + shift) % count) for dev in away]
-        self.z_up = [(dev, dev + 8) for dev in range(count - 8) if dev % 8 < 4]
+        self.z_up_near = [(dev, dev + 8) for dev in range(count - 8) if dev % 8 < 4]
+        self.z_up_far = [(dev, dev + 8) for dev in range(count - 8) if dev % 8 >= 4]
         self.back_x = [(dev, dev - 2) for dev in range(count) if dev % 4 >= 2]
 
     def is_home(self, dev):
@@ -83,30 +84,37 @@
         out_shape=[jax.ShapeDtypeStruct(shape, F32), jax.ShapeDtypeStruct(shape, BF16)],
         in_specs=[vmem(), vmem()],
         out_specs=[vmem(), vmem()],
+        compiler_params=grant(10),
         cost_estimate=pl.CostEstimate(flops=low.size, bytes_accessed=12 * low.size, transcendentals=0),
     )(low, arrived)
 
 
-def update_kernel(part, crossed, weights, momentum, total, applied):
-    grads = part[0] + crossed[0].astype(F32)
-    total[...] = grads
-    applied[...] = updated(weights[...], momentum[...], grads)[0].astype(BF16)
-
-
-def update_pair(part, crossed, weights, momentum):
+def update_kernel(part, crossed, w_own, w_near, m_own, m_near, total, applied):
+    owned = w_own.shape[1]
+    for idx, (weights, momentum) in enumerate(((w_own, m_own), (w_near, m_near))):
+        rows = slice(idx * owned, (idx + 1) * owned)
+        grads = part[0, :, rows] + crossed[0, :, rows].astype(F32)
+        total[idx] = grads
+        applied[:, rows] = updated(weights[...], momentum[...], grads)[0].astype(BF16)
+
+
+def update_pair(part, crossed, *pairs):
+    shape = pairs[0].shape
+    rows = (shape[0], 2 * shape[1], shape[2])
     return pl.pallas_call(
         update_kernel,
         out_shape=[
-            jax.ShapeDtypeStruct(weights.shape, F32),
-            jax.ShapeDtypeStruct(weights.shape, BF16),
+            jax.ShapeDtypeStruct((2,) + shape, F32),
+            jax.ShapeDtypeStruct(rows, BF16),
         ],
-        in_specs=[vmem()] * 4,
+        in_specs=[vmem()] * 6,
         out_specs=[vmem()] * 2,
+        compiler_params=grant(10),
         cost_estimate=pl.CostEstimate(
-            flops=10 * weights.size, bytes_accessed=20 * weights.size, transcendentals=0
+            flops=20 * math.prod(shape), bytes_accessed=40 * math.prod(shape), transcendentals=0
         ),
         name="update",
-    )(part, crossed, weights, momentum)
+    )(part, crossed, *pairs)
 
 
 def nt_dot(left, right):
@@ -121,15 +129,20 @@
     return pl.BlockSpec(memory_space=pltpu.VMEM)
 
 
+def grant(mebibytes):
+    return pltpu.CompilerParams(vmem_limit_bytes=mebibytes << 20)
+
+
 def key_kernel(grad_scale, *refs):
-    k_own, v_own, k_near, v_near, rates = refs[:5]
-    units = refs[5:-5]
+    k_own, v_own, k_near, v_near, r_own, r_near = refs[:6]
+    units = refs[6:-5]
     out, keys, ograd, pair, down = refs[-5:]
     tokens = k_own.shape[1]
     parts = len(units)
     step = units[0].shape[1]
     rows = parts * step
-    by_token = jnp.transpose(rates[...] * (-grad_scale))
+    rates = jnp.concatenate([r_own[...], r_near[...]], axis=0)
+    by_token = jnp.transpose(rates * (-grad_scale))
     for idx, (k_ref, v_ref) in enumerate(((k_own, v_own), (k_near, v_near))):
         for side in range(2):
             at = (2 * idx + side) * tokens
@@ -157,15 +170,15 @@
         out[idx, 2] = second[at : at + step].astype(out.dtype)
 
 
-def key_side(grad_scale, k_own, v_own, k_near, v_near, rates, units, kind):
-    _, tokens, width = k_own.shape
+def key_side(grad_scale, tokens_in, units, kind):
+    _, tokens, width = tokens_in[0].shape
     parts = len(units)
     step = units[0].shape[1]
     rows = parts * step
     return pl.pallas_call(
         lambda *refs: key_kernel(grad_scale, *refs),
         out_shape=jax.ShapeDtypeStruct((parts, 3, step, width), kind),
-        in_specs=[vmem()] * (5 + parts),
+        in_specs=[vmem()] * (6 + parts),
         out_specs=vmem(),
         scratch_shapes=[
             pltpu.VMEM((4 * tokens, width), BF16),
@@ -173,12 +186,13 @@
             pltpu.VMEM((2 * rows, width), BF16),
             pltpu.VMEM((rows, width), BF16),
         ],
+        compiler_params=grant(30),
         cost_estimate=pl.CostEstimate(
             flops=12 * 4 * tokens * rows * width,
             bytes_accessed=16 * tokens * width,
             transcendentals=0,
         ),
-    )(k_own, v_own, k_near, v_near, rates, *units)
+    )(*tokens_in, *units)
 
 
 def load_rows(pieces, weights):
@@ -188,7 +202,7 @@
 
 
 def fast_product(quer_in, weights):
-    quer = jnp.concatenate([quer_in[0], quer_in[1]], axis=0)
+    quer = jnp.concatenate([part[...] for part in quer_in], axis=0)
     gate = nt_dot(quer, weights[0])
     up = nt_dot(quer, weights[1])
     hidden = (gate * jax.nn.sigmoid(gate) * up).astype(BF16)
@@ -196,36 +210,37 @@
 
 
 def query_first_kernel(count, *refs):
-    quer_in = refs[0]
-    out, weights = refs[1 + count :]
-    load_rows(refs[1 : 1 + count], weights)
+    quer_in = refs[:2]
+    out, weights = refs[2 + count :]
+    load_rows(refs[2 : 2 + count], weights)
     out[...] = fast_product(quer_in, weights)
 
 
 def query_first(quer_in, pieces):
-    _, tokens, width = quer_in.shape
+    tokens, width = quer_in[0].shape
     count = len(pieces)
     rows = pieces[0].shape[1]
     return pl.pallas_call(
         lambda *refs: query_first_kernel(count, *refs),
         out_shape=jax.ShapeDtypeStruct((2 * tokens, width), F32),
-        in_specs=[vmem()] * (1 + count),
+        in_specs=[vmem()] * (2 + count),
         out_specs=vmem(),
         scratch_shapes=[pltpu.VMEM((3, count * rows, width), BF16)],
+        compiler_params=grant(24),
         cost_estimate=pl.CostEstimate(
             flops=12 * tokens * count * rows * width,
             bytes_accessed=6 * count * rows * width,
             transcendentals=0,
         ),
         name="query_first",
-    )(quer_in, *pieces)
+    )(*quer_in, *pieces)
 
 
 def query_last_kernel(count, *refs):
-    where, quer_in = refs[:2]
-    sums, gain, att_a, att_b, own, other, weights = refs[2 + count :]
+    where, quer_in = refs[0], refs[1:3]
+    sums, gain, att_a, att_b, own, other, weights = refs[3 + count :]
     tokens, width = other.shape
-    load_rows(refs[2 : 2 + count], weights)
+    load_rows(refs[3 : 3 + count], weights)
     fast = sums[...] + fast_product(quer_in, weights)
     scale = lax.rsqrt(jnp.mean(fast * fast, axis=-1, keepdims=True) + EPS)
     normed = fast * scale * gain[...]
@@ -240,7 +255,7 @@
 
 
 def query_last(where, quer_in, pieces, sums, gain, atts):
-    _, tokens, width = quer_in.shape
+    tokens, width = quer_in[0].shape
     count = len(pieces)
     rows = pieces[0].shape[1]
     return pl.pallas_call(
@@ -249,21 +264,22 @@
             jax.ShapeDtypeStruct((tokens, 2 * width), BF16),
             jax.ShapeDtypeStruct((tokens, width), BF16),
         ],
-        in_specs=[pl.BlockSpec(memory_space=pltpu.SMEM)] + [vmem()] * (5 + count),
+        in_specs=[pl.BlockSpec(memory_space=pltpu.SMEM)] + [vmem()] * (6 + count),
         out_specs=[vmem()] * 2,
         scratch_shapes=[pltpu.VMEM((3, count * rows, width), BF16)],
+        compiler_params=grant(24),
         cost_estimate=pl.CostEstimate(
             flops=12 * tokens * count * rows * width,
             bytes_accessed=6 * count * rows * width,
             transcendentals=0,
         ),
         name="query_last",
-    )(where, quer_in, *pieces, sums, gain, *atts)
-
-
-def att_kernel(low, where, quer_in, k_own, v_own, k_near, v_near, two, back, out,
+    )(where, *quer_in, *pieces, sums, gain, *atts)
+
+
+def att_kernel(low, where, q_kept, q_came, k_own, v_own, k_near, v_near, two, back, out,
                quer, keys, vals, bias):
-    tokens = quer_in.shape[1]
+    tokens = q_kept.shape[0]
     span = 2 * tokens
     reach = WINDOW + span
     wide = out.shape[1]
@@ -276,7 +292,7 @@
         dest[pl.ds(pl.multiple_of(base + mine, tokens), tokens), :] = first
         dest[pl.ds(pl.multiple_of(base + theirs, tokens), tokens), :] = second
 
-    put(quer, 0, quer_in[0, :, cols], quer_in[1, :, cols])
+    put(quer, 0, q_kept[:, cols], q_came[:, cols])
     for idx, (dest, own, near) in enumerate(((keys, k_own, k_near), (vals, v_own, v_near))):
         put(dest, 2 * span, own[0, :, cols], own[1, :, cols])
         put(dest, 0, two[2 * idx], two[2 * idx + 1])
@@ -305,7 +321,7 @@
 
 
 def attention(where, quer_in, k_own, v_own, k_near, v_near, two, back, low):
-    _, tokens, _ = quer_in.shape
+    tokens = quer_in[0].shape[0]
     wide = two.shape[2]
     span = 2 * tokens
     reach = WINDOW + span
@@ -313,7 +329,7 @@
     return pl.pallas_call(
         lambda *refs: att_kernel(low, *refs),
         out_shape=jax.ShapeDtypeStruct((span, wide), F32),
-        in_specs=[pl.BlockSpec(memory_space=pltpu.SMEM)] + [vmem()] * 7,
+        in_specs=[pl.BlockSpec(memory_space=pltpu.SMEM)] + [vmem()] * 8,
         out_specs=vmem(),
         scratch_shapes=[
             pltpu.VMEM((span, wide), BF16),
@@ -321,12 +337,13 @@
             pltpu.VMEM((reach, wide), BF16),
             pltpu.VMEM((span, reach), F32),
         ],
+        compiler_params=grant(30),
         cost_estimate=pl.CostEstimate(
             flops=4 * span * reach * wide,
             bytes_accessed=40 * tokens * wide,
             transcendentals=span * reach * wide // ATT_DIM,
         ),
-    )(where, quer_in, k_own, v_own, k_near, v_near, two, back)
+    )(where, *quer_in, k_own, v_own, k_near, v_near, two, back)
 
 
 def updated(weights, momentum, grads):
@@ -344,7 +361,6 @@
     routes = Routes(count)
     local_tokens = queries.shape[0]
     heads, width = step_rates.shape[0], fast_weights.shape[2]
-    owned = fast_weights.shape[1]
     assert heads == 2
     here = lax.axis_index("seq")
     core = here % 2
@@ -354,63 +370,66 @@
 
     my_rate = lax.dynamic_slice_in_dim(step_rates, core, 1, 0)
     their_rate = lax.dynamic_slice_in_dim(step_rates, 1 - core, 1, 0)
-    rates = jnp.concatenate([my_rate, send(their_rate, routes.partner)], axis=0)
-    rates = jnp.concatenate([rates, send(rates, routes.x_swap)], axis=0)
+    r_own = jnp.concatenate([my_rate, send(their_rate, routes.partner)], axis=0)
+    r_near = send(r_own, routes.x_swap)
 
     def by_core(array):
         kept = lax.dynamic_slice_in_dim(array, core * width, width, 1)
         sent = lax.dynamic_slice_in_dim(array, (1 - core) * width, width, 1)
-        return jnp.stack([kept, send(sent, routes.partner)])
-
-    k_own = by_core(key_rows)
-    v_own = by_core(value_rows)
+        return kept, send(sent, routes.partner)
+
+    k_own = jnp.stack(by_core(key_rows))
+    v_own = jnp.stack(by_core(value_rows))
     q_own = by_core(queries)
 
-    pair_weights = jnp.concatenate([fast_weights, send(fast_weights, routes.pair_in)], axis=1)
+    their_weights = send(fast_weights, routes.pair_in)
+    their_momentum = send(momentum, routes.pair_in)
 
     k_near = send(k_own, routes.x_swap)
     v_near = send(v_own, routes.x_swap)
-    cut = 3 * ATT_DIM
+    cut = 2 * ATT_DIM
     early = jnp.concatenate([k_own[:, :, :cut], v_own[:, :, :cut]], axis=0)
     late = jnp.concatenate([k_own[:, :, cut:], v_own[:, :, cut:]], axis=0)
-    unit = pair_weights.astype(BF16)
+    unit = jnp.concatenate([fast_weights.astype(BF16), their_weights.astype(BF16)], axis=1)
     units = gather_z(unit, routes, is_home)
     side_units = [send(part, routes.y_swap) for part in units]
     grad_scale = 1.0 / math.sqrt(local_tokens * count)
-    tokens_in = (k_own, v_own, k_near, v_near, rates)
+    tokens_in = (k_own, v_own, k_near, v_near, r_own, r_near)
 
     upper = chip // 2 % 2 == 1
     early_y = send(early, routes.y_swap)
-    early_z = send(early_y, routes.z_up)
+    early_z = send(early_y, routes.z_up_near)
     early_two = jnp.where(upper, early_y, early_z)
     early_back = send(early_two, routes.back_x)
-    late, _ = lax.optimization_barrier((late, side_units))
-    late_y = send(late, routes.y_swap)
-    late_z = send(late_y, routes.z_up)
-    late_two = jnp.where(upper, late_y, late_z)
+    late_in, _ = lax.optimization_barrier((late, units))
+    late_z = send(late_in, routes.z_up_far)
+
+    side_grads = key_side(grad_scale, tokens_in, side_units, BF16)
+    side_in = send(side_grads, routes.y_swap)
+    own_grads = key_side(grad_scale, tokens_in, units, F32)
+    late_turn = jnp.where(upper, late_z, late)
+    side_in, late_turn = lax.optimization_barrier((side_in, late_turn))
+    late_two = send(late_turn, routes.y_swap)
     late_back = send(late_two, routes.back_x)
-
-    side_grads = key_side(grad_scale, *tokens_in, side_units, BF16)
-    side_in = send(side_grads, routes.y_swap)
-    own_grads = key_side(grad_scale, *tokens_in, units, F32)
     part, sent = fold(own_grads, side_in)
     for bit in reversed(routes.bits):
         part, sent = fold(part, send(sent, routes.z_swap[bit]))
     crossed = send(sent, routes.cross_back)
-    their_momentum = send(momentum, routes.pair_in)
-    pair_momentum = jnp.concatenate([momentum, their_momentum], axis=1)
     att_in = (where, q_own, k_own, v_own, k_near, v_near)
     early_att = attention(*att_in, early_two, early_back, 0)
     late_att = attention(*att_in, late_two, late_back, cut)
 
-    total, pair_new = update_pair(part, crossed, pair_weights, pair_momentum)
+    total, pair_new = update_pair(
+        part, crossed, fast_weights, their_weights, momentum, their_momentum
+    )
     applied = gather_plane(gather_z(pair_new, routes, is_home), routes)
-    partner_grads = send(total[:, owned:], routes.pair_out)
-    grads = jnp.where(is_home, total[:, :owned], partner_grads)
+    partner_grads = send(total[1], routes.pair_out)
+    grads = jnp.where(is_home, total[0], partner_grads)
     new_weights, new_momentum = updated(fast_weights, momentum, grads)
     gain = lax.dynamic_slice_in_dim(out_gain, core * width, width, 0).reshape(1, width)
-    soon = [piece for idx, piece in enumerate(applied) if idx % 4 != 3]
-    last = applied[3::4]
+    soon = [piece for idx, piece in enumerate(applied) if idx % 4 < 2]
+    last = [piece for idx, piece in enumerate(applied) if idx % 4 >= 2]
+    new_weights, new_momentum, gain = lax.optimization_barrier((new_weights, new_momentum, gain))
     sums = query_first(q_own, soon)
     own, other = query_last(where, q_own, last, sums, gain, (early_att, late_att))
     arrived = send(other, routes.partner)

time: 171 us -> 148 us (0.87)
  Pallas kernels: 39.8 us -> 20.9 us
  starting transfers between devices: 62 us -> 54.4 us
  waiting for transfers between devices: 50.5 us -> 56.9 us
    ppermute x34, starting transfers between devices: 62 us -> 54.4 us  [send(): return lax.ppermute(array, 'seq', route)]
    ppermute x34, waiting for transfers between devices: 50.5 us -> 56.9 us  [send(): return lax.ppermute(array, 'seq', route)]
    pallas_call x2, Pallas kernels: 9.61 us -> 4.94 us  [key_side(): pl.pallas_call(lambda *refs: key_kernel(grad_scale, *refs), out_shape=jax...]
    pallas_call x2, Pallas kernels: 4.56 us -> 0.23 us  [fold(): pl.pallas_call(lambda *refs: fold_kernel(0, count - half, *refs), out_sha...]
    pallas_call x2, Pallas kernels: 14.8 us -> 10.5 us  [attention(): pl.pallas_call(lambda *refs: att_kernel(low, *refs), out_shape=jax.ShapeD...]
    pallas_call x1, Pallas kernels: 4.17 us -> 1.31 us  [query_first(): pl.pallas_call(lambda *refs: query_first_kernel(count, *refs), out_shape=...]
    unnamed x51 -> x46, local copies, waits for them, and re-layouts: 4.65 us -> 3.71 us
  transfers between devices with their start and end apart: 34 -> 34, of which waited for: 10 -> 11; matrix products, arithmetic and copies ran while one was open for 6% -> 6% of each run, Pallas kernels for 21% -> 12%
where the time goes in v3:
time: 148 us; the launch traced here: 147 us
  waiting for transfers between devices  56.9 us (38%)
  starting transfers between devices  54.4 us (37%)
  Pallas kernels  20.9 us (14%)
  local copies, waits for them, and re-layouts  7.39 us (5%)
  other arithmetic  6.55 us (4%)
    ppermute x34, waiting for transfers between devices, send(): return lax.ppermute(array, 'seq', route)  56.9 us
    ppermute x34, starting transfers between devices, send(): return lax.ppermute(array, 'seq', route)  54.4 us
    pallas_call x2, Pallas kernels, attention(): pl.pallas_call(lambda *refs: att_kernel(low, *refs), out_shape=jax.ShapeD...  10.5 us
    pallas_call x2, Pallas kernels, key_side(): pl.pallas_call(lambda *refs: key_kernel(grad_scale, *refs), out_shape=jax...  4.94 us
    unnamed x46, local copies, waits for them, and re-layouts  3.71 us
  transfers between devices with their start and end apart: 34, of which 11 were waited for; matrix products, arithmetic and copies ran while one was open for 6% of the time, Pallas kernels for 12%

profile of v3, /device:TPU:1, one launch (start us, length us, event | category | flops | bytes accessed | tf_op | source)
XLA Modules:
  0.0 147.4 jit_solution(15597283035315500874)
XLA Ops:
  0.7 0.8 constant_dynamic-slice_fusion.1
  1.4 2.4 %collective-permute-start.7 = (f32[3,40,640]{2,1,0:T(8,128)}, f32[3,40,640]{2,1,0:T(8,128)S(1)}, u32[]{:S(2)}, u32[]{:S(2)}) collective-permute-start(f32[3,40,640]{2,1,0:T(8,128)} %w_own.1), channel_id=1, source_target_pairs={{1,0},{3,2},{5,4},{7,6},{9,8},{11,10},{13,12},{15,14},{16,17},{18,... | collective-permute-start | bytes 921608 | tf_op jit(solution)/shard_map/ppermute | solution.py:47
  3.9 1.2 dynamic-slice_bitcast_fusion.1
  5.3 0.5 collective-permute-start.2
  5.9 2.3 %collective-permute-start.6 = (f32[2,256]{1,0:T(2,128)S(1)}, f32[2,256]{1,0:T(2,128)S(1)}, u32[]{:S(2)}, u32[]{:S(2)}) collective-permute-start(f32[2,256]{1,0:T(2,128)S(1)} %pad_maximum_fusion.5.refs_4_), channel_id=1, source_target_pairs={{0,2},{1,3},{2,0},{3,1},{4,6},{5,7},{6,4},{7,5},{8,10},{9,11},{10,... | collective-permute-start | bytes 6152 | tf_op jit(solution)/shard_map/ppermute | solution.py:47
  8.2 0.7 collective-permute-start.9
  8.9 1.3 collective-permute-start.8
  10.4 0.5 copy-done.17
  10.9 0.1 copy-done.15
  11.1 0.1 collective-permute-start.4
  11.2 1.4 collective-permute-start.3
  12.6 1.0 fusion
  13.6 1.0 pad_maximum_fusion.2
  14.6 8.0 %collective-permute-done.8 = bf16[3,80,640]{2,1,0:T(8,128)(2,1)S(1)} collective-permute-done((bf16[3,80,640]{2,1,0:T(8,128)(2,1)S(1)}, bf16[3,80,640]{2,1,0:T(8,128)(2,1)S(1)}, u32[]{:S(2)}, u32[]{:S(2)}) %collective-permute-start.8) | collective-permute-done | bytes 307232 | tf_op jit(solution)/shard_map/ppermute | solution.py:47
  22.6 1.9 %collective-permute-start.10 = (bf16[3,80,640]{2,1,0:T(8,128)(2,1)S(1)}, bf16[3,80,640]{2,1,0:T(8,128)(2,1)S(1)}, u32[]{:S(2)}, u32[]{:S(2)}) collective-permute-start(bf16[3,80,640]{2,1,0:T(8,128)(2,1)S(1)} %collective-permute-done.8), channel_id=1, source_target_pairs={{1,9},{3,11},{5,13},{7,15},{9,1},{11,3},{13,5},{15,7},{16,24},{18,... | collective-permute-start | bytes 921608 | tf_op jit(solution)/shard_map/ppermute | solution.py:47
  24.7 1.3 collective-permute-start.11
  26.0 4.5 %collective-permute-done.10 = bf16[3,80,640]{2,1,0:T(8,128)(2,1)S(1)} collective-permute-done((bf16[3,80,640]{2,1,0:T(8,128)(2,1)S(1)}, bf16[3,80,640]{2,1,0:T(8,128)(2,1)S(1)}, u32[]{:S(2)}, u32[]{:S(2)}) %collective-permute-start.10) | collective-permute-done | bytes 307232 | tf_op jit(solution)/shard_map/ppermute | solution.py:47
  30.5 1.3 collective-permute-start.12
  31.8 1.5 %collective-permute-start.14 = (bf16[4,256,384]{2,1,0:T(8,128)(2,1)}, bf16[4,256,384]{2,1,0:T(8,128)(2,1)}, u32[]{:S(2)}, u32[]{:S(2)}) collective-permute-start(bf16[4,256,384]{2,1,0:T(8,128)(2,1)} %pad_maximum_fusion.2), channel_id=1, source_target_pairs={{4,12},{5,13},{6,14},{7,15},{12,20},{13,21},{14,22},{15,23},{20,28... | collective-permute-start | bytes 2359304 | tf_op jit(solution)/shard_map/ppermute | solution.py:47
  33.4 0.8 pad_maximum_fusion.3
  34.3 1.5 %collective-permute-start.28 = (bf16[4,256,256]{2,1,0:T(8,128)(2,1)}, bf16[4,256,256]{2,1,0:T(8,128)(2,1)}, u32[]{:S(2)}, u32[]{:S(2)}) collective-permute-start(bf16[4,256,256]{2,1,0:T(8,128)(2,1)} %pad_maximum_fusion.3), channel_id=1, source_target_pairs={{0,4},{1,5},{2,6},{3,7},{4,0},{5,1},{6,2},{7,3},{8,12},{9,13},{10,... | collective-permute-start | bytes 1572872 | tf_op jit(solution)/shard_map/ppermute | solution.py:47
  35.7 1.8 %collective-permute-done.3.refs_2_.refs_5_ = bf16[2,256,640]{2,1,0:T(8,128)(2,1)S(1)} collective-permute-done((bf16[2,256,640]{2,1,0:T(8,128)(2,1)S(1)}, bf16[2,256,640]{2,1,0:T(8,128)(2,1)S(1)}, u32[]{:S(2)}, u32[]{:S(2)}) %collective-permute-start.3) | collective-permute-done | bytes 655392 | tf_op jit(solution)/shard_map/ppermute | solution.py:47
  37.6 3.2 %collective-permute-done.12.refs_7_ = bf16[3,80,640]{2,1,0:T(8,128)(2,1)S(1)} collective-permute-done((bf16[3,80,640]{2,1,0:T(8,128)(2,1)S(1)}, bf16[3,80,640]{2,1,0:T(8,128)(2,1)S(1)}, u32[]{:S(2)}, u32[]{:S(2)}) %collective-permute-start.12) | collective-permute-done | bytes 307232 | tf_op jit(solution)/shard_map/ppermute | solution.py:47
  40.7 2.9 %shard_map.95 = bf16[2,3,80,640]{3,2,1,0:T(8,128)(2,1)} custom-call(bf16[2,256,640]{2,1,0:T(8,128)(2,1)S(1)} %pad_maximum_fusion.refs_0_.refs_3_, bf16[2,256,640]{2,1,0:T(8,128)(2,1)S(1)} %pad_maximum_fusion.1.refs_1_.refs_4_, bf16[2,256,640]{2,1,0:T(8,128)(2,1)S(1)} %collective-permute-done.3.refs_2_.refs_5_, ...), custom_call_target="tpu_custom_call" | custom-call | flops 1258291200 | bytes 2621440 | tf_op jit(solution)/shard_map/pallas_call | solution.py:178
  43.6 1.0 collective-permute-start.13
  44.6 3.4 %collective-permute-done.28 = bf16[4,256,256]{2,1,0:T(8,128)(2,1)} collective-permute-done((bf16[4,256,256]{2,1,0:T(8,128)(2,1)}, bf16[4,256,256]{2,1,0:T(8,128)(2,1)}, u32[]{:S(2)}, u32[]{:S(2)}) %collective-permute-start.28) | collective-permute-done | bytes 524320 | tf_op jit(solution)/shard_map/ppermute | solution.py:47
  48.0 3.6 %collective-permute-start.29 = (bf16[4,256,256]{2,1,0:T(8,128)(2,1)}, bf16[4,256,256]{2,1,0:T(8,128)(2,1)S(1)}, u32[]{:S(2)}, u32[]{:S(2)}) collective-permute-start(bf16[4,256,256]{2,1,0:T(8,128)(2,1)} %collective-permute-done.28), channel_id=1, source_target_pairs={{0,8},{1,9},{2,10},{3,11},{8,16},{9,17},{10,18},{11,19},{16,24},{1... | collective-permute-start | bytes 1572872 | tf_op jit(solution)/shard_map/ppermute | solution.py:47
  51.6 1.1 copy-done.2
  52.7 2.0 %shard_map.94.refs_0_ = f32[2,3,80,640]{3,2,1,0:T(8,128)S(1)} custom-call(bf16[2,256,640]{2,1,0:T(8,128)(2,1)S(1)} %pad_maximum_fusion.refs_0_.refs_3_, bf16[2,256,640]{2,1,0:T(8,128)(2,1)S(1)} %pad_maximum_fusion.1.refs_1_.refs_4_, bf16[2,256,640]{2,1,0:T(8,128)(2,1)S(1)} %copy-done.2, bf16[2,256,640]{2,1,0:T(8,128)(2,1)S(1)} %collective-permute-done.4.refs_3_.refs_6_, ...), custom_call_target="tpu_custom_call" | custom-call | flops 1258291200 | bytes 2621440 | tf_op jit(solution)/shard_map/pallas_call | solution.py:178
  54.8 1.0 broadcast_select_fusion
  55.9 5.0 %collective-permute-done.13.refs_1_ = bf16[2,3,80,640]{3,2,1,0:T(8,128)(2,1)S(1)} collective-permute-done((bf16[2,3,80,640]{3,2,1,0:T(8,128)(2,1)}, bf16[2,3,80,640]{3,2,1,0:T(8,128)(2,1)S(1)}, u32[]{:S(2)}, u32[]{:S(2)}) %collective-permute-start.13) | collective-permute-done | bytes 614432 | tf_op jit(solution)/shard_map/ppermute | solution.py:47
  60.9 0.1 shard_map.96
  61.1 1.9 %collective-permute-start.15 = (bf16[1,3,80,640]{3,2,1,0:T(8,128)(2,1)S(1)}, bf16[1,3,80,640]{3,2,1,0:T(8,128)(2,1)S(1)}, u32[]{:S(2)}, u32[]{:S(2)}) collective-permute-start(bf16[1,3,80,640]{3,2,1,0:T(8,128)(2,1)S(1)} %get-tuple-element.20), channel_id=1, source_target_pairs={{0,8},{1,9},{2,10},{3,11},{4,12},{5,13},{6,14},{7,15},{8,0},{9,1},... | collective-permute-start | bytes 921608 | tf_op jit(solution)/shard_map/ppermute | solution.py:47
  63.0 4.6 %collective-permute-start.17 = (f32[3,40,640]{2,1,0:T(8,128)S(1)}, f32[3,40,640]{2,1,0:T(8,128)S(1)}, u32[]{:S(2)}, u32[]{:S(2)}) collective-permute-start(f32[3,40,640]{2,1,0:T(8,128)S(1)} %copy-done.7), channel_id=1, source_target_pairs={{1,0},{3,2},{5,4},{7,6},{9,8},{11,10},{13,12},{15,14},{16,17},{18,... | collective-permute-start | bytes 921608 | tf_op jit(solution)/shard_map/ppermute | solution.py:47
  67.6 0.5 collective-permute-done.15.refs_1_
  68.3 7.2 %collective-permute-start.16 = (bf16[1,3,80,640]{3,2,1,0:T(8,128)(2,1)S(1)}, bf16[1,3,80,640]{3,2,1,0:T(8,128)(2,1)S(1)}, u32[]{:S(2)}, u32[]{:S(2)}) collective-permute-start(bf16[1,3,80,640]{3,2,1,0:T(8,128)(2,1)S(1)} %get-tuple-element.22), channel_id=1, source_target_pairs={{1,17},{3,19},{5,21},{7,23},{9,25},{11,27},{13,29},{15,31},{16,0},... | collective-permute-start | bytes 921608 | tf_op jit(solution)/shard_map/ppermute | solution.py:47
  75.5 1.3 collective-permute-start.30
  76.8 1.9 %collective-permute-start.31 = (bf16[4,256,384]{2,1,0:T(8,128)(2,1)}, bf16[4,256,384]{2,1,0:T(8,128)(2,1)}, u32[]{:S(2)}, u32[]{:S(2)}) collective-permute-start(bf16[4,256,384]{2,1,0:T(8,128)(2,1)} %broadcast_select_fusion), channel_id=1, source_target_pairs={{0,4},{1,5},{2,6},{3,7},{4,0},{5,1},{6,2},{7,3},{8,12},{9,13},{10,... | collective-permute-start | bytes 2359304 | tf_op jit(solution)/shard_map/ppermute | solution.py:47
  78.7 0.8 constant_dynamic-slice_fusion.4
  79.6 1.1 update.1
  80.6 0.8 copy-done.9
  81.4 1.3 collective-permute-start.18
  82.9 6.3 %collective-permute-done.30.refs_8_ = bf16[4,256,256]{2,1,0:T(8,128)(2,1)} collective-permute-done((bf16[4,256,256]{2,1,0:T(8,128)(2,1)S(1)}, bf16[4,256,256]{2,1,0:T(8,128)(2,1)}, u32[]{:S(2)}, u32[]{:S(2)}) %collective-permute-start.30) | collective-permute-done | bytes 524320 | tf_op jit(solution)/shard_map/ppermute | solution.py:47
  89.2 1.1 copy-done.3
  90.3 4.7 %shard_map.98.refs_9_ = f32[512,256]{1,0:T(8,128)S(1)} custom-call(s32[3]{0:T(128)S(1)} %pad_add_fusion.refs_0_, bf16[256,640]{1,0:T(8,128)(2,1)S(1)} %get-tuple-element.39.refs_0_.refs_1_, bf16[256,640]{1,0:T(8,128)(2,1)S(1)} %collective-permute-done.refs_1_.refs_2_, bf16[2,256,640]{2,1,0:T(8,128)(2,1)S(1)} %pad_maximum_fusion.refs_0_.refs_3_, ...), custom_call_target="tpu_custom_call" | custom-call | flops 805306368 | bytes 2621440 | tf_op jit(solution)/shard_map/pallas_call | solution.py:329
  95.1 0.8 collective-permute-start.22
  95.9 3.4 %collective-permute-start.23 = (bf16[3,80,640]{2,1,0:T(8,128)(2,1)}, bf16[3,80,640]{2,1,0:T(8,128)(2,1)S(1)}, u32[]{:S(2)}, u32[]{:S(2)}) collective-permute-start(bf16[3,80,640]{2,1,0:T(8,128)(2,1)} %collective-permute-done.18), channel_id=1, source_target_pairs={{1,9},{3,11},{5,13},{7,15},{9,1},{11,3},{13,5},{15,7},{16,24},{18,... | collective-permute-start | bytes 921608 | tf_op jit(solution)/shard_map/ppermute | solution.py:47
  99.4 1.3 collective-permute-start.27
  100.7 1.5 collective-permute-start.32
  102.2 1.0 broadcast_select_fusion.3.refs_2_
  103.2 2.2 %collective-permute-start.20 = (bf16[3,80,640]{2,1,0:T(8,128)(2,1)S(1)}, bf16[3,80,640]{2,1,0:T(8,128)(2,1)S(1)}, u32[]{:S(2)}, u32[]{:S(2)}) collective-permute-start(bf16[3,80,640]{2,1,0:T(8,128)(2,1)S(1)} %broadcast_select_fusion.3.refs_2_), channel_id=1, source_target_pairs={{0,2},{1,3},{2,0},{3,1},{4,6},{5,7},{6,4},{7,5},{8,10},{9,11},{10,... | collective-permute-start | bytes 921608 | tf_op jit(solution)/shard_map/ppermute | solution.py:47
  105.4 1.9 %collective-permute-start.19 = (bf16[3,80,640]{2,1,0:T(8,128)(2,1)S(1)}, bf16[3,80,640]{2,1,0:T(8,128)(2,1)S(1)}, u32[]{:S(2)}, u32[]{:S(2)}) collective-permute-start(bf16[3,80,640]{2,1,0:T(8,128)(2,1)S(1)} %broadcast_select_fusion.3.refs_2_), channel_id=1, source_target_pairs={{0,4},{1,5},{2,6},{3,7},{4,0},{5,1},{6,2},{7,3},{8,12},{9,13},{10,... | collective-permute-start | bytes 921608 | tf_op jit(solution)/shard_map/ppermute | solution.py:47
  107.3 0.3 collective-permute-start.25
  107.6 0.2 multiply_reduce_fusion.1
  107.9 19.5 %collective-permute-done.20.refs_3_ = bf16[3,80,640]{2,1,0:T(8,128)(2,1)S(1)} collective-permute-done((bf16[3,80,640]{2,1,0:T(8,128)(2,1)S(1)}, bf16[3,80,640]{2,1,0:T(8,128)(2,1)S(1)}, u32[]{:S(2)}, u32[]{:S(2)}) %collective-permute-start.20) | collective-permute-done | bytes 307232 | tf_op jit(solution)/shard_map/ppermute | solution.py:47
  127.3 1.9 %collective-permute-start.21 = (bf16[3,80,640]{2,1,0:T(8,128)(2,1)S(1)}, bf16[3,80,640]{2,1,0:T(8,128)(2,1)S(1)}, u32[]{:S(2)}, u32[]{:S(2)}) collective-permute-start(bf16[3,80,640]{2,1,0:T(8,128)(2,1)S(1)} %collective-permute-done.20.refs_3_), channel_id=1, source_target_pairs={{0,4},{1,5},{2,6},{3,7},{4,0},{5,1},{6,2},{7,3},{8,12},{9,13},{10,... | collective-permute-start | bytes 921608 | tf_op jit(solution)/shard_map/ppermute | solution.py:47
  129.2 0.8 multiply_multiply_fusion
  130.0 1.3 query_first.1.refs_7_
  131.4 5.8 %shard_map.99.refs_10_ = f32[512,384]{1,0:T(8,128)S(1)} custom-call(s32[3]{0:T(128)S(1)} %pad_add_fusion.refs_0_, bf16[256,640]{1,0:T(8,128)(2,1)S(1)} %get-tuple-element.39.refs_0_.refs_1_, bf16[256,640]{1,0:T(8,128)(2,1)S(1)} %collective-permute-done.refs_1_.refs_2_, bf16[2,256,640]{2,1,0:T(8,128)(2,1)S(1)} %pad_maximum_fusion.refs_0_.refs_3_, ...), custom_call_target="tpu_custom_call" | custom-call | flops 1207959552 | bytes 3932160 | tf_op jit(solution)/shard_map/pallas_call | solution.py:329
  137.2 3.3 %collective-permute-done.26.refs_6_ = bf16[3,80,640]{2,1,0:T(8,128)(2,1)S(1)} collective-permute-done((bf16[3,80,640]{2,1,0:T(8,128)(2,1)S(1)}, bf16[3,80,640]{2,1,0:T(8,128)(2,1)S(1)}, u32[]{:S(2)}, u32[]{:S(2)}) %collective-permute-start.26) | collective-permute-done | bytes 307232 | tf_op jit(solution)/shard_map/ppermute | solution.py:47
  140.5 2.9 %query_last.1 = (bf16[256,1280]{1,0:T(8,128)(2,1)}, bf16[256,640]{1,0:T(8,128)(2,1)S(1)}) custom-call(s32[3]{0:T(128)S(1)} %pad_add_fusion.refs_0_, bf16[256,640]{1,0:T(8,128)(2,1)S(1)} %get-tuple-element.39.refs_0_.refs_1_, bf16[256,640]{1,0:T(8,128)(2,1)S(1)} %collective-permute-done.refs_1_.refs_2_, ...), custom_call_target="tpu_custom_call" | custom-call | flops 629145600 | bytes 1228800 | tf_op jit(solution)/shard_map/query_last/pallas_call | solution.py:261
  143.4 2.0 %collective-permute-start.33 = (bf16[256,640]{1,0:T(8,128)(2,1)S(1)}, bf16[256,640]{1,0:T(8,128)(2,1)S(1)}, u32[]{:S(2)}, u32[]{:S(2)}) collective-permute-start(bf16[256,640]{1,0:T(8,128)(2,1)S(1)} %get-tuple-element.28), channel_id=1, source_target_pairs={{0,1},{1,0},{2,3},{3,2},{4,5},{5,4},{6,7},{7,6},{8,9},{9,8},{10,11... | collective-permute-start | bytes 983048 | tf_op jit(solution)/shard_map/ppermute | solution.py:47
  145.4 1.3 collective-permute-done.33
  146.6 0.8 constant_dynamic-update-slice_fusion
  (89 shorter events, 1.3 us)
Async XLA Ops:
  0.6 4.5 %copy-start.20 = (bf16[256,1280]{1,0:T(8,128)(2,1)S(1)}, bf16[256,1280]{1,0:T(8,128)(2,1)}, u32[]{:S(2)}) copy-start(bf16[256,1280]{1,0:T(8,128)(2,1)} %param.9) | copy-start | bytes 1966084
  1.4 4.4 %collective-permute-start.5 = (f32[1,256]{1,0:T(1,128)S(1)}, f32[1,256]{1,0:T(1,128)S(1)}, u32[]{:S(2)}, u32[]{:S(2)}) collective-permute-start(f32[1,256]{1,0:T(1,128)S(1)} %get-tuple-element.41), channel_id=1, source_target_pairs={{0,1},{1,0},{2,3},{3,2},{4,5},{5,4},{6,7},{7,6},{8,9},{9,8},{10,11... | collective-permute-start | bytes 3080 | tf_op jit(solution)/shard_map/ppermute | solution.py:47
  1.4 6.7 %collective-permute-start.7 = (f32[3,40,640]{2,1,0:T(8,128)}, f32[3,40,640]{2,1,0:T(8,128)S(1)}, u32[]{:S(2)}, u32[]{:S(2)}) collective-permute-start(f32[3,40,640]{2,1,0:T(8,128)} %w_own.1), channel_id=1, source_target_pairs={{1,0},{3,2},{5,4},{7,6},{9,8},{11,10},{13,12},{15,14},{16,17},{18,... | collective-permute-start | bytes 921608 | tf_op jit(solution)/shard_map/ppermute | solution.py:47
  3.9 1.9 %copy-start = (f32[3,40,640]{2,1,0:T(8,128)S(1)}, f32[3,40,640]{2,1,0:T(8,128)}, u32[]{:S(2)}) copy-start(f32[3,40,640]{2,1,0:T(8,128)} %w_own.1) | copy-start | bytes 921604
  5.1 5.1 %collective-permute-start.1 = (bf16[256,640]{1,0:T(8,128)(2,1)S(1)}, bf16[256,640]{1,0:T(8,128)(2,1)S(1)}, u32[]{:S(2)}, u32[]{:S(2)}) collective-permute-start(bf16[256,640]{1,0:T(8,128)(2,1)S(1)} %get-tuple-element.37), channel_id=1, source_target_pairs={{0,1},{1,0},{2,3},{3,2},{4,5},{5,4},{6,7},{7,6},{8,9},{9,8},{10,11... | collective-permute-start | bytes 983048 | tf_op jit(solution)/shard_map/ppermute | solution.py:47
  5.3 5.0 %collective-permute-start.2 = (bf16[256,640]{1,0:T(8,128)(2,1)S(1)}, bf16[256,640]{1,0:T(8,128)(2,1)S(1)}, u32[]{:S(2)}, u32[]{:S(2)}) collective-permute-start(bf16[256,640]{1,0:T(8,128)(2,1)S(1)} %get-tuple-element.35), channel_id=1, source_target_pairs={{0,1},{1,0},{2,3},{3,2},{4,5},{5,4},{6,7},{7,6},{8,9},{9,8},{10,11... | collective-permute-start | bytes 983048 | tf_op jit(solution)/shard_map/ppermute | solution.py:47
  5.9 26.0 %collective-permute-start.6 = (f32[2,256]{1,0:T(2,128)S(1)}, f32[2,256]{1,0:T(2,128)S(1)}, u32[]{:S(2)}, u32[]{:S(2)}) collective-permute-start(f32[2,256]{1,0:T(2,128)S(1)} %pad_maximum_fusion.5.refs_4_), channel_id=1, source_target_pairs={{0,2},{1,3},{2,0},{3,1},{4,6},{5,7},{6,4},{7,5},{8,10},{9,11},{10,... | collective-permute-start | bytes 6152 | tf_op jit(solution)/shard_map/ppermute | solution.py:47
  8.1 2.3 %copy-start.5 = (f32[3,40,640]{2,1,0:T(8,128)}, f32[3,40,640]{2,1,0:T(8,128)S(1)}, u32[]{:S(2)}) copy-start(f32[3,40,640]{2,1,0:T(8,128)S(1)} %collective-permute-done.7.w_near) | copy-start | bytes 921604
  8.2 16.5 %collective-permute-start.9 = (bf16[3,80,640]{2,1,0:T(8,128)(2,1)S(1)}, bf16[3,80,640]{2,1,0:T(8,128)(2,1)S(1)}, u32[]{:S(2)}, u32[]{:S(2)}) collective-permute-start(bf16[3,80,640]{2,1,0:T(8,128)(2,1)S(1)} %pad_maximum_fusion.4), channel_id=1, source_target_pairs={{0,8},{2,10},{4,12},{6,14},{8,0},{10,2},{12,4},{14,6},{17,25},{19,... | collective-permute-start | bytes 921608 | tf_op jit(solution)/shard_map/ppermute | solution.py:47
  8.9 13.7 %collective-permute-start.8 = (bf16[3,80,640]{2,1,0:T(8,128)(2,1)S(1)}, bf16[3,80,640]{2,1,0:T(8,128)(2,1)S(1)}, u32[]{:S(2)}, u32[]{:S(2)}) collective-permute-start(bf16[3,80,640]{2,1,0:T(8,128)(2,1)S(1)} %pad_maximum_fusion.4), channel_id=1, source_target_pairs={{0,16},{2,18},{4,20},{6,22},{8,24},{10,26},{12,28},{14,30},{17,1},... | collective-permute-start | bytes 921608 | tf_op jit(solution)/shard_map/ppermute | solution.py:47
  10.2 0.7 copy-start.17
  10.3 0.7 copy-start.15
  11.1 13.5 %copy-start.11 = (bf16[2,256,384]{2,1,0:T(8,128)(2,1)}, bf16[2,256,384]{2,1,0:T(8,128)(2,1)S(1)}, u32[]{:S(2)}) copy-start(bf16[2,256,384]{2,1,0:T(8,128)(2,1)S(1)} %fusion.1) | copy-start | bytes 1179652
  11.1 13.5 %copy-start.18 = (bf16[256,640]{1,0:T(8,128)(2,1)S(1)}, bf16[256,640]{1,0:T(8,128)(2,1)}, u32[]{:S(2)}) copy-start(bf16[256,640]{1,0:T(8,128)(2,1)} %copy-done.17) | copy-start | bytes 983044
  11.1 24.7 %collective-permute-start.4 = (bf16[2,256,640]{2,1,0:T(8,128)(2,1)S(1)}, bf16[2,256,640]{2,1,0:T(8,128)(2,1)S(1)}, u32[]{:S(2)}, u32[]{:S(2)}) collective-permute-start(bf16[2,256,640]{2,1,0:T(8,128)(2,1)S(1)} %pad_maximum_fusion.1.refs_1_.refs_4_), channel_id=1, source_target_pairs={{0,2},{1,3},{2,0},{3,1},{4,6},{5,7},{6,4},{7,5},{8,10},{9,11},{10,... | collective-permute-start | bytes 1966088 | tf_op jit(solution)/shard_map/ppermute | solution.py:47
  11.2 26.4 %collective-permute-start.3 = (bf16[2,256,640]{2,1,0:T(8,128)(2,1)S(1)}, bf16[2,256,640]{2,1,0:T(8,128)(2,1)S(1)}, u32[]{:S(2)}, u32[]{:S(2)}) collective-permute-start(bf16[2,256,640]{2,1,0:T(8,128)(2,1)S(1)} %pad_maximum_fusion.refs_0_.refs_3_), channel_id=1, source_target_pairs={{0,2},{1,3},{2,0},{3,1},{4,6},{5,7},{6,4},{7,5},{8,10},{9,11},{10,... | collective-permute-start | bytes 1966088 | tf_op jit(solution)/shard_map/ppermute | solution.py:47
  13.6 11.1 %copy-start.13 = (bf16[2,256,384]{2,1,0:T(8,128)(2,1)}, bf16[2,256,384]{2,1,0:T(8,128)(2,1)S(1)}, u32[]{:S(2)}) copy-start(bf16[2,256,384]{2,1,0:T(8,128)(2,1)S(1)} %fusion) | copy-start | bytes 1179652
  14.6 18.8 %copy-start.16 = (bf16[256,640]{1,0:T(8,128)(2,1)S(1)}, bf16[256,640]{1,0:T(8,128)(2,1)}, u32[]{:S(2)}) copy-start(bf16[256,640]{1,0:T(8,128)(2,1)} %copy-done.15) | copy-start | bytes 983044
  22.6 7.9 %collective-permute-start.10 = (bf16[3,80,640]{2,1,0:T(8,128)(2,1)S(1)}, bf16[3,80,640]{2,1,0:T(8,128)(2,1)S(1)}, u32[]{:S(2)}, u32[]{:S(2)}) collective-permute-start(bf16[3,80,640]{2,1,0:T(8,128)(2,1)S(1)} %collective-permute-done.8), channel_id=1, source_target_pairs={{1,9},{3,11},{5,13},{7,15},{9,1},{11,3},{13,5},{15,7},{16,24},{18,... | collective-permute-start | bytes 921608 | tf_op jit(solution)/shard_map/ppermute | solution.py:47
  24.7 9.6 %collective-permute-start.11 = (bf16[3,80,640]{2,1,0:T(8,128)(2,1)S(1)}, bf16[3,80,640]{2,1,0:T(8,128)(2,1)S(1)}, u32[]{:S(2)}, u32[]{:S(2)}) collective-permute-start(bf16[3,80,640]{2,1,0:T(8,128)(2,1)S(1)} %broadcast_select_fusion.5.refs_6_), channel_id=1, source_target_pairs={{0,4},{1,5},{2,6},{3,7},{4,0},{5,1},{6,2},{7,3},{8,12},{9,13},{10,... | collective-permute-start | bytes 921608 | tf_op jit(solution)/shard_map/ppermute | solution.py:47
  30.5 10.2 %collective-permute-start.12 = (bf16[3,80,640]{2,1,0:T(8,128)(2,1)S(1)}, bf16[3,80,640]{2,1,0:T(8,128)(2,1)S(1)}, u32[]{:S(2)}, u32[]{:S(2)}) collective-permute-start(bf16[3,80,640]{2,1,0:T(8,128)(2,1)S(1)} %broadcast_select_fusion.4.refs_7_), channel_id=1, source_target_pairs={{0,4},{1,5},{2,6},{3,7},{4,0},{5,1},{6,2},{7,3},{8,12},{9,13},{10,... | collective-permute-start | bytes 921608 | tf_op jit(solution)/shard_map/ppermute | solution.py:47
  31.8 22.9 %collective-permute-start.14 = (bf16[4,256,384]{2,1,0:T(8,128)(2,1)}, bf16[4,256,384]{2,1,0:T(8,128)(2,1)}, u32[]{:S(2)}, u32[]{:S(2)}) collective-permute-start(bf16[4,256,384]{2,1,0:T(8,128)(2,1)} %pad_maximum_fusion.2), channel_id=1, source_target_pairs={{4,12},{5,13},{6,14},{7,15},{12,20},{13,21},{14,22},{15,23},{20,28... | collective-permute-start | bytes 2359304 | tf_op jit(solution)/shard_map/ppermute | solution.py:47
  34.3 13.7 %collective-permute-start.28 = (bf16[4,256,256]{2,1,0:T(8,128)(2,1)}, bf16[4,256,256]{2,1,0:T(8,128)(2,1)}, u32[]{:S(2)}, u32[]{:S(2)}) collective-permute-start(bf16[4,256,256]{2,1,0:T(8,128)(2,1)} %pad_maximum_fusion.3), channel_id=1, source_target_pairs={{0,4},{1,5},{2,6},{3,7},{4,0},{5,1},{6,2},{7,3},{8,12},{9,13},{10,... | collective-permute-start | bytes 1572872 | tf_op jit(solution)/shard_map/ppermute | solution.py:47
  37.6 6.1 %copy-start.1 = (bf16[2,256,640]{2,1,0:T(8,128)(2,1)}, bf16[2,256,640]{2,1,0:T(8,128)(2,1)S(1)}, u32[]{:S(2)}) copy-start(bf16[2,256,640]{2,1,0:T(8,128)(2,1)S(1)} %collective-permute-done.3.refs_2_.refs_5_) | copy-start | bytes 1966084
  43.6 17.3 %collective-permute-start.13 = (bf16[2,3,80,640]{3,2,1,0:T(8,128)(2,1)}, bf16[2,3,80,640]{3,2,1,0:T(8,128)(2,1)S(1)}, u32[]{:S(2)}, u32[]{:S(2)}) collective-permute-start(bf16[2,3,80,640]{3,2,1,0:T(8,128)(2,1)} %shard_map.95), channel_id=1, source_target_pairs={{0,4},{1,5},{2,6},{3,7},{4,0},{5,1},{6,2},{7,3},{8,12},{9,13},{10,... | collective-permute-start | bytes 1843208 | tf_op jit(solution)/shard_map/ppermute | solution.py:47
  48.0 27.5 %collective-permute-start.29 = (bf16[4,256,256]{2,1,0:T(8,128)(2,1)}, bf16[4,256,256]{2,1,0:T(8,128)(2,1)S(1)}, u32[]{:S(2)}, u32[]{:S(2)}) collective-permute-start(bf16[4,256,256]{2,1,0:T(8,128)(2,1)} %collective-permute-done.28), channel_id=1, source_target_pairs={{0,8},{1,9},{2,10},{3,11},{8,16},{9,17},{10,18},{11,19},{16,24},{1... | collective-permute-start | bytes 1572872 | tf_op jit(solution)/shard_map/ppermute | solution.py:47
  51.6 1.1 copy-start.2
  52.7 2.1 %copy-start.12 = (bf16[2,256,384]{2,1,0:T(8,128)(2,1)S(1)}, bf16[2,256,384]{2,1,0:T(8,128)(2,1)}, u32[]{:S(2)}) copy-start(bf16[2,256,384]{2,1,0:T(8,128)(2,1)} %copy-done.11) | copy-start | bytes 1179652
  52.7 2.1 %copy-start.14 = (bf16[2,256,384]{2,1,0:T(8,128)(2,1)S(1)}, bf16[2,256,384]{2,1,0:T(8,128)(2,1)}, u32[]{:S(2)}) copy-start(bf16[2,256,384]{2,1,0:T(8,128)(2,1)} %copy-done.13) | copy-start | bytes 1179652
  55.9 7.1 %copy-start.7 = (f32[3,40,640]{2,1,0:T(8,128)S(1)}, f32[3,40,640]{2,1,0:T(8,128)}, u32[]{:S(2)}) copy-start(f32[3,40,640]{2,1,0:T(8,128)} %m_own.1) | copy-start | bytes 921604
  61.0 17.7 %copy-start.21 = (bf16[256,1280]{1,0:T(8,128)(2,1)S(1)}, bf16[256,1280]{1,0:T(8,128)(2,1)}, u32[]{:S(2)}) copy-start(bf16[256,1280]{1,0:T(8,128)(2,1)} %param.7) | copy-start | bytes 1966084
  61.1 7.1 %collective-permute-start.15 = (bf16[1,3,80,640]{3,2,1,0:T(8,128)(2,1)S(1)}, bf16[1,3,80,640]{3,2,1,0:T(8,128)(2,1)S(1)}, u32[]{:S(2)}, u32[]{:S(2)}) collective-permute-start(bf16[1,3,80,640]{3,2,1,0:T(8,128)(2,1)S(1)} %get-tuple-element.20), channel_id=1, source_target_pairs={{0,8},{1,9},{2,10},{3,11},{4,12},{5,13},{6,14},{7,15},{8,0},{9,1},... | collective-permute-start | bytes 921608 | tf_op jit(solution)/shard_map/ppermute | solution.py:47
  63.0 16.5 %collective-permute-start.17 = (f32[3,40,640]{2,1,0:T(8,128)S(1)}, f32[3,40,640]{2,1,0:T(8,128)S(1)}, u32[]{:S(2)}, u32[]{:S(2)}) collective-permute-start(f32[3,40,640]{2,1,0:T(8,128)S(1)} %copy-done.7), channel_id=1, source_target_pairs={{1,0},{3,2},{5,4},{7,6},{9,8},{11,10},{13,12},{15,14},{16,17},{18,... | collective-permute-start | bytes 921608 | tf_op jit(solution)/shard_map/ppermute | solution.py:47
  68.3 11.3 %copy-start.6 = (f32[3,40,640]{2,1,0:T(8,128)S(1)}, f32[3,40,640]{2,1,0:T(8,128)}, u32[]{:S(2)}) copy-start(f32[3,40,640]{2,1,0:T(8,128)} %copy-done.5) | copy-start | bytes 921604
  68.3 11.2 %collective-permute-start.16 = (bf16[1,3,80,640]{3,2,1,0:T(8,128)(2,1)S(1)}, bf16[1,3,80,640]{3,2,1,0:T(8,128)(2,1)S(1)}, u32[]{:S(2)}, u32[]{:S(2)}) collective-permute-start(bf16[1,3,80,640]{3,2,1,0:T(8,128)(2,1)S(1)} %get-tuple-element.22), channel_id=1, source_target_pairs={{1,17},{3,19},{5,21},{7,23},{9,25},{11,27},{13,29},{15,31},{16,0},... | collective-permute-start | bytes 921608 | tf_op jit(solution)/shard_map/ppermute | solution.py:47
  75.5 13.7 %collective-permute-start.30 = (bf16[4,256,256]{2,1,0:T(8,128)(2,1)S(1)}, bf16[4,256,256]{2,1,0:T(8,128)(2,1)}, u32[]{:S(2)}, u32[]{:S(2)}) collective-permute-start(bf16[4,256,256]{2,1,0:T(8,128)(2,1)S(1)} %broadcast_select_fusion.1.refs_7_), channel_id=1, source_target_pairs={{2,0},{3,1},{6,4},{7,5},{10,8},{11,9},{14,12},{15,13},{18,16},{19,... | collective-permute-start | bytes 1572872 | tf_op jit(solution)/shard_map/ppermute | solution.py:47
  76.8 23.8 %collective-permute-start.31 = (bf16[4,256,384]{2,1,0:T(8,128)(2,1)}, bf16[4,256,384]{2,1,0:T(8,128)(2,1)}, u32[]{:S(2)}, u32[]{:S(2)}) collective-permute-start(bf16[4,256,384]{2,1,0:T(8,128)(2,1)} %broadcast_select_fusion), channel_id=1, source_target_pairs={{0,4},{1,5},{2,6},{3,7},{4,0},{5,1},{6,2},{7,3},{8,12},{9,13},{10,... | collective-permute-start | bytes 2359304 | tf_op jit(solution)/shard_map/ppermute | solution.py:47
  79.5 3.2 %copy-start.22 = (f32[1280]{0:T(1024)S(1)}, f32[1280]{0:T(1024)}, u32[]{:S(2)}) copy-start(f32[1280]{0:T(1024)} %param.13) | copy-start | bytes 15364
  79.5 3.4 %collective-permute-start = (bf16[256,640]{1,0:T(8,128)(2,1)}, bf16[256,640]{1,0:T(8,128)(2,1)S(1)}, u32[]{:S(2)}, u32[]{:S(2)}) collective-permute-start(bf16[256,640]{1,0:T(8,128)(2,1)} %get-tuple-element.38), channel_id=1, source_target_pairs={{0,1},{1,0},{2,3},{3,2},{4,5},{5,4},{6,7},{7,6},{8,9},{9,8},{10,11... | collective-permute-start | bytes 983048 | tf_op jit(solution)/shard_map/ppermute | solution.py:47
  80.6 0.8 copy-start.9
  81.4 14.5 %collective-permute-start.18 = (bf16[3,80,640]{2,1,0:T(8,128)(2,1)}, bf16[3,80,640]{2,1,0:T(8,128)(2,1)}, u32[]{:S(2)}, u32[]{:S(2)}) collective-permute-start(bf16[3,80,640]{2,1,0:T(8,128)(2,1)} %get-tuple-element.23), channel_id=1, source_target_pairs={{0,16},{2,18},{4,20},{6,22},{8,24},{10,26},{12,28},{14,30},{17,1},... | collective-permute-start | bytes 921608 | tf_op jit(solution)/shard_map/ppermute | solution.py:47
  89.2 1.1 copy-start.3
  90.3 9.0 %copy-start.10 = (f32[2,3,40,640]{3,2,1,0:T(8,128)S(1)}, f32[2,3,40,640]{3,2,1,0:T(8,128)}, u32[]{:S(2)}) copy-start(f32[2,3,40,640]{3,2,1,0:T(8,128)} %copy-done.9) | copy-start | bytes 1843204
  95.1 12.5 %copy-start.8 = (f32[3,40,640]{2,1,0:T(8,128)S(1)}, f32[3,40,640]{2,1,0:T(8,128)}, u32[]{:S(2)}) copy-start(f32[3,40,640]{2,1,0:T(8,128)} %m_own.1) | copy-start | bytes 921604
  95.1 10.3 %collective-permute-start.22 = (bf16[3,80,640]{2,1,0:T(8,128)(2,1)}, bf16[3,80,640]{2,1,0:T(8,128)(2,1)S(1)}, u32[]{:S(2)}, u32[]{:S(2)}) collective-permute-start(bf16[3,80,640]{2,1,0:T(8,128)(2,1)} %get-tuple-element.23), channel_id=1, source_target_pairs={{0,8},{2,10},{4,12},{6,14},{8,0},{10,2},{12,4},{14,6},{17,25},{19,... | collective-permute-start | bytes 921608 | tf_op jit(solution)/shard_map/ppermute | solution.py:47
  95.9 11.3 %collective-permute-start.23 = (bf16[3,80,640]{2,1,0:T(8,128)(2,1)}, bf16[3,80,640]{2,1,0:T(8,128)(2,1)S(1)}, u32[]{:S(2)}, u32[]{:S(2)}) collective-permute-start(bf16[3,80,640]{2,1,0:T(8,128)(2,1)} %collective-permute-done.18), channel_id=1, source_target_pairs={{1,9},{3,11},{5,13},{7,15},{9,1},{11,3},{13,5},{15,7},{16,24},{18,... | collective-permute-start | bytes 921608 | tf_op jit(solution)/shard_map/ppermute | solution.py:47
  99.4 8.2 %collective-permute-start.27 = (f32[3,40,640]{2,1,0:T(8,128)S(1)}, f32[3,40,640]{2,1,0:T(8,128)S(1)}, u32[]{:S(2)}, u32[]{:S(2)}) collective-permute-start(f32[3,40,640]{2,1,0:T(8,128)S(1)} %slice_bitcast_fusion), channel_id=1, source_target_pairs={{0,1},{2,3},{4,5},{6,7},{8,9},{10,11},{12,13},{14,15},{17,16},{19,... | collective-permute-start | bytes 921608 | tf_op jit(solution)/shard_map/ppermute | solution.py:47
  100.7 30.7 %collective-permute-start.32 = (bf16[4,256,384]{2,1,0:T(8,128)(2,1)}, bf16[4,256,384]{2,1,0:T(8,128)(2,1)S(1)}, u32[]{:S(2)}, u32[]{:S(2)}) collective-permute-start(bf16[4,256,384]{2,1,0:T(8,128)(2,1)} %collective-permute-done.31.refs_7_), channel_id=1, source_target_pairs={{2,0},{3,1},{6,4},{7,5},{10,8},{11,9},{14,12},{15,13},{18,16},{19,... | collective-permute-start | bytes 2359304 | tf_op jit(solution)/shard_map/ppermute | solution.py:47
  103.2 24.1 %collective-permute-start.20 = (bf16[3,80,640]{2,1,0:T(8,128)(2,1)S(1)}, bf16[3,80,640]{2,1,0:T(8,128)(2,1)S(1)}, u32[]{:S(2)}, u32[]{:S(2)}) collective-permute-start(bf16[3,80,640]{2,1,0:T(8,128)(2,1)S(1)} %broadcast_select_fusion.3.refs_2_), channel_id=1, source_target_pairs={{0,2},{1,3},{2,0},{3,1},{4,6},{5,7},{6,4},{7,5},{8,10},{9,11},{10,... | collective-permute-start | bytes 921608 | tf_op jit(solution)/shard_map/ppermute | solution.py:47
  105.4 31.8 %collective-permute-start.19 = (bf16[3,80,640]{2,1,0:T(8,128)(2,1)S(1)}, bf16[3,80,640]{2,1,0:T(8,128)(2,1)S(1)}, u32[]{:S(2)}, u32[]{:S(2)}) collective-permute-start(bf16[3,80,640]{2,1,0:T(8,128)(2,1)S(1)} %broadcast_select_fusion.3.refs_2_), channel_id=1, source_target_pairs={{0,4},{1,5},{2,6},{3,7},{4,0},{5,1},{6,2},{7,3},{8,12},{9,13},{10,... | collective-permute-start | bytes 921608 | tf_op jit(solution)/shard_map/ppermute | solution.py:47
  107.3 21.9 %collective-permute-start.25 = (bf16[3,80,640]{2,1,0:T(8,128)(2,1)S(1)}, bf16[3,80,640]{2,1,0:T(8,128)(2,1)S(1)}, u32[]{:S(2)}, u32[]{:S(2)}) collective-permute-start(bf16[3,80,640]{2,1,0:T(8,128)(2,1)S(1)} %broadcast_select_fusion.2.refs_4_), channel_id=1, source_target_pairs={{0,4},{1,5},{2,6},{3,7},{4,0},{5,1},{6,2},{7,3},{8,12},{9,13},{10,... | collective-permute-start | bytes 921608 | tf_op jit(solution)/shard_map/ppermute | solution.py:47
  107.7 23.6 %copy-start.19 = (f32[3,40,640]{2,1,0:T(8,128)}, f32[3,40,640]{2,1,0:T(8,128)S(1)}, u32[]{:S(2)}) copy-start(f32[3,40,640]{2,1,0:T(8,128)S(1)} %get-tuple-element.16) | copy-start | bytes 921604
  107.8 29.4 %collective-permute-start.24 = (bf16[3,80,640]{2,1,0:T(8,128)(2,1)S(1)}, bf16[3,80,640]{2,1,0:T(8,128)(2,1)S(1)}, u32[]{:S(2)}, u32[]{:S(2)}) collective-permute-start(bf16[3,80,640]{2,1,0:T(8,128)(2,1)S(1)} %broadcast_select_fusion.2.refs_4_), channel_id=1, source_target_pairs={{0,2},{1,3},{2,0},{3,1},{4,6},{5,7},{6,4},{7,5},{8,10},{9,11},{10,... | collective-permute-start | bytes 921608 | tf_op jit(solution)/shard_map/ppermute | solution.py:47
  127.3 9.8 %collective-permute-start.21 = (bf16[3,80,640]{2,1,0:T(8,128)(2,1)S(1)}, bf16[3,80,640]{2,1,0:T(8,128)(2,1)S(1)}, u32[]{:S(2)}, u32[]{:S(2)}) collective-permute-start(bf16[3,80,640]{2,1,0:T(8,128)(2,1)S(1)} %collective-permute-done.20.refs_3_), channel_id=1, source_target_pairs={{0,4},{1,5},{2,6},{3,7},{4,0},{5,1},{6,2},{7,3},{8,12},{9,13},{10,... | collective-permute-start | bytes 921608 | tf_op jit(solution)/shard_map/ppermute | solution.py:47
  129.2 11.3 %collective-permute-start.26 = (bf16[3,80,640]{2,1,0:T(8,128)(2,1)S(1)}, bf16[3,80,640]{2,1,0:T(8,128)(2,1)S(1)}, u32[]{:S(2)}, u32[]{:S(2)}) collective-permute-start(bf16[3,80,640]{2,1,0:T(8,128)(2,1)S(1)} %collective-permute-done.25.refs_5_), channel_id=1, source_target_pairs={{0,2},{1,3},{2,0},{3,1},{4,6},{5,7},{6,4},{7,5},{8,10},{9,11},{10,... | collective-permute-start | bytes 921608 | tf_op jit(solution)/shard_map/ppermute | solution.py:47
  130.0 1.3 copy-start.4
  143.4 3.3 %collective-permute-start.33 = (bf16[256,640]{1,0:T(8,128)(2,1)S(1)}, bf16[256,640]{1,0:T(8,128)(2,1)S(1)}, u32[]{:S(2)}, u32[]{:S(2)}) collective-permute-start(bf16[256,640]{1,0:T(8,128)(2,1)S(1)} %get-tuple-element.28), channel_id=1, source_target_pairs={{0,1},{1,0},{2,3},{3,2},{4,5},{5,4},{6,7},{7,6},{8,9},{9,8},{10,11... | collective-permute-start | bytes 983048 | tf_op jit(solution)/shard_map/ppermute | solution.py:47

commit v4 on v3

--- a/solution.py
+++ b/solution.py
@@ -387,9 +387,10 @@
 
     k_near = send(k_own, routes.x_swap)
     v_near = send(v_own, routes.x_swap)
-    cut = 2 * ATT_DIM
-    early = jnp.concatenate([k_own[:, :, :cut], v_own[:, :, :cut]], axis=0)
-    late = jnp.concatenate([k_own[:, :, cut:], v_own[:, :, cut:]], axis=0)
+    cut = 3 * ATT_DIM
+    k_held, v_held = lax.optimization_barrier((k_own, v_own))
+    early = jnp.concatenate([k_held[:, :, :cut], v_held[:, :, :cut]], axis=0)
+    late = jnp.concatenate([k_held[:, :, cut:], v_held[:, :, cut:]], axis=0)
     unit = jnp.concatenate([fast_weights.astype(BF16), their_weights.astype(BF16)], axis=1)
     units = gather_z(unit, routes, is_home)
     side_units = [send(part, routes.y_swap) for part in units]
@@ -423,14 +424,15 @@
         part, crossed, fast_weights, their_weights, momentum, their_momentum
     )
     applied = gather_plane(gather_z(pair_new, routes, is_home), routes)
+    gain = lax.dynamic_slice_in_dim(out_gain, core * width, width, 0).reshape(1, width)
+    soon = [piece for idx, piece in enumerate(applied) if idx % 4 < 2]
+    last = [piece for idx, piece in enumerate(applied) if idx % 4 >= 2]
+    sums = query_first(q_own, soon)
+    total, sums, late_att = lax.optimization_barrier((total, sums, late_att))
     partner_grads = send(total[1], routes.pair_out)
     grads = jnp.where(is_home, total[0], partner_grads)
     new_weights, new_momentum = updated(fast_weights, momentum, grads)
-    gain = lax.dynamic_slice_in_dim(out_gain, core * width, width, 0).reshape(1, width)
-    soon = [piece for idx, piece in enumerate(applied) if idx % 4 < 2]
-    last = [piece for idx, piece in enumerate(applied) if idx % 4 >= 2]
     new_weights, new_momentum, gain = lax.optimization_barrier((new_weights, new_momentum, gain))
-    sums = query_first(q_own, soon)
     own, other = query_last(where, q_own, last, sums, gain, (early_att, late_att))
     arrived = send(other, routes.partner)
     layer_out = lax.dynamic_update_slice_in_dim(own, arrived, (1 - core) * width, 1)

time: 148 us -> 167 us (1.13)
  the two profiles are of different devices: /device:TPU:1 before, /device:TPU:29 now
where the time goes in v4:
time: 167 us; the launch traced here: 166 us
  starting transfers between devices  67.9 us (41%)
  waiting for transfers between devices  62.4 us (37%)
  Pallas kernels  22.9 us (14%)
  local copies, waits for them, and re-layouts  6.87 us (4%)
  other arithmetic  5.27 us (3%)
    ppermute x34, starting transfers between devices, send(): return lax.ppermute(array, 'seq', route)  67.9 us
    ppermute x34, waiting for transfers between devices, send(): return lax.ppermute(array, 'seq', route)  62.4 us
    pallas_call x2, Pallas kernels, attention(): pl.pallas_call(lambda *refs: att_kernel(low, *refs), out_shape=jax.ShapeD...  10.8 us
    pallas_call x2, Pallas kernels, key_side(): pl.pallas_call(lambda *refs: key_kernel(grad_scale, *refs), out_shape=jax...  5.02 us
  transfers between devices with their start and end apart: 34, of which 14 were waited for; matrix products, arithmetic and copies ran while one was open for 5% of the time, Pallas kernels for 12%

profile of v4, /device:TPU:29, one launch (start us, length us, event | category | flops | bytes accessed | tf_op | source)
XLA Modules:
  0.0 166.5 jit_solution(6212295112487367718)
XLA Ops:
  0.6 1.4 collective-permute-start.7
  2.1 1.2 dynamic-slice_bitcast_fusion.1
  3.3 1.2 collective-permute-start.1
  4.5 0.8 dynamic-slice_bitcast_fusion
  5.4 0.8 pad_maximum_fusion.4
  6.2 3.3 %collective-permute-start.8 = (bf16[3,80,640]{2,1,0:T(8,128)(2,1)}, bf16[3,80,640]{2,1,0:T(8,128)(2,1)}, u32[]{:S(2)}, u32[]{:S(2)}) collective-permute-start(bf16[3,80,640]{2,1,0:T(8,128)(2,1)} %pad_maximum_fusion.4), channel_id=1, source_target_pairs={{0,16},{2,18},{4,20},{6,22},{8,24},{10,26},{12,28},{14,30},{17,1},... | collective-permute-start | bytes 921608 | tf_op jit(solution)/shard_map/ppermute | solution.py:47
  9.5 2.1 %collective-permute-start.9 = (bf16[3,80,640]{2,1,0:T(8,128)(2,1)}, bf16[3,80,640]{2,1,0:T(8,128)(2,1)S(1)}, u32[]{:S(2)}, u32[]{:S(2)}) collective-permute-start(bf16[3,80,640]{2,1,0:T(8,128)(2,1)} %pad_maximum_fusion.4), channel_id=1, source_target_pairs={{0,8},{2,10},{4,12},{6,14},{8,0},{10,2},{12,4},{14,6},{17,25},{19,... | collective-permute-start | bytes 921608 | tf_op jit(solution)/shard_map/ppermute | solution.py:47
  11.7 1.3 collective-permute-start.3
  13.0 0.7 collective-permute-start.10
  13.8 1.2 collective-permute-start.4
  15.1 0.3 collective-permute-start.11
  15.3 5.4 %collective-permute-done.9 = bf16[3,80,640]{2,1,0:T(8,128)(2,1)S(1)} collective-permute-done((bf16[3,80,640]{2,1,0:T(8,128)(2,1)}, bf16[3,80,640]{2,1,0:T(8,128)(2,1)S(1)}, u32[]{:S(2)}, u32[]{:S(2)}) %collective-permute-start.9) | collective-permute-done | bytes 307232 | tf_op jit(solution)/shard_map/ppermute | solution.py:47
  21.1 8.4 %collective-permute-start.5 = (f32[1,256]{1,0:T(1,128)S(1)}, f32[1,256]{1,0:T(1,128)S(1)}, u32[]{:S(2)}, u32[]{:S(2)}) collective-permute-start(f32[1,256]{1,0:T(1,128)S(1)} %get-tuple-element.51), channel_id=1, source_target_pairs={{0,1},{1,0},{2,3},{3,2},{4,5},{5,4},{6,7},{7,6},{8,9},{9,8},{10,11... | collective-permute-start | bytes 3080 | tf_op jit(solution)/shard_map/ppermute | solution.py:47
  29.5 0.8 collective-permute-done.5
  30.4 1.2 collective-permute-start.6
  31.7 0.9 pad_maximum_fusion.3
  32.6 7.3 %collective-permute-done.6.refs_5_ = f32[2,256]{1,0:T(2,128)S(1)} collective-permute-done((f32[2,256]{1,0:T(2,128)S(1)}, f32[2,256]{1,0:T(2,128)S(1)}, u32[]{:S(2)}, u32[]{:S(2)}) %collective-permute-start.6) | collective-permute-done | bytes 2080 | tf_op jit(solution)/shard_map/ppermute | solution.py:47
  39.9 1.3 collective-permute-start.14
  41.2 2.9 %shard_map.95 = bf16[2,3,80,640]{3,2,1,0:T(8,128)(2,1)} custom-call(bf16[2,256,640]{2,1,0:T(8,128)(2,1)S(1)} %pad_maximum_fusion.1.refs_0_.refs_3_, bf16[2,256,640]{2,1,0:T(8,128)(2,1)S(1)} %pad_maximum_fusion.2.refs_1_.refs_4_, bf16[2,256,640]{2,1,0:T(8,128)(2,1)S(1)} %collective-permute-done.3.refs_2_.refs_5_, ...), custom_call_target="tpu_custom_call" | custom-call | flops 1258291200 | bytes 2621440 | tf_op jit(solution)/shard_map/pallas_call | solution.py:178
  44.2 0.4 collective-permute-start.13
  44.8 1.2 collective-permute-start.30
  46.0 2.1 %shard_map.94.refs_0_ = f32[2,3,80,640]{3,2,1,0:T(8,128)S(1)} custom-call(bf16[2,256,640]{2,1,0:T(8,128)(2,1)S(1)} %pad_maximum_fusion.1.refs_0_.refs_3_, bf16[2,256,640]{2,1,0:T(8,128)(2,1)S(1)} %pad_maximum_fusion.2.refs_1_.refs_4_, bf16[2,256,640]{2,1,0:T(8,128)(2,1)S(1)} %collective-permute-done.3.refs_2_.refs_5_, ...), custom_call_target="tpu_custom_call" | custom-call | flops 1258291200 | bytes 2621440 | tf_op jit(solution)/shard_map/pallas_call | solution.py:178
  48.0 7.8 %collective-permute-done.14 = bf16[4,256,256]{2,1,0:T(8,128)(2,1)} collective-permute-done((bf16[4,256,256]{2,1,0:T(8,128)(2,1)}, bf16[4,256,256]{2,1,0:T(8,128)(2,1)}, u32[]{:S(2)}, u32[]{:S(2)}) %collective-permute-start.14) | collective-permute-done | bytes 524320 | tf_op jit(solution)/shard_map/ppermute | solution.py:47
  55.8 1.1 broadcast_select_fusion.1
  57.0 3.2 %collective-permute-done.13.refs_1_ = bf16[2,3,80,640]{3,2,1,0:T(8,128)(2,1)} collective-permute-done((bf16[2,3,80,640]{3,2,1,0:T(8,128)(2,1)}, bf16[2,3,80,640]{3,2,1,0:T(8,128)(2,1)}, u32[]{:S(2)}, u32[]{:S(2)}) %collective-permute-start.13) | collective-permute-done | bytes 614432 | tf_op jit(solution)/shard_map/ppermute | solution.py:47
  60.2 1.2 shard_map.96
  61.4 1.9 %collective-permute-start.15 = (bf16[1,3,80,640]{3,2,1,0:T(8,128)(2,1)S(1)}, bf16[1,3,80,640]{3,2,1,0:T(8,128)(2,1)S(1)}, u32[]{:S(2)}, u32[]{:S(2)}) collective-permute-start(bf16[1,3,80,640]{3,2,1,0:T(8,128)(2,1)S(1)} %get-tuple-element.27), channel_id=1, source_target_pairs={{0,8},{1,9},{2,10},{3,11},{4,12},{5,13},{6,14},{7,15},{8,0},{9,1},... | collective-permute-start | bytes 921608 | tf_op jit(solution)/shard_map/ppermute | solution.py:47
  63.3 1.3 collective-permute-start.17
  64.5 5.0 %collective-permute-done.15.refs_1_ = bf16[1,3,80,640]{3,2,1,0:T(8,128)(2,1)S(1)} collective-permute-done((bf16[1,3,80,640]{3,2,1,0:T(8,128)(2,1)S(1)}, bf16[1,3,80,640]{3,2,1,0:T(8,128)(2,1)S(1)}, u32[]{:S(2)}, u32[]{:S(2)}) %collective-permute-start.15) | collective-permute-done | bytes 307232 | tf_op jit(solution)/shard_map/ppermute | solution.py:47
  69.6 1.4 collective-permute-start.16
  71.1 0.9 collective-permute-start.27
  72.0 9.6 %collective-permute-done.16.crossed = bf16[1,3,80,640]{3,2,1,0:T(8,128)(2,1)S(1)} collective-permute-done((bf16[1,3,80,640]{3,2,1,0:T(8,128)(2,1)S(1)}, bf16[1,3,80,640]{3,2,1,0:T(8,128)(2,1)S(1)}, u32[]{:S(2)}, u32[]{:S(2)}) %collective-permute-start.16) | collective-permute-done | bytes 307232 | tf_op jit(solution)/shard_map/ppermute | solution.py:47
  81.6 0.3 update.1
  81.9 0.8 copy-done.8
  82.7 1.5 collective-permute-start.18
  84.2 0.7 collective-permute-start.31
  84.9 1.9 %collective-permute-start.22 = (bf16[3,80,640]{2,1,0:T(8,128)(2,1)S(1)}, bf16[3,80,640]{2,1,0:T(8,128)(2,1)S(1)}, u32[]{:S(2)}, u32[]{:S(2)}) collective-permute-start(bf16[3,80,640]{2,1,0:T(8,128)(2,1)S(1)} %get-tuple-element.30), channel_id=1, source_target_pairs={{0,8},{2,10},{4,12},{6,14},{8,0},{10,2},{12,4},{14,6},{17,25},{19,... | collective-permute-start | bytes 921608 | tf_op jit(solution)/shard_map/ppermute | solution.py:47
  86.8 1.1 collective-permute-done.18
  88.0 0.7 collective-permute-start.23
  88.6 0.8 constant_dynamic-slice_fusion.4
  89.4 7.4 %collective-permute-start = (bf16[256,640]{1,0:T(8,128)(2,1)}, bf16[256,640]{1,0:T(8,128)(2,1)S(1)}, u32[]{:S(2)}, u32[]{:S(2)}) collective-permute-start(bf16[256,640]{1,0:T(8,128)(2,1)} %get-tuple-element.48), channel_id=1, source_target_pairs={{0,1},{1,0},{2,3},{3,2},{4,5},{5,4},{6,7},{7,6},{8,9},{9,8},{10,11... | collective-permute-start | bytes 983048 | tf_op jit(solution)/shard_map/ppermute | solution.py:47
  96.8 1.3 collective-permute-start.28
  98.1 2.9 %collective-permute-start.20 = (bf16[3,80,640]{2,1,0:T(8,128)(2,1)S(1)}, bf16[3,80,640]{2,1,0:T(8,128)(2,1)}, u32[]{:S(2)}, u32[]{:S(2)}) collective-permute-start(bf16[3,80,640]{2,1,0:T(8,128)(2,1)S(1)} %broadcast_select_fusion.3.refs_2_), channel_id=1, source_target_pairs={{0,2},{1,3},{2,0},{3,1},{4,6},{5,7},{6,4},{7,5},{8,10},{9,11},{10,... | collective-permute-start | bytes 921608 | tf_op jit(solution)/shard_map/ppermute | solution.py:47
  101.1 0.7 broadcast_select_fusion.2.refs_4_
  101.8 13.0 %collective-permute-start.25 = (bf16[3,80,640]{2,1,0:T(8,128)(2,1)}, bf16[3,80,640]{2,1,0:T(8,128)(2,1)}, u32[]{:S(2)}, u32[]{:S(2)}) collective-permute-start(bf16[3,80,640]{2,1,0:T(8,128)(2,1)} %broadcast_select_fusion.2.refs_4_), channel_id=1, source_target_pairs={{0,4},{1,5},{2,6},{3,7},{4,0},{5,1},{6,2},{7,3},{8,12},{9,13},{10,... | collective-permute-start | bytes 921608 | tf_op jit(solution)/shard_map/ppermute | solution.py:47
  115.0 1.3 collective-permute-start.32
  116.4 1.1 copy-done.2
  117.5 1.1 copy-done.4
  118.6 5.0 %shard_map.98.refs_10_ = f32[512,256]{1,0:T(8,128)S(1)} custom-call(s32[3]{0:T(128)S(1)} %pad_add_fusion.refs_0_, bf16[256,640]{1,0:T(8,128)(2,1)S(1)} %get-tuple-element.49.refs_0_.refs_1_, bf16[256,640]{1,0:T(8,128)(2,1)S(1)} %collective-permute-done.refs_1_.refs_2_, bf16[2,256,640]{2,1,0:T(8,128)(2,1)S(1)} %pad_maximum_fusion.1.refs_0_.refs_3_, ...), custom_call_target="tpu_custom_call" | custom-call | flops 805306368 | bytes 2621440 | tf_op jit(solution)/shard_map/pallas_call | solution.py:329
  123.7 2.5 %query_first.1.refs_7_ = f32[512,640]{1,0:T(8,128)S(1)} custom-call(bf16[256,640]{1,0:T(8,128)(2,1)S(1)} %get-tuple-element.49.refs_0_.refs_1_, bf16[256,640]{1,0:T(8,128)(2,1)S(1)} %collective-permute-done.refs_1_.refs_2_, bf16[3,80,640]{2,1,0:T(8,128)(2,1)S(1)} %broadcast_select_fusion.3.refs_2_, bf16[3,80,640]{2,1,0:T(8,128)(2,1)} %collective-permute-done.20.refs_3_, ...), custom_call_target="tpu_custom_call" | custom-call | flops 629145600 | bytes 1228800 | tf_op jit(solution)/shard_map/query_first/pallas_call | solution.py:223
  126.2 1.3 collective-permute-start.29
  127.7 8.5 %collective-permute-done.32.refs_8_ = bf16[4,256,384]{2,1,0:T(8,128)(2,1)} collective-permute-done((bf16[4,256,384]{2,1,0:T(8,128)(2,1)S(1)}, bf16[4,256,384]{2,1,0:T(8,128)(2,1)}, u32[]{:S(2)}, u32[]{:S(2)}) %collective-permute-start.32) | collective-permute-done | bytes 786464 | tf_op jit(solution)/shard_map/ppermute | solution.py:47
  136.2 5.8 %shard_map.99.refs_9_ = f32[512,384]{1,0:T(8,128)S(1)} custom-call(s32[3]{0:T(128)S(1)} %pad_add_fusion.refs_0_, bf16[256,640]{1,0:T(8,128)(2,1)S(1)} %get-tuple-element.49.refs_0_.refs_1_, bf16[256,640]{1,0:T(8,128)(2,1)S(1)} %collective-permute-done.refs_1_.refs_2_, bf16[2,256,640]{2,1,0:T(8,128)(2,1)S(1)} %pad_maximum_fusion.1.refs_0_.refs_3_, ...), custom_call_target="tpu_custom_call" | custom-call | flops 1207959552 | bytes 3932160 | tf_op jit(solution)/shard_map/pallas_call | solution.py:329
  142.0 3.1 %collective-permute-start.19 = (bf16[3,80,640]{2,1,0:T(8,128)(2,1)S(1)}, bf16[3,80,640]{2,1,0:T(8,128)(2,1)S(1)}, u32[]{:S(2)}, u32[]{:S(2)}) collective-permute-start(bf16[3,80,640]{2,1,0:T(8,128)(2,1)S(1)} %broadcast_select_fusion.3.refs_2_), channel_id=1, source_target_pairs={{0,4},{1,5},{2,6},{3,7},{4,0},{5,1},{6,2},{7,3},{8,12},{9,13},{10,... | collective-permute-start | bytes 921608 | tf_op jit(solution)/shard_map/ppermute | solution.py:47
  145.3 1.4 collective-permute-start.26
  146.9 0.8 multiply_multiply_fusion
  147.7 4.7 %collective-permute-done.19.refs_3_ = bf16[3,80,640]{2,1,0:T(8,128)(2,1)S(1)} collective-permute-done((bf16[3,80,640]{2,1,0:T(8,128)(2,1)S(1)}, bf16[3,80,640]{2,1,0:T(8,128)(2,1)S(1)}, u32[]{:S(2)}, u32[]{:S(2)}) %collective-permute-start.19) | collective-permute-done | bytes 307232 | tf_op jit(solution)/shard_map/ppermute | solution.py:47
  152.4 1.1 collective-permute-done.24.refs_5_
  153.5 5.5 %collective-permute-done.21.refs_4_ = bf16[3,80,640]{2,1,0:T(8,128)(2,1)S(1)} collective-permute-done((bf16[3,80,640]{2,1,0:T(8,128)(2,1)}, bf16[3,80,640]{2,1,0:T(8,128)(2,1)S(1)}, u32[]{:S(2)}, u32[]{:S(2)}) %collective-permute-start.21) | collective-permute-done | bytes 307232 | tf_op jit(solution)/shard_map/ppermute | solution.py:47
  159.0 1.1 collective-permute-done.26.refs_6_
  160.1 2.9 %query_last.1 = (bf16[256,1280]{1,0:T(8,128)(2,1)}, bf16[256,640]{1,0:T(8,128)(2,1)S(1)}) custom-call(s32[3]{0:T(128)S(1)} %pad_add_fusion.refs_0_, bf16[256,640]{1,0:T(8,128)(2,1)S(1)} %get-tuple-element.49.refs_0_.refs_1_, bf16[256,640]{1,0:T(8,128)(2,1)S(1)} %collective-permute-done.refs_1_.refs_2_, ...), custom_call_target="tpu_custom_call" | custom-call | flops 629145600 | bytes 1228800 | tf_op jit(solution)/shard_map/query_last/pallas_call | solution.py:261
  163.0 1.5 collective-permute-start.33
  164.5 1.3 collective-permute-done.33
  165.7 0.8 constant_dynamic-update-slice_fusion
  (93 shorter events, 1.8 us)
Async XLA Ops:
  0.6 3.9 %copy-start.21 = (bf16[256,1280]{1,0:T(8,128)(2,1)S(1)}, bf16[256,1280]{1,0:T(8,128)(2,1)}, u32[]{:S(2)}) copy-start(bf16[256,1280]{1,0:T(8,128)(2,1)} %param.9) | copy-start | bytes 1966084
  0.6 4.7 %collective-permute-start.7 = (f32[3,40,640]{2,1,0:T(8,128)}, f32[3,40,640]{2,1,0:T(8,128)S(1)}, u32[]{:S(2)}, u32[]{:S(2)}) collective-permute-start(f32[3,40,640]{2,1,0:T(8,128)} %w_own.1), channel_id=1, source_target_pairs={{1,0},{3,2},{5,4},{7,6},{9,8},{11,10},{13,12},{15,14},{16,17},{18,... | collective-permute-start | bytes 921608 | tf_op jit(solution)/shard_map/ppermute | solution.py:47
  2.1 3.2 %copy-start = (f32[3,40,640]{2,1,0:T(8,128)S(1)}, f32[3,40,640]{2,1,0:T(8,128)}, u32[]{:S(2)}) copy-start(f32[3,40,640]{2,1,0:T(8,128)} %w_own.1) | copy-start | bytes 921604
  3.3 8.3 %collective-permute-start.1 = (bf16[256,640]{1,0:T(8,128)(2,1)S(1)}, bf16[256,640]{1,0:T(8,128)(2,1)S(1)}, u32[]{:S(2)}, u32[]{:S(2)}) collective-permute-start(bf16[256,640]{1,0:T(8,128)(2,1)S(1)} %get-tuple-element.47), channel_id=1, source_target_pairs={{0,1},{1,0},{2,3},{3,2},{4,5},{5,4},{6,7},{7,6},{8,9},{9,8},{10,11... | collective-permute-start | bytes 983048 | tf_op jit(solution)/shard_map/ppermute | solution.py:47
  5.3 8.3 %collective-permute-start.2 = (bf16[256,640]{1,0:T(8,128)(2,1)}, bf16[256,640]{1,0:T(8,128)(2,1)S(1)}, u32[]{:S(2)}, u32[]{:S(2)}) collective-permute-start(bf16[256,640]{1,0:T(8,128)(2,1)} %get-tuple-element.45), channel_id=1, source_target_pairs={{0,1},{1,0},{2,3},{3,2},{4,5},{5,4},{6,7},{7,6},{8,9},{9,8},{10,11... | collective-permute-start | bytes 983048 | tf_op jit(solution)/shard_map/ppermute | solution.py:47
  5.3 6.2 %copy-start.16 = (bf16[3,40,640]{2,1,0:T(8,128)(2,1)}, bf16[3,40,640]{2,1,0:T(8,128)(2,1)S(1)}, u32[]{:S(2)}) copy-start(bf16[3,40,640]{2,1,0:T(8,128)(2,1)S(1)} %convert_element_type.6) | copy-start | bytes 460804
  5.4 6.2 %copy-start.18 = (bf16[3,40,640]{2,1,0:T(8,128)(2,1)}, bf16[3,40,640]{2,1,0:T(8,128)(2,1)S(1)}, u32[]{:S(2)}) copy-start(bf16[3,40,640]{2,1,0:T(8,128)(2,1)S(1)} %convert_element_type.7) | copy-start | bytes 460804
  6.2 6.8 %collective-permute-start.8 = (bf16[3,80,640]{2,1,0:T(8,128)(2,1)}, bf16[3,80,640]{2,1,0:T(8,128)(2,1)}, u32[]{:S(2)}, u32[]{:S(2)}) collective-permute-start(bf16[3,80,640]{2,1,0:T(8,128)(2,1)} %pad_maximum_fusion.4), channel_id=1, source_target_pairs={{0,16},{2,18},{4,20},{6,22},{8,24},{10,26},{12,28},{14,30},{17,1},... | collective-permute-start | bytes 921608 | tf_op jit(solution)/shard_map/ppermute | solution.py:47
  9.5 11.3 %collective-permute-start.9 = (bf16[3,80,640]{2,1,0:T(8,128)(2,1)}, bf16[3,80,640]{2,1,0:T(8,128)(2,1)S(1)}, u32[]{:S(2)}, u32[]{:S(2)}) collective-permute-start(bf16[3,80,640]{2,1,0:T(8,128)(2,1)} %pad_maximum_fusion.4), channel_id=1, source_target_pairs={{0,8},{2,10},{4,12},{6,14},{8,0},{10,2},{12,4},{14,6},{17,25},{19,... | collective-permute-start | bytes 921608 | tf_op jit(solution)/shard_map/ppermute | solution.py:47
  11.6 3.4 %copy-start.17 = (bf16[3,40,640]{2,1,0:T(8,128)(2,1)S(1)}, bf16[3,40,640]{2,1,0:T(8,128)(2,1)}, u32[]{:S(2)}) copy-start(bf16[3,40,640]{2,1,0:T(8,128)(2,1)} %copy-done.16) | copy-start | bytes 460804
  11.6 3.4 %copy-start.19 = (bf16[3,40,640]{2,1,0:T(8,128)(2,1)S(1)}, bf16[3,40,640]{2,1,0:T(8,128)(2,1)}, u32[]{:S(2)}) copy-start(bf16[3,40,640]{2,1,0:T(8,128)(2,1)} %copy-done.18) | copy-start | bytes 460804
  11.7 29.5 %collective-permute-start.3 = (bf16[2,256,640]{2,1,0:T(8,128)(2,1)S(1)}, bf16[2,256,640]{2,1,0:T(8,128)(2,1)S(1)}, u32[]{:S(2)}, u32[]{:S(2)}) collective-permute-start(bf16[2,256,640]{2,1,0:T(8,128)(2,1)S(1)} %pad_maximum_fusion.1.refs_0_.refs_3_), channel_id=1, source_target_pairs={{0,2},{1,3},{2,0},{3,1},{4,6},{5,7},{6,4},{7,5},{8,10},{9,11},{10,... | collective-permute-start | bytes 1966088 | tf_op jit(solution)/shard_map/ppermute | solution.py:47
  13.0 7.8 %collective-permute-start.10 = (bf16[3,80,640]{2,1,0:T(8,128)(2,1)}, bf16[3,80,640]{2,1,0:T(8,128)(2,1)S(1)}, u32[]{:S(2)}, u32[]{:S(2)}) collective-permute-start(bf16[3,80,640]{2,1,0:T(8,128)(2,1)} %collective-permute-done.8), channel_id=1, source_target_pairs={{1,9},{3,11},{5,13},{7,15},{9,1},{11,3},{13,5},{15,7},{16,24},{18,... | collective-permute-start | bytes 921608 | tf_op jit(solution)/shard_map/ppermute | solution.py:47
  13.7 7.5 %copy-start.24 = (f32[2,256]{1,0:T(2,128)S(1)}, f32[2,256]{1,0:T(2,128)}, u32[]{:S(2)}) copy-start(f32[2,256]{1,0:T(2,128)} %param.10) | copy-start | bytes 6148
  13.8 27.4 %collective-permute-start.4 = (bf16[2,256,640]{2,1,0:T(8,128)(2,1)S(1)}, bf16[2,256,640]{2,1,0:T(8,128)(2,1)S(1)}, u32[]{:S(2)}, u32[]{:S(2)}) collective-permute-start(bf16[2,256,640]{2,1,0:T(8,128)(2,1)S(1)} %pad_maximum_fusion.2.refs_1_.refs_4_), channel_id=1, source_target_pairs={{0,2},{1,3},{2,0},{3,1},{4,6},{5,7},{6,4},{7,5},{8,10},{9,11},{10,... | collective-permute-start | bytes 1966088 | tf_op jit(solution)/shard_map/ppermute | solution.py:47
  15.1 26.1 %collective-permute-start.11 = (bf16[3,80,640]{2,1,0:T(8,128)(2,1)S(1)}, bf16[3,80,640]{2,1,0:T(8,128)(2,1)S(1)}, u32[]{:S(2)}, u32[]{:S(2)}) collective-permute-start(bf16[3,80,640]{2,1,0:T(8,128)(2,1)S(1)} %broadcast_select_fusion.5.refs_6_), channel_id=1, source_target_pairs={{0,4},{1,5},{2,6},{3,7},{4,0},{5,1},{6,2},{7,3},{8,12},{9,13},{10,... | collective-permute-start | bytes 921608 | tf_op jit(solution)/shard_map/ppermute | solution.py:47
  20.8 20.4 %copy-start.10 = (bf16[3,80,640]{2,1,0:T(8,128)(2,1)}, bf16[3,80,640]{2,1,0:T(8,128)(2,1)S(1)}, u32[]{:S(2)}) copy-start(bf16[3,80,640]{2,1,0:T(8,128)(2,1)S(1)} %broadcast_select_fusion.4.refs_7_) | copy-start | bytes 921604
  20.8 20.4 %collective-permute-start.12 = (bf16[3,80,640]{2,1,0:T(8,128)(2,1)S(1)}, bf16[3,80,640]{2,1,0:T(8,128)(2,1)S(1)}, u32[]{:S(2)}, u32[]{:S(2)}) collective-permute-start(bf16[3,80,640]{2,1,0:T(8,128)(2,1)S(1)} %broadcast_select_fusion.4.refs_7_), channel_id=1, source_target_pairs={{0,4},{1,5},{2,6},{3,7},{4,0},{5,1},{6,2},{7,3},{8,12},{9,13},{10,... | collective-permute-start | bytes 921608 | tf_op jit(solution)/shard_map/ppermute | solution.py:47
  21.1 9.2 %collective-permute-start.5 = (f32[1,256]{1,0:T(1,128)S(1)}, f32[1,256]{1,0:T(1,128)S(1)}, u32[]{:S(2)}, u32[]{:S(2)}) collective-permute-start(f32[1,256]{1,0:T(1,128)S(1)} %get-tuple-element.51), channel_id=1, source_target_pairs={{0,1},{1,0},{2,3},{3,2},{4,5},{5,4},{6,7},{7,6},{8,9},{9,8},{10,11... | collective-permute-start | bytes 3080 | tf_op jit(solution)/shard_map/ppermute | solution.py:47
  30.4 9.5 %collective-permute-start.6 = (f32[2,256]{1,0:T(2,128)S(1)}, f32[2,256]{1,0:T(2,128)S(1)}, u32[]{:S(2)}, u32[]{:S(2)}) collective-permute-start(f32[2,256]{1,0:T(2,128)S(1)} %pad_maximum_fusion.5.refs_4_), channel_id=1, source_target_pairs={{0,2},{1,3},{2,0},{3,1},{4,6},{5,7},{6,4},{7,5},{8,10},{9,11},{10,... | collective-permute-start | bytes 6152 | tf_op jit(solution)/shard_map/ppermute | solution.py:47
  31.6 12.6 %copy-start.12 = (bf16[2,256,256]{2,1,0:T(8,128)(2,1)}, bf16[2,256,256]{2,1,0:T(8,128)(2,1)S(1)}, u32[]{:S(2)}) copy-start(bf16[2,256,256]{2,1,0:T(8,128)(2,1)S(1)} %slice.18) | copy-start | bytes 786436
  31.6 12.5 %copy-start.14 = (bf16[2,256,256]{2,1,0:T(8,128)(2,1)}, bf16[2,256,256]{2,1,0:T(8,128)(2,1)S(1)}, u32[]{:S(2)}) copy-start(bf16[2,256,256]{2,1,0:T(8,128)(2,1)S(1)} %slice.19) | copy-start | bytes 786436
  39.9 15.9 %collective-permute-start.14 = (bf16[4,256,256]{2,1,0:T(8,128)(2,1)}, bf16[4,256,256]{2,1,0:T(8,128)(2,1)}, u32[]{:S(2)}, u32[]{:S(2)}) collective-permute-start(bf16[4,256,256]{2,1,0:T(8,128)(2,1)} %pad_maximum_fusion.3), channel_id=1, source_target_pairs={{4,12},{5,13},{6,14},{7,15},{12,20},{13,21},{14,22},{15,23},{20,28... | collective-permute-start | bytes 1572872 | tf_op jit(solution)/shard_map/ppermute | solution.py:47
  41.2 4.8 %copy-start.1 = (bf16[2,256,640]{2,1,0:T(8,128)(2,1)}, bf16[2,256,640]{2,1,0:T(8,128)(2,1)S(1)}, u32[]{:S(2)}) copy-start(bf16[2,256,640]{2,1,0:T(8,128)(2,1)S(1)} %collective-permute-done.3.refs_2_.refs_5_) | copy-start | bytes 1966084
  41.2 4.7 %copy-start.3 = (bf16[2,256,640]{2,1,0:T(8,128)(2,1)}, bf16[2,256,640]{2,1,0:T(8,128)(2,1)S(1)}, u32[]{:S(2)}) copy-start(bf16[2,256,640]{2,1,0:T(8,128)(2,1)S(1)} %collective-permute-done.4.refs_3_.refs_6_) | copy-start | bytes 1966084
  44.2 16.0 %collective-permute-start.13 = (bf16[2,3,80,640]{3,2,1,0:T(8,128)(2,1)}, bf16[2,3,80,640]{3,2,1,0:T(8,128)(2,1)}, u32[]{:S(2)}, u32[]{:S(2)}) collective-permute-start(bf16[2,3,80,640]{3,2,1,0:T(8,128)(2,1)} %shard_map.95), channel_id=1, source_target_pairs={{0,4},{1,5},{2,6},{3,7},{4,0},{5,1},{6,2},{7,3},{8,12},{9,13},{10,... | collective-permute-start | bytes 1843208 | tf_op jit(solution)/shard_map/ppermute | solution.py:47
  44.6 1.4 copy-start.11
  44.7 11.1 %copy-start.13 = (bf16[2,256,256]{2,1,0:T(8,128)(2,1)S(1)}, bf16[2,256,256]{2,1,0:T(8,128)(2,1)}, u32[]{:S(2)}) copy-start(bf16[2,256,256]{2,1,0:T(8,128)(2,1)} %copy-done.12) | copy-start | bytes 786436
  44.8 11.1 %copy-start.15 = (bf16[2,256,256]{2,1,0:T(8,128)(2,1)S(1)}, bf16[2,256,256]{2,1,0:T(8,128)(2,1)}, u32[]{:S(2)}) copy-start(bf16[2,256,256]{2,1,0:T(8,128)(2,1)} %copy-done.14) | copy-start | bytes 786436
  44.8 39.4 %collective-permute-start.30 = (bf16[4,256,384]{2,1,0:T(8,128)(2,1)S(1)}, bf16[4,256,384]{2,1,0:T(8,128)(2,1)S(1)}, u32[]{:S(2)}, u32[]{:S(2)}) collective-permute-start(bf16[4,256,384]{2,1,0:T(8,128)(2,1)S(1)} %pad_maximum_fusion), channel_id=1, source_target_pairs={{0,4},{1,5},{2,6},{3,7},{4,0},{5,1},{6,2},{7,3},{8,12},{9,13},{10,... | collective-permute-start | bytes 2359304 | tf_op jit(solution)/shard_map/ppermute | solution.py:47
  57.0 6.3 %copy-start.6 = (f32[3,40,640]{2,1,0:T(8,128)S(1)}, f32[3,40,640]{2,1,0:T(8,128)}, u32[]{:S(2)}) copy-start(f32[3,40,640]{2,1,0:T(8,128)} %m_own.1) | copy-start | bytes 921604
  61.4 8.1 %collective-permute-start.15 = (bf16[1,3,80,640]{3,2,1,0:T(8,128)(2,1)S(1)}, bf16[1,3,80,640]{3,2,1,0:T(8,128)(2,1)S(1)}, u32[]{:S(2)}, u32[]{:S(2)}) collective-permute-start(bf16[1,3,80,640]{3,2,1,0:T(8,128)(2,1)S(1)} %get-tuple-element.27), channel_id=1, source_target_pairs={{0,8},{1,9},{2,10},{3,11},{4,12},{5,13},{6,14},{7,15},{8,0},{9,1},... | collective-permute-start | bytes 921608 | tf_op jit(solution)/shard_map/ppermute | solution.py:47
  63.3 8.7 %collective-permute-start.17 = (f32[3,40,640]{2,1,0:T(8,128)S(1)}, f32[3,40,640]{2,1,0:T(8,128)S(1)}, u32[]{:S(2)}, u32[]{:S(2)}) collective-permute-start(f32[3,40,640]{2,1,0:T(8,128)S(1)} %copy-done.6), channel_id=1, source_target_pairs={{1,0},{3,2},{5,4},{7,6},{9,8},{11,10},{13,12},{15,14},{16,17},{18,... | collective-permute-start | bytes 921608 | tf_op jit(solution)/shard_map/ppermute | solution.py:47
  69.5 19.1 %copy-start.22 = (bf16[256,1280]{1,0:T(8,128)(2,1)S(1)}, bf16[256,1280]{1,0:T(8,128)(2,1)}, u32[]{:S(2)}) copy-start(bf16[256,1280]{1,0:T(8,128)(2,1)} %param.7) | copy-start | bytes 1966084
  69.6 11.9 %collective-permute-start.16 = (bf16[1,3,80,640]{3,2,1,0:T(8,128)(2,1)S(1)}, bf16[1,3,80,640]{3,2,1,0:T(8,128)(2,1)S(1)}, u32[]{:S(2)}, u32[]{:S(2)}) collective-permute-start(bf16[1,3,80,640]{3,2,1,0:T(8,128)(2,1)S(1)} %get-tuple-element.29), channel_id=1, source_target_pairs={{1,17},{3,19},{5,21},{7,23},{9,25},{11,27},{13,29},{15,31},{16,0},... | collective-permute-start | bytes 921608 | tf_op jit(solution)/shard_map/ppermute | solution.py:47
  71.1 25.7 %collective-permute-start.27 = (bf16[4,256,256]{2,1,0:T(8,128)(2,1)S(1)}, bf16[4,256,256]{2,1,0:T(8,128)(2,1)}, u32[]{:S(2)}, u32[]{:S(2)}) collective-permute-start(bf16[4,256,256]{2,1,0:T(8,128)(2,1)S(1)} %broadcast_select_fusion.1), channel_id=1, source_target_pairs={{0,4},{1,5},{2,6},{3,7},{4,0},{5,1},{6,2},{7,3},{8,12},{9,13},{10,... | collective-permute-start | bytes 1572872 | tf_op jit(solution)/shard_map/ppermute | solution.py:47
  81.9 0.8 copy-start.8
  82.7 5.2 %collective-permute-start.18 = (bf16[3,80,640]{2,1,0:T(8,128)(2,1)S(1)}, bf16[3,80,640]{2,1,0:T(8,128)(2,1)S(1)}, u32[]{:S(2)}, u32[]{:S(2)}) collective-permute-start(bf16[3,80,640]{2,1,0:T(8,128)(2,1)S(1)} %get-tuple-element.30), channel_id=1, source_target_pairs={{0,16},{2,18},{4,20},{6,22},{8,24},{10,26},{12,28},{14,30},{17,1},... | collective-permute-start | bytes 921608 | tf_op jit(solution)/shard_map/ppermute | solution.py:47
  84.2 30.7 %collective-permute-start.31 = (bf16[4,256,384]{2,1,0:T(8,128)(2,1)S(1)}, bf16[4,256,384]{2,1,0:T(8,128)(2,1)S(1)}, u32[]{:S(2)}, u32[]{:S(2)}) collective-permute-start(bf16[4,256,384]{2,1,0:T(8,128)(2,1)S(1)} %collective-permute-done.30), channel_id=1, source_target_pairs={{0,8},{1,9},{2,10},{3,11},{8,16},{9,17},{10,18},{11,19},{16,24},{1... | collective-permute-start | bytes 2359304 | tf_op jit(solution)/shard_map/ppermute | solution.py:47
  84.9 13.2 %collective-permute-start.22 = (bf16[3,80,640]{2,1,0:T(8,128)(2,1)S(1)}, bf16[3,80,640]{2,1,0:T(8,128)(2,1)S(1)}, u32[]{:S(2)}, u32[]{:S(2)}) collective-permute-start(bf16[3,80,640]{2,1,0:T(8,128)(2,1)S(1)} %get-tuple-element.30), channel_id=1, source_target_pairs={{0,8},{2,10},{4,12},{6,14},{8,0},{10,2},{12,4},{14,6},{17,25},{19,... | collective-permute-start | bytes 921608 | tf_op jit(solution)/shard_map/ppermute | solution.py:47
  88.0 13.1 %collective-permute-start.23 = (bf16[3,80,640]{2,1,0:T(8,128)(2,1)S(1)}, bf16[3,80,640]{2,1,0:T(8,128)(2,1)S(1)}, u32[]{:S(2)}, u32[]{:S(2)}) collective-permute-start(bf16[3,80,640]{2,1,0:T(8,128)(2,1)S(1)} %collective-permute-done.18), channel_id=1, source_target_pairs={{1,9},{3,11},{5,13},{7,15},{9,1},{11,3},{13,5},{15,7},{16,24},{18,... | collective-permute-start | bytes 921608 | tf_op jit(solution)/shard_map/ppermute | solution.py:47
  89.4 27.0 %collective-permute-start = (bf16[256,640]{1,0:T(8,128)(2,1)}, bf16[256,640]{1,0:T(8,128)(2,1)S(1)}, u32[]{:S(2)}, u32[]{:S(2)}) collective-permute-start(bf16[256,640]{1,0:T(8,128)(2,1)} %get-tuple-element.48), channel_id=1, source_target_pairs={{0,1},{1,0},{2,3},{3,2},{4,5},{5,4},{6,7},{7,6},{8,9},{9,8},{10,11... | collective-permute-start | bytes 983048 | tf_op jit(solution)/shard_map/ppermute | solution.py:47
  96.8 19.6 %collective-permute-start.28 = (bf16[4,256,256]{2,1,0:T(8,128)(2,1)}, bf16[4,256,256]{2,1,0:T(8,128)(2,1)}, u32[]{:S(2)}, u32[]{:S(2)}) collective-permute-start(bf16[4,256,256]{2,1,0:T(8,128)(2,1)} %collective-permute-done.27.refs_7_), channel_id=1, source_target_pairs={{2,0},{3,1},{6,4},{7,5},{10,8},{11,9},{14,12},{15,13},{18,16},{19,... | collective-permute-start | bytes 1572872 | tf_op jit(solution)/shard_map/ppermute | solution.py:47
  98.1 25.5 %collective-permute-start.20 = (bf16[3,80,640]{2,1,0:T(8,128)(2,1)S(1)}, bf16[3,80,640]{2,1,0:T(8,128)(2,1)}, u32[]{:S(2)}, u32[]{:S(2)}) collective-permute-start(bf16[3,80,640]{2,1,0:T(8,128)(2,1)S(1)} %broadcast_select_fusion.3.refs_2_), channel_id=1, source_target_pairs={{0,2},{1,3},{2,0},{3,1},{4,6},{5,7},{6,4},{7,5},{8,10},{9,11},{10,... | collective-permute-start | bytes 921608 | tf_op jit(solution)/shard_map/ppermute | solution.py:47
  101.8 21.8 %collective-permute-start.25 = (bf16[3,80,640]{2,1,0:T(8,128)(2,1)}, bf16[3,80,640]{2,1,0:T(8,128)(2,1)}, u32[]{:S(2)}, u32[]{:S(2)}) collective-permute-start(bf16[3,80,640]{2,1,0:T(8,128)(2,1)} %broadcast_select_fusion.2.refs_4_), channel_id=1, source_target_pairs={{0,4},{1,5},{2,6},{3,7},{4,0},{5,1},{6,2},{7,3},{8,12},{9,13},{10,... | collective-permute-start | bytes 921608 | tf_op jit(solution)/shard_map/ppermute | solution.py:47
  115.0 21.2 %collective-permute-start.32 = (bf16[4,256,384]{2,1,0:T(8,128)(2,1)S(1)}, bf16[4,256,384]{2,1,0:T(8,128)(2,1)}, u32[]{:S(2)}, u32[]{:S(2)}) collective-permute-start(bf16[4,256,384]{2,1,0:T(8,128)(2,1)S(1)} %broadcast_select_fusion.refs_7_), channel_id=1, source_target_pairs={{2,0},{3,1},{6,4},{7,5},{10,8},{11,9},{14,12},{15,13},{18,16},{19,... | collective-permute-start | bytes 2359304 | tf_op jit(solution)/shard_map/ppermute | solution.py:47
  116.4 1.1 copy-start.2
  117.5 1.1 copy-start.4
  123.6 2.6 %copy-start.9 = (f32[2,3,40,640]{3,2,1,0:T(8,128)S(1)}, f32[2,3,40,640]{3,2,1,0:T(8,128)}, u32[]{:S(2)}) copy-start(f32[2,3,40,640]{3,2,1,0:T(8,128)} %copy-done.8) | copy-start | bytes 1843204
  123.6 4.0 %copy-start.23 = (f32[1280]{0:T(1024)S(1)}, f32[1280]{0:T(1024)}, u32[]{:S(2)}) copy-start(f32[1280]{0:T(1024)} %param.13) | copy-start | bytes 15364
  123.6 12.6 %copy-start.5 = (bf16[2,256,640]{2,1,0:T(8,128)(2,1)S(1)}, bf16[2,256,640]{2,1,0:T(8,128)(2,1)}, u32[]{:S(2)}) copy-start(bf16[2,256,640]{2,1,0:T(8,128)(2,1)} %copy-done.3) | copy-start | bytes 1966084
  126.2 20.4 %collective-permute-start.29 = (f32[3,40,640]{2,1,0:T(8,128)S(1)}, f32[3,40,640]{2,1,0:T(8,128)S(1)}, u32[]{:S(2)}, u32[]{:S(2)}) collective-permute-start(f32[3,40,640]{2,1,0:T(8,128)S(1)} %slice_bitcast_fusion), channel_id=1, source_target_pairs={{0,1},{2,3},{4,5},{6,7},{8,9},{10,11},{12,13},{14,15},{17,16},{19,... | collective-permute-start | bytes 921608 | tf_op jit(solution)/shard_map/ppermute | solution.py:47
  127.7 19.0 %copy-start.7 = (f32[3,40,640]{2,1,0:T(8,128)S(1)}, f32[3,40,640]{2,1,0:T(8,128)}, u32[]{:S(2)}) copy-start(f32[3,40,640]{2,1,0:T(8,128)} %m_own.1) | copy-start | bytes 921604
  142.0 10.4 %collective-permute-start.19 = (bf16[3,80,640]{2,1,0:T(8,128)(2,1)S(1)}, bf16[3,80,640]{2,1,0:T(8,128)(2,1)S(1)}, u32[]{:S(2)}, u32[]{:S(2)}) collective-permute-start(bf16[3,80,640]{2,1,0:T(8,128)(2,1)S(1)} %broadcast_select_fusion.3.refs_2_), channel_id=1, source_target_pairs={{0,4},{1,5},{2,6},{3,7},{4,0},{5,1},{6,2},{7,3},{8,12},{9,13},{10,... | collective-permute-start | bytes 921608 | tf_op jit(solution)/shard_map/ppermute | solution.py:47
  145.1 8.4 %collective-permute-start.24 = (bf16[3,80,640]{2,1,0:T(8,128)(2,1)}, bf16[3,80,640]{2,1,0:T(8,128)(2,1)S(1)}, u32[]{:S(2)}, u32[]{:S(2)}) collective-permute-start(bf16[3,80,640]{2,1,0:T(8,128)(2,1)} %broadcast_select_fusion.2.refs_4_), channel_id=1, source_target_pairs={{0,2},{1,3},{2,0},{3,1},{4,6},{5,7},{6,4},{7,5},{8,10},{9,11},{10,... | collective-permute-start | bytes 921608 | tf_op jit(solution)/shard_map/ppermute | solution.py:47
  145.1 13.8 %collective-permute-start.21 = (bf16[3,80,640]{2,1,0:T(8,128)(2,1)}, bf16[3,80,640]{2,1,0:T(8,128)(2,1)S(1)}, u32[]{:S(2)}, u32[]{:S(2)}) collective-permute-start(bf16[3,80,640]{2,1,0:T(8,128)(2,1)} %collective-permute-done.20.refs_3_), channel_id=1, source_target_pairs={{0,4},{1,5},{2,6},{3,7},{4,0},{5,1},{6,2},{7,3},{8,12},{9,13},{10,... | collective-permute-start | bytes 921608 | tf_op jit(solution)/shard_map/ppermute | solution.py:47
  145.3 14.8 %collective-permute-start.26 = (bf16[3,80,640]{2,1,0:T(8,128)(2,1)}, bf16[3,80,640]{2,1,0:T(8,128)(2,1)S(1)}, u32[]{:S(2)}, u32[]{:S(2)}) collective-permute-start(bf16[3,80,640]{2,1,0:T(8,128)(2,1)} %collective-permute-done.25.refs_5_), channel_id=1, source_target_pairs={{0,2},{1,3},{2,0},{3,1},{4,6},{5,7},{6,4},{7,5},{8,10},{9,11},{10,... | collective-permute-start | bytes 921608 | tf_op jit(solution)/shard_map/ppermute | solution.py:47
  146.8 16.1 %copy-start.20 = (f32[3,40,640]{2,1,0:T(8,128)}, f32[3,40,640]{2,1,0:T(8,128)S(1)}, u32[]{:S(2)}) copy-start(f32[3,40,640]{2,1,0:T(8,128)S(1)} %get-tuple-element.21) | copy-start | bytes 921604
  163.0 2.8 %collective-permute-start.33 = (bf16[256,640]{1,0:T(8,128)(2,1)S(1)}, bf16[256,640]{1,0:T(8,128)(2,1)S(1)}, u32[]{:S(2)}, u32[]{:S(2)}) collective-permute-start(bf16[256,640]{1,0:T(8,128)(2,1)S(1)} %get-tuple-element.38), channel_id=1, source_target_pairs={{0,1},{1,0},{2,3},{3,2},{4,5},{5,4},{6,7},{7,6},{8,9},{9,8},{10,11... | collective-permute-start | bytes 983048 | tf_op jit(solution)/shard_map/ppermute | solution.py:47

commit v5 on v4

--- a/solution.py
+++ b/solution.py
@@ -33,8 +33,9 @@
         self.cross_out = [(dev, (dev + shift) % count) for dev in home]
         self.home_swap = [[(dev, dev ^ (8 * k)) for dev in home] for k in range(half)]
         self.away_swap = [[(dev, dev ^ (8 * k)) for dev in away] for k in range(half)]
-        self.z_swap = [[(dev, dev ^ (8 * k)) for dev in range(count)] for k in range(half)]
-        self.cross_back = [(dev, (dev + shift) % count) for dev in away]
+        self.cross_back = [
+            [(dev, ((dev ^ (8 * k)) + shift) % count) for dev in away] for k in range(half)
+        ]
         self.z_up_near = [(dev, dev + 8) for dev in range(count - 8) if dev % 8 < 4]
         self.z_up_far = [(dev, dev + 8) for dev in range(count - 8) if dev % 8 >= 4]
         self.back_x = [(dev, dev - 2) for dev in range(count) if dev % 4 >= 2]
@@ -68,37 +69,42 @@
     return pieces
 
 
-def fold_kernel(keep_from, send_from, low, arrived, keep, sent):
-    count = keep.shape[0]
-    total = low[...] + arrived[...].astype(F32)
-    keep[...] = total[keep_from : keep_from + count]
-    sent[...] = total[send_from : send_from + count].astype(BF16)
+def fold_kernel(low, arrived, keep, *sent):
+    for idx, ref in enumerate(sent):
+        total = low[idx] + arrived[idx].astype(F32)
+        ref[...] = total.astype(BF16)
+        if idx == 0:
+            keep[...] = total
 
 
 def fold(low, arrived):
-    count = low.shape[0]
-    half = max(count // 2, 1)
-    shape = (half,) + low.shape[1:]
-    return pl.pallas_call(
-        lambda *refs: fold_kernel(0, count - half, *refs),
-        out_shape=[jax.ShapeDtypeStruct(shape, F32), jax.ShapeDtypeStruct(shape, BF16)],
+    shape = low.shape[1:]
+    sent = [jax.ShapeDtypeStruct(shape, BF16)] * low.shape[0]
+    return pl.pallas_call(
+        fold_kernel,
+        out_shape=[jax.ShapeDtypeStruct(shape, F32)] + sent,
         in_specs=[vmem(), vmem()],
-        out_specs=[vmem(), vmem()],
+        out_specs=[vmem()] * (1 + len(sent)),
         compiler_params=grant(10),
         cost_estimate=pl.CostEstimate(flops=low.size, bytes_accessed=12 * low.size, transcendentals=0),
+        name="fold",
     )(low, arrived)
 
 
-def update_kernel(part, crossed, w_own, w_near, m_own, m_near, total, applied):
+def update_kernel(part, *refs):
+    arrived = refs[:-6]
+    w_own, w_near, m_own, m_near, total, applied = refs[-6:]
     owned = w_own.shape[1]
     for idx, (weights, momentum) in enumerate(((w_own, m_own), (w_near, m_near))):
         rows = slice(idx * owned, (idx + 1) * owned)
-        grads = part[0, :, rows] + crossed[0, :, rows].astype(F32)
+        grads = part[:, rows]
+        for came in arrived:
+            grads = grads + came[:, rows].astype(F32)
         total[idx] = grads
         applied[:, rows] = updated(weights[...], momentum[...], grads)[0].astype(BF16)
 
 
-def update_pair(part, crossed, *pairs):
+def update_pair(part, arrived, *pairs):
     shape = pairs[0].shape
     rows = (shape[0], 2 * shape[1], shape[2])
     return pl.pallas_call(
@@ -107,14 +113,14 @@
             jax.ShapeDtypeStruct((2,) + shape, F32),
             jax.ShapeDtypeStruct(rows, BF16),
         ],
-        in_specs=[vmem()] * 6,
+        in_specs=[vmem()] * (5 + len(arrived)),
         out_specs=[vmem()] * 2,
-        compiler_params=grant(10),
+        compiler_params=grant(12),
         cost_estimate=pl.CostEstimate(
             flops=20 * math.prod(shape), bytes_accessed=40 * math.prod(shape), transcendentals=0
         ),
         name="update",
-    )(part, crossed, *pairs)
+    )(part, *arrived, *pairs)
 
 
 def nt_dot(left, right):
@@ -412,24 +418,26 @@
     side_in, late_turn = lax.optimization_barrier((side_in, late_turn))
     late_two = send(late_turn, routes.y_swap)
     late_back = send(late_two, routes.back_x)
-    part, sent = fold(own_grads, side_in)
-    for bit in reversed(routes.bits):
-        part, sent = fold(part, send(sent, routes.z_swap[bit]))
-    crossed = send(sent, routes.cross_back)
+    part, *sent = fold(own_grads, side_in)
+    arrived = []
+    for k in range(len(sent)):
+        arrived.append(send(sent[k], routes.cross_back[k]))
+    for k in range(1, len(sent)):
+        arrived.append(send(sent[k], routes.home_swap[k]))
     att_in = (where, q_own, k_own, v_own, k_near, v_near)
     early_att = attention(*att_in, early_two, early_back, 0)
     late_att = attention(*att_in, late_two, late_back, cut)
 
     total, pair_new = update_pair(
-        part, crossed, fast_weights, their_weights, momentum, their_momentum
+        part, arrived, fast_weights, their_weights, momentum, their_momentum
     )
     applied = gather_plane(gather_z(pair_new, routes, is_home), routes)
+    partner_grads = send(total[1], routes.pair_out)
     gain = lax.dynamic_slice_in_dim(out_gain, core * width, width, 0).reshape(1, width)
     soon = [piece for idx, piece in enumerate(applied) if idx % 4 < 2]
     last = [piece for idx, piece in enumerate(applied) if idx % 4 >= 2]
     sums = query_first(q_own, soon)
-    total, sums, late_att = lax.optimization_barrier((total, sums, late_att))
-    partner_grads = send(total[1], routes.pair_out)
+    partner_grads, sums = lax.optimization_barrier((partner_grads, sums))
     grads = jnp.where(is_home, total[0], partner_grads)
     new_weights, new_momentum = updated(fast_weights, momentum, grads)
     new_weights, new_momentum, gain = lax.optimization_barrier((new_weights, new_momentum, gain))

time: 167 us -> 165 us (0.988)
  the two profiles are of different devices: /device:TPU:29 before, /device:TPU:1 now
where the time goes in v5:
time: 165 us; the launch traced here: 164 us
  waiting for transfers between devices  70 us (42%)
  starting transfers between devices  55.2 us (33%)
  Pallas kernels  22.6 us (14%)
  other arithmetic  8.23 us (5%)
  local copies, waits for them, and re-layouts  6.45 us (4%)
    ppermute x35, waiting for transfers between devices, send(): return lax.ppermute(array, 'seq', route)  70 us
    ppermute x35, starting transfers between devices, send(): return lax.ppermute(array, 'seq', route)  55.2 us
    pallas_call x2, Pallas kernels, attention(): pl.pallas_call(lambda *refs: att_kernel(low, *refs), out_shape=jax.ShapeD...  10 us
    pallas_call x2, Pallas kernels, key_side(): pl.pallas_call(lambda *refs: key_kernel(grad_scale, *refs), out_shape=jax...  5.03 us
  transfers between devices with their start and end apart: 35, of which 13 were waited for; matrix products, arithmetic and copies ran while one was open for 7% of the time, Pallas kernels for 12%

profile of v5, /device:TPU:1, one launch (start us, length us, event | category | flops | bytes accessed | tf_op | source)
XLA Modules:
  0.0 163.7 jit_solution(18175966554727153047)
XLA Ops:
  0.6 2.1 %collective-permute-start.7 = (f32[3,40,640]{2,1,0:T(8,128)}, f32[3,40,640]{2,1,0:T(8,128)S(1)}, u32[]{:S(2)}, u32[]{:S(2)}) collective-permute-start(f32[3,40,640]{2,1,0:T(8,128)} %refs_3_.1), channel_id=1, source_target_pairs={{1,0},{3,2},{5,4},{7,6},{9,8},{11,10},{13,12},{15,14},{16,17},{18,... | collective-permute-start | bytes 921608 | tf_op jit(solution)/shard_map/ppermute | solution.py:48
  2.8 1.9 %dynamic-slice_bitcast_fusion.1 = (bf16[1,256,640]{2,1,0:T(8,128)(2,1)S(1)}, bf16[256,640]{1,0:T(8,128)(2,1)}) fusion(bf16[256,1280]{1,0:T(8,128)(2,1)} %param.8, s32[]{:T(128)S(6)} %select_n.90, s32[]{:T(128)S(6)} %select_n.91), kind=kLoop, calls=%fused_computation.7 | loop fusion | bytes 1310728 | tf_op jit(solution)/shard_map/stack | solution.py:387
  4.7 0.1 dynamic-slice_bitcast_fusion
  4.8 0.5 collective-permute-start.2
  5.4 0.8 pad_maximum_fusion.4
  6.2 1.3 collective-permute-start.8
  7.5 5.3 %collective-permute-start.5 = (f32[1,256]{1,0:T(1,128)S(1)}, f32[1,256]{1,0:T(1,128)S(1)}, u32[]{:S(2)}, u32[]{:S(2)}) collective-permute-start(f32[1,256]{1,0:T(1,128)S(1)} %get-tuple-element.47), channel_id=1, source_target_pairs={{0,1},{1,0},{2,3},{3,2},{4,5},{5,4},{6,7},{7,6},{8,9},{9,8},{10,11... | collective-permute-start | bytes 3080 | tf_op jit(solution)/shard_map/ppermute | solution.py:48
  12.8 0.8 collective-permute-done.5
  13.6 1.2 collective-permute-start.6
  14.8 0.7 collective-permute-start.9
  15.6 0.3 collective-permute-start.3
  15.9 2.5 %collective-permute-done.8 = bf16[3,80,640]{2,1,0:T(8,128)(2,1)} collective-permute-done((bf16[3,80,640]{2,1,0:T(8,128)(2,1)}, bf16[3,80,640]{2,1,0:T(8,128)(2,1)}, u32[]{:S(2)}, u32[]{:S(2)}) %collective-permute-start.8) | collective-permute-done | bytes 307232 | tf_op jit(solution)/shard_map/ppermute | solution.py:48
  18.4 1.9 %collective-permute-start.10 = (bf16[3,80,640]{2,1,0:T(8,128)(2,1)}, bf16[3,80,640]{2,1,0:T(8,128)(2,1)S(1)}, u32[]{:S(2)}, u32[]{:S(2)}) collective-permute-start(bf16[3,80,640]{2,1,0:T(8,128)(2,1)} %collective-permute-done.8), channel_id=1, source_target_pairs={{1,9},{3,11},{5,13},{7,15},{9,1},{11,3},{13,5},{15,7},{16,24},{18,... | collective-permute-start | bytes 921608 | tf_op jit(solution)/shard_map/ppermute | solution.py:48
  20.5 2.6 %collective-permute-start.4 = (bf16[2,256,640]{2,1,0:T(8,128)(2,1)S(1)}, bf16[2,256,640]{2,1,0:T(8,128)(2,1)S(1)}, u32[]{:S(2)}, u32[]{:S(2)}) collective-permute-start(bf16[2,256,640]{2,1,0:T(8,128)(2,1)S(1)} %pad_maximum_fusion.2.refs_1_.refs_4_), channel_id=1, source_target_pairs={{0,2},{1,3},{2,0},{3,1},{4,6},{5,7},{6,4},{7,5},{8,10},{9,11},{10,... | collective-permute-start | bytes 1966088 | tf_op jit(solution)/shard_map/ppermute | solution.py:48
  23.1 1.1 broadcast_select_fusion.5.refs_6_
  24.2 1.3 collective-permute-start.11
  25.5 1.8 %collective-permute-done.10 = bf16[3,80,640]{2,1,0:T(8,128)(2,1)S(1)} collective-permute-done((bf16[3,80,640]{2,1,0:T(8,128)(2,1)}, bf16[3,80,640]{2,1,0:T(8,128)(2,1)S(1)}, u32[]{:S(2)}, u32[]{:S(2)}) %collective-permute-start.10) | collective-permute-done | bytes 307232 | tf_op jit(solution)/shard_map/ppermute | solution.py:48
  27.4 1.8 %collective-permute-start.12 = (bf16[3,80,640]{2,1,0:T(8,128)(2,1)S(1)}, bf16[3,80,640]{2,1,0:T(8,128)(2,1)S(1)}, u32[]{:S(2)}, u32[]{:S(2)}) collective-permute-start(bf16[3,80,640]{2,1,0:T(8,128)(2,1)S(1)} %broadcast_select_fusion.4.refs_7_), channel_id=1, source_target_pairs={{0,4},{1,5},{2,6},{3,7},{4,0},{5,1},{6,2},{7,3},{8,12},{9,13},{10,... | collective-permute-start | bytes 921608 | tf_op jit(solution)/shard_map/ppermute | solution.py:48
  29.2 1.0 pad_maximum_fusion
  30.2 0.7 copy-done.10
  30.9 0.9 pad_maximum_fusion.3
  31.8 0.2 collective-permute-done.11.refs_6_
  32.0 1.4 collective-permute-start.14
  33.5 9.2 %collective-permute-done.4.refs_3_.refs_6_ = bf16[2,256,640]{2,1,0:T(8,128)(2,1)S(1)} collective-permute-done((bf16[2,256,640]{2,1,0:T(8,128)(2,1)S(1)}, bf16[2,256,640]{2,1,0:T(8,128)(2,1)S(1)}, u32[]{:S(2)}, u32[]{:S(2)}) %collective-permute-start.4) | collective-permute-done | bytes 655392 | tf_op jit(solution)/shard_map/ppermute | solution.py:48
  42.7 2.9 %shard_map.95 = bf16[2,3,80,640]{3,2,1,0:T(8,128)(2,1)} custom-call(bf16[2,256,640]{2,1,0:T(8,128)(2,1)S(1)} %pad_maximum_fusion.1.refs_0_.refs_3_, bf16[2,256,640]{2,1,0:T(8,128)(2,1)S(1)} %pad_maximum_fusion.2.refs_1_.refs_4_, bf16[2,256,640]{2,1,0:T(8,128)(2,1)S(1)} %collective-permute-done.3.refs_2_.refs_5_, ...), custom_call_target="tpu_custom_call" | custom-call | flops 1258291200 | bytes 2621440 | tf_op jit(solution)/shard_map/pallas_call | solution.py:184
  45.6 1.2 collective-permute-start.13
  46.9 7.1 %collective-permute-start.18 = (f32[3,40,640]{2,1,0:T(8,128)S(1)}, f32[3,40,640]{2,1,0:T(8,128)}, u32[]{:S(2)}, u32[]{:S(2)}) collective-permute-start(f32[3,40,640]{2,1,0:T(8,128)S(1)} %copy-done.3), channel_id=1, source_target_pairs={{1,0},{3,2},{5,4},{7,6},{9,8},{11,10},{13,12},{15,14},{16,17},{18,... | collective-permute-start | bytes 921608 | tf_op jit(solution)/shard_map/ppermute | solution.py:48
  54.0 1.0 copy-done.7
  54.9 1.0 copy-done.9
  55.9 2.1 %shard_map.94.low = f32[2,3,80,640]{3,2,1,0:T(8,128)S(1)} custom-call(bf16[2,256,640]{2,1,0:T(8,128)(2,1)S(1)} %pad_maximum_fusion.1.refs_0_.refs_3_, bf16[2,256,640]{2,1,0:T(8,128)(2,1)S(1)} %pad_maximum_fusion.2.refs_1_.refs_4_, bf16[2,256,640]{2,1,0:T(8,128)(2,1)S(1)} %collective-permute-done.3.refs_2_.refs_5_, ...), custom_call_target="tpu_custom_call" | custom-call | flops 1258291200 | bytes 2621440 | tf_op jit(solution)/shard_map/pallas_call | solution.py:184
  58.0 4.1 %collective-permute-start.30 = (bf16[4,256,384]{2,1,0:T(8,128)(2,1)}, bf16[4,256,384]{2,1,0:T(8,128)(2,1)}, u32[]{:S(2)}, u32[]{:S(2)}) collective-permute-start(bf16[4,256,384]{2,1,0:T(8,128)(2,1)} %collective-permute-done.29), channel_id=1, source_target_pairs={{0,8},{1,9},{2,10},{3,11},{8,16},{9,17},{10,18},{11,19},{16,24},{1... | collective-permute-start | bytes 2359304 | tf_op jit(solution)/shard_map/ppermute | solution.py:48
  62.1 0.9 broadcast_select_fusion.1
  63.0 5.7 %collective-permute-done.13.arrived = bf16[2,3,80,640]{3,2,1,0:T(8,128)(2,1)} collective-permute-done((bf16[2,3,80,640]{3,2,1,0:T(8,128)(2,1)}, bf16[2,3,80,640]{3,2,1,0:T(8,128)(2,1)}, u32[]{:S(2)}, u32[]{:S(2)}) %collective-permute-start.13) | collective-permute-done | bytes 614432 | tf_op jit(solution)/shard_map/ppermute | solution.py:48
  68.7 1.2 fold.1
  70.0 1.3 collective-permute-start.15
  71.3 3.3 %collective-permute-start.16 = (bf16[3,80,640]{2,1,0:T(8,128)(2,1)S(1)}, bf16[3,80,640]{2,1,0:T(8,128)(2,1)S(1)}, u32[]{:S(2)}, u32[]{:S(2)}) collective-permute-start(bf16[3,80,640]{2,1,0:T(8,128)(2,1)S(1)} %get-tuple-element.26), channel_id=1, source_target_pairs={{1,25},{3,27},{5,29},{7,31},{9,17},{11,19},{13,21},{15,23},{16,8},... | collective-permute-start | bytes 921608 | tf_op jit(solution)/shard_map/ppermute | solution.py:48
  74.6 0.7 collective-permute-start.17
  75.3 7.5 %collective-permute-done.15.refs_0_ = bf16[3,80,640]{2,1,0:T(8,128)(2,1)S(1)} collective-permute-done((bf16[3,80,640]{2,1,0:T(8,128)(2,1)S(1)}, bf16[3,80,640]{2,1,0:T(8,128)(2,1)S(1)}, u32[]{:S(2)}, u32[]{:S(2)}) %collective-permute-start.15) | collective-permute-done | bytes 307232 | tf_op jit(solution)/shard_map/ppermute | solution.py:48
  82.8 5.9 %collective-permute-done.16.refs_1_ = bf16[3,80,640]{2,1,0:T(8,128)(2,1)S(1)} collective-permute-done((bf16[3,80,640]{2,1,0:T(8,128)(2,1)S(1)}, bf16[3,80,640]{2,1,0:T(8,128)(2,1)S(1)}, u32[]{:S(2)}, u32[]{:S(2)}) %collective-permute-start.16) | collective-permute-done | bytes 307232 | tf_op jit(solution)/shard_map/ppermute | solution.py:48
  88.7 2.2 %update.1 = (f32[2,3,40,640]{3,2,1,0:T(8,128)S(1)}, bf16[3,80,640]{2,1,0:T(8,128)(2,1)}) custom-call(f32[3,80,640]{2,1,0:T(8,128)S(1)} %get-tuple-element.24.part, bf16[3,80,640]{2,1,0:T(8,128)(2,1)S(1)} %collective-permute-done.15.refs_0_, bf16[3,80,640]{2,1,0:T(8,128)(2,1)S(1)} %collective-permute-done.16.refs_1_, ...), custom_call_target="tpu_custom_call" | custom-call | flops 1536000 | bytes 3072000 | tf_op jit(solution)/shard_map/update/pallas_call | solution.py:110
  90.8 1.4 collective-permute-start.19
  92.3 0.8 constant_dynamic-slice_fusion.4
  93.1 5.2 %collective-permute-start = (bf16[256,640]{1,0:T(8,128)(2,1)}, bf16[256,640]{1,0:T(8,128)(2,1)S(1)}, u32[]{:S(2)}, u32[]{:S(2)}) collective-permute-start(bf16[256,640]{1,0:T(8,128)(2,1)} %get-tuple-element.44), channel_id=1, source_target_pairs={{0,1},{1,0},{2,3},{3,2},{4,5},{5,4},{6,7},{7,6},{8,9},{9,8},{10,11... | collective-permute-start | bytes 983048 | tf_op jit(solution)/shard_map/ppermute | solution.py:48
  98.4 0.7 collective-permute-start.23
  99.0 6.1 %collective-permute-done.19 = bf16[3,80,640]{2,1,0:T(8,128)(2,1)} collective-permute-done((bf16[3,80,640]{2,1,0:T(8,128)(2,1)}, bf16[3,80,640]{2,1,0:T(8,128)(2,1)}, u32[]{:S(2)}, u32[]{:S(2)}) %collective-permute-start.19) | collective-permute-done | bytes 307232 | tf_op jit(solution)/shard_map/ppermute | solution.py:48
  105.1 1.9 %collective-permute-start.24 = (bf16[3,80,640]{2,1,0:T(8,128)(2,1)}, bf16[3,80,640]{2,1,0:T(8,128)(2,1)S(1)}, u32[]{:S(2)}, u32[]{:S(2)}) collective-permute-start(bf16[3,80,640]{2,1,0:T(8,128)(2,1)} %collective-permute-done.19), channel_id=1, source_target_pairs={{1,9},{3,11},{5,13},{7,15},{9,1},{11,3},{13,5},{15,7},{16,24},{18,... | collective-permute-start | bytes 921608 | tf_op jit(solution)/shard_map/ppermute | solution.py:48
  107.0 1.2 broadcast_select_fusion.refs_7_
  108.3 1.4 collective-permute-start.31
  109.7 1.3 collective-permute-start.33
  111.0 1.0 broadcast_select_fusion.3.refs_2_
  112.1 2.2 %collective-permute-start.21 = (bf16[3,80,640]{2,1,0:T(8,128)(2,1)S(1)}, bf16[3,80,640]{2,1,0:T(8,128)(2,1)S(1)}, u32[]{:S(2)}, u32[]{:S(2)}) collective-permute-start(bf16[3,80,640]{2,1,0:T(8,128)(2,1)S(1)} %broadcast_select_fusion.3.refs_2_), channel_id=1, source_target_pairs={{0,2},{1,3},{2,0},{3,1},{4,6},{5,7},{6,4},{7,5},{8,10},{9,11},{10,... | collective-permute-start | bytes 921608 | tf_op jit(solution)/shard_map/ppermute | solution.py:48
  114.5 1.3 collective-permute-start.28
  115.8 14.0 %collective-permute-done.31.refs_8_ = bf16[4,256,384]{2,1,0:T(8,128)(2,1)S(1)} collective-permute-done((bf16[4,256,384]{2,1,0:T(8,128)(2,1)S(1)}, bf16[4,256,384]{2,1,0:T(8,128)(2,1)S(1)}, u32[]{:S(2)}, u32[]{:S(2)}) %collective-permute-start.31) | collective-permute-done | bytes 786464 | tf_op jit(solution)/shard_map/ppermute | solution.py:48
  129.9 5.3 %shard_map.96.refs_9_ = f32[512,384]{1,0:T(8,128)S(1)} custom-call(s32[3]{0:T(128)S(1)} %pad_add_fusion.refs_0_, bf16[256,640]{1,0:T(8,128)(2,1)S(1)} %get-tuple-element.45.refs_0_.refs_1_, bf16[256,640]{1,0:T(8,128)(2,1)S(1)} %collective-permute-done.refs_1_.refs_2_, bf16[2,256,640]{2,1,0:T(8,128)(2,1)S(1)} %pad_maximum_fusion.1.refs_0_.refs_3_, ...), custom_call_target="tpu_custom_call" | custom-call | flops 1207959552 | bytes 3932160 | tf_op jit(solution)/shard_map/pallas_call | solution.py:335
  135.2 8.9 %collective-permute-done.21.refs_3_ = bf16[3,80,640]{2,1,0:T(8,128)(2,1)S(1)} collective-permute-done((bf16[3,80,640]{2,1,0:T(8,128)(2,1)S(1)}, bf16[3,80,640]{2,1,0:T(8,128)(2,1)S(1)}, u32[]{:S(2)}, u32[]{:S(2)}) %collective-permute-start.21) | collective-permute-done | bytes 307232 | tf_op jit(solution)/shard_map/ppermute | solution.py:48
  144.2 4.7 %shard_map.97.refs_10_ = f32[512,256]{1,0:T(8,128)S(1)} custom-call(s32[3]{0:T(128)S(1)} %pad_add_fusion.refs_0_, bf16[256,640]{1,0:T(8,128)(2,1)S(1)} %get-tuple-element.45.refs_0_.refs_1_, bf16[256,640]{1,0:T(8,128)(2,1)S(1)} %collective-permute-done.refs_1_.refs_2_, bf16[2,256,640]{2,1,0:T(8,128)(2,1)S(1)} %pad_maximum_fusion.1.refs_0_.refs_3_, ...), custom_call_target="tpu_custom_call" | custom-call | flops 805306368 | bytes 2621440 | tf_op jit(solution)/shard_map/pallas_call | solution.py:335
  148.9 1.3 query_first.1.refs_7_
  150.2 0.2 multiply_reduce_fusion.1
  150.4 1.5 collective-permute-start.27
  151.9 0.9 multiply_multiply_fusion
  152.8 5.7 %collective-permute-done.27.refs_6_ = bf16[3,80,640]{2,1,0:T(8,128)(2,1)S(1)} collective-permute-done((bf16[3,80,640]{2,1,0:T(8,128)(2,1)S(1)}, bf16[3,80,640]{2,1,0:T(8,128)(2,1)S(1)}, u32[]{:S(2)}, u32[]{:S(2)}) %collective-permute-start.27) | collective-permute-done | bytes 307232 | tf_op jit(solution)/shard_map/ppermute | solution.py:48
  158.4 2.9 %query_last.1 = (bf16[256,1280]{1,0:T(8,128)(2,1)}, bf16[256,640]{1,0:T(8,128)(2,1)S(1)}) custom-call(s32[3]{0:T(128)S(1)} %pad_add_fusion.refs_0_, bf16[256,640]{1,0:T(8,128)(2,1)S(1)} %get-tuple-element.45.refs_0_.refs_1_, bf16[256,640]{1,0:T(8,128)(2,1)S(1)} %collective-permute-done.refs_1_.refs_2_, ...), custom_call_target="tpu_custom_call" | custom-call | flops 629145600 | bytes 1228800 | tf_op jit(solution)/shard_map/query_last/pallas_call | solution.py:267
  161.3 1.6 collective-permute-done.34
  162.9 0.8 constant_dynamic-update-slice_fusion
  (86 shorter events, 0.9 us)
Async XLA Ops:
  0.6 4.0 %copy-start.17 = (bf16[256,1280]{1,0:T(8,128)(2,1)S(1)}, bf16[256,1280]{1,0:T(8,128)(2,1)}, u32[]{:S(2)}) copy-start(bf16[256,1280]{1,0:T(8,128)(2,1)} %param.9) | copy-start | bytes 1966084
  0.6 4.7 %collective-permute-start.7 = (f32[3,40,640]{2,1,0:T(8,128)}, f32[3,40,640]{2,1,0:T(8,128)S(1)}, u32[]{:S(2)}, u32[]{:S(2)}) collective-permute-start(f32[3,40,640]{2,1,0:T(8,128)} %refs_3_.1), channel_id=1, source_target_pairs={{1,0},{3,2},{5,4},{7,6},{9,8},{11,10},{13,12},{15,14},{16,17},{18,... | collective-permute-start | bytes 921608 | tf_op jit(solution)/shard_map/ppermute | solution.py:48
  2.7 2.6 %copy-start = (f32[3,40,640]{2,1,0:T(8,128)S(1)}, f32[3,40,640]{2,1,0:T(8,128)}, u32[]{:S(2)}) copy-start(f32[3,40,640]{2,1,0:T(8,128)} %refs_3_.1) | copy-start | bytes 921604
  4.7 2.8 %copy-start.20 = (f32[2,256]{1,0:T(2,128)S(1)}, f32[2,256]{1,0:T(2,128)}, u32[]{:S(2)}) copy-start(f32[2,256]{1,0:T(2,128)} %param.10) | copy-start | bytes 6148
  4.7 10.9 %collective-permute-start.1 = (bf16[256,640]{1,0:T(8,128)(2,1)}, bf16[256,640]{1,0:T(8,128)(2,1)S(1)}, u32[]{:S(2)}, u32[]{:S(2)}) collective-permute-start(bf16[256,640]{1,0:T(8,128)(2,1)} %get-tuple-element.43), channel_id=1, source_target_pairs={{0,1},{1,0},{2,3},{3,2},{4,5},{5,4},{6,7},{7,6},{8,9},{9,8},{10,11... | collective-permute-start | bytes 983048 | tf_op jit(solution)/shard_map/ppermute | solution.py:48
  4.8 15.6 %collective-permute-start.2 = (bf16[256,640]{1,0:T(8,128)(2,1)S(1)}, bf16[256,640]{1,0:T(8,128)(2,1)S(1)}, u32[]{:S(2)}, u32[]{:S(2)}) collective-permute-start(bf16[256,640]{1,0:T(8,128)(2,1)S(1)} %get-tuple-element.41), channel_id=1, source_target_pairs={{0,1},{1,0},{2,3},{3,2},{4,5},{5,4},{6,7},{7,6},{8,9},{9,8},{10,11... | collective-permute-start | bytes 983048 | tf_op jit(solution)/shard_map/ppermute | solution.py:48
  5.4 10.1 %copy-start.14 = (bf16[3,40,640]{2,1,0:T(8,128)(2,1)}, bf16[3,40,640]{2,1,0:T(8,128)(2,1)S(1)}, u32[]{:S(2)}) copy-start(bf16[3,40,640]{2,1,0:T(8,128)(2,1)S(1)} %convert_element_type.7) | copy-start | bytes 460804
  6.2 12.3 %collective-permute-start.8 = (bf16[3,80,640]{2,1,0:T(8,128)(2,1)}, bf16[3,80,640]{2,1,0:T(8,128)(2,1)}, u32[]{:S(2)}, u32[]{:S(2)}) collective-permute-start(bf16[3,80,640]{2,1,0:T(8,128)(2,1)} %pad_maximum_fusion.4), channel_id=1, source_target_pairs={{0,16},{2,18},{4,20},{6,22},{8,24},{10,26},{12,28},{14,30},{17,1},... | collective-permute-start | bytes 921608 | tf_op jit(solution)/shard_map/ppermute | solution.py:48
  7.5 6.2 %collective-permute-start.5 = (f32[1,256]{1,0:T(1,128)S(1)}, f32[1,256]{1,0:T(1,128)S(1)}, u32[]{:S(2)}, u32[]{:S(2)}) collective-permute-start(f32[1,256]{1,0:T(1,128)S(1)} %get-tuple-element.47), channel_id=1, source_target_pairs={{0,1},{1,0},{2,3},{3,2},{4,5},{5,4},{6,7},{7,6},{8,9},{9,8},{10,11... | collective-permute-start | bytes 3080 | tf_op jit(solution)/shard_map/ppermute | solution.py:48
  13.6 16.5 %collective-permute-start.6 = (f32[2,256]{1,0:T(2,128)S(1)}, f32[2,256]{1,0:T(2,128)S(1)}, u32[]{:S(2)}, u32[]{:S(2)}) collective-permute-start(f32[2,256]{1,0:T(2,128)S(1)} %pad_maximum_fusion.5.refs_4_), channel_id=1, source_target_pairs={{0,2},{1,3},{2,0},{3,1},{4,6},{5,7},{6,4},{7,5},{8,10},{9,11},{10,... | collective-permute-start | bytes 6152 | tf_op jit(solution)/shard_map/ppermute | solution.py:48
  14.8 9.4 %collective-permute-start.9 = (bf16[3,80,640]{2,1,0:T(8,128)(2,1)}, bf16[3,80,640]{2,1,0:T(8,128)(2,1)S(1)}, u32[]{:S(2)}, u32[]{:S(2)}) collective-permute-start(bf16[3,80,640]{2,1,0:T(8,128)(2,1)} %pad_maximum_fusion.4), channel_id=1, source_target_pairs={{0,8},{2,10},{4,12},{6,14},{8,0},{10,2},{12,4},{14,6},{17,25},{19,... | collective-permute-start | bytes 921608 | tf_op jit(solution)/shard_map/ppermute | solution.py:48
  15.6 17.9 %collective-permute-start.3 = (bf16[2,256,640]{2,1,0:T(8,128)(2,1)S(1)}, bf16[2,256,640]{2,1,0:T(8,128)(2,1)S(1)}, u32[]{:S(2)}, u32[]{:S(2)}) collective-permute-start(bf16[2,256,640]{2,1,0:T(8,128)(2,1)S(1)} %pad_maximum_fusion.1.refs_0_.refs_3_), channel_id=1, source_target_pairs={{0,2},{1,3},{2,0},{3,1},{4,6},{5,7},{6,4},{7,5},{8,10},{9,11},{10,... | collective-permute-start | bytes 1966088 | tf_op jit(solution)/shard_map/ppermute | solution.py:48
  18.4 8.9 %collective-permute-start.10 = (bf16[3,80,640]{2,1,0:T(8,128)(2,1)}, bf16[3,80,640]{2,1,0:T(8,128)(2,1)S(1)}, u32[]{:S(2)}, u32[]{:S(2)}) collective-permute-start(bf16[3,80,640]{2,1,0:T(8,128)(2,1)} %collective-permute-done.8), channel_id=1, source_target_pairs={{1,9},{3,11},{5,13},{7,15},{9,1},{11,3},{13,5},{15,7},{16,24},{18,... | collective-permute-start | bytes 921608 | tf_op jit(solution)/shard_map/ppermute | solution.py:48
  20.4 2.8 %copy-start.15 = (bf16[3,40,640]{2,1,0:T(8,128)(2,1)S(1)}, bf16[3,40,640]{2,1,0:T(8,128)(2,1)}, u32[]{:S(2)}) copy-start(bf16[3,40,640]{2,1,0:T(8,128)(2,1)} %copy-done.14) | copy-start | bytes 460804
  20.5 22.2 %collective-permute-start.4 = (bf16[2,256,640]{2,1,0:T(8,128)(2,1)S(1)}, bf16[2,256,640]{2,1,0:T(8,128)(2,1)S(1)}, u32[]{:S(2)}, u32[]{:S(2)}) collective-permute-start(bf16[2,256,640]{2,1,0:T(8,128)(2,1)S(1)} %pad_maximum_fusion.2.refs_1_.refs_4_), channel_id=1, source_target_pairs={{0,2},{1,3},{2,0},{3,1},{4,6},{5,7},{6,4},{7,5},{8,10},{9,11},{10,... | collective-permute-start | bytes 1966088 | tf_op jit(solution)/shard_map/ppermute | solution.py:48
  24.2 6.0 %copy-start.6 = (bf16[3,80,640]{2,1,0:T(8,128)(2,1)}, bf16[3,80,640]{2,1,0:T(8,128)(2,1)S(1)}, u32[]{:S(2)}) copy-start(bf16[3,80,640]{2,1,0:T(8,128)(2,1)S(1)} %broadcast_select_fusion.5.refs_6_) | copy-start | bytes 921604
  24.2 7.8 %collective-permute-start.11 = (bf16[3,80,640]{2,1,0:T(8,128)(2,1)S(1)}, bf16[3,80,640]{2,1,0:T(8,128)(2,1)S(1)}, u32[]{:S(2)}, u32[]{:S(2)}) collective-permute-start(bf16[3,80,640]{2,1,0:T(8,128)(2,1)S(1)} %broadcast_select_fusion.5.refs_6_), channel_id=1, source_target_pairs={{0,4},{1,5},{2,6},{3,7},{4,0},{5,1},{6,2},{7,3},{8,12},{9,13},{10,... | collective-permute-start | bytes 921608 | tf_op jit(solution)/shard_map/ppermute | solution.py:48
  27.3 2.9 %copy-start.8 = (bf16[3,80,640]{2,1,0:T(8,128)(2,1)}, bf16[3,80,640]{2,1,0:T(8,128)(2,1)S(1)}, u32[]{:S(2)}) copy-start(bf16[3,80,640]{2,1,0:T(8,128)(2,1)S(1)} %broadcast_select_fusion.4.refs_7_) | copy-start | bytes 921604
  27.4 15.3 %collective-permute-start.12 = (bf16[3,80,640]{2,1,0:T(8,128)(2,1)S(1)}, bf16[3,80,640]{2,1,0:T(8,128)(2,1)S(1)}, u32[]{:S(2)}, u32[]{:S(2)}) collective-permute-start(bf16[3,80,640]{2,1,0:T(8,128)(2,1)S(1)} %broadcast_select_fusion.4.refs_7_), channel_id=1, source_target_pairs={{0,4},{1,5},{2,6},{3,7},{4,0},{5,1},{6,2},{7,3},{8,12},{9,13},{10,... | collective-permute-start | bytes 921608 | tf_op jit(solution)/shard_map/ppermute | solution.py:48
  30.1 27.9 %collective-permute-start.29 = (bf16[4,256,384]{2,1,0:T(8,128)(2,1)}, bf16[4,256,384]{2,1,0:T(8,128)(2,1)}, u32[]{:S(2)}, u32[]{:S(2)}) collective-permute-start(bf16[4,256,384]{2,1,0:T(8,128)(2,1)} %pad_maximum_fusion), channel_id=1, source_target_pairs={{0,4},{1,5},{2,6},{3,7},{4,0},{5,1},{6,2},{7,3},{8,12},{9,13},{10,... | collective-permute-start | bytes 2359304 | tf_op jit(solution)/shard_map/ppermute | solution.py:48
  30.2 0.7 copy-start.10
  30.9 11.8 %copy-start.12 = (bf16[2,256,256]{2,1,0:T(8,128)(2,1)}, bf16[2,256,256]{2,1,0:T(8,128)(2,1)S(1)}, u32[]{:S(2)}) copy-start(bf16[2,256,256]{2,1,0:T(8,128)(2,1)S(1)} %slice.19) | copy-start | bytes 786436
  31.8 15.1 %copy-start.3 = (f32[3,40,640]{2,1,0:T(8,128)S(1)}, f32[3,40,640]{2,1,0:T(8,128)}, u32[]{:S(2)}) copy-start(f32[3,40,640]{2,1,0:T(8,128)} %refs_5_.1) | copy-start | bytes 921604
  32.0 30.1 %collective-permute-start.14 = (bf16[4,256,256]{2,1,0:T(8,128)(2,1)}, bf16[4,256,256]{2,1,0:T(8,128)(2,1)}, u32[]{:S(2)}, u32[]{:S(2)}) collective-permute-start(bf16[4,256,256]{2,1,0:T(8,128)(2,1)} %pad_maximum_fusion.3), channel_id=1, source_target_pairs={{4,12},{5,13},{6,14},{7,15},{12,20},{13,21},{14,22},{15,23},{20,28... | collective-permute-start | bytes 1572872 | tf_op jit(solution)/shard_map/ppermute | solution.py:48
  42.7 11.3 %copy-start.1 = (bf16[2,256,640]{2,1,0:T(8,128)(2,1)}, bf16[2,256,640]{2,1,0:T(8,128)(2,1)S(1)}, u32[]{:S(2)}) copy-start(bf16[2,256,640]{2,1,0:T(8,128)(2,1)S(1)} %collective-permute-done.4.refs_3_.refs_6_) | copy-start | bytes 1966084
  45.6 23.1 %collective-permute-start.13 = (bf16[2,3,80,640]{3,2,1,0:T(8,128)(2,1)}, bf16[2,3,80,640]{3,2,1,0:T(8,128)(2,1)}, u32[]{:S(2)}, u32[]{:S(2)}) collective-permute-start(bf16[2,3,80,640]{3,2,1,0:T(8,128)(2,1)} %shard_map.95), channel_id=1, source_target_pairs={{0,4},{1,5},{2,6},{3,7},{4,0},{5,1},{6,2},{7,3},{8,12},{9,13},{10,... | collective-permute-start | bytes 1843208 | tf_op jit(solution)/shard_map/ppermute | solution.py:48
  46.9 28.4 %collective-permute-start.18 = (f32[3,40,640]{2,1,0:T(8,128)S(1)}, f32[3,40,640]{2,1,0:T(8,128)}, u32[]{:S(2)}, u32[]{:S(2)}) collective-permute-start(f32[3,40,640]{2,1,0:T(8,128)S(1)} %copy-done.3), channel_id=1, source_target_pairs={{1,0},{3,2},{5,4},{7,6},{9,8},{11,10},{13,12},{15,14},{16,17},{18,... | collective-permute-start | bytes 921608 | tf_op jit(solution)/shard_map/ppermute | solution.py:48
  54.0 1.0 copy-start.7
  54.9 1.0 copy-start.9
  55.9 6.2 %copy-start.11 = (bf16[2,256,256]{2,1,0:T(8,128)(2,1)S(1)}, bf16[2,256,256]{2,1,0:T(8,128)(2,1)}, u32[]{:S(2)}) copy-start(bf16[2,256,256]{2,1,0:T(8,128)(2,1)} %copy-done.10) | copy-start | bytes 786436
  55.9 6.2 %copy-start.13 = (bf16[2,256,256]{2,1,0:T(8,128)(2,1)S(1)}, bf16[2,256,256]{2,1,0:T(8,128)(2,1)}, u32[]{:S(2)}) copy-start(bf16[2,256,256]{2,1,0:T(8,128)(2,1)} %copy-done.12) | copy-start | bytes 786436
  58.0 49.0 %collective-permute-start.30 = (bf16[4,256,384]{2,1,0:T(8,128)(2,1)}, bf16[4,256,384]{2,1,0:T(8,128)(2,1)}, u32[]{:S(2)}, u32[]{:S(2)}) collective-permute-start(bf16[4,256,384]{2,1,0:T(8,128)(2,1)} %collective-permute-done.29), channel_id=1, source_target_pairs={{0,8},{1,9},{2,10},{3,11},{8,16},{9,17},{10,18},{11,19},{16,24},{1... | collective-permute-start | bytes 2359304 | tf_op jit(solution)/shard_map/ppermute | solution.py:48
  70.0 12.8 %collective-permute-start.15 = (bf16[3,80,640]{2,1,0:T(8,128)(2,1)S(1)}, bf16[3,80,640]{2,1,0:T(8,128)(2,1)S(1)}, u32[]{:S(2)}, u32[]{:S(2)}) collective-permute-start(bf16[3,80,640]{2,1,0:T(8,128)(2,1)S(1)} %get-tuple-element.25), channel_id=1, source_target_pairs={{1,17},{3,19},{5,21},{7,23},{9,25},{11,27},{13,29},{15,31},{16,0},... | collective-permute-start | bytes 921608 | tf_op jit(solution)/shard_map/ppermute | solution.py:48
  71.3 17.4 %collective-permute-start.16 = (bf16[3,80,640]{2,1,0:T(8,128)(2,1)S(1)}, bf16[3,80,640]{2,1,0:T(8,128)(2,1)S(1)}, u32[]{:S(2)}, u32[]{:S(2)}) collective-permute-start(bf16[3,80,640]{2,1,0:T(8,128)(2,1)S(1)} %get-tuple-element.26), channel_id=1, source_target_pairs={{1,25},{3,27},{5,29},{7,31},{9,17},{11,19},{13,21},{15,23},{16,8},... | collective-permute-start | bytes 921608 | tf_op jit(solution)/shard_map/ppermute | solution.py:48
  74.6 14.1 %collective-permute-start.17 = (bf16[3,80,640]{2,1,0:T(8,128)(2,1)S(1)}, bf16[3,80,640]{2,1,0:T(8,128)(2,1)S(1)}, u32[]{:S(2)}, u32[]{:S(2)}) collective-permute-start(bf16[3,80,640]{2,1,0:T(8,128)(2,1)S(1)} %get-tuple-element.26), channel_id=1, source_target_pairs={{0,8},{2,10},{4,12},{6,14},{8,0},{10,2},{12,4},{14,6},{17,25},{19,... | collective-permute-start | bytes 921608 | tf_op jit(solution)/shard_map/ppermute | solution.py:48
  88.7 3.7 %copy-start.18 = (bf16[256,1280]{1,0:T(8,128)(2,1)S(1)}, bf16[256,1280]{1,0:T(8,128)(2,1)}, u32[]{:S(2)}) copy-start(bf16[256,1280]{1,0:T(8,128)(2,1)} %param.7) | copy-start | bytes 1966084
  90.8 2.3 %copy-start.4 = (f32[2,3,40,640]{3,2,1,0:T(8,128)}, f32[2,3,40,640]{3,2,1,0:T(8,128)S(1)}, u32[]{:S(2)}) copy-start(f32[2,3,40,640]{3,2,1,0:T(8,128)S(1)} %get-tuple-element.28) | copy-start | bytes 1843204
  90.8 7.4 %copy-start.19 = (f32[1280]{0:T(1024)S(1)}, f32[1280]{0:T(1024)}, u32[]{:S(2)}) copy-start(f32[1280]{0:T(1024)} %param.13) | copy-start | bytes 15364
  90.8 14.3 %collective-permute-start.19 = (bf16[3,80,640]{2,1,0:T(8,128)(2,1)}, bf16[3,80,640]{2,1,0:T(8,128)(2,1)}, u32[]{:S(2)}, u32[]{:S(2)}) collective-permute-start(bf16[3,80,640]{2,1,0:T(8,128)(2,1)} %get-tuple-element.27), channel_id=1, source_target_pairs={{0,16},{2,18},{4,20},{6,22},{8,24},{10,26},{12,28},{14,30},{17,1},... | collective-permute-start | bytes 921608 | tf_op jit(solution)/shard_map/ppermute | solution.py:48
  92.3 17.5 %collective-permute-start.32 = (bf16[4,256,256]{2,1,0:T(8,128)(2,1)}, bf16[4,256,256]{2,1,0:T(8,128)(2,1)}, u32[]{:S(2)}, u32[]{:S(2)}) collective-permute-start(bf16[4,256,256]{2,1,0:T(8,128)(2,1)} %broadcast_select_fusion.1), channel_id=1, source_target_pairs={{0,4},{1,5},{2,6},{3,7},{4,0},{5,1},{6,2},{7,3},{8,12},{9,13},{10,... | collective-permute-start | bytes 1572872 | tf_op jit(solution)/shard_map/ppermute | solution.py:48
  93.1 21.3 %collective-permute-start = (bf16[256,640]{1,0:T(8,128)(2,1)}, bf16[256,640]{1,0:T(8,128)(2,1)S(1)}, u32[]{:S(2)}, u32[]{:S(2)}) collective-permute-start(bf16[256,640]{1,0:T(8,128)(2,1)} %get-tuple-element.44), channel_id=1, source_target_pairs={{0,1},{1,0},{2,3},{3,2},{4,5},{5,4},{6,7},{7,6},{8,9},{9,8},{10,11... | collective-permute-start | bytes 983048 | tf_op jit(solution)/shard_map/ppermute | solution.py:48
  98.4 13.7 %collective-permute-start.23 = (bf16[3,80,640]{2,1,0:T(8,128)(2,1)}, bf16[3,80,640]{2,1,0:T(8,128)(2,1)S(1)}, u32[]{:S(2)}, u32[]{:S(2)}) collective-permute-start(bf16[3,80,640]{2,1,0:T(8,128)(2,1)} %get-tuple-element.27), channel_id=1, source_target_pairs={{0,8},{2,10},{4,12},{6,14},{8,0},{10,2},{12,4},{14,6},{17,25},{19,... | collective-permute-start | bytes 921608 | tf_op jit(solution)/shard_map/ppermute | solution.py:48
  105.1 9.2 %collective-permute-start.24 = (bf16[3,80,640]{2,1,0:T(8,128)(2,1)}, bf16[3,80,640]{2,1,0:T(8,128)(2,1)S(1)}, u32[]{:S(2)}, u32[]{:S(2)}) collective-permute-start(bf16[3,80,640]{2,1,0:T(8,128)(2,1)} %collective-permute-done.19), channel_id=1, source_target_pairs={{1,9},{3,11},{5,13},{7,15},{9,1},{11,3},{13,5},{15,7},{16,24},{18,... | collective-permute-start | bytes 921608 | tf_op jit(solution)/shard_map/ppermute | solution.py:48
  108.3 6.1 %copy-start.5 = (f32[2,3,40,640]{3,2,1,0:T(8,128)S(1)}, f32[2,3,40,640]{3,2,1,0:T(8,128)}, u32[]{:S(2)}) copy-start(f32[2,3,40,640]{3,2,1,0:T(8,128)} %copy-done.4) | copy-start | bytes 1843204
  108.3 21.6 %copy-start.2 = (bf16[2,256,640]{2,1,0:T(8,128)(2,1)S(1)}, bf16[2,256,640]{2,1,0:T(8,128)(2,1)}, u32[]{:S(2)}) copy-start(bf16[2,256,640]{2,1,0:T(8,128)(2,1)} %copy-done.1) | copy-start | bytes 1966084
  108.3 21.6 %collective-permute-start.31 = (bf16[4,256,384]{2,1,0:T(8,128)(2,1)S(1)}, bf16[4,256,384]{2,1,0:T(8,128)(2,1)S(1)}, u32[]{:S(2)}, u32[]{:S(2)}) collective-permute-start(bf16[4,256,384]{2,1,0:T(8,128)(2,1)S(1)} %broadcast_select_fusion.refs_7_), channel_id=1, source_target_pairs={{2,0},{3,1},{6,4},{7,5},{10,8},{11,9},{14,12},{15,13},{18,16},{19,... | collective-permute-start | bytes 2359304 | tf_op jit(solution)/shard_map/ppermute | solution.py:48
  109.7 34.4 %collective-permute-start.33 = (bf16[4,256,256]{2,1,0:T(8,128)(2,1)}, bf16[4,256,256]{2,1,0:T(8,128)(2,1)S(1)}, u32[]{:S(2)}, u32[]{:S(2)}) collective-permute-start(bf16[4,256,256]{2,1,0:T(8,128)(2,1)} %collective-permute-done.32.refs_7_), channel_id=1, source_target_pairs={{2,0},{3,1},{6,4},{7,5},{10,8},{11,9},{14,12},{15,13},{18,16},{19,... | collective-permute-start | bytes 1572872 | tf_op jit(solution)/shard_map/ppermute | solution.py:48
  112.1 32.1 %collective-permute-start.21 = (bf16[3,80,640]{2,1,0:T(8,128)(2,1)S(1)}, bf16[3,80,640]{2,1,0:T(8,128)(2,1)S(1)}, u32[]{:S(2)}, u32[]{:S(2)}) collective-permute-start(bf16[3,80,640]{2,1,0:T(8,128)(2,1)S(1)} %broadcast_select_fusion.3.refs_2_), channel_id=1, source_target_pairs={{0,2},{1,3},{2,0},{3,1},{4,6},{5,7},{6,4},{7,5},{8,10},{9,11},{10,... | collective-permute-start | bytes 921608 | tf_op jit(solution)/shard_map/ppermute | solution.py:48
  114.3 34.5 %collective-permute-start.26 = (bf16[3,80,640]{2,1,0:T(8,128)(2,1)S(1)}, bf16[3,80,640]{2,1,0:T(8,128)(2,1)S(1)}, u32[]{:S(2)}, u32[]{:S(2)}) collective-permute-start(bf16[3,80,640]{2,1,0:T(8,128)(2,1)S(1)} %broadcast_select_fusion.2.refs_4_), channel_id=1, source_target_pairs={{0,4},{1,5},{2,6},{3,7},{4,0},{5,1},{6,2},{7,3},{8,12},{9,13},{10,... | collective-permute-start | bytes 921608 | tf_op jit(solution)/shard_map/ppermute | solution.py:48
  114.5 35.7 %collective-permute-start.28 = (f32[3,40,640]{2,1,0:T(8,128)S(1)}, f32[3,40,640]{2,1,0:T(8,128)S(1)}, u32[]{:S(2)}, u32[]{:S(2)}) collective-permute-start(f32[3,40,640]{2,1,0:T(8,128)S(1)} %slice_bitcast_fusion), channel_id=1, source_target_pairs={{0,1},{2,3},{4,5},{6,7},{8,9},{10,11},{12,13},{14,15},{17,16},{19,... | collective-permute-start | bytes 921608 | tf_op jit(solution)/shard_map/ppermute | solution.py:48
  129.9 22.9 %collective-permute-start.20 = (bf16[3,80,640]{2,1,0:T(8,128)(2,1)S(1)}, bf16[3,80,640]{2,1,0:T(8,128)(2,1)S(1)}, u32[]{:S(2)}, u32[]{:S(2)}) collective-permute-start(bf16[3,80,640]{2,1,0:T(8,128)(2,1)S(1)} %broadcast_select_fusion.3.refs_2_), channel_id=1, source_target_pairs={{0,4},{1,5},{2,6},{3,7},{4,0},{5,1},{6,2},{7,3},{8,12},{9,13},{10,... | collective-permute-start | bytes 921608 | tf_op jit(solution)/shard_map/ppermute | solution.py:48
  144.1 8.6 %collective-permute-start.25 = (bf16[3,80,640]{2,1,0:T(8,128)(2,1)S(1)}, bf16[3,80,640]{2,1,0:T(8,128)(2,1)S(1)}, u32[]{:S(2)}, u32[]{:S(2)}) collective-permute-start(bf16[3,80,640]{2,1,0:T(8,128)(2,1)S(1)} %broadcast_select_fusion.2.refs_4_), channel_id=1, source_target_pairs={{0,2},{1,3},{2,0},{3,1},{4,6},{5,7},{6,4},{7,5},{8,10},{9,11},{10,... | collective-permute-start | bytes 921608 | tf_op jit(solution)/shard_map/ppermute | solution.py:48
  144.1 8.6 %collective-permute-start.22 = (bf16[3,80,640]{2,1,0:T(8,128)(2,1)S(1)}, bf16[3,80,640]{2,1,0:T(8,128)(2,1)S(1)}, u32[]{:S(2)}, u32[]{:S(2)}) collective-permute-start(bf16[3,80,640]{2,1,0:T(8,128)(2,1)S(1)} %collective-permute-done.21.refs_3_), channel_id=1, source_target_pairs={{0,4},{1,5},{2,6},{3,7},{4,0},{5,1},{6,2},{7,3},{8,12},{9,13},{10,... | collective-permute-start | bytes 921608 | tf_op jit(solution)/shard_map/ppermute | solution.py:48
  150.4 10.9 %copy-start.16 = (f32[3,40,640]{2,1,0:T(8,128)}, f32[3,40,640]{2,1,0:T(8,128)S(1)}, u32[]{:S(2)}) copy-start(f32[3,40,640]{2,1,0:T(8,128)S(1)} %get-tuple-element.19) | copy-start | bytes 921604
  150.4 8.0 %collective-permute-start.27 = (bf16[3,80,640]{2,1,0:T(8,128)(2,1)S(1)}, bf16[3,80,640]{2,1,0:T(8,128)(2,1)S(1)}, u32[]{:S(2)}, u32[]{:S(2)}) collective-permute-start(bf16[3,80,640]{2,1,0:T(8,128)(2,1)S(1)} %collective-permute-done.26.refs_5_), channel_id=1, source_target_pairs={{0,2},{1,3},{2,0},{3,1},{4,6},{5,7},{6,4},{7,5},{8,10},{9,11},{10,... | collective-permute-start | bytes 921608 | tf_op jit(solution)/shard_map/ppermute | solution.py:48
  161.3 1.6 collective-permute-start.34

commit v6 on v5

--- a/solution.py
+++ b/solution.py
@@ -284,7 +284,7 @@
 
 
 def att_kernel(low, where, q_kept, q_came, k_own, v_own, k_near, v_near, two, back, out,
-               quer, keys, vals, bias):
+               quer, keys, vals, bias, arrivals):
     tokens = q_kept.shape[0]
     span = 2 * tokens
     reach = WINDOW + span
@@ -294,18 +294,29 @@
     mine = core * tokens
     theirs = (1 - core) * tokens
 
+    copies = []
+    for idx, (dest, near) in enumerate(((keys, k_near), (vals, v_near))):
+        for side, at in enumerate((mine, theirs)):
+            rows = pl.ds(pl.multiple_of(span + at, tokens), tokens)
+            copies.append(
+                pltpu.make_async_copy(
+                    near.at[side, :, pl.ds(low, wide)], dest.at[rows], arrivals.at[2 * idx + side]
+                )
+            )
+
+    @pl.when(odd == 1)
+    def _():
+        for copy in copies:
+            copy.start()
+
     def put(dest, base, first, second):
         dest[pl.ds(pl.multiple_of(base + mine, tokens), tokens), :] = first
         dest[pl.ds(pl.multiple_of(base + theirs, tokens), tokens), :] = second
 
     put(quer, 0, q_kept[:, cols], q_came[:, cols])
-    for idx, (dest, own, near) in enumerate(((keys, k_own, k_near), (vals, v_own, v_near))):
+    for idx, (dest, own) in enumerate(((keys, k_own), (vals, v_own))):
         put(dest, 2 * span, own[0, :, cols], own[1, :, cols])
         put(dest, 0, two[2 * idx], two[2 * idx + 1])
-
-        @pl.when(odd == 1)
-        def _():
-            put(dest, span, near[0, :, cols], near[1, :, cols])
 
         @pl.when(odd == 0)
         def _():
@@ -316,6 +327,12 @@
     col = lax.broadcasted_iota(jnp.int32, (span, reach), 1)
     seen = (col > row) & (col <= row + WINDOW) & (chip * span - WINDOW + col >= 0)
     bias[...] = jnp.where(seen, 0.0, MASKED)
+
+    @pl.when(odd == 1)
+    def _():
+        for copy in copies:
+            copy.wait()
+
     for head in range(wide // ATT_DIM):
         at = slice(head * ATT_DIM, (head + 1) * ATT_DIM)
         scores = nt_dot(quer[:, at], keys[:, at]) + bias[...]
@@ -335,13 +352,17 @@
     return pl.pallas_call(
         lambda *refs: att_kernel(low, *refs),
         out_shape=jax.ShapeDtypeStruct((span, wide), F32),
-        in_specs=[pl.BlockSpec(memory_space=pltpu.SMEM)] + [vmem()] * 8,
+        in_specs=[pl.BlockSpec(memory_space=pltpu.SMEM)]
+        + [vmem()] * 4
+        + [pl.BlockSpec(memory_space=pl.ANY)] * 2
+        + [vmem()] * 2,
         out_specs=vmem(),
         scratch_shapes=[
             pltpu.VMEM((span, wide), BF16),
             pltpu.VMEM((reach, wide), BF16),
             pltpu.VMEM((reach, wide), BF16),
             pltpu.VMEM((span, reach), F32),
+            pltpu.SemaphoreType.DMA((4,)),
         ],
         compiler_params=grant(30),
         cost_estimate=pl.CostEstimate(

time: 165 us -> 166 us (level)
  transfers between devices with their start and end apart: 35 -> 35, of which waited for: 13 -> 13; matrix products, arithmetic and copies ran while one was open for 7% -> 7% of each run, Pallas kernels for 12% -> 13%
where the time goes in v6:
time: 166 us; the launch traced here: 164 us
  waiting for transfers between devices  69.5 us (42%)
  starting transfers between devices  55.2 us (33%)
  Pallas kernels  23.4 us (14%)
  other arithmetic  8.23 us (5%)
  local copies, waits for them, and re-layouts  6.45 us (4%)
    ppermute x35, waiting for transfers between devices, send(): return lax.ppermute(array, 'seq', route)  69.5 us
    ppermute x35, starting transfers between devices, send(): return lax.ppermute(array, 'seq', route)  55.2 us
    pallas_call x2, Pallas kernels, attention(): pl.pallas_call(lambda *refs: att_kernel(low, *refs), out_shape=jax.ShapeD...  10.8 us
    pallas_call x2, Pallas kernels, key_side(): pl.pallas_call(lambda *refs: key_kernel(grad_scale, *refs), out_shape=jax...  5.03 us
  transfers between devices with their start and end apart: 35, of which 13 were waited for; matrix products, arithmetic and copies ran while one was open for 7% of the time, Pallas kernels for 13%

profile of v6, /device:TPU:1, one launch (start us, length us, event | category | flops | bytes accessed | tf_op | source)
XLA Modules:
  0.0 164.1 jit_solution(8845066130475187229)
XLA Ops:
  0.6 2.1 %collective-permute-start.7 = (f32[3,40,640]{2,1,0:T(8,128)}, f32[3,40,640]{2,1,0:T(8,128)S(1)}, u32[]{:S(2)}, u32[]{:S(2)}) collective-permute-start(f32[3,40,640]{2,1,0:T(8,128)} %refs_3_.1), channel_id=1, source_target_pairs={{1,0},{3,2},{5,4},{7,6},{9,8},{11,10},{13,12},{15,14},{16,17},{18,... | collective-permute-start | bytes 921608 | tf_op jit(solution)/shard_map/ppermute | solution.py:48
  2.8 1.9 %dynamic-slice_bitcast_fusion.1 = (bf16[1,256,640]{2,1,0:T(8,128)(2,1)S(1)}, bf16[256,640]{1,0:T(8,128)(2,1)}) fusion(bf16[256,1280]{1,0:T(8,128)(2,1)} %param.8, s32[]{:T(128)S(6)} %select_n.90, s32[]{:T(128)S(6)} %select_n.91), kind=kLoop, calls=%fused_computation.7 | loop fusion | bytes 1310728 | tf_op jit(solution)/shard_map/stack | solution.py:408
  4.7 0.1 dynamic-slice_bitcast_fusion
  4.8 0.5 collective-permute-start.2
  5.4 0.8 pad_maximum_fusion.4
  6.2 1.3 collective-permute-start.8
  7.5 5.3 %collective-permute-start.5 = (f32[1,256]{1,0:T(1,128)S(1)}, f32[1,256]{1,0:T(1,128)S(1)}, u32[]{:S(2)}, u32[]{:S(2)}) collective-permute-start(f32[1,256]{1,0:T(1,128)S(1)} %get-tuple-element.47), channel_id=1, source_target_pairs={{0,1},{1,0},{2,3},{3,2},{4,5},{5,4},{6,7},{7,6},{8,9},{9,8},{10,11... | collective-permute-start | bytes 3080 | tf_op jit(solution)/shard_map/ppermute | solution.py:48
  12.8 0.8 collective-permute-done.5
  13.6 1.2 collective-permute-start.6
  14.8 0.7 collective-permute-start.9
  15.6 0.3 collective-permute-start.3
  15.9 2.5 %collective-permute-done.8 = bf16[3,80,640]{2,1,0:T(8,128)(2,1)} collective-permute-done((bf16[3,80,640]{2,1,0:T(8,128)(2,1)}, bf16[3,80,640]{2,1,0:T(8,128)(2,1)}, u32[]{:S(2)}, u32[]{:S(2)}) %collective-permute-start.8) | collective-permute-done | bytes 307232 | tf_op jit(solution)/shard_map/ppermute | solution.py:48
  18.4 1.9 %collective-permute-start.10 = (bf16[3,80,640]{2,1,0:T(8,128)(2,1)}, bf16[3,80,640]{2,1,0:T(8,128)(2,1)S(1)}, u32[]{:S(2)}, u32[]{:S(2)}) collective-permute-start(bf16[3,80,640]{2,1,0:T(8,128)(2,1)} %collective-permute-done.8), channel_id=1, source_target_pairs={{1,9},{3,11},{5,13},{7,15},{9,1},{11,3},{13,5},{15,7},{16,24},{18,... | collective-permute-start | bytes 921608 | tf_op jit(solution)/shard_map/ppermute | solution.py:48
  20.5 2.6 %collective-permute-start.4 = (bf16[2,256,640]{2,1,0:T(8,128)(2,1)S(1)}, bf16[2,256,640]{2,1,0:T(8,128)(2,1)S(1)}, u32[]{:S(2)}, u32[]{:S(2)}) collective-permute-start(bf16[2,256,640]{2,1,0:T(8,128)(2,1)S(1)} %pad_maximum_fusion.2.refs_1_.refs_4_), channel_id=1, source_target_pairs={{0,2},{1,3},{2,0},{3,1},{4,6},{5,7},{6,4},{7,5},{8,10},{9,11},{10,... | collective-permute-start | bytes 1966088 | tf_op jit(solution)/shard_map/ppermute | solution.py:48
  23.1 1.1 broadcast_select_fusion.5.refs_6_
  24.2 1.3 collective-permute-start.11
  25.5 1.8 %collective-permute-done.10 = bf16[3,80,640]{2,1,0:T(8,128)(2,1)S(1)} collective-permute-done((bf16[3,80,640]{2,1,0:T(8,128)(2,1)}, bf16[3,80,640]{2,1,0:T(8,128)(2,1)S(1)}, u32[]{:S(2)}, u32[]{:S(2)}) %collective-permute-start.10) | collective-permute-done | bytes 307232 | tf_op jit(solution)/shard_map/ppermute | solution.py:48
  27.4 1.8 %collective-permute-start.12 = (bf16[3,80,640]{2,1,0:T(8,128)(2,1)S(1)}, bf16[3,80,640]{2,1,0:T(8,128)(2,1)S(1)}, u32[]{:S(2)}, u32[]{:S(2)}) collective-permute-start(bf16[3,80,640]{2,1,0:T(8,128)(2,1)S(1)} %broadcast_select_fusion.4.refs_7_), channel_id=1, source_target_pairs={{0,4},{1,5},{2,6},{3,7},{4,0},{5,1},{6,2},{7,3},{8,12},{9,13},{10,... | collective-permute-start | bytes 921608 | tf_op jit(solution)/shard_map/ppermute | solution.py:48
  29.2 1.0 pad_maximum_fusion
  30.2 0.7 copy-done.10
  30.9 0.9 pad_maximum_fusion.3
  31.8 0.2 collective-permute-done.11.refs_6_
  32.0 1.4 collective-permute-start.14
  33.5 9.2 %collective-permute-done.4.refs_3_.refs_6_ = bf16[2,256,640]{2,1,0:T(8,128)(2,1)S(1)} collective-permute-done((bf16[2,256,640]{2,1,0:T(8,128)(2,1)S(1)}, bf16[2,256,640]{2,1,0:T(8,128)(2,1)S(1)}, u32[]{:S(2)}, u32[]{:S(2)}) %collective-permute-start.4) | collective-permute-done | bytes 655392 | tf_op jit(solution)/shard_map/ppermute | solution.py:48
  42.7 2.9 %shard_map.95 = bf16[2,3,80,640]{3,2,1,0:T(8,128)(2,1)} custom-call(bf16[2,256,640]{2,1,0:T(8,128)(2,1)S(1)} %pad_maximum_fusion.1.refs_0_.refs_3_, bf16[2,256,640]{2,1,0:T(8,128)(2,1)S(1)} %pad_maximum_fusion.2.refs_1_.refs_4_, bf16[2,256,640]{2,1,0:T(8,128)(2,1)S(1)} %collective-permute-done.3.refs_2_.refs_5_, ...), custom_call_target="tpu_custom_call" | custom-call | flops 1258291200 | bytes 2621440 | tf_op jit(solution)/shard_map/pallas_call | solution.py:184
  45.6 1.2 collective-permute-start.13
  46.9 7.1 %collective-permute-start.18 = (f32[3,40,640]{2,1,0:T(8,128)S(1)}, f32[3,40,640]{2,1,0:T(8,128)}, u32[]{:S(2)}, u32[]{:S(2)}) collective-permute-start(f32[3,40,640]{2,1,0:T(8,128)S(1)} %copy-done.3), channel_id=1, source_target_pairs={{1,0},{3,2},{5,4},{7,6},{9,8},{11,10},{13,12},{15,14},{16,17},{18,... | collective-permute-start | bytes 921608 | tf_op jit(solution)/shard_map/ppermute | solution.py:48
  54.0 1.0 copy-done.7
  54.9 1.0 copy-done.9
  55.9 2.1 %shard_map.94.low = f32[2,3,80,640]{3,2,1,0:T(8,128)S(1)} custom-call(bf16[2,256,640]{2,1,0:T(8,128)(2,1)S(1)} %pad_maximum_fusion.1.refs_0_.refs_3_, bf16[2,256,640]{2,1,0:T(8,128)(2,1)S(1)} %pad_maximum_fusion.2.refs_1_.refs_4_, bf16[2,256,640]{2,1,0:T(8,128)(2,1)S(1)} %collective-permute-done.3.refs_2_.refs_5_, ...), custom_call_target="tpu_custom_call" | custom-call | flops 1258291200 | bytes 2621440 | tf_op jit(solution)/shard_map/pallas_call | solution.py:184
  58.0 4.1 %collective-permute-start.30 = (bf16[4,256,384]{2,1,0:T(8,128)(2,1)}, bf16[4,256,384]{2,1,0:T(8,128)(2,1)}, u32[]{:S(2)}, u32[]{:S(2)}) collective-permute-start(bf16[4,256,384]{2,1,0:T(8,128)(2,1)} %collective-permute-done.29), channel_id=1, source_target_pairs={{0,8},{1,9},{2,10},{3,11},{8,16},{9,17},{10,18},{11,19},{16,24},{1... | collective-permute-start | bytes 2359304 | tf_op jit(solution)/shard_map/ppermute | solution.py:48
  62.1 0.9 broadcast_select_fusion.1
  63.0 5.7 %collective-permute-done.13.arrived = bf16[2,3,80,640]{3,2,1,0:T(8,128)(2,1)} collective-permute-done((bf16[2,3,80,640]{3,2,1,0:T(8,128)(2,1)}, bf16[2,3,80,640]{3,2,1,0:T(8,128)(2,1)}, u32[]{:S(2)}, u32[]{:S(2)}) %collective-permute-start.13) | collective-permute-done | bytes 614432 | tf_op jit(solution)/shard_map/ppermute | solution.py:48
  68.7 1.2 fold.1
  70.0 1.3 collective-permute-start.15
  71.3 3.3 %collective-permute-start.16 = (bf16[3,80,640]{2,1,0:T(8,128)(2,1)S(1)}, bf16[3,80,640]{2,1,0:T(8,128)(2,1)S(1)}, u32[]{:S(2)}, u32[]{:S(2)}) collective-permute-start(bf16[3,80,640]{2,1,0:T(8,128)(2,1)S(1)} %get-tuple-element.26), channel_id=1, source_target_pairs={{1,25},{3,27},{5,29},{7,31},{9,17},{11,19},{13,21},{15,23},{16,8},... | collective-permute-start | bytes 921608 | tf_op jit(solution)/shard_map/ppermute | solution.py:48
  74.6 0.7 collective-permute-start.17
  75.3 7.5 %collective-permute-done.15.refs_0_ = bf16[3,80,640]{2,1,0:T(8,128)(2,1)S(1)} collective-permute-done((bf16[3,80,640]{2,1,0:T(8,128)(2,1)S(1)}, bf16[3,80,640]{2,1,0:T(8,128)(2,1)S(1)}, u32[]{:S(2)}, u32[]{:S(2)}) %collective-permute-start.15) | collective-permute-done | bytes 307232 | tf_op jit(solution)/shard_map/ppermute | solution.py:48
  82.8 5.9 %collective-permute-done.16.refs_1_ = bf16[3,80,640]{2,1,0:T(8,128)(2,1)S(1)} collective-permute-done((bf16[3,80,640]{2,1,0:T(8,128)(2,1)S(1)}, bf16[3,80,640]{2,1,0:T(8,128)(2,1)S(1)}, u32[]{:S(2)}, u32[]{:S(2)}) %collective-permute-start.16) | collective-permute-done | bytes 307232 | tf_op jit(solution)/shard_map/ppermute | solution.py:48
  88.7 2.2 %update.1 = (f32[2,3,40,640]{3,2,1,0:T(8,128)S(1)}, bf16[3,80,640]{2,1,0:T(8,128)(2,1)}) custom-call(f32[3,80,640]{2,1,0:T(8,128)S(1)} %get-tuple-element.24.part, bf16[3,80,640]{2,1,0:T(8,128)(2,1)S(1)} %collective-permute-done.15.refs_0_, bf16[3,80,640]{2,1,0:T(8,128)(2,1)S(1)} %collective-permute-done.16.refs_1_, ...), custom_call_target="tpu_custom_call" | custom-call | flops 1536000 | bytes 3072000 | tf_op jit(solution)/shard_map/update/pallas_call | solution.py:110
  90.8 1.4 collective-permute-start.19
  92.3 0.8 constant_dynamic-slice_fusion.4
  93.1 5.2 %collective-permute-start = (bf16[256,640]{1,0:T(8,128)(2,1)}, bf16[256,640]{1,0:T(8,128)(2,1)S(1)}, u32[]{:S(2)}, u32[]{:S(2)}) collective-permute-start(bf16[256,640]{1,0:T(8,128)(2,1)} %get-tuple-element.44), channel_id=1, source_target_pairs={{0,1},{1,0},{2,3},{3,2},{4,5},{5,4},{6,7},{7,6},{8,9},{9,8},{10,11... | collective-permute-start | bytes 983048 | tf_op jit(solution)/shard_map/ppermute | solution.py:48
  98.4 0.7 collective-permute-start.23
  99.0 6.1 %collective-permute-done.19 = bf16[3,80,640]{2,1,0:T(8,128)(2,1)} collective-permute-done((bf16[3,80,640]{2,1,0:T(8,128)(2,1)}, bf16[3,80,640]{2,1,0:T(8,128)(2,1)}, u32[]{:S(2)}, u32[]{:S(2)}) %collective-permute-start.19) | collective-permute-done | bytes 307232 | tf_op jit(solution)/shard_map/ppermute | solution.py:48
  105.1 1.9 %collective-permute-start.24 = (bf16[3,80,640]{2,1,0:T(8,128)(2,1)}, bf16[3,80,640]{2,1,0:T(8,128)(2,1)S(1)}, u32[]{:S(2)}, u32[]{:S(2)}) collective-permute-start(bf16[3,80,640]{2,1,0:T(8,128)(2,1)} %collective-permute-done.19), channel_id=1, source_target_pairs={{1,9},{3,11},{5,13},{7,15},{9,1},{11,3},{13,5},{15,7},{16,24},{18,... | collective-permute-start | bytes 921608 | tf_op jit(solution)/shard_map/ppermute | solution.py:48
  107.0 1.2 broadcast_select_fusion.refs_7_
  108.3 1.4 collective-permute-start.31
  109.7 1.3 collective-permute-start.33
  111.0 1.0 broadcast_select_fusion.3.refs_2_
  112.1 2.2 %collective-permute-start.21 = (bf16[3,80,640]{2,1,0:T(8,128)(2,1)S(1)}, bf16[3,80,640]{2,1,0:T(8,128)(2,1)S(1)}, u32[]{:S(2)}, u32[]{:S(2)}) collective-permute-start(bf16[3,80,640]{2,1,0:T(8,128)(2,1)S(1)} %broadcast_select_fusion.3.refs_2_), channel_id=1, source_target_pairs={{0,2},{1,3},{2,0},{3,1},{4,6},{5,7},{6,4},{7,5},{8,10},{9,11},{10,... | collective-permute-start | bytes 921608 | tf_op jit(solution)/shard_map/ppermute | solution.py:48
  114.5 1.3 collective-permute-start.28
  115.8 14.0 %collective-permute-done.31.refs_8_ = bf16[4,256,384]{2,1,0:T(8,128)(2,1)S(1)} collective-permute-done((bf16[4,256,384]{2,1,0:T(8,128)(2,1)S(1)}, bf16[4,256,384]{2,1,0:T(8,128)(2,1)S(1)}, u32[]{:S(2)}, u32[]{:S(2)}) %collective-permute-start.31) | collective-permute-done | bytes 786464 | tf_op jit(solution)/shard_map/ppermute | solution.py:48
  129.9 5.8 %shard_map.96.refs_9_ = f32[512,384]{1,0:T(8,128)S(1)} custom-call(s32[3]{0:T(128)S(1)} %pad_add_fusion.refs_0_, bf16[256,640]{1,0:T(8,128)(2,1)S(1)} %get-tuple-element.45.refs_0_.refs_1_, bf16[256,640]{1,0:T(8,128)(2,1)S(1)} %collective-permute-done.refs_1_.refs_2_, bf16[2,256,640]{2,1,0:T(8,128)(2,1)S(1)} %pad_maximum_fusion.1.refs_0_.refs_3_, ...), custom_call_target="tpu_custom_call" | custom-call | flops 1207959552 | bytes 3932160 | tf_op jit(solution)/shard_map/pallas_call | solution.py:352
  135.7 8.5 %collective-permute-done.21.refs_3_ = bf16[3,80,640]{2,1,0:T(8,128)(2,1)S(1)} collective-permute-done((bf16[3,80,640]{2,1,0:T(8,128)(2,1)S(1)}, bf16[3,80,640]{2,1,0:T(8,128)(2,1)S(1)}, u32[]{:S(2)}, u32[]{:S(2)}) %collective-permute-start.21) | collective-permute-done | bytes 307232 | tf_op jit(solution)/shard_map/ppermute | solution.py:48
  144.2 5.1 %shard_map.97.refs_10_ = f32[512,256]{1,0:T(8,128)S(1)} custom-call(s32[3]{0:T(128)S(1)} %pad_add_fusion.refs_0_, bf16[256,640]{1,0:T(8,128)(2,1)S(1)} %get-tuple-element.45.refs_0_.refs_1_, bf16[256,640]{1,0:T(8,128)(2,1)S(1)} %collective-permute-done.refs_1_.refs_2_, bf16[2,256,640]{2,1,0:T(8,128)(2,1)S(1)} %pad_maximum_fusion.1.refs_0_.refs_3_, ...), custom_call_target="tpu_custom_call" | custom-call | flops 805306368 | bytes 2621440 | tf_op jit(solution)/shard_map/pallas_call | solution.py:352
  149.2 1.3 query_first.1.refs_7_
  150.6 0.2 multiply_reduce_fusion.1
  150.8 1.5 collective-permute-start.27
  152.3 0.9 multiply_multiply_fusion
  153.2 5.7 %collective-permute-done.27.refs_6_ = bf16[3,80,640]{2,1,0:T(8,128)(2,1)S(1)} collective-permute-done((bf16[3,80,640]{2,1,0:T(8,128)(2,1)S(1)}, bf16[3,80,640]{2,1,0:T(8,128)(2,1)S(1)}, u32[]{:S(2)}, u32[]{:S(2)}) %collective-permute-start.27) | collective-permute-done | bytes 307232 | tf_op jit(solution)/shard_map/ppermute | solution.py:48
  158.8 2.9 %query_last.1 = (bf16[256,1280]{1,0:T(8,128)(2,1)}, bf16[256,640]{1,0:T(8,128)(2,1)S(1)}) custom-call(s32[3]{0:T(128)S(1)} %pad_add_fusion.refs_0_, bf16[256,640]{1,0:T(8,128)(2,1)S(1)} %get-tuple-element.45.refs_0_.refs_1_, bf16[256,640]{1,0:T(8,128)(2,1)S(1)} %collective-permute-done.refs_1_.refs_2_, ...), custom_call_target="tpu_custom_call" | custom-call | flops 629145600 | bytes 1228800 | tf_op jit(solution)/shard_map/query_last/pallas_call | solution.py:267
  161.7 1.6 collective-permute-done.34
  163.3 0.8 constant_dynamic-update-slice_fusion
  (86 shorter events, 0.9 us)
Async XLA Ops:
  0.6 4.0 %copy-start.17 = (bf16[256,1280]{1,0:T(8,128)(2,1)S(1)}, bf16[256,1280]{1,0:T(8,128)(2,1)}, u32[]{:S(2)}) copy-start(bf16[256,1280]{1,0:T(8,128)(2,1)} %param.9) | copy-start | bytes 1966084
  0.6 4.7 %collective-permute-start.7 = (f32[3,40,640]{2,1,0:T(8,128)}, f32[3,40,640]{2,1,0:T(8,128)S(1)}, u32[]{:S(2)}, u32[]{:S(2)}) collective-permute-start(f32[3,40,640]{2,1,0:T(8,128)} %refs_3_.1), channel_id=1, source_target_pairs={{1,0},{3,2},{5,4},{7,6},{9,8},{11,10},{13,12},{15,14},{16,17},{18,... | collective-permute-start | bytes 921608 | tf_op jit(solution)/shard_map/ppermute | solution.py:48
  2.7 2.6 %copy-start = (f32[3,40,640]{2,1,0:T(8,128)S(1)}, f32[3,40,640]{2,1,0:T(8,128)}, u32[]{:S(2)}) copy-start(f32[3,40,640]{2,1,0:T(8,128)} %refs_3_.1) | copy-start | bytes 921604
  4.7 2.8 %copy-start.20 = (f32[2,256]{1,0:T(2,128)S(1)}, f32[2,256]{1,0:T(2,128)}, u32[]{:S(2)}) copy-start(f32[2,256]{1,0:T(2,128)} %param.10) | copy-start | bytes 6148
  4.7 10.9 %collective-permute-start.1 = (bf16[256,640]{1,0:T(8,128)(2,1)}, bf16[256,640]{1,0:T(8,128)(2,1)S(1)}, u32[]{:S(2)}, u32[]{:S(2)}) collective-permute-start(bf16[256,640]{1,0:T(8,128)(2,1)} %get-tuple-element.43), channel_id=1, source_target_pairs={{0,1},{1,0},{2,3},{3,2},{4,5},{5,4},{6,7},{7,6},{8,9},{9,8},{10,11... | collective-permute-start | bytes 983048 | tf_op jit(solution)/shard_map/ppermute | solution.py:48
  4.8 15.6 %collective-permute-start.2 = (bf16[256,640]{1,0:T(8,128)(2,1)S(1)}, bf16[256,640]{1,0:T(8,128)(2,1)S(1)}, u32[]{:S(2)}, u32[]{:S(2)}) collective-permute-start(bf16[256,640]{1,0:T(8,128)(2,1)S(1)} %get-tuple-element.41), channel_id=1, source_target_pairs={{0,1},{1,0},{2,3},{3,2},{4,5},{5,4},{6,7},{7,6},{8,9},{9,8},{10,11... | collective-permute-start | bytes 983048 | tf_op jit(solution)/shard_map/ppermute | solution.py:48
  5.4 10.1 %copy-start.14 = (bf16[3,40,640]{2,1,0:T(8,128)(2,1)}, bf16[3,40,640]{2,1,0:T(8,128)(2,1)S(1)}, u32[]{:S(2)}) copy-start(bf16[3,40,640]{2,1,0:T(8,128)(2,1)S(1)} %convert_element_type.7) | copy-start | bytes 460804
  6.2 12.3 %collective-permute-start.8 = (bf16[3,80,640]{2,1,0:T(8,128)(2,1)}, bf16[3,80,640]{2,1,0:T(8,128)(2,1)}, u32[]{:S(2)}, u32[]{:S(2)}) collective-permute-start(bf16[3,80,640]{2,1,0:T(8,128)(2,1)} %pad_maximum_fusion.4), channel_id=1, source_target_pairs={{0,16},{2,18},{4,20},{6,22},{8,24},{10,26},{12,28},{14,30},{17,1},... | collective-permute-start | bytes 921608 | tf_op jit(solution)/shard_map/ppermute | solution.py:48
  7.5 6.2 %collective-permute-start.5 = (f32[1,256]{1,0:T(1,128)S(1)}, f32[1,256]{1,0:T(1,128)S(1)}, u32[]{:S(2)}, u32[]{:S(2)}) collective-permute-start(f32[1,256]{1,0:T(1,128)S(1)} %get-tuple-element.47), channel_id=1, source_target_pairs={{0,1},{1,0},{2,3},{3,2},{4,5},{5,4},{6,7},{7,6},{8,9},{9,8},{10,11... | collective-permute-start | bytes 3080 | tf_op jit(solution)/shard_map/ppermute | solution.py:48
  13.6 16.5 %collective-permute-start.6 = (f32[2,256]{1,0:T(2,128)S(1)}, f32[2,256]{1,0:T(2,128)S(1)}, u32[]{:S(2)}, u32[]{:S(2)}) collective-permute-start(f32[2,256]{1,0:T(2,128)S(1)} %pad_maximum_fusion.5.refs_4_), channel_id=1, source_target_pairs={{0,2},{1,3},{2,0},{3,1},{4,6},{5,7},{6,4},{7,5},{8,10},{9,11},{10,... | collective-permute-start | bytes 6152 | tf_op jit(solution)/shard_map/ppermute | solution.py:48
  14.8 9.4 %collective-permute-start.9 = (bf16[3,80,640]{2,1,0:T(8,128)(2,1)}, bf16[3,80,640]{2,1,0:T(8,128)(2,1)S(1)}, u32[]{:S(2)}, u32[]{:S(2)}) collective-permute-start(bf16[3,80,640]{2,1,0:T(8,128)(2,1)} %pad_maximum_fusion.4), channel_id=1, source_target_pairs={{0,8},{2,10},{4,12},{6,14},{8,0},{10,2},{12,4},{14,6},{17,25},{19,... | collective-permute-start | bytes 921608 | tf_op jit(solution)/shard_map/ppermute | solution.py:48
  15.6 17.9 %collective-permute-start.3 = (bf16[2,256,640]{2,1,0:T(8,128)(2,1)S(1)}, bf16[2,256,640]{2,1,0:T(8,128)(2,1)S(1)}, u32[]{:S(2)}, u32[]{:S(2)}) collective-permute-start(bf16[2,256,640]{2,1,0:T(8,128)(2,1)S(1)} %pad_maximum_fusion.1.refs_0_.refs_3_), channel_id=1, source_target_pairs={{0,2},{1,3},{2,0},{3,1},{4,6},{5,7},{6,4},{7,5},{8,10},{9,11},{10,... | collective-permute-start | bytes 1966088 | tf_op jit(solution)/shard_map/ppermute | solution.py:48
  18.4 8.9 %collective-permute-start.10 = (bf16[3,80,640]{2,1,0:T(8,128)(2,1)}, bf16[3,80,640]{2,1,0:T(8,128)(2,1)S(1)}, u32[]{:S(2)}, u32[]{:S(2)}) collective-permute-start(bf16[3,80,640]{2,1,0:T(8,128)(2,1)} %collective-permute-done.8), channel_id=1, source_target_pairs={{1,9},{3,11},{5,13},{7,15},{9,1},{11,3},{13,5},{15,7},{16,24},{18,... | collective-permute-start | bytes 921608 | tf_op jit(solution)/shard_map/ppermute | solution.py:48
  20.4 2.8 %copy-start.15 = (bf16[3,40,640]{2,1,0:T(8,128)(2,1)S(1)}, bf16[3,40,640]{2,1,0:T(8,128)(2,1)}, u32[]{:S(2)}) copy-start(bf16[3,40,640]{2,1,0:T(8,128)(2,1)} %copy-done.14) | copy-start | bytes 460804
  20.5 22.2 %collective-permute-start.4 = (bf16[2,256,640]{2,1,0:T(8,128)(2,1)S(1)}, bf16[2,256,640]{2,1,0:T(8,128)(2,1)S(1)}, u32[]{:S(2)}, u32[]{:S(2)}) collective-permute-start(bf16[2,256,640]{2,1,0:T(8,128)(2,1)S(1)} %pad_maximum_fusion.2.refs_1_.refs_4_), channel_id=1, source_target_pairs={{0,2},{1,3},{2,0},{3,1},{4,6},{5,7},{6,4},{7,5},{8,10},{9,11},{10,... | collective-permute-start | bytes 1966088 | tf_op jit(solution)/shard_map/ppermute | solution.py:48
  24.2 6.0 %copy-start.6 = (bf16[3,80,640]{2,1,0:T(8,128)(2,1)}, bf16[3,80,640]{2,1,0:T(8,128)(2,1)S(1)}, u32[]{:S(2)}) copy-start(bf16[3,80,640]{2,1,0:T(8,128)(2,1)S(1)} %broadcast_select_fusion.5.refs_6_) | copy-start | bytes 921604
  24.2 7.8 %collective-permute-start.11 = (bf16[3,80,640]{2,1,0:T(8,128)(2,1)S(1)}, bf16[3,80,640]{2,1,0:T(8,128)(2,1)S(1)}, u32[]{:S(2)}, u32[]{:S(2)}) collective-permute-start(bf16[3,80,640]{2,1,0:T(8,128)(2,1)S(1)} %broadcast_select_fusion.5.refs_6_), channel_id=1, source_target_pairs={{0,4},{1,5},{2,6},{3,7},{4,0},{5,1},{6,2},{7,3},{8,12},{9,13},{10,... | collective-permute-start | bytes 921608 | tf_op jit(solution)/shard_map/ppermute | solution.py:48
  27.3 2.9 %copy-start.8 = (bf16[3,80,640]{2,1,0:T(8,128)(2,1)}, bf16[3,80,640]{2,1,0:T(8,128)(2,1)S(1)}, u32[]{:S(2)}) copy-start(bf16[3,80,640]{2,1,0:T(8,128)(2,1)S(1)} %broadcast_select_fusion.4.refs_7_) | copy-start | bytes 921604
  27.4 15.3 %collective-permute-start.12 = (bf16[3,80,640]{2,1,0:T(8,128)(2,1)S(1)}, bf16[3,80,640]{2,1,0:T(8,128)(2,1)S(1)}, u32[]{:S(2)}, u32[]{:S(2)}) collective-permute-start(bf16[3,80,640]{2,1,0:T(8,128)(2,1)S(1)} %broadcast_select_fusion.4.refs_7_), channel_id=1, source_target_pairs={{0,4},{1,5},{2,6},{3,7},{4,0},{5,1},{6,2},{7,3},{8,12},{9,13},{10,... | collective-permute-start | bytes 921608 | tf_op jit(solution)/shard_map/ppermute | solution.py:48
  30.1 27.9 %collective-permute-start.29 = (bf16[4,256,384]{2,1,0:T(8,128)(2,1)}, bf16[4,256,384]{2,1,0:T(8,128)(2,1)}, u32[]{:S(2)}, u32[]{:S(2)}) collective-permute-start(bf16[4,256,384]{2,1,0:T(8,128)(2,1)} %pad_maximum_fusion), channel_id=1, source_target_pairs={{0,4},{1,5},{2,6},{3,7},{4,0},{5,1},{6,2},{7,3},{8,12},{9,13},{10,... | collective-permute-start | bytes 2359304 | tf_op jit(solution)/shard_map/ppermute | solution.py:48
  30.2 0.7 copy-start.10
  30.9 11.8 %copy-start.12 = (bf16[2,256,256]{2,1,0:T(8,128)(2,1)}, bf16[2,256,256]{2,1,0:T(8,128)(2,1)S(1)}, u32[]{:S(2)}) copy-start(bf16[2,256,256]{2,1,0:T(8,128)(2,1)S(1)} %slice.19) | copy-start | bytes 786436
  31.8 15.1 %copy-start.3 = (f32[3,40,640]{2,1,0:T(8,128)S(1)}, f32[3,40,640]{2,1,0:T(8,128)}, u32[]{:S(2)}) copy-start(f32[3,40,640]{2,1,0:T(8,128)} %refs_5_.1) | copy-start | bytes 921604
  32.0 30.1 %collective-permute-start.14 = (bf16[4,256,256]{2,1,0:T(8,128)(2,1)}, bf16[4,256,256]{2,1,0:T(8,128)(2,1)}, u32[]{:S(2)}, u32[]{:S(2)}) collective-permute-start(bf16[4,256,256]{2,1,0:T(8,128)(2,1)} %pad_maximum_fusion.3), channel_id=1, source_target_pairs={{4,12},{5,13},{6,14},{7,15},{12,20},{13,21},{14,22},{15,23},{20,28... | collective-permute-start | bytes 1572872 | tf_op jit(solution)/shard_map/ppermute | solution.py:48
  42.7 11.3 %copy-start.1 = (bf16[2,256,640]{2,1,0:T(8,128)(2,1)}, bf16[2,256,640]{2,1,0:T(8,128)(2,1)S(1)}, u32[]{:S(2)}) copy-start(bf16[2,256,640]{2,1,0:T(8,128)(2,1)S(1)} %collective-permute-done.4.refs_3_.refs_6_) | copy-start | bytes 1966084
  45.6 23.1 %collective-permute-start.13 = (bf16[2,3,80,640]{3,2,1,0:T(8,128)(2,1)}, bf16[2,3,80,640]{3,2,1,0:T(8,128)(2,1)}, u32[]{:S(2)}, u32[]{:S(2)}) collective-permute-start(bf16[2,3,80,640]{3,2,1,0:T(8,128)(2,1)} %shard_map.95), channel_id=1, source_target_pairs={{0,4},{1,5},{2,6},{3,7},{4,0},{5,1},{6,2},{7,3},{8,12},{9,13},{10,... | collective-permute-start | bytes 1843208 | tf_op jit(solution)/shard_map/ppermute | solution.py:48
  46.9 28.4 %collective-permute-start.18 = (f32[3,40,640]{2,1,0:T(8,128)S(1)}, f32[3,40,640]{2,1,0:T(8,128)}, u32[]{:S(2)}, u32[]{:S(2)}) collective-permute-start(f32[3,40,640]{2,1,0:T(8,128)S(1)} %copy-done.3), channel_id=1, source_target_pairs={{1,0},{3,2},{5,4},{7,6},{9,8},{11,10},{13,12},{15,14},{16,17},{18,... | collective-permute-start | bytes 921608 | tf_op jit(solution)/shard_map/ppermute | solution.py:48
  54.0 1.0 copy-start.7
  54.9 1.0 copy-start.9
  55.9 6.2 %copy-start.11 = (bf16[2,256,256]{2,1,0:T(8,128)(2,1)S(1)}, bf16[2,256,256]{2,1,0:T(8,128)(2,1)}, u32[]{:S(2)}) copy-start(bf16[2,256,256]{2,1,0:T(8,128)(2,1)} %copy-done.10) | copy-start | bytes 786436
  55.9 6.2 %copy-start.13 = (bf16[2,256,256]{2,1,0:T(8,128)(2,1)S(1)}, bf16[2,256,256]{2,1,0:T(8,128)(2,1)}, u32[]{:S(2)}) copy-start(bf16[2,256,256]{2,1,0:T(8,128)(2,1)} %copy-done.12) | copy-start | bytes 786436
  58.0 49.0 %collective-permute-start.30 = (bf16[4,256,384]{2,1,0:T(8,128)(2,1)}, bf16[4,256,384]{2,1,0:T(8,128)(2,1)}, u32[]{:S(2)}, u32[]{:S(2)}) collective-permute-start(bf16[4,256,384]{2,1,0:T(8,128)(2,1)} %collective-permute-done.29), channel_id=1, source_target_pairs={{0,8},{1,9},{2,10},{3,11},{8,16},{9,17},{10,18},{11,19},{16,24},{1... | collective-permute-start | bytes 2359304 | tf_op jit(solution)/shard_map/ppermute | solution.py:48
  70.0 12.8 %collective-permute-start.15 = (bf16[3,80,640]{2,1,0:T(8,128)(2,1)S(1)}, bf16[3,80,640]{2,1,0:T(8,128)(2,1)S(1)}, u32[]{:S(2)}, u32[]{:S(2)}) collective-permute-start(bf16[3,80,640]{2,1,0:T(8,128)(2,1)S(1)} %get-tuple-element.25), channel_id=1, source_target_pairs={{1,17},{3,19},{5,21},{7,23},{9,25},{11,27},{13,29},{15,31},{16,0},... | collective-permute-start | bytes 921608 | tf_op jit(solution)/shard_map/ppermute | solution.py:48
  71.3 17.4 %collective-permute-start.16 = (bf16[3,80,640]{2,1,0:T(8,128)(2,1)S(1)}, bf16[3,80,640]{2,1,0:T(8,128)(2,1)S(1)}, u32[]{:S(2)}, u32[]{:S(2)}) collective-permute-start(bf16[3,80,640]{2,1,0:T(8,128)(2,1)S(1)} %get-tuple-element.26), channel_id=1, source_target_pairs={{1,25},{3,27},{5,29},{7,31},{9,17},{11,19},{13,21},{15,23},{16,8},... | collective-permute-start | bytes 921608 | tf_op jit(solution)/shard_map/ppermute | solution.py:48
  74.6 14.1 %collective-permute-start.17 = (bf16[3,80,640]{2,1,0:T(8,128)(2,1)S(1)}, bf16[3,80,640]{2,1,0:T(8,128)(2,1)S(1)}, u32[]{:S(2)}, u32[]{:S(2)}) collective-permute-start(bf16[3,80,640]{2,1,0:T(8,128)(2,1)S(1)} %get-tuple-element.26), channel_id=1, source_target_pairs={{0,8},{2,10},{4,12},{6,14},{8,0},{10,2},{12,4},{14,6},{17,25},{19,... | collective-permute-start | bytes 921608 | tf_op jit(solution)/shard_map/ppermute | solution.py:48
  88.7 3.7 %copy-start.18 = (bf16[256,1280]{1,0:T(8,128)(2,1)S(1)}, bf16[256,1280]{1,0:T(8,128)(2,1)}, u32[]{:S(2)}) copy-start(bf16[256,1280]{1,0:T(8,128)(2,1)} %param.7) | copy-start | bytes 1966084
  90.8 2.3 %copy-start.4 = (f32[2,3,40,640]{3,2,1,0:T(8,128)}, f32[2,3,40,640]{3,2,1,0:T(8,128)S(1)}, u32[]{:S(2)}) copy-start(f32[2,3,40,640]{3,2,1,0:T(8,128)S(1)} %get-tuple-element.28) | copy-start | bytes 1843204
  90.8 7.4 %copy-start.19 = (f32[1280]{0:T(1024)S(1)}, f32[1280]{0:T(1024)}, u32[]{:S(2)}) copy-start(f32[1280]{0:T(1024)} %param.13) | copy-start | bytes 15364
  90.8 14.3 %collective-permute-start.19 = (bf16[3,80,640]{2,1,0:T(8,128)(2,1)}, bf16[3,80,640]{2,1,0:T(8,128)(2,1)}, u32[]{:S(2)}, u32[]{:S(2)}) collective-permute-start(bf16[3,80,640]{2,1,0:T(8,128)(2,1)} %get-tuple-element.27), channel_id=1, source_target_pairs={{0,16},{2,18},{4,20},{6,22},{8,24},{10,26},{12,28},{14,30},{17,1},... | collective-permute-start | bytes 921608 | tf_op jit(solution)/shard_map/ppermute | solution.py:48
  92.3 17.5 %collective-permute-start.32 = (bf16[4,256,256]{2,1,0:T(8,128)(2,1)}, bf16[4,256,256]{2,1,0:T(8,128)(2,1)}, u32[]{:S(2)}, u32[]{:S(2)}) collective-permute-start(bf16[4,256,256]{2,1,0:T(8,128)(2,1)} %broadcast_select_fusion.1), channel_id=1, source_target_pairs={{0,4},{1,5},{2,6},{3,7},{4,0},{5,1},{6,2},{7,3},{8,12},{9,13},{10,... | collective-permute-start | bytes 1572872 | tf_op jit(solution)/shard_map/ppermute | solution.py:48
  93.1 21.3 %collective-permute-start = (bf16[256,640]{1,0:T(8,128)(2,1)}, bf16[256,640]{1,0:T(8,128)(2,1)S(1)}, u32[]{:S(2)}, u32[]{:S(2)}) collective-permute-start(bf16[256,640]{1,0:T(8,128)(2,1)} %get-tuple-element.44), channel_id=1, source_target_pairs={{0,1},{1,0},{2,3},{3,2},{4,5},{5,4},{6,7},{7,6},{8,9},{9,8},{10,11... | collective-permute-start | bytes 983048 | tf_op jit(solution)/shard_map/ppermute | solution.py:48
  98.4 13.7 %collective-permute-start.23 = (bf16[3,80,640]{2,1,0:T(8,128)(2,1)}, bf16[3,80,640]{2,1,0:T(8,128)(2,1)S(1)}, u32[]{:S(2)}, u32[]{:S(2)}) collective-permute-start(bf16[3,80,640]{2,1,0:T(8,128)(2,1)} %get-tuple-element.27), channel_id=1, source_target_pairs={{0,8},{2,10},{4,12},{6,14},{8,0},{10,2},{12,4},{14,6},{17,25},{19,... | collective-permute-start | bytes 921608 | tf_op jit(solution)/shard_map/ppermute | solution.py:48
  105.1 9.2 %collective-permute-start.24 = (bf16[3,80,640]{2,1,0:T(8,128)(2,1)}, bf16[3,80,640]{2,1,0:T(8,128)(2,1)S(1)}, u32[]{:S(2)}, u32[]{:S(2)}) collective-permute-start(bf16[3,80,640]{2,1,0:T(8,128)(2,1)} %collective-permute-done.19), channel_id=1, source_target_pairs={{1,9},{3,11},{5,13},{7,15},{9,1},{11,3},{13,5},{15,7},{16,24},{18,... | collective-permute-start | bytes 921608 | tf_op jit(solution)/shard_map/ppermute | solution.py:48
  108.3 6.1 %copy-start.5 = (f32[2,3,40,640]{3,2,1,0:T(8,128)S(1)}, f32[2,3,40,640]{3,2,1,0:T(8,128)}, u32[]{:S(2)}) copy-start(f32[2,3,40,640]{3,2,1,0:T(8,128)} %copy-done.4) | copy-start | bytes 1843204
  108.3 21.6 %copy-start.2 = (bf16[2,256,640]{2,1,0:T(8,128)(2,1)S(1)}, bf16[2,256,640]{2,1,0:T(8,128)(2,1)}, u32[]{:S(2)}) copy-start(bf16[2,256,640]{2,1,0:T(8,128)(2,1)} %copy-done.1) | copy-start | bytes 1966084
  108.3 21.6 %collective-permute-start.31 = (bf16[4,256,384]{2,1,0:T(8,128)(2,1)S(1)}, bf16[4,256,384]{2,1,0:T(8,128)(2,1)S(1)}, u32[]{:S(2)}, u32[]{:S(2)}) collective-permute-start(bf16[4,256,384]{2,1,0:T(8,128)(2,1)S(1)} %broadcast_select_fusion.refs_7_), channel_id=1, source_target_pairs={{2,0},{3,1},{6,4},{7,5},{10,8},{11,9},{14,12},{15,13},{18,16},{19,... | collective-permute-start | bytes 2359304 | tf_op jit(solution)/shard_map/ppermute | solution.py:48
  109.7 34.4 %collective-permute-start.33 = (bf16[4,256,256]{2,1,0:T(8,128)(2,1)}, bf16[4,256,256]{2,1,0:T(8,128)(2,1)S(1)}, u32[]{:S(2)}, u32[]{:S(2)}) collective-permute-start(bf16[4,256,256]{2,1,0:T(8,128)(2,1)} %collective-permute-done.32.refs_7_), channel_id=1, source_target_pairs={{2,0},{3,1},{6,4},{7,5},{10,8},{11,9},{14,12},{15,13},{18,16},{19,... | collective-permute-start | bytes 1572872 | tf_op jit(solution)/shard_map/ppermute | solution.py:48
  112.1 32.1 %collective-permute-start.21 = (bf16[3,80,640]{2,1,0:T(8,128)(2,1)S(1)}, bf16[3,80,640]{2,1,0:T(8,128)(2,1)S(1)}, u32[]{:S(2)}, u32[]{:S(2)}) collective-permute-start(bf16[3,80,640]{2,1,0:T(8,128)(2,1)S(1)} %broadcast_select_fusion.3.refs_2_), channel_id=1, source_target_pairs={{0,2},{1,3},{2,0},{3,1},{4,6},{5,7},{6,4},{7,5},{8,10},{9,11},{10,... | collective-permute-start | bytes 921608 | tf_op jit(solution)/shard_map/ppermute | solution.py:48
  114.3 34.9 %collective-permute-start.26 = (bf16[3,80,640]{2,1,0:T(8,128)(2,1)S(1)}, bf16[3,80,640]{2,1,0:T(8,128)(2,1)S(1)}, u32[]{:S(2)}, u32[]{:S(2)}) collective-permute-start(bf16[3,80,640]{2,1,0:T(8,128)(2,1)S(1)} %broadcast_select_fusion.2.refs_4_), channel_id=1, source_target_pairs={{0,4},{1,5},{2,6},{3,7},{4,0},{5,1},{6,2},{7,3},{8,12},{9,13},{10,... | collective-permute-start | bytes 921608 | tf_op jit(solution)/shard_map/ppermute | solution.py:48
  114.5 36.1 %collective-permute-start.28 = (f32[3,40,640]{2,1,0:T(8,128)S(1)}, f32[3,40,640]{2,1,0:T(8,128)S(1)}, u32[]{:S(2)}, u32[]{:S(2)}) collective-permute-start(f32[3,40,640]{2,1,0:T(8,128)S(1)} %slice_bitcast_fusion), channel_id=1, source_target_pairs={{0,1},{2,3},{4,5},{6,7},{8,9},{10,11},{12,13},{14,15},{17,16},{19,... | collective-permute-start | bytes 921608 | tf_op jit(solution)/shard_map/ppermute | solution.py:48
  129.9 23.3 %collective-permute-start.20 = (bf16[3,80,640]{2,1,0:T(8,128)(2,1)S(1)}, bf16[3,80,640]{2,1,0:T(8,128)(2,1)S(1)}, u32[]{:S(2)}, u32[]{:S(2)}) collective-permute-start(bf16[3,80,640]{2,1,0:T(8,128)(2,1)S(1)} %broadcast_select_fusion.3.refs_2_), channel_id=1, source_target_pairs={{0,4},{1,5},{2,6},{3,7},{4,0},{5,1},{6,2},{7,3},{8,12},{9,13},{10,... | collective-permute-start | bytes 921608 | tf_op jit(solution)/shard_map/ppermute | solution.py:48
  144.1 9.0 %collective-permute-start.25 = (bf16[3,80,640]{2,1,0:T(8,128)(2,1)S(1)}, bf16[3,80,640]{2,1,0:T(8,128)(2,1)S(1)}, u32[]{:S(2)}, u32[]{:S(2)}) collective-permute-start(bf16[3,80,640]{2,1,0:T(8,128)(2,1)S(1)} %broadcast_select_fusion.2.refs_4_), channel_id=1, source_target_pairs={{0,2},{1,3},{2,0},{3,1},{4,6},{5,7},{6,4},{7,5},{8,10},{9,11},{10,... | collective-permute-start | bytes 921608 | tf_op jit(solution)/shard_map/ppermute | solution.py:48
  144.1 9.0 %collective-permute-start.22 = (bf16[3,80,640]{2,1,0:T(8,128)(2,1)S(1)}, bf16[3,80,640]{2,1,0:T(8,128)(2,1)S(1)}, u32[]{:S(2)}, u32[]{:S(2)}) collective-permute-start(bf16[3,80,640]{2,1,0:T(8,128)(2,1)S(1)} %collective-permute-done.21.refs_3_), channel_id=1, source_target_pairs={{0,4},{1,5},{2,6},{3,7},{4,0},{5,1},{6,2},{7,3},{8,12},{9,13},{10,... | collective-permute-start | bytes 921608 | tf_op jit(solution)/shard_map/ppermute | solution.py:48
  150.8 11.0 %copy-start.16 = (f32[3,40,640]{2,1,0:T(8,128)}, f32[3,40,640]{2,1,0:T(8,128)S(1)}, u32[]{:S(2)}) copy-start(f32[3,40,640]{2,1,0:T(8,128)S(1)} %get-tuple-element.19) | copy-start | bytes 921604
  150.8 8.1 %collective-permute-start.27 = (bf16[3,80,640]{2,1,0:T(8,128)(2,1)S(1)}, bf16[3,80,640]{2,1,0:T(8,128)(2,1)S(1)}, u32[]{:S(2)}, u32[]{:S(2)}) collective-permute-start(bf16[3,80,640]{2,1,0:T(8,128)(2,1)S(1)} %collective-permute-done.26.refs_5_), channel_id=1, source_target_pairs={{0,2},{1,3},{2,0},{3,1},{4,6},{5,7},{6,4},{7,5},{8,10},{9,11},{10,... | collective-permute-start | bytes 921608 | tf_op jit(solution)/shard_map/ppermute | solution.py:48
  161.7 1.6 collective-permute-start.34

commit v7 on v6

--- a/solution.py
+++ b/solution.py
@@ -91,20 +91,23 @@
     )(low, arrived)
 
 
-def update_kernel(part, *refs):
+def update_kernel(where, part, *refs):
     arrived = refs[:-6]
     w_own, w_near, m_own, m_near, total, applied = refs[-6:]
     owned = w_own.shape[1]
-    for idx, (weights, momentum) in enumerate(((w_own, m_own), (w_near, m_near))):
-        rows = slice(idx * owned, (idx + 1) * owned)
-        grads = part[:, rows]
-        for came in arrived:
-            grads = grads + came[:, rows].astype(F32)
-        total[idx] = grads
-        applied[:, rows] = updated(weights[...], momentum[...], grads)[0].astype(BF16)
-
-
-def update_pair(part, arrived, *pairs):
+
+    @pl.when(where[3] == 1)
+    def _():
+        for idx, (weights, momentum) in enumerate(((w_own, m_own), (w_near, m_near))):
+            rows = slice(idx * owned, (idx + 1) * owned)
+            grads = part[:, rows]
+            for came in arrived:
+                grads = grads + came[:, rows].astype(F32)
+            total[idx] = grads
+            applied[:, rows] = updated(weights[...], momentum[...], grads)[0].astype(BF16)
+
+
+def update_pair(where, part, arrived, *pairs):
     shape = pairs[0].shape
     rows = (shape[0], 2 * shape[1], shape[2])
     return pl.pallas_call(
@@ -113,14 +116,14 @@
             jax.ShapeDtypeStruct((2,) + shape, F32),
             jax.ShapeDtypeStruct(rows, BF16),
         ],
-        in_specs=[vmem()] * (5 + len(arrived)),
+        in_specs=[pl.BlockSpec(memory_space=pltpu.SMEM)] + [vmem()] * (5 + len(arrived)),
         out_specs=[vmem()] * 2,
         compiler_params=grant(12),
         cost_estimate=pl.CostEstimate(
             flops=20 * math.prod(shape), bytes_accessed=40 * math.prod(shape), transcendentals=0
         ),
         name="update",
-    )(part, *arrived, *pairs)
+    )(where, part, *arrived, *pairs)
 
 
 def nt_dot(left, right):
@@ -343,7 +346,7 @@
         out[:, at] = att * lax.rsqrt(jnp.mean(att * att, axis=-1, keepdims=True) + EPS)
 
 
-def attention(where, quer_in, k_own, v_own, k_near, v_near, two, back, low):
+def attention(where, quer_in, k_own, v_own, k_near, v_near, two, back, low, space):
     tokens = quer_in[0].shape[0]
     wide = two.shape[2]
     span = 2 * tokens
@@ -354,7 +357,7 @@
         out_shape=jax.ShapeDtypeStruct((span, wide), F32),
         in_specs=[pl.BlockSpec(memory_space=pltpu.SMEM)]
         + [vmem()] * 4
-        + [pl.BlockSpec(memory_space=pl.ANY)] * 2
+        + [pl.BlockSpec(memory_space=space)] * 2
         + [vmem()] * 2,
         out_specs=vmem(),
         scratch_shapes=[
@@ -393,7 +396,7 @@
     core = here % 2
     chip = here // 2
     is_home = core == (2 * here) // count
-    where = jnp.stack([core, chip % 2, chip]).astype(jnp.int32)
+    where = jnp.stack([core, chip % 2, chip, is_home.astype(jnp.int32)]).astype(jnp.int32)
 
     my_rate = lax.dynamic_slice_in_dim(step_rates, core, 1, 0)
     their_rate = lax.dynamic_slice_in_dim(step_rates, 1 - core, 1, 0)
@@ -446,11 +449,11 @@
     for k in range(1, len(sent)):
         arrived.append(send(sent[k], routes.home_swap[k]))
     att_in = (where, q_own, k_own, v_own, k_near, v_near)
-    early_att = attention(*att_in, early_two, early_back, 0)
-    late_att = attention(*att_in, late_two, late_back, cut)
+    early_att = attention(*att_in, early_two, early_back, 0, pl.ANY)
+    late_att = attention(*att_in, late_two, late_back, cut, pltpu.VMEM)
 
     total, pair_new = update_pair(
-        part, arrived, fast_weights, their_weights, momentum, their_momentum
+        where, part, arrived, fast_weights, their_weights, momentum, their_momentum
     )
     applied = gather_plane(gather_z(pair_new, routes, is_home), routes)
     partner_grads = send(total[1], routes.pair_out)

time: 166 us -> 168 us (1.012)
  local copies, waits for them, and re-layouts: 6.45 us -> 8.35 us
    unnamed x42, local copies, waits for them, and re-layouts: 2.69 us -> 5.29 us
  transfers between devices with their start and end apart: 35 -> 35, of which waited for: 13 -> 14; matrix products, arithmetic and copies ran while one was open for 7% -> 6% of each run, Pallas kernels for 13% -> 12%
where the time goes in v7:
time: 168 us; the launch traced here: 166 us
  waiting for transfers between devices  68.6 us (41%)
  starting transfers between devices  56.6 us (34%)
  Pallas kernels  22.9 us (14%)
  local copies, waits for them, and re-layouts  8.35 us (5%)
  other arithmetic  8.25 us (5%)
    ppermute x35, waiting for transfers between devices, send(): return lax.ppermute(array, 'seq', route)  68.6 us
    ppermute x35, starting transfers between devices, send(): return lax.ppermute(array, 'seq', route)  56.6 us
    pallas_call x2, Pallas kernels, attention(): pl.pallas_call(lambda *refs: att_kernel(low, *refs), out_shape=jax.ShapeD...  10.3 us
    unnamed x42, local copies, waits for them, and re-layouts  5.29 us
    pallas_call x2, Pallas kernels, key_side(): pl.pallas_call(lambda *refs: key_kernel(grad_scale, *refs), out_shape=jax...  5 us
  transfers between devices with their start and end apart: 35, of which 14 were waited for; matrix products, arithmetic and copies ran while one was open for 6% of the time, Pallas kernels for 12%

profile of v7, /device:TPU:1, one launch (start us, length us, event | category | flops | bytes accessed | tf_op | source)
XLA Modules:
  0.0 165.9 jit_solution(4397076403702135230)
XLA Ops:
  0.6 2.1 %collective-permute-start.7 = (f32[3,40,640]{2,1,0:T(8,128)}, f32[3,40,640]{2,1,0:T(8,128)S(1)}, u32[]{:S(2)}, u32[]{:S(2)}) collective-permute-start(f32[3,40,640]{2,1,0:T(8,128)} %refs_3_.1), channel_id=1, source_target_pairs={{1,0},{3,2},{5,4},{7,6},{9,8},{11,10},{13,12},{15,14},{16,17},{18,... | collective-permute-start | bytes 921608 | tf_op jit(solution)/shard_map/ppermute | solution.py:48
  2.8 1.2 dynamic-slice_bitcast_fusion.1
  4.0 0.8 dynamic-slice_bitcast_fusion
  4.9 0.4 collective-permute-start.2
  5.4 0.8 pad_maximum_fusion.4
  6.2 1.3 collective-permute-start.8
  7.5 5.3 %collective-permute-start.5 = (f32[1,256]{1,0:T(1,128)S(1)}, f32[1,256]{1,0:T(1,128)S(1)}, u32[]{:S(2)}, u32[]{:S(2)}) collective-permute-start(f32[1,256]{1,0:T(1,128)S(1)} %get-tuple-element.47), channel_id=1, source_target_pairs={{0,1},{1,0},{2,3},{3,2},{4,5},{5,4},{6,7},{7,6},{8,9},{9,8},{10,11... | collective-permute-start | bytes 3080 | tf_op jit(solution)/shard_map/ppermute | solution.py:48
  12.8 0.8 collective-permute-done.5
  13.6 1.2 collective-permute-start.6
  14.8 0.7 collective-permute-start.9
  15.9 2.5 %collective-permute-done.8 = bf16[3,80,640]{2,1,0:T(8,128)(2,1)} collective-permute-done((bf16[3,80,640]{2,1,0:T(8,128)(2,1)}, bf16[3,80,640]{2,1,0:T(8,128)(2,1)}, u32[]{:S(2)}, u32[]{:S(2)}) %collective-permute-start.8) | collective-permute-done | bytes 307232 | tf_op jit(solution)/shard_map/ppermute | solution.py:48
  18.4 1.9 %collective-permute-start.10 = (bf16[3,80,640]{2,1,0:T(8,128)(2,1)}, bf16[3,80,640]{2,1,0:T(8,128)(2,1)S(1)}, u32[]{:S(2)}, u32[]{:S(2)}) collective-permute-start(bf16[3,80,640]{2,1,0:T(8,128)(2,1)} %collective-permute-done.8), channel_id=1, source_target_pairs={{1,9},{3,11},{5,13},{7,15},{9,1},{11,3},{13,5},{15,7},{16,24},{18,... | collective-permute-start | bytes 921608 | tf_op jit(solution)/shard_map/ppermute | solution.py:48
  20.4 0.7 copy-done.18
  21.1 1.1 pad_maximum_fusion.2.refs_1_.refs_4_
  22.2 2.6 %collective-permute-start.4 = (bf16[2,256,640]{2,1,0:T(8,128)(2,1)S(1)}, bf16[2,256,640]{2,1,0:T(8,128)(2,1)S(1)}, u32[]{:S(2)}, u32[]{:S(2)}) collective-permute-start(bf16[2,256,640]{2,1,0:T(8,128)(2,1)S(1)} %pad_maximum_fusion.2.refs_1_.refs_4_), channel_id=1, source_target_pairs={{0,2},{1,3},{2,0},{3,1},{4,6},{5,7},{6,4},{7,5},{8,10},{9,11},{10,... | collective-permute-start | bytes 1966088 | tf_op jit(solution)/shard_map/ppermute | solution.py:48
  24.9 1.1 broadcast_select_fusion.5.refs_6_
  25.9 1.3 collective-permute-start.11
  27.4 1.8 %collective-permute-start.12 = (bf16[3,80,640]{2,1,0:T(8,128)(2,1)S(1)}, bf16[3,80,640]{2,1,0:T(8,128)(2,1)S(1)}, u32[]{:S(2)}, u32[]{:S(2)}) collective-permute-start(bf16[3,80,640]{2,1,0:T(8,128)(2,1)S(1)} %broadcast_select_fusion.4.refs_7_), channel_id=1, source_target_pairs={{0,4},{1,5},{2,6},{3,7},{4,0},{5,1},{6,2},{7,3},{8,12},{9,13},{10,... | collective-permute-start | bytes 921608 | tf_op jit(solution)/shard_map/ppermute | solution.py:48
  29.2 1.0 pad_maximum_fusion
  30.2 0.7 copy-done.8
  30.9 0.9 pad_maximum_fusion.3
  31.8 3.3 %collective-permute-done.11.refs_6_ = bf16[3,80,640]{2,1,0:T(8,128)(2,1)S(1)} collective-permute-done((bf16[3,80,640]{2,1,0:T(8,128)(2,1)S(1)}, bf16[3,80,640]{2,1,0:T(8,128)(2,1)S(1)}, u32[]{:S(2)}, u32[]{:S(2)}) %collective-permute-start.11) | collective-permute-done | bytes 307232 | tf_op jit(solution)/shard_map/ppermute | solution.py:48
  35.2 1.5 collective-permute-start.14
  36.6 6.1 %collective-permute-done.4.refs_3_.refs_6_ = bf16[2,256,640]{2,1,0:T(8,128)(2,1)S(1)} collective-permute-done((bf16[2,256,640]{2,1,0:T(8,128)(2,1)S(1)}, bf16[2,256,640]{2,1,0:T(8,128)(2,1)S(1)}, u32[]{:S(2)}, u32[]{:S(2)}) %collective-permute-start.4) | collective-permute-done | bytes 655392 | tf_op jit(solution)/shard_map/ppermute | solution.py:48
  42.7 2.9 %shard_map.95 = bf16[2,3,80,640]{3,2,1,0:T(8,128)(2,1)} custom-call(bf16[2,256,640]{2,1,0:T(8,128)(2,1)S(1)} %pad_maximum_fusion.1.refs_0_.refs_3_, bf16[2,256,640]{2,1,0:T(8,128)(2,1)S(1)} %pad_maximum_fusion.2.refs_1_.refs_4_, bf16[2,256,640]{2,1,0:T(8,128)(2,1)S(1)} %collective-permute-done.3.refs_2_.refs_5_, ...), custom_call_target="tpu_custom_call" | custom-call | flops 1258291200 | bytes 2621440 | tf_op jit(solution)/shard_map/pallas_call | solution.py:187
  45.6 1.2 collective-permute-start.13
  46.9 7.1 %collective-permute-start.18 = (f32[3,40,640]{2,1,0:T(8,128)S(1)}, f32[3,40,640]{2,1,0:T(8,128)}, u32[]{:S(2)}, u32[]{:S(2)}) collective-permute-start(f32[3,40,640]{2,1,0:T(8,128)S(1)} %copy-done.1), channel_id=1, source_target_pairs={{1,0},{3,2},{5,4},{7,6},{9,8},{11,10},{13,12},{15,14},{16,17},{18,... | collective-permute-start | bytes 921608 | tf_op jit(solution)/shard_map/ppermute | solution.py:48
  54.0 1.0 copy-done.5
  54.9 1.0 copy-done.7
  55.9 2.1 %shard_map.94.low = f32[2,3,80,640]{3,2,1,0:T(8,128)S(1)} custom-call(bf16[2,256,640]{2,1,0:T(8,128)(2,1)S(1)} %pad_maximum_fusion.1.refs_0_.refs_3_, bf16[2,256,640]{2,1,0:T(8,128)(2,1)S(1)} %pad_maximum_fusion.2.refs_1_.refs_4_, bf16[2,256,640]{2,1,0:T(8,128)(2,1)S(1)} %collective-permute-done.3.refs_2_.refs_5_, ...), custom_call_target="tpu_custom_call" | custom-call | flops 1258291200 | bytes 2621440 | tf_op jit(solution)/shard_map/pallas_call | solution.py:187
  58.0 0.7 collective-permute-done.29
  58.7 3.6 %collective-permute-start.30 = (bf16[4,256,384]{2,1,0:T(8,128)(2,1)}, bf16[4,256,384]{2,1,0:T(8,128)(2,1)}, u32[]{:S(2)}, u32[]{:S(2)}) collective-permute-start(bf16[4,256,384]{2,1,0:T(8,128)(2,1)} %collective-permute-done.29), channel_id=1, source_target_pairs={{0,8},{1,9},{2,10},{3,11},{8,16},{9,17},{10,18},{11,19},{16,24},{1... | collective-permute-start | bytes 2359304 | tf_op jit(solution)/shard_map/ppermute | solution.py:48
  62.3 0.9 broadcast_select_fusion.1
  63.2 8.7 %collective-permute-done.13.arrived = bf16[2,3,80,640]{3,2,1,0:T(8,128)(2,1)} collective-permute-done((bf16[2,3,80,640]{3,2,1,0:T(8,128)(2,1)}, bf16[2,3,80,640]{3,2,1,0:T(8,128)(2,1)}, u32[]{:S(2)}, u32[]{:S(2)}) %collective-permute-start.13) | collective-permute-done | bytes 614432 | tf_op jit(solution)/shard_map/ppermute | solution.py:48
  71.9 2.0 %fold.1 = (f32[3,80,640]{2,1,0:T(8,128)S(1)}, bf16[3,80,640]{2,1,0:T(8,128)(2,1)}, bf16[3,80,640]{2,1,0:T(8,128)(2,1)}) custom-call(f32[2,3,80,640]{3,2,1,0:T(8,128)S(1)} %shard_map.94.low, bf16[2,3,80,640]{3,2,1,0:T(8,128)(2,1)} %collective-permute-done.13.arrived), custom_call_target="tpu_custom_call" | custom-call | flops 307200 | bytes 3686400 | tf_op jit(solution)/shard_map/fold/pallas_call | solution.py:83
  73.8 0.8 copy-done.2
  74.7 2.0 %collective-permute-start.15 = (bf16[3,80,640]{2,1,0:T(8,128)(2,1)}, bf16[3,80,640]{2,1,0:T(8,128)(2,1)}, u32[]{:S(2)}, u32[]{:S(2)}) collective-permute-start(bf16[3,80,640]{2,1,0:T(8,128)(2,1)} %get-tuple-element.25), channel_id=1, source_target_pairs={{1,17},{3,19},{5,21},{7,23},{9,25},{11,27},{13,29},{15,31},{16,0},... | collective-permute-start | bytes 921608 | tf_op jit(solution)/shard_map/ppermute | solution.py:48
  76.7 2.0 %collective-permute-start.16 = (bf16[3,80,640]{2,1,0:T(8,128)(2,1)}, bf16[3,80,640]{2,1,0:T(8,128)(2,1)}, u32[]{:S(2)}, u32[]{:S(2)}) collective-permute-start(bf16[3,80,640]{2,1,0:T(8,128)(2,1)} %get-tuple-element.26), channel_id=1, source_target_pairs={{1,25},{3,27},{5,29},{7,31},{9,17},{11,19},{13,21},{15,23},{16,8},... | collective-permute-start | bytes 921608 | tf_op jit(solution)/shard_map/ppermute | solution.py:48
  78.7 1.4 collective-permute-start.17
  80.1 2.2 %collective-permute-done.15.refs_0_ = bf16[3,80,640]{2,1,0:T(8,128)(2,1)} collective-permute-done((bf16[3,80,640]{2,1,0:T(8,128)(2,1)}, bf16[3,80,640]{2,1,0:T(8,128)(2,1)}, u32[]{:S(2)}, u32[]{:S(2)}) %collective-permute-start.15) | collective-permute-done | bytes 307232 | tf_op jit(solution)/shard_map/ppermute | solution.py:48
  82.4 6.6 %collective-permute-done.16.refs_1_ = bf16[3,80,640]{2,1,0:T(8,128)(2,1)} collective-permute-done((bf16[3,80,640]{2,1,0:T(8,128)(2,1)}, bf16[3,80,640]{2,1,0:T(8,128)(2,1)}, u32[]{:S(2)}, u32[]{:S(2)}) %collective-permute-start.16) | collective-permute-done | bytes 307232 | tf_op jit(solution)/shard_map/ppermute | solution.py:48
  89.0 1.1 copy-done.3
  90.1 1.4 update.1
  91.4 1.3 collective-permute-start.19
  92.9 6.4 %collective-permute-start = (bf16[256,640]{1,0:T(8,128)(2,1)S(1)}, bf16[256,640]{1,0:T(8,128)(2,1)S(1)}, u32[]{:S(2)}, u32[]{:S(2)}) collective-permute-start(bf16[256,640]{1,0:T(8,128)(2,1)S(1)} %get-tuple-element.44), channel_id=1, source_target_pairs={{0,1},{1,0},{2,3},{3,2},{4,5},{5,4},{6,7},{7,6},{8,9},{9,8},{10,11... | collective-permute-start | bytes 983048 | tf_op jit(solution)/shard_map/ppermute | solution.py:48
  99.3 0.7 collective-permute-start.23
  99.9 5.7 %collective-permute-done.19 = bf16[3,80,640]{2,1,0:T(8,128)(2,1)S(1)} collective-permute-done((bf16[3,80,640]{2,1,0:T(8,128)(2,1)S(1)}, bf16[3,80,640]{2,1,0:T(8,128)(2,1)S(1)}, u32[]{:S(2)}, u32[]{:S(2)}) %collective-permute-start.19) | collective-permute-done | bytes 307232 | tf_op jit(solution)/shard_map/ppermute | solution.py:48
  105.6 1.9 %collective-permute-start.24 = (bf16[3,80,640]{2,1,0:T(8,128)(2,1)S(1)}, bf16[3,80,640]{2,1,0:T(8,128)(2,1)S(1)}, u32[]{:S(2)}, u32[]{:S(2)}) collective-permute-start(bf16[3,80,640]{2,1,0:T(8,128)(2,1)S(1)} %collective-permute-done.19), channel_id=1, source_target_pairs={{1,9},{3,11},{5,13},{7,15},{9,1},{11,3},{13,5},{15,7},{16,24},{18,... | collective-permute-start | bytes 921608 | tf_op jit(solution)/shard_map/ppermute | solution.py:48
  107.5 1.2 broadcast_select_fusion.refs_7_
  108.8 1.3 collective-permute-start.31
  110.1 1.3 collective-permute-start.33
  111.5 2.2 %collective-permute-start.21 = (bf16[3,80,640]{2,1,0:T(8,128)(2,1)S(1)}, bf16[3,80,640]{2,1,0:T(8,128)(2,1)S(1)}, u32[]{:S(2)}, u32[]{:S(2)}) collective-permute-start(bf16[3,80,640]{2,1,0:T(8,128)(2,1)S(1)} %broadcast_select_fusion.3.refs_2_), channel_id=1, source_target_pairs={{0,2},{1,3},{2,0},{3,1},{4,6},{5,7},{6,4},{7,5},{8,10},{9,11},{10,... | collective-permute-start | bytes 921608 | tf_op jit(solution)/shard_map/ppermute | solution.py:48
  113.9 1.3 collective-permute-start.28
  115.3 15.0 %collective-permute-done.31.refs_8_ = bf16[4,256,384]{2,1,0:T(8,128)(2,1)S(1)} collective-permute-done((bf16[4,256,384]{2,1,0:T(8,128)(2,1)S(1)}, bf16[4,256,384]{2,1,0:T(8,128)(2,1)S(1)}, u32[]{:S(2)}, u32[]{:S(2)}) %collective-permute-start.31) | collective-permute-done | bytes 786464 | tf_op jit(solution)/shard_map/ppermute | solution.py:48
  130.3 5.8 %shard_map.96.refs_9_ = f32[512,384]{1,0:T(8,128)S(1)} custom-call(s32[4]{0:T(128)S(1)} %pad_add_fusion.where.refs_0_, bf16[256,640]{1,0:T(8,128)(2,1)S(1)} %get-tuple-element.45.refs_0_.refs_1_, bf16[256,640]{1,0:T(8,128)(2,1)S(1)} %collective-permute-done.refs_1_.refs_2_, bf16[2,256,640]{2,1,0:T(8,128)(2,1)S(1)} %pad_maximum_fusion.1.refs_0_.refs_3_, ...), custom_call_target="tpu_custom_call" | custom-call | flops 1207959552 | bytes 3932160 | tf_op jit(solution)/shard_map/pallas_call | solution.py:355
  136.0 8.7 %collective-permute-done.21.refs_3_ = bf16[3,80,640]{2,1,0:T(8,128)(2,1)S(1)} collective-permute-done((bf16[3,80,640]{2,1,0:T(8,128)(2,1)S(1)}, bf16[3,80,640]{2,1,0:T(8,128)(2,1)S(1)}, u32[]{:S(2)}, u32[]{:S(2)}) %collective-permute-start.21) | collective-permute-done | bytes 307232 | tf_op jit(solution)/shard_map/ppermute | solution.py:48
  145.1 4.6 %shard_map.97.refs_10_ = f32[512,256]{1,0:T(8,128)S(1)} custom-call(s32[4]{0:T(128)S(1)} %pad_add_fusion.where.refs_0_, bf16[256,640]{1,0:T(8,128)(2,1)S(1)} %get-tuple-element.45.refs_0_.refs_1_, bf16[256,640]{1,0:T(8,128)(2,1)S(1)} %collective-permute-done.refs_1_.refs_2_, bf16[2,256,640]{2,1,0:T(8,128)(2,1)S(1)} %pad_maximum_fusion.1.refs_0_.refs_3_, ...), custom_call_target="tpu_custom_call" | custom-call | flops 805306368 | bytes 2621440 | tf_op jit(solution)/shard_map/pallas_call | solution.py:355
  149.7 1.3 query_first.1.refs_7_
  151.2 1.5 collective-permute-start.27
  152.7 0.9 multiply_multiply_fusion
  153.6 6.9 %collective-permute-done.27.refs_6_ = bf16[3,80,640]{2,1,0:T(8,128)(2,1)S(1)} collective-permute-done((bf16[3,80,640]{2,1,0:T(8,128)(2,1)S(1)}, bf16[3,80,640]{2,1,0:T(8,128)(2,1)S(1)}, u32[]{:S(2)}, u32[]{:S(2)}) %collective-permute-start.27) | collective-permute-done | bytes 307232 | tf_op jit(solution)/shard_map/ppermute | solution.py:48
  160.5 2.9 %query_last.1 = (bf16[256,1280]{1,0:T(8,128)(2,1)}, bf16[256,640]{1,0:T(8,128)(2,1)S(1)}) custom-call(s32[4]{0:T(128)S(1)} %pad_add_fusion.where.refs_0_, bf16[256,640]{1,0:T(8,128)(2,1)S(1)} %get-tuple-element.45.refs_0_.refs_1_, bf16[256,640]{1,0:T(8,128)(2,1)S(1)} %collective-permute-done.refs_1_.refs_2_, ...), custom_call_target="tpu_custom_call" | custom-call | flops 629145600 | bytes 1228800 | tf_op jit(solution)/shard_map/query_last/pallas_call | solution.py:270
  163.9 1.3 collective-permute-done.34
  165.1 0.8 constant_dynamic-update-slice_fusion
  (86 shorter events, 2.4 us)
Async XLA Ops:
  0.6 3.4 %copy-start.15 = (bf16[256,1280]{1,0:T(8,128)(2,1)S(1)}, bf16[256,1280]{1,0:T(8,128)(2,1)}, u32[]{:S(2)}) copy-start(bf16[256,1280]{1,0:T(8,128)(2,1)} %param.9) | copy-start | bytes 1966084
  0.6 4.7 %collective-permute-start.7 = (f32[3,40,640]{2,1,0:T(8,128)}, f32[3,40,640]{2,1,0:T(8,128)S(1)}, u32[]{:S(2)}, u32[]{:S(2)}) collective-permute-start(f32[3,40,640]{2,1,0:T(8,128)} %refs_3_.1), channel_id=1, source_target_pairs={{1,0},{3,2},{5,4},{7,6},{9,8},{11,10},{13,12},{15,14},{16,17},{18,... | collective-permute-start | bytes 921608 | tf_op jit(solution)/shard_map/ppermute | solution.py:48
  2.7 2.6 %copy-start = (f32[3,40,640]{2,1,0:T(8,128)S(1)}, f32[3,40,640]{2,1,0:T(8,128)}, u32[]{:S(2)}) copy-start(f32[3,40,640]{2,1,0:T(8,128)} %refs_3_.1) | copy-start | bytes 921604
  3.9 3.5 %copy-start.20 = (f32[2,256]{1,0:T(2,128)S(1)}, f32[2,256]{1,0:T(2,128)}, u32[]{:S(2)}) copy-start(f32[2,256]{1,0:T(2,128)} %param.10) | copy-start | bytes 6148
  3.9 11.6 %collective-permute-start.1 = (bf16[256,640]{1,0:T(8,128)(2,1)S(1)}, bf16[256,640]{1,0:T(8,128)(2,1)S(1)}, u32[]{:S(2)}, u32[]{:S(2)}) collective-permute-start(bf16[256,640]{1,0:T(8,128)(2,1)S(1)} %get-tuple-element.43), channel_id=1, source_target_pairs={{0,1},{1,0},{2,3},{3,2},{4,5},{5,4},{6,7},{7,6},{8,9},{9,8},{10,11... | collective-permute-start | bytes 983048 | tf_op jit(solution)/shard_map/ppermute | solution.py:48
  4.9 15.5 %collective-permute-start.2 = (bf16[256,640]{1,0:T(8,128)(2,1)}, bf16[256,640]{1,0:T(8,128)(2,1)S(1)}, u32[]{:S(2)}, u32[]{:S(2)}) collective-permute-start(bf16[256,640]{1,0:T(8,128)(2,1)} %get-tuple-element.41), channel_id=1, source_target_pairs={{0,1},{1,0},{2,3},{3,2},{4,5},{5,4},{6,7},{7,6},{8,9},{9,8},{10,11... | collective-permute-start | bytes 983048 | tf_op jit(solution)/shard_map/ppermute | solution.py:48
  5.4 10.1 %copy-start.12 = (bf16[3,40,640]{2,1,0:T(8,128)(2,1)}, bf16[3,40,640]{2,1,0:T(8,128)(2,1)S(1)}, u32[]{:S(2)}) copy-start(bf16[3,40,640]{2,1,0:T(8,128)(2,1)S(1)} %convert_element_type.8) | copy-start | bytes 460804
  6.2 12.3 %collective-permute-start.8 = (bf16[3,80,640]{2,1,0:T(8,128)(2,1)}, bf16[3,80,640]{2,1,0:T(8,128)(2,1)}, u32[]{:S(2)}, u32[]{:S(2)}) collective-permute-start(bf16[3,80,640]{2,1,0:T(8,128)(2,1)} %pad_maximum_fusion.4), channel_id=1, source_target_pairs={{0,16},{2,18},{4,20},{6,22},{8,24},{10,26},{12,28},{14,30},{17,1},... | collective-permute-start | bytes 921608 | tf_op jit(solution)/shard_map/ppermute | solution.py:48
  7.5 6.2 %collective-permute-start.5 = (f32[1,256]{1,0:T(1,128)S(1)}, f32[1,256]{1,0:T(1,128)S(1)}, u32[]{:S(2)}, u32[]{:S(2)}) collective-permute-start(f32[1,256]{1,0:T(1,128)S(1)} %get-tuple-element.47), channel_id=1, source_target_pairs={{0,1},{1,0},{2,3},{3,2},{4,5},{5,4},{6,7},{7,6},{8,9},{9,8},{10,11... | collective-permute-start | bytes 3080 | tf_op jit(solution)/shard_map/ppermute | solution.py:48
  13.6 16.5 %collective-permute-start.6 = (f32[2,256]{1,0:T(2,128)S(1)}, f32[2,256]{1,0:T(2,128)S(1)}, u32[]{:S(2)}, u32[]{:S(2)}) collective-permute-start(f32[2,256]{1,0:T(2,128)S(1)} %pad_maximum_fusion.5.refs_4_), channel_id=1, source_target_pairs={{0,2},{1,3},{2,0},{3,1},{4,6},{5,7},{6,4},{7,5},{8,10},{9,11},{10,... | collective-permute-start | bytes 6152 | tf_op jit(solution)/shard_map/ppermute | solution.py:48
  14.8 11.1 %collective-permute-start.9 = (bf16[3,80,640]{2,1,0:T(8,128)(2,1)}, bf16[3,80,640]{2,1,0:T(8,128)(2,1)S(1)}, u32[]{:S(2)}, u32[]{:S(2)}) collective-permute-start(bf16[3,80,640]{2,1,0:T(8,128)(2,1)} %pad_maximum_fusion.4), channel_id=1, source_target_pairs={{0,8},{2,10},{4,12},{6,14},{8,0},{10,2},{12,4},{14,6},{17,25},{19,... | collective-permute-start | bytes 921608 | tf_op jit(solution)/shard_map/ppermute | solution.py:48
  15.6 21.0 %collective-permute-start.3 = (bf16[2,256,640]{2,1,0:T(8,128)(2,1)S(1)}, bf16[2,256,640]{2,1,0:T(8,128)(2,1)S(1)}, u32[]{:S(2)}, u32[]{:S(2)}) collective-permute-start(bf16[2,256,640]{2,1,0:T(8,128)(2,1)S(1)} %pad_maximum_fusion.1.refs_0_.refs_3_), channel_id=1, source_target_pairs={{0,2},{1,3},{2,0},{3,1},{4,6},{5,7},{6,4},{7,5},{8,10},{9,11},{10,... | collective-permute-start | bytes 1966088 | tf_op jit(solution)/shard_map/ppermute | solution.py:48
  18.4 8.9 %collective-permute-start.10 = (bf16[3,80,640]{2,1,0:T(8,128)(2,1)}, bf16[3,80,640]{2,1,0:T(8,128)(2,1)S(1)}, u32[]{:S(2)}, u32[]{:S(2)}) collective-permute-start(bf16[3,80,640]{2,1,0:T(8,128)(2,1)} %collective-permute-done.8), channel_id=1, source_target_pairs={{1,9},{3,11},{5,13},{7,15},{9,1},{11,3},{13,5},{15,7},{16,24},{18,... | collective-permute-start | bytes 921608 | tf_op jit(solution)/shard_map/ppermute | solution.py:48
  20.3 0.7 copy-start.18
  21.1 3.8 %copy-start.13 = (bf16[3,40,640]{2,1,0:T(8,128)(2,1)S(1)}, bf16[3,40,640]{2,1,0:T(8,128)(2,1)}, u32[]{:S(2)}) copy-start(bf16[3,40,640]{2,1,0:T(8,128)(2,1)} %copy-done.12) | copy-start | bytes 460804
  22.2 20.5 %collective-permute-start.4 = (bf16[2,256,640]{2,1,0:T(8,128)(2,1)S(1)}, bf16[2,256,640]{2,1,0:T(8,128)(2,1)S(1)}, u32[]{:S(2)}, u32[]{:S(2)}) collective-permute-start(bf16[2,256,640]{2,1,0:T(8,128)(2,1)S(1)} %pad_maximum_fusion.2.refs_1_.refs_4_), channel_id=1, source_target_pairs={{0,2},{1,3},{2,0},{3,1},{4,6},{5,7},{6,4},{7,5},{8,10},{9,11},{10,... | collective-permute-start | bytes 1966088 | tf_op jit(solution)/shard_map/ppermute | solution.py:48
  25.9 4.3 %copy-start.4 = (bf16[3,80,640]{2,1,0:T(8,128)(2,1)}, bf16[3,80,640]{2,1,0:T(8,128)(2,1)S(1)}, u32[]{:S(2)}) copy-start(bf16[3,80,640]{2,1,0:T(8,128)(2,1)S(1)} %broadcast_select_fusion.5.refs_6_) | copy-start | bytes 921604
  25.9 9.2 %collective-permute-start.11 = (bf16[3,80,640]{2,1,0:T(8,128)(2,1)S(1)}, bf16[3,80,640]{2,1,0:T(8,128)(2,1)S(1)}, u32[]{:S(2)}, u32[]{:S(2)}) collective-permute-start(bf16[3,80,640]{2,1,0:T(8,128)(2,1)S(1)} %broadcast_select_fusion.5.refs_6_), channel_id=1, source_target_pairs={{0,4},{1,5},{2,6},{3,7},{4,0},{5,1},{6,2},{7,3},{8,12},{9,13},{10,... | collective-permute-start | bytes 921608 | tf_op jit(solution)/shard_map/ppermute | solution.py:48
  27.4 2.9 %copy-start.6 = (bf16[3,80,640]{2,1,0:T(8,128)(2,1)}, bf16[3,80,640]{2,1,0:T(8,128)(2,1)S(1)}, u32[]{:S(2)}) copy-start(bf16[3,80,640]{2,1,0:T(8,128)(2,1)S(1)} %broadcast_select_fusion.4.refs_7_) | copy-start | bytes 921604
  27.4 15.3 %collective-permute-start.12 = (bf16[3,80,640]{2,1,0:T(8,128)(2,1)S(1)}, bf16[3,80,640]{2,1,0:T(8,128)(2,1)S(1)}, u32[]{:S(2)}, u32[]{:S(2)}) collective-permute-start(bf16[3,80,640]{2,1,0:T(8,128)(2,1)S(1)} %broadcast_select_fusion.4.refs_7_), channel_id=1, source_target_pairs={{0,4},{1,5},{2,6},{3,7},{4,0},{5,1},{6,2},{7,3},{8,12},{9,13},{10,... | collective-permute-start | bytes 921608 | tf_op jit(solution)/shard_map/ppermute | solution.py:48
  30.1 28.6 %collective-permute-start.29 = (bf16[4,256,384]{2,1,0:T(8,128)(2,1)}, bf16[4,256,384]{2,1,0:T(8,128)(2,1)}, u32[]{:S(2)}, u32[]{:S(2)}) collective-permute-start(bf16[4,256,384]{2,1,0:T(8,128)(2,1)} %pad_maximum_fusion), channel_id=1, source_target_pairs={{0,4},{1,5},{2,6},{3,7},{4,0},{5,1},{6,2},{7,3},{8,12},{9,13},{10,... | collective-permute-start | bytes 2359304 | tf_op jit(solution)/shard_map/ppermute | solution.py:48
  30.2 0.7 copy-start.8
  30.9 11.8 %copy-start.10 = (bf16[2,256,256]{2,1,0:T(8,128)(2,1)}, bf16[2,256,256]{2,1,0:T(8,128)(2,1)S(1)}, u32[]{:S(2)}) copy-start(bf16[2,256,256]{2,1,0:T(8,128)(2,1)S(1)} %slice.19) | copy-start | bytes 786436
  31.8 15.1 %copy-start.1 = (f32[3,40,640]{2,1,0:T(8,128)S(1)}, f32[3,40,640]{2,1,0:T(8,128)}, u32[]{:S(2)}) copy-start(f32[3,40,640]{2,1,0:T(8,128)} %refs_5_.1) | copy-start | bytes 921604
  35.2 27.1 %collective-permute-start.14 = (bf16[4,256,256]{2,1,0:T(8,128)(2,1)}, bf16[4,256,256]{2,1,0:T(8,128)(2,1)}, u32[]{:S(2)}, u32[]{:S(2)}) collective-permute-start(bf16[4,256,256]{2,1,0:T(8,128)(2,1)} %pad_maximum_fusion.3), channel_id=1, source_target_pairs={{4,12},{5,13},{6,14},{7,15},{12,20},{13,21},{14,22},{15,23},{20,28... | collective-permute-start | bytes 1572872 | tf_op jit(solution)/shard_map/ppermute | solution.py:48
  45.6 26.2 %collective-permute-start.13 = (bf16[2,3,80,640]{3,2,1,0:T(8,128)(2,1)}, bf16[2,3,80,640]{3,2,1,0:T(8,128)(2,1)}, u32[]{:S(2)}, u32[]{:S(2)}) collective-permute-start(bf16[2,3,80,640]{3,2,1,0:T(8,128)(2,1)} %shard_map.95), channel_id=1, source_target_pairs={{0,4},{1,5},{2,6},{3,7},{4,0},{5,1},{6,2},{7,3},{8,12},{9,13},{10,... | collective-permute-start | bytes 1843208 | tf_op jit(solution)/shard_map/ppermute | solution.py:48
  46.9 33.3 %collective-permute-start.18 = (f32[3,40,640]{2,1,0:T(8,128)S(1)}, f32[3,40,640]{2,1,0:T(8,128)}, u32[]{:S(2)}, u32[]{:S(2)}) collective-permute-start(f32[3,40,640]{2,1,0:T(8,128)S(1)} %copy-done.1), channel_id=1, source_target_pairs={{1,0},{3,2},{5,4},{7,6},{9,8},{11,10},{13,12},{15,14},{16,17},{18,... | collective-permute-start | bytes 921608 | tf_op jit(solution)/shard_map/ppermute | solution.py:48
  54.0 1.0 copy-start.5
  54.9 1.0 copy-start.7
  55.9 6.4 %copy-start.9 = (bf16[2,256,256]{2,1,0:T(8,128)(2,1)S(1)}, bf16[2,256,256]{2,1,0:T(8,128)(2,1)}, u32[]{:S(2)}) copy-start(bf16[2,256,256]{2,1,0:T(8,128)(2,1)} %copy-done.8) | copy-start | bytes 786436
  55.9 6.4 %copy-start.11 = (bf16[2,256,256]{2,1,0:T(8,128)(2,1)S(1)}, bf16[2,256,256]{2,1,0:T(8,128)(2,1)}, u32[]{:S(2)}) copy-start(bf16[2,256,256]{2,1,0:T(8,128)(2,1)} %copy-done.10) | copy-start | bytes 786436
  58.7 48.8 %collective-permute-start.30 = (bf16[4,256,384]{2,1,0:T(8,128)(2,1)}, bf16[4,256,384]{2,1,0:T(8,128)(2,1)}, u32[]{:S(2)}, u32[]{:S(2)}) collective-permute-start(bf16[4,256,384]{2,1,0:T(8,128)(2,1)} %collective-permute-done.29), channel_id=1, source_target_pairs={{0,8},{1,9},{2,10},{3,11},{8,16},{9,17},{10,18},{11,19},{16,24},{1... | collective-permute-start | bytes 2359304 | tf_op jit(solution)/shard_map/ppermute | solution.py:48
  73.8 0.8 copy-start.2
  74.7 7.7 %collective-permute-start.15 = (bf16[3,80,640]{2,1,0:T(8,128)(2,1)}, bf16[3,80,640]{2,1,0:T(8,128)(2,1)}, u32[]{:S(2)}, u32[]{:S(2)}) collective-permute-start(bf16[3,80,640]{2,1,0:T(8,128)(2,1)} %get-tuple-element.25), channel_id=1, source_target_pairs={{1,17},{3,19},{5,21},{7,23},{9,25},{11,27},{13,29},{15,31},{16,0},... | collective-permute-start | bytes 921608 | tf_op jit(solution)/shard_map/ppermute | solution.py:48
  76.7 12.3 %collective-permute-start.16 = (bf16[3,80,640]{2,1,0:T(8,128)(2,1)}, bf16[3,80,640]{2,1,0:T(8,128)(2,1)}, u32[]{:S(2)}, u32[]{:S(2)}) collective-permute-start(bf16[3,80,640]{2,1,0:T(8,128)(2,1)} %get-tuple-element.26), channel_id=1, source_target_pairs={{1,25},{3,27},{5,29},{7,31},{9,17},{11,19},{13,21},{15,23},{16,8},... | collective-permute-start | bytes 921608 | tf_op jit(solution)/shard_map/ppermute | solution.py:48
  78.7 10.3 %collective-permute-start.17 = (bf16[3,80,640]{2,1,0:T(8,128)(2,1)}, bf16[3,80,640]{2,1,0:T(8,128)(2,1)}, u32[]{:S(2)}, u32[]{:S(2)}) collective-permute-start(bf16[3,80,640]{2,1,0:T(8,128)(2,1)} %get-tuple-element.26), channel_id=1, source_target_pairs={{0,8},{2,10},{4,12},{6,14},{8,0},{10,2},{12,4},{14,6},{17,25},{19,... | collective-permute-start | bytes 921608 | tf_op jit(solution)/shard_map/ppermute | solution.py:48
  89.0 1.1 copy-start.3
  90.0 2.7 %copy-start.17 = (bf16[4,256,256]{2,1,0:T(8,128)(2,1)S(1)}, bf16[4,256,256]{2,1,0:T(8,128)(2,1)}, u32[]{:S(2)}) copy-start(bf16[4,256,256]{2,1,0:T(8,128)(2,1)} %broadcast_select_fusion.1) | copy-start | bytes 1572868
  90.1 2.8 %copy-start.16 = (bf16[256,1280]{1,0:T(8,128)(2,1)S(1)}, bf16[256,1280]{1,0:T(8,128)(2,1)}, u32[]{:S(2)}) copy-start(bf16[256,1280]{1,0:T(8,128)(2,1)} %param.7) | copy-start | bytes 1966084
  91.4 14.2 %collective-permute-start.19 = (bf16[3,80,640]{2,1,0:T(8,128)(2,1)S(1)}, bf16[3,80,640]{2,1,0:T(8,128)(2,1)S(1)}, u32[]{:S(2)}, u32[]{:S(2)}) collective-permute-start(bf16[3,80,640]{2,1,0:T(8,128)(2,1)S(1)} %get-tuple-element.27), channel_id=1, source_target_pairs={{0,16},{2,18},{4,20},{6,22},{8,24},{10,26},{12,28},{14,30},{17,1},... | collective-permute-start | bytes 921608 | tf_op jit(solution)/shard_map/ppermute | solution.py:48
  92.7 17.4 %collective-permute-start.32 = (bf16[4,256,256]{2,1,0:T(8,128)(2,1)S(1)}, bf16[4,256,256]{2,1,0:T(8,128)(2,1)S(1)}, u32[]{:S(2)}, u32[]{:S(2)}) collective-permute-start(bf16[4,256,256]{2,1,0:T(8,128)(2,1)S(1)} %copy-done.17), channel_id=1, source_target_pairs={{0,4},{1,5},{2,6},{3,7},{4,0},{5,1},{6,2},{7,3},{8,12},{9,13},{10,... | collective-permute-start | bytes 1572872 | tf_op jit(solution)/shard_map/ppermute | solution.py:48
  92.9 21.0 %collective-permute-start = (bf16[256,640]{1,0:T(8,128)(2,1)S(1)}, bf16[256,640]{1,0:T(8,128)(2,1)S(1)}, u32[]{:S(2)}, u32[]{:S(2)}) collective-permute-start(bf16[256,640]{1,0:T(8,128)(2,1)S(1)} %get-tuple-element.44), channel_id=1, source_target_pairs={{0,1},{1,0},{2,3},{3,2},{4,5},{5,4},{6,7},{7,6},{8,9},{9,8},{10,11... | collective-permute-start | bytes 983048 | tf_op jit(solution)/shard_map/ppermute | solution.py:48
  99.3 12.2 %collective-permute-start.23 = (bf16[3,80,640]{2,1,0:T(8,128)(2,1)S(1)}, bf16[3,80,640]{2,1,0:T(8,128)(2,1)S(1)}, u32[]{:S(2)}, u32[]{:S(2)}) collective-permute-start(bf16[3,80,640]{2,1,0:T(8,128)(2,1)S(1)} %get-tuple-element.27), channel_id=1, source_target_pairs={{0,8},{2,10},{4,12},{6,14},{8,0},{10,2},{12,4},{14,6},{17,25},{19,... | collective-permute-start | bytes 921608 | tf_op jit(solution)/shard_map/ppermute | solution.py:48
  105.6 8.1 %collective-permute-start.24 = (bf16[3,80,640]{2,1,0:T(8,128)(2,1)S(1)}, bf16[3,80,640]{2,1,0:T(8,128)(2,1)S(1)}, u32[]{:S(2)}, u32[]{:S(2)}) collective-permute-start(bf16[3,80,640]{2,1,0:T(8,128)(2,1)S(1)} %collective-permute-done.19), channel_id=1, source_target_pairs={{1,9},{3,11},{5,13},{7,15},{9,1},{11,3},{13,5},{15,7},{16,24},{18,... | collective-permute-start | bytes 921608 | tf_op jit(solution)/shard_map/ppermute | solution.py:48
  108.8 6.4 %copy-start.19 = (f32[1280]{0:T(1024)S(1)}, f32[1280]{0:T(1024)}, u32[]{:S(2)}) copy-start(f32[1280]{0:T(1024)} %param.13) | copy-start | bytes 15364
  108.8 21.5 %collective-permute-start.31 = (bf16[4,256,384]{2,1,0:T(8,128)(2,1)S(1)}, bf16[4,256,384]{2,1,0:T(8,128)(2,1)S(1)}, u32[]{:S(2)}, u32[]{:S(2)}) collective-permute-start(bf16[4,256,384]{2,1,0:T(8,128)(2,1)S(1)} %broadcast_select_fusion.refs_7_), channel_id=1, source_target_pairs={{2,0},{3,1},{6,4},{7,5},{10,8},{11,9},{14,12},{15,13},{18,16},{19,... | collective-permute-start | bytes 2359304 | tf_op jit(solution)/shard_map/ppermute | solution.py:48
  110.1 34.7 %collective-permute-start.33 = (bf16[4,256,256]{2,1,0:T(8,128)(2,1)S(1)}, bf16[4,256,256]{2,1,0:T(8,128)(2,1)S(1)}, u32[]{:S(2)}, u32[]{:S(2)}) collective-permute-start(bf16[4,256,256]{2,1,0:T(8,128)(2,1)S(1)} %collective-permute-done.32.refs_7_), channel_id=1, source_target_pairs={{2,0},{3,1},{6,4},{7,5},{10,8},{11,9},{14,12},{15,13},{18,16},{19,... | collective-permute-start | bytes 1572872 | tf_op jit(solution)/shard_map/ppermute | solution.py:48
  111.5 33.3 %collective-permute-start.21 = (bf16[3,80,640]{2,1,0:T(8,128)(2,1)S(1)}, bf16[3,80,640]{2,1,0:T(8,128)(2,1)S(1)}, u32[]{:S(2)}, u32[]{:S(2)}) collective-permute-start(bf16[3,80,640]{2,1,0:T(8,128)(2,1)S(1)} %broadcast_select_fusion.3.refs_2_), channel_id=1, source_target_pairs={{0,2},{1,3},{2,0},{3,1},{4,6},{5,7},{6,4},{7,5},{8,10},{9,11},{10,... | collective-permute-start | bytes 921608 | tf_op jit(solution)/shard_map/ppermute | solution.py:48
  113.7 35.9 %collective-permute-start.26 = (bf16[3,80,640]{2,1,0:T(8,128)(2,1)S(1)}, bf16[3,80,640]{2,1,0:T(8,128)(2,1)S(1)}, u32[]{:S(2)}, u32[]{:S(2)}) collective-permute-start(bf16[3,80,640]{2,1,0:T(8,128)(2,1)S(1)} %broadcast_select_fusion.2.refs_4_), channel_id=1, source_target_pairs={{0,4},{1,5},{2,6},{3,7},{4,0},{5,1},{6,2},{7,3},{8,12},{9,13},{10,... | collective-permute-start | bytes 921608 | tf_op jit(solution)/shard_map/ppermute | solution.py:48
  113.9 37.1 %collective-permute-start.28 = (f32[3,40,640]{2,1,0:T(8,128)S(1)}, f32[3,40,640]{2,1,0:T(8,128)S(1)}, u32[]{:S(2)}, u32[]{:S(2)}) collective-permute-start(f32[3,40,640]{2,1,0:T(8,128)S(1)} %slice_bitcast_fusion), channel_id=1, source_target_pairs={{0,1},{2,3},{4,5},{6,7},{8,9},{10,11},{12,13},{14,15},{17,16},{19,... | collective-permute-start | bytes 921608 | tf_op jit(solution)/shard_map/ppermute | solution.py:48
  130.2 23.4 %collective-permute-start.20 = (bf16[3,80,640]{2,1,0:T(8,128)(2,1)S(1)}, bf16[3,80,640]{2,1,0:T(8,128)(2,1)S(1)}, u32[]{:S(2)}, u32[]{:S(2)}) collective-permute-start(bf16[3,80,640]{2,1,0:T(8,128)(2,1)S(1)} %broadcast_select_fusion.3.refs_2_), channel_id=1, source_target_pairs={{0,4},{1,5},{2,6},{3,7},{4,0},{5,1},{6,2},{7,3},{8,12},{9,13},{10,... | collective-permute-start | bytes 921608 | tf_op jit(solution)/shard_map/ppermute | solution.py:48
  144.8 8.8 %collective-permute-start.25 = (bf16[3,80,640]{2,1,0:T(8,128)(2,1)S(1)}, bf16[3,80,640]{2,1,0:T(8,128)(2,1)S(1)}, u32[]{:S(2)}, u32[]{:S(2)}) collective-permute-start(bf16[3,80,640]{2,1,0:T(8,128)(2,1)S(1)} %broadcast_select_fusion.2.refs_4_), channel_id=1, source_target_pairs={{0,2},{1,3},{2,0},{3,1},{4,6},{5,7},{6,4},{7,5},{8,10},{9,11},{10,... | collective-permute-start | bytes 921608 | tf_op jit(solution)/shard_map/ppermute | solution.py:48
  144.8 8.8 %collective-permute-start.22 = (bf16[3,80,640]{2,1,0:T(8,128)(2,1)S(1)}, bf16[3,80,640]{2,1,0:T(8,128)(2,1)S(1)}, u32[]{:S(2)}, u32[]{:S(2)}) collective-permute-start(bf16[3,80,640]{2,1,0:T(8,128)(2,1)S(1)} %collective-permute-done.21.refs_3_), channel_id=1, source_target_pairs={{0,4},{1,5},{2,6},{3,7},{4,0},{5,1},{6,2},{7,3},{8,12},{9,13},{10,... | collective-permute-start | bytes 921608 | tf_op jit(solution)/shard_map/ppermute | solution.py:48
  151.2 12.2 %copy-start.14 = (f32[3,40,640]{2,1,0:T(8,128)}, f32[3,40,640]{2,1,0:T(8,128)S(1)}, u32[]{:S(2)}) copy-start(f32[3,40,640]{2,1,0:T(8,128)S(1)} %get-tuple-element.19) | copy-start | bytes 921604
  151.2 9.3 %collective-permute-start.27 = (bf16[3,80,640]{2,1,0:T(8,128)(2,1)S(1)}, bf16[3,80,640]{2,1,0:T(8,128)(2,1)S(1)}, u32[]{:S(2)}, u32[]{:S(2)}) collective-permute-start(bf16[3,80,640]{2,1,0:T(8,128)(2,1)S(1)} %collective-permute-done.26.refs_5_), channel_id=1, source_target_pairs={{0,2},{1,3},{2,0},{3,1},{4,6},{5,7},{6,4},{7,5},{8,10},{9,11},{10,... | collective-permute-start | bytes 921608 | tf_op jit(solution)/shard_map/ppermute | solution.py:48
  163.4 1.7 %collective-permute-start.34 = (bf16[256,640]{1,0:T(8,128)(2,1)S(1)}, bf16[256,640]{1,0:T(8,128)(2,1)S(1)}, u32[]{:S(2)}, u32[]{:S(2)}) collective-permute-start(bf16[256,640]{1,0:T(8,128)(2,1)S(1)} %get-tuple-element.34), channel_id=1, source_target_pairs={{0,1},{1,0},{2,3},{3,2},{4,5},{5,4},{6,7},{7,6},{8,9},{9,8},{10,11... | collective-permute-start | bytes 983048 | tf_op jit(solution)/shard_map/ppermute | solution.py:48

commit v8 on v7

--- a/solution.py
+++ b/solution.py
@@ -245,52 +245,45 @@
     )(*quer_in, *pieces)
 
 
-def query_last_kernel(count, *refs):
-    where, quer_in = refs[0], refs[1:3]
-    sums, gain, att_a, att_b, own, other, weights = refs[3 + count :]
-    tokens, width = other.shape
-    load_rows(refs[3 : 3 + count], weights)
-    fast = sums[...] + fast_product(quer_in, weights)
+def query_last_kernel(count, side, where, quer_in, *refs):
+    sums, gain, att_a, att_b, out, weights = refs[count:]
+    tokens, width = quer_in.shape
+    load_rows(refs[:count], weights)
+    fast = sums[side * tokens : (side + 1) * tokens, :] + fast_product([quer_in], weights)
     scale = lax.rsqrt(jnp.mean(fast * fast, axis=-1, keepdims=True) + EPS)
-    normed = fast * scale * gain[...]
-    here = pl.multiple_of(where[0] * width, ATT_DIM)
-    at = [pl.multiple_of(core * tokens, tokens) for core in (where[0], 1 - where[0])]
-    att = [
-        jnp.concatenate([ref[pl.ds(base, tokens), :] for ref in (att_a, att_b)], axis=1)
-        for base in at
-    ]
-    own[:, pl.ds(here, width)] = (normed[:tokens] + att[0]).astype(BF16)
-    other[...] = (normed[tokens:] + att[1]).astype(BF16)
-
-
-def query_last(where, quer_in, pieces, sums, gain, atts):
-    tokens, width = quer_in[0].shape
+    core = where[0] if side == 0 else 1 - where[0]
+    rows = pl.ds(pl.multiple_of(core * tokens, tokens), tokens)
+    att = jnp.concatenate([att_a[rows, :], att_b[rows, :]], axis=1)
+    result = (fast * scale * gain[...] + att).astype(BF16)
+    if side == 0:
+        out[:, pl.ds(pl.multiple_of(where[0] * width, ATT_DIM), width)] = result
+    else:
+        out[...] = result
+
+
+def query_last(where, quer_in, pieces, sums, gain, atts, side):
+    tokens, width = quer_in.shape
     count = len(pieces)
     rows = pieces[0].shape[1]
     return pl.pallas_call(
-        lambda *refs: query_last_kernel(count, *refs),
-        out_shape=[
-            jax.ShapeDtypeStruct((tokens, 2 * width), BF16),
-            jax.ShapeDtypeStruct((tokens, width), BF16),
-        ],
-        in_specs=[pl.BlockSpec(memory_space=pltpu.SMEM)] + [vmem()] * (6 + count),
-        out_specs=[vmem()] * 2,
+        lambda *refs: query_last_kernel(count, side, *refs),
+        out_shape=jax.ShapeDtypeStruct((tokens, (2 - side) * width), BF16),
+        in_specs=[pl.BlockSpec(memory_space=pltpu.SMEM)] + [vmem()] * (5 + count),
+        out_specs=vmem(),
         scratch_shapes=[pltpu.VMEM((3, count * rows, width), BF16)],
         compiler_params=grant(24),
         cost_estimate=pl.CostEstimate(
-            flops=12 * tokens * count * rows * width,
+            flops=6 * tokens * count * rows * width,
             bytes_accessed=6 * count * rows * width,
             transcendentals=0,
         ),
-        name="query_last",
-    )(where, *quer_in, *pieces, sums, gain, *atts)
+    )(where, quer_in, *pieces, sums, gain, *atts)
 
 
 def att_kernel(low, where, q_kept, q_came, k_own, v_own, k_near, v_near, two, back, out,
                quer, keys, vals, bias, arrivals):
     tokens = q_kept.shape[0]
     span = 2 * tokens
-    reach = WINDOW + span
     wide = out.shape[1]
     cols = slice(low, low + wide)
     core, odd, chip = where[0], where[1], where[2]
@@ -326,10 +319,11 @@
             put(dest, span, back[2 * idx], back[2 * idx + 1])
 
     scale = 1.0 / math.sqrt(ATT_DIM)
-    row = lax.broadcasted_iota(jnp.int32, (span, reach), 0)
-    col = lax.broadcasted_iota(jnp.int32, (span, reach), 1)
-    seen = (col > row) & (col <= row + WINDOW) & (chip * span - WINDOW + col >= 0)
-    bias[...] = jnp.where(seen, 0.0, MASKED)
+    row = lax.broadcasted_iota(jnp.int32, (span, span), 0)
+    col = lax.broadcasted_iota(jnp.int32, (span, span), 1)
+    bias[0] = jnp.where((col > row) & (chip >= 2), 0.0, MASKED)
+    bias[1] = jnp.where(col <= row, 0.0, MASKED)
+    middle = jnp.where(chip >= 1, 0.0, MASKED)
 
     @pl.when(odd == 1)
     def _():
@@ -338,11 +332,15 @@
 
     for head in range(wide // ATT_DIM):
         at = slice(head * ATT_DIM, (head + 1) * ATT_DIM)
-        scores = nt_dot(quer[:, at], keys[:, at]) + bias[...]
-        top = jnp.max(scores, axis=-1, keepdims=True)
-        probs = jnp.exp((scores - top) * scale)
-        norm = jnp.sum(probs, axis=-1, keepdims=True)
-        att = nn_dot(probs.astype(BF16), vals[:, at]) / norm
+        blocks = [slice(idx * span, (idx + 1) * span) for idx in range(3)]
+        scores = [nt_dot(quer[:, at], keys[rows, at]) for rows in blocks]
+        scores = [scores[0] + bias[0], scores[1] + middle, scores[2] + bias[1]]
+        tops = [jnp.max(part, axis=-1, keepdims=True) for part in scores]
+        top = jnp.maximum(jnp.maximum(tops[0], tops[1]), tops[2])
+        probs = [jnp.exp((part - top) * scale) for part in scores]
+        norm = sum(jnp.sum(part, axis=-1, keepdims=True) for part in probs)
+        att = sum(nn_dot(part.astype(BF16), vals[rows, at]) for part, rows in zip(probs, blocks))
+        att = att / norm
         out[:, at] = att * lax.rsqrt(jnp.mean(att * att, axis=-1, keepdims=True) + EPS)
 
 
@@ -364,7 +362,7 @@
             pltpu.VMEM((span, wide), BF16),
             pltpu.VMEM((reach, wide), BF16),
             pltpu.VMEM((reach, wide), BF16),
-            pltpu.VMEM((span, reach), F32),
+            pltpu.VMEM((2, span, span), F32),
             pltpu.SemaphoreType.DMA((4,)),
         ],
         compiler_params=grant(30),
@@ -410,14 +408,13 @@
 
     k_own = jnp.stack(by_core(key_rows))
     v_own = jnp.stack(by_core(value_rows))
-    q_own = by_core(queries)
 
     their_weights = send(fast_weights, routes.pair_in)
     their_momentum = send(momentum, routes.pair_in)
 
     k_near = send(k_own, routes.x_swap)
     v_near = send(v_own, routes.x_swap)
-    cut = 3 * ATT_DIM
+    cut = 2 * ATT_DIM
     k_held, v_held = lax.optimization_barrier((k_own, v_own))
     early = jnp.concatenate([k_held[:, :, :cut], v_held[:, :, :cut]], axis=0)
     late = jnp.concatenate([k_held[:, :, cut:], v_held[:, :, cut:]], axis=0)
@@ -436,6 +433,8 @@
     late_z = send(late_in, routes.z_up_far)
 
     side_grads = key_side(grad_scale, tokens_in, side_units, BF16)
+    queries, side_grads = lax.optimization_barrier((queries, side_grads))
+    q_own = by_core(queries)
     side_in = send(side_grads, routes.y_swap)
     own_grads = key_side(grad_scale, tokens_in, units, F32)
     late_turn = jnp.where(upper, late_z, late)
@@ -465,8 +464,10 @@
     grads = jnp.where(is_home, total[0], partner_grads)
     new_weights, new_momentum = updated(fast_weights, momentum, grads)
     new_weights, new_momentum, gain = lax.optimization_barrier((new_weights, new_momentum, gain))
-    own, other = query_last(where, q_own, last, sums, gain, (early_att, late_att))
+    last_in = (last, sums, gain, (early_att, late_att))
+    other = query_last(where, q_own[1], *last_in, 1)
     arrived = send(other, routes.partner)
+    own = query_last(where, q_own[0], *last_in, 0)
     layer_out = lax.dynamic_update_slice_in_dim(own, arrived, (1 - core) * width, 1)
     return (layer_out, new_weights, new_momentum)
 

time: 168 us -> 169 us (level)
  waiting for transfers between devices: 68.6 us -> 50.5 us
  starting transfers between devices: 56.6 us -> 74.4 us
    ppermute x35, waiting for transfers between devices: 68.6 us -> 50.5 us  [send(): return lax.ppermute(array, 'seq', route)]
    ppermute x35, starting transfers between devices: 56.6 us -> 74.4 us  [send(): return lax.ppermute(array, 'seq', route)]
    pallas_call x1 -> x2, Pallas kernels: 2.89 us -> 3.88 us  [query_last(): pl.pallas_call(lambda *refs: query_last_kernel(count, side, *refs), out_s...]
    unnamed x42 -> x38, local copies, waits for them, and re-layouts: 5.29 us -> 5.33 us
  transfers between devices with their start and end apart: 35 -> 35, of which waited for: 14 -> 12; matrix products, arithmetic and copies ran while one was open for 6% -> 7% of each run, Pallas kernels for 12% -> 13%
where the time goes in v8:
time: 169 us; the launch traced here: 166 us
  starting transfers between devices  74.4 us (44%)
  waiting for transfers between devices  50.5 us (30%)
  Pallas kernels  22.6 us (13%)
  other arithmetic  8.93 us (5%)
  local copies, waits for them, and re-layouts  8.38 us (5%)
    ppermute x35, starting transfers between devices, send(): return lax.ppermute(array, 'seq', route)  74.4 us
    ppermute x35, waiting for transfers between devices, send(): return lax.ppermute(array, 'seq', route)  50.5 us
    pallas_call x2, Pallas kernels, attention(): pl.pallas_call(lambda *refs: att_kernel(low, *refs), out_shape=jax.ShapeD...  9.13 us
    unnamed x38, local copies, waits for them, and re-layouts  5.33 us
    pallas_call x2, Pallas kernels, key_side(): pl.pallas_call(lambda *refs: key_kernel(grad_scale, *refs), out_shape=jax...  4.99 us
    pallas_call x2, Pallas kernels, query_last(): pl.pallas_call(lambda *refs: query_last_kernel(count, side, *refs), out_s...  3.88 us
  transfers between devices with their start and end apart: 35, of which 12 were waited for; matrix products, arithmetic and copies ran while one was open for 7% of the time, Pallas kernels for 13%

profile of v8, /device:TPU:1, one launch (start us, length us, event | category | flops | bytes accessed | tf_op | source)
XLA Modules:
  0.0 166.0 jit_solution(15652355974119295345)
XLA Ops:
  0.6 2.1 %collective-permute-start.6 = (f32[3,40,640]{2,1,0:T(8,128)}, f32[3,40,640]{2,1,0:T(8,128)S(1)}, u32[]{:S(2)}, u32[]{:S(2)}) collective-permute-start(f32[3,40,640]{2,1,0:T(8,128)} %refs_3_.1), channel_id=1, source_target_pairs={{1,0},{3,2},{5,4},{7,6},{9,8},{11,10},{13,12},{15,14},{16,17},{18,... | collective-permute-start | bytes 921608 | tf_op jit(solution)/shard_map/ppermute | solution.py:48
  2.8 1.2 dynamic-slice_bitcast_fusion
  4.0 0.8 dynamic-slice_bitcast_fusion.1
  5.4 0.7 pad_maximum_fusion.4
  6.1 1.3 collective-permute-start.7
  7.5 5.3 %collective-permute-start.4 = (f32[1,256]{1,0:T(1,128)S(1)}, f32[1,256]{1,0:T(1,128)}, u32[]{:S(2)}, u32[]{:S(2)}) collective-permute-start(f32[1,256]{1,0:T(1,128)S(1)} %get-tuple-element.47), channel_id=1, source_target_pairs={{0,1},{1,0},{2,3},{3,2},{4,5},{5,4},{6,7},{7,6},{8,9},{9,8},{10,11... | collective-permute-start | bytes 3080 | tf_op jit(solution)/shard_map/ppermute | solution.py:48
  13.5 1.3 collective-permute-start.3
  14.8 0.7 copy-done.16
  15.5 1.0 pad_maximum_fusion.1.refs_0_.refs_3_
  17.0 1.4 collective-permute-done.7
  18.5 1.9 %collective-permute-start.10 = (bf16[3,80,640]{2,1,0:T(8,128)(2,1)}, bf16[3,80,640]{2,1,0:T(8,128)(2,1)S(1)}, u32[]{:S(2)}, u32[]{:S(2)}) collective-permute-start(bf16[3,80,640]{2,1,0:T(8,128)(2,1)} %collective-permute-done.7), channel_id=1, source_target_pairs={{1,9},{3,11},{5,13},{7,15},{9,1},{11,3},{13,5},{15,7},{16,24},{18,... | collective-permute-start | bytes 921608 | tf_op jit(solution)/shard_map/ppermute | solution.py:48
  20.4 1.0 pad_maximum_fusion
  21.4 1.1 broadcast_select_fusion.5.refs_6_
  22.5 4.1 %collective-permute-done.10 = bf16[3,80,640]{2,1,0:T(8,128)(2,1)S(1)} collective-permute-done((bf16[3,80,640]{2,1,0:T(8,128)(2,1)}, bf16[3,80,640]{2,1,0:T(8,128)(2,1)S(1)}, u32[]{:S(2)}, u32[]{:S(2)}) %collective-permute-start.10) | collective-permute-done | bytes 307232 | tf_op jit(solution)/shard_map/ppermute | solution.py:48
  26.6 1.6 collective-permute-start.13
  28.2 0.7 pad_maximum_fusion.5.refs_4_
  28.8 2.6 %collective-permute-start.5 = (f32[2,256]{1,0:T(2,128)S(1)}, f32[2,256]{1,0:T(2,128)S(1)}, u32[]{:S(2)}, u32[]{:S(2)}) collective-permute-start(f32[2,256]{1,0:T(2,128)S(1)} %pad_maximum_fusion.5.refs_4_), channel_id=1, source_target_pairs={{0,2},{1,3},{2,0},{3,1},{4,6},{5,7},{6,4},{7,5},{8,10},{9,11},{10,... | collective-permute-start | bytes 6152 | tf_op jit(solution)/shard_map/ppermute | solution.py:48
  31.4 2.5 %collective-permute-start.8 = (bf16[3,80,640]{2,1,0:T(8,128)(2,1)S(1)}, bf16[3,80,640]{2,1,0:T(8,128)(2,1)S(1)}, u32[]{:S(2)}, u32[]{:S(2)}) collective-permute-start(bf16[3,80,640]{2,1,0:T(8,128)(2,1)S(1)} %broadcast_select_fusion.5.refs_6_), channel_id=1, source_target_pairs={{0,4},{1,5},{2,6},{3,7},{4,0},{5,1},{6,2},{7,3},{8,12},{9,13},{10,... | collective-permute-start | bytes 921608 | tf_op jit(solution)/shard_map/ppermute | solution.py:48
  33.9 7.2 %collective-permute-done.5.refs_5_ = f32[2,256]{1,0:T(2,128)S(1)} collective-permute-done((f32[2,256]{1,0:T(2,128)S(1)}, f32[2,256]{1,0:T(2,128)S(1)}, u32[]{:S(2)}, u32[]{:S(2)}) %collective-permute-start.5) | collective-permute-done | bytes 2080 | tf_op jit(solution)/shard_map/ppermute | solution.py:48
  41.1 1.2 collective-permute-start.11
  42.4 0.7 copy-done.6
  43.1 3.7 %collective-permute-done.11.refs_7_ = bf16[3,80,640]{2,1,0:T(8,128)(2,1)S(1)} collective-permute-done((bf16[3,80,640]{2,1,0:T(8,128)(2,1)S(1)}, bf16[3,80,640]{2,1,0:T(8,128)(2,1)S(1)}, u32[]{:S(2)}, u32[]{:S(2)}) %collective-permute-start.11) | collective-permute-done | bytes 307232 | tf_op jit(solution)/shard_map/ppermute | solution.py:48
  46.8 2.9 %shard_map.94 = bf16[2,3,80,640]{3,2,1,0:T(8,128)(2,1)} custom-call(bf16[2,256,640]{2,1,0:T(8,128)(2,1)S(1)} %pad_maximum_fusion.1.refs_0_.refs_3_, bf16[2,256,640]{2,1,0:T(8,128)(2,1)S(1)} %pad_maximum_fusion.2.refs_1_.refs_4_, bf16[2,256,640]{2,1,0:T(8,128)(2,1)S(1)} %collective-permute-done.2.refs_2_.refs_5_, ...), custom_call_target="tpu_custom_call" | custom-call | flops 1258291200 | bytes 2621440 | tf_op jit(solution)/shard_map/pallas_call | solution.py:187
  49.7 1.3 collective-permute-start.12
  51.0 0.9 pad_maximum_fusion.3
  52.1 8.1 %collective-permute-start.17 = (f32[3,40,640]{2,1,0:T(8,128)S(1)}, f32[3,40,640]{2,1,0:T(8,128)}, u32[]{:S(2)}, u32[]{:S(2)}) collective-permute-start(f32[3,40,640]{2,1,0:T(8,128)S(1)} %copy-done.1), channel_id=1, source_target_pairs={{1,0},{3,2},{5,4},{7,6},{9,8},{11,10},{13,12},{15,14},{16,17},{18,... | collective-permute-start | bytes 921608 | tf_op jit(solution)/shard_map/ppermute | solution.py:48
  60.2 1.0 copy-done.5
  61.1 1.0 copy-done.7
  62.1 2.1 %shard_map.95.low = f32[2,3,80,640]{3,2,1,0:T(8,128)S(1)} custom-call(bf16[2,256,640]{2,1,0:T(8,128)(2,1)S(1)} %pad_maximum_fusion.1.refs_0_.refs_3_, bf16[2,256,640]{2,1,0:T(8,128)(2,1)S(1)} %pad_maximum_fusion.2.refs_1_.refs_4_, bf16[2,256,640]{2,1,0:T(8,128)(2,1)S(1)} %collective-permute-done.2.refs_2_.refs_5_, ...), custom_call_target="tpu_custom_call" | custom-call | flops 1258291200 | bytes 2621440 | tf_op jit(solution)/shard_map/pallas_call | solution.py:187
  64.2 1.1 broadcast_select_fusion
  65.3 2.0 %fold.1 = (f32[3,80,640]{2,1,0:T(8,128)S(1)}, bf16[3,80,640]{2,1,0:T(8,128)(2,1)}, bf16[3,80,640]{2,1,0:T(8,128)(2,1)}) custom-call(f32[2,3,80,640]{3,2,1,0:T(8,128)S(1)} %shard_map.95.low, bf16[2,3,80,640]{3,2,1,0:T(8,128)(2,1)} %collective-permute-done.12.arrived), custom_call_target="tpu_custom_call" | custom-call | flops 307200 | bytes 3686400 | tf_op jit(solution)/shard_map/fold/pallas_call | solution.py:83
  67.3 0.8 copy-done.2
  68.1 9.7 %collective-permute-start.14 = (bf16[3,80,640]{2,1,0:T(8,128)(2,1)}, bf16[3,80,640]{2,1,0:T(8,128)(2,1)}, u32[]{:S(2)}, u32[]{:S(2)}) collective-permute-start(bf16[3,80,640]{2,1,0:T(8,128)(2,1)} %get-tuple-element.27), channel_id=1, source_target_pairs={{1,17},{3,19},{5,21},{7,23},{9,25},{11,27},{13,29},{15,31},{16,0},... | collective-permute-start | bytes 921608 | tf_op jit(solution)/shard_map/ppermute | solution.py:48
  77.8 2.1 %collective-permute-start.15 = (bf16[3,80,640]{2,1,0:T(8,128)(2,1)}, bf16[3,80,640]{2,1,0:T(8,128)(2,1)}, u32[]{:S(2)}, u32[]{:S(2)}) collective-permute-start(bf16[3,80,640]{2,1,0:T(8,128)(2,1)} %get-tuple-element.28), channel_id=1, source_target_pairs={{1,25},{3,27},{5,29},{7,31},{9,17},{11,19},{13,21},{15,23},{16,8},... | collective-permute-start | bytes 921608 | tf_op jit(solution)/shard_map/ppermute | solution.py:48
  80.0 1.4 collective-permute-start.16
  81.3 3.7 %collective-permute-start.30 = (bf16[4,256,256]{2,1,0:T(8,128)(2,1)}, bf16[4,256,256]{2,1,0:T(8,128)(2,1)}, u32[]{:S(2)}, u32[]{:S(2)}) collective-permute-start(bf16[4,256,256]{2,1,0:T(8,128)(2,1)} %collective-permute-done.29), channel_id=1, source_target_pairs={{0,8},{1,9},{2,10},{3,11},{8,16},{9,17},{10,18},{11,19},{16,24},{1... | collective-permute-start | bytes 1572872 | tf_op jit(solution)/shard_map/ppermute | solution.py:48
  85.1 2.3 %collective-permute-done.15.refs_1_ = bf16[3,80,640]{2,1,0:T(8,128)(2,1)} collective-permute-done((bf16[3,80,640]{2,1,0:T(8,128)(2,1)}, bf16[3,80,640]{2,1,0:T(8,128)(2,1)}, u32[]{:S(2)}, u32[]{:S(2)}) %collective-permute-start.15) | collective-permute-done | bytes 307232 | tf_op jit(solution)/shard_map/ppermute | solution.py:48
  87.4 1.1 copy-done.3
  88.5 1.3 update.1
  89.8 1.4 collective-permute-start.18
  91.3 7.2 %collective-permute-start.28 = (bf16[256,640]{1,0:T(8,128)(2,1)S(1)}, bf16[256,640]{1,0:T(8,128)(2,1)S(1)}, u32[]{:S(2)}, u32[]{:S(2)}) collective-permute-start(bf16[256,640]{1,0:T(8,128)(2,1)S(1)} %get-tuple-element.40), channel_id=1, source_target_pairs={{0,1},{1,0},{2,3},{3,2},{4,5},{5,4},{6,7},{7,6},{8,9},{9,8},{10,11... | collective-permute-start | bytes 983048 | tf_op jit(solution)/shard_map/ppermute | solution.py:48
  99.2 10.9 %collective-permute-done.18 = bf16[3,80,640]{2,1,0:T(8,128)(2,1)S(1)} collective-permute-done((bf16[3,80,640]{2,1,0:T(8,128)(2,1)S(1)}, bf16[3,80,640]{2,1,0:T(8,128)(2,1)S(1)}, u32[]{:S(2)}, u32[]{:S(2)}) %collective-permute-start.18) | collective-permute-done | bytes 307232 | tf_op jit(solution)/shard_map/ppermute | solution.py:48
  110.1 1.9 %collective-permute-start.23 = (bf16[3,80,640]{2,1,0:T(8,128)(2,1)S(1)}, bf16[3,80,640]{2,1,0:T(8,128)(2,1)S(1)}, u32[]{:S(2)}, u32[]{:S(2)}) collective-permute-start(bf16[3,80,640]{2,1,0:T(8,128)(2,1)S(1)} %collective-permute-done.18), channel_id=1, source_target_pairs={{1,9},{3,11},{5,13},{7,15},{9,1},{11,3},{13,5},{15,7},{16,24},{18,... | collective-permute-start | bytes 921608 | tf_op jit(solution)/shard_map/ppermute | solution.py:48
  112.0 1.1 broadcast_select_fusion.1.refs_7_
  113.1 1.3 collective-permute-start.31
  114.6 2.2 %collective-permute-start.20 = (bf16[3,80,640]{2,1,0:T(8,128)(2,1)S(1)}, bf16[3,80,640]{2,1,0:T(8,128)(2,1)S(1)}, u32[]{:S(2)}, u32[]{:S(2)}) collective-permute-start(bf16[3,80,640]{2,1,0:T(8,128)(2,1)S(1)} %broadcast_select_fusion.3.refs_2_), channel_id=1, source_target_pairs={{0,2},{1,3},{2,0},{3,1},{4,6},{5,7},{6,4},{7,5},{8,10},{9,11},{10,... | collective-permute-start | bytes 921608 | tf_op jit(solution)/shard_map/ppermute | solution.py:48
  116.7 1.2 collective-permute-done.23
  118.3 1.3 collective-permute-start.27
  119.7 4.8 %collective-permute-done.31.refs_8_ = bf16[4,256,256]{2,1,0:T(8,128)(2,1)S(1)} collective-permute-done((bf16[4,256,256]{2,1,0:T(8,128)(2,1)S(1)}, bf16[4,256,256]{2,1,0:T(8,128)(2,1)S(1)}, u32[]{:S(2)}, u32[]{:S(2)}) %collective-permute-start.31) | collective-permute-done | bytes 524320 | tf_op jit(solution)/shard_map/ppermute | solution.py:48
  124.5 4.1 %shard_map.96.refs_8_ = f32[512,256]{1,0:T(8,128)S(1)} custom-call(s32[4]{0:T(128)S(1)} %pad_add_fusion.where.refs_0_, bf16[256,640]{1,0:T(8,128)(2,1)S(1)} %get-tuple-element.41.refs_0_.refs_1_, bf16[256,640]{1,0:T(8,128)(2,1)S(1)} %collective-permute-done.28.refs_1_.refs_2_, bf16[2,256,640]{2,1,0:T(8,128)(2,1)S(1)} %pad_maximum_fusion.1.refs_0_.refs_3_, ...), custom_call_target="tpu_custom_call" | custom-call | flops 805306368 | bytes 2621440 | tf_op jit(solution)/shard_map/pallas_call | solution.py:353
  128.6 0.9 collective-permute-start.19
  129.5 1.6 collective-permute-done.32.refs_7_
  131.0 1.5 collective-permute-start.33
  132.5 3.9 %collective-permute-start.24 = (bf16[3,80,640]{2,1,0:T(8,128)(2,1)S(1)}, bf16[3,80,640]{2,1,0:T(8,128)(2,1)S(1)}, u32[]{:S(2)}, u32[]{:S(2)}) collective-permute-start(bf16[3,80,640]{2,1,0:T(8,128)(2,1)S(1)} %broadcast_select_fusion.2.refs_4_), channel_id=1, source_target_pairs={{0,2},{1,3},{2,0},{3,1},{4,6},{5,7},{6,4},{7,5},{8,10},{9,11},{10,... | collective-permute-start | bytes 921608 | tf_op jit(solution)/shard_map/ppermute | solution.py:48
  136.5 1.2 collective-permute-done.25.refs_5_
  138.0 1.3 query_first.1.refs_6_
  139.4 3.7 %collective-permute-start.26 = (bf16[3,80,640]{2,1,0:T(8,128)(2,1)S(1)}, bf16[3,80,640]{2,1,0:T(8,128)(2,1)S(1)}, u32[]{:S(2)}, u32[]{:S(2)}) collective-permute-start(bf16[3,80,640]{2,1,0:T(8,128)(2,1)S(1)} %collective-permute-done.25.refs_5_), channel_id=1, source_target_pairs={{0,2},{1,3},{2,0},{3,1},{4,6},{5,7},{6,4},{7,5},{8,10},{9,11},{10,... | collective-permute-start | bytes 921608 | tf_op jit(solution)/shard_map/ppermute | solution.py:48
  143.2 0.9 multiply_multiply_fusion
  144.1 10.1 %collective-permute-done.33.refs_8_ = bf16[4,256,384]{2,1,0:T(8,128)(2,1)S(1)} collective-permute-done((bf16[4,256,384]{2,1,0:T(8,128)(2,1)S(1)}, bf16[4,256,384]{2,1,0:T(8,128)(2,1)S(1)}, u32[]{:S(2)}, u32[]{:S(2)}) %collective-permute-start.33) | collective-permute-done | bytes 786464 | tf_op jit(solution)/shard_map/ppermute | solution.py:48
  154.2 5.1 %shard_map.97.refs_9_ = f32[512,384]{1,0:T(8,128)S(1)} custom-call(s32[4]{0:T(128)S(1)} %pad_add_fusion.where.refs_0_, bf16[256,640]{1,0:T(8,128)(2,1)S(1)} %get-tuple-element.41.refs_0_.refs_1_, bf16[256,640]{1,0:T(8,128)(2,1)S(1)} %collective-permute-done.28.refs_1_.refs_2_, bf16[2,256,640]{2,1,0:T(8,128)(2,1)S(1)} %pad_maximum_fusion.1.refs_0_.refs_3_, ...), custom_call_target="tpu_custom_call" | custom-call | flops 1207959552 | bytes 3932160 | tf_op jit(solution)/shard_map/pallas_call | solution.py:353
  159.3 1.9 %collective-permute-done.26.refs_5_ = bf16[3,80,640]{2,1,0:T(8,128)(2,1)S(1)} collective-permute-done((bf16[3,80,640]{2,1,0:T(8,128)(2,1)S(1)}, bf16[3,80,640]{2,1,0:T(8,128)(2,1)S(1)}, u32[]{:S(2)}, u32[]{:S(2)}) %collective-permute-start.26) | collective-permute-done | bytes 307232 | tf_op jit(solution)/shard_map/ppermute | solution.py:48
  161.3 1.5 shard_map.99
  162.9 2.4 %shard_map.98 = bf16[256,1280]{1,0:T(8,128)(2,1)} custom-call(s32[4]{0:T(128)S(1)} %pad_add_fusion.where.refs_0_, bf16[256,640]{1,0:T(8,128)(2,1)S(1)} %get-tuple-element.41.refs_0_.refs_1_, bf16[3,80,640]{2,1,0:T(8,128)(2,1)S(1)} %collective-permute-done.19.refs_2_, bf16[3,80,640]{2,1,0:T(8,128)(2,1)S(1)} %collective-permute-done.21.refs_3_, ...), custom_call_target="tpu_custom_call" | custom-call | flops 314572800 | bytes 1228800 | tf_op jit(solution)/shard_map/pallas_call | solution.py:268
  165.3 0.8 constant_dynamic-update-slice_fusion
  (83 shorter events, 4.2 us)
Async XLA Ops:
  0.6 3.4 %copy-start.14 = (bf16[256,1280]{1,0:T(8,128)(2,1)S(1)}, bf16[256,1280]{1,0:T(8,128)(2,1)}, u32[]{:S(2)}) copy-start(bf16[256,1280]{1,0:T(8,128)(2,1)} %param.8) | copy-start | bytes 1966084
  0.6 4.7 %collective-permute-start.6 = (f32[3,40,640]{2,1,0:T(8,128)}, f32[3,40,640]{2,1,0:T(8,128)S(1)}, u32[]{:S(2)}, u32[]{:S(2)}) collective-permute-start(f32[3,40,640]{2,1,0:T(8,128)} %refs_3_.1), channel_id=1, source_target_pairs={{1,0},{3,2},{5,4},{7,6},{9,8},{11,10},{13,12},{15,14},{16,17},{18,... | collective-permute-start | bytes 921608 | tf_op jit(solution)/shard_map/ppermute | solution.py:48
  2.7 2.6 %copy-start = (f32[3,40,640]{2,1,0:T(8,128)S(1)}, f32[3,40,640]{2,1,0:T(8,128)}, u32[]{:S(2)}) copy-start(f32[3,40,640]{2,1,0:T(8,128)} %refs_3_.1) | copy-start | bytes 921604
  3.9 3.5 %copy-start.18 = (f32[2,256]{1,0:T(2,128)S(1)}, f32[2,256]{1,0:T(2,128)}, u32[]{:S(2)}) copy-start(f32[2,256]{1,0:T(2,128)} %param.10) | copy-start | bytes 6148
  3.9 9.5 %collective-permute-start.1 = (bf16[256,640]{1,0:T(8,128)(2,1)S(1)}, bf16[256,640]{1,0:T(8,128)(2,1)S(1)}, u32[]{:S(2)}, u32[]{:S(2)}) collective-permute-start(bf16[256,640]{1,0:T(8,128)(2,1)S(1)} %get-tuple-element.43), channel_id=1, source_target_pairs={{0,1},{1,0},{2,3},{3,2},{4,5},{5,4},{6,7},{7,6},{8,9},{9,8},{10,11... | collective-permute-start | bytes 983048 | tf_op jit(solution)/shard_map/ppermute | solution.py:48
  4.9 10.0 %collective-permute-start = (bf16[256,640]{1,0:T(8,128)(2,1)}, bf16[256,640]{1,0:T(8,128)(2,1)S(1)}, u32[]{:S(2)}, u32[]{:S(2)}) collective-permute-start(bf16[256,640]{1,0:T(8,128)(2,1)} %get-tuple-element.45), channel_id=1, source_target_pairs={{0,1},{1,0},{2,3},{3,2},{4,5},{5,4},{6,7},{7,6},{8,9},{9,8},{10,11... | collective-permute-start | bytes 983048 | tf_op jit(solution)/shard_map/ppermute | solution.py:48
  6.1 12.3 %collective-permute-start.7 = (bf16[3,80,640]{2,1,0:T(8,128)(2,1)}, bf16[3,80,640]{2,1,0:T(8,128)(2,1)}, u32[]{:S(2)}, u32[]{:S(2)}) collective-permute-start(bf16[3,80,640]{2,1,0:T(8,128)(2,1)} %pad_maximum_fusion.4), channel_id=1, source_target_pairs={{0,16},{2,18},{4,20},{6,22},{8,24},{10,26},{12,28},{14,30},{17,1},... | collective-permute-start | bytes 921608 | tf_op jit(solution)/shard_map/ppermute | solution.py:48
  7.5 20.7 %collective-permute-start.4 = (f32[1,256]{1,0:T(1,128)S(1)}, f32[1,256]{1,0:T(1,128)}, u32[]{:S(2)}, u32[]{:S(2)}) collective-permute-start(f32[1,256]{1,0:T(1,128)S(1)} %get-tuple-element.47), channel_id=1, source_target_pairs={{0,1},{1,0},{2,3},{3,2},{4,5},{5,4},{6,7},{7,6},{8,9},{9,8},{10,11... | collective-permute-start | bytes 3080 | tf_op jit(solution)/shard_map/ppermute | solution.py:48
  12.8 9.7 %collective-permute-start.9 = (bf16[3,80,640]{2,1,0:T(8,128)(2,1)}, bf16[3,80,640]{2,1,0:T(8,128)(2,1)S(1)}, u32[]{:S(2)}, u32[]{:S(2)}) collective-permute-start(bf16[3,80,640]{2,1,0:T(8,128)(2,1)} %pad_maximum_fusion.4), channel_id=1, source_target_pairs={{0,8},{2,10},{4,12},{6,14},{8,0},{10,2},{12,4},{14,6},{17,25},{19,... | collective-permute-start | bytes 921608 | tf_op jit(solution)/shard_map/ppermute | solution.py:48
  13.5 29.6 %collective-permute-start.3 = (bf16[2,256,640]{2,1,0:T(8,128)(2,1)S(1)}, bf16[2,256,640]{2,1,0:T(8,128)(2,1)S(1)}, u32[]{:S(2)}, u32[]{:S(2)}) collective-permute-start(bf16[2,256,640]{2,1,0:T(8,128)(2,1)S(1)} %pad_maximum_fusion.2.refs_1_.refs_4_), channel_id=1, source_target_pairs={{0,2},{1,3},{2,0},{3,1},{4,6},{5,7},{6,4},{7,5},{8,10},{9,11},{10,... | collective-permute-start | bytes 1966088 | tf_op jit(solution)/shard_map/ppermute | solution.py:48
  14.8 0.7 copy-start.16
  16.6 26.5 %collective-permute-start.2 = (bf16[2,256,640]{2,1,0:T(8,128)(2,1)S(1)}, bf16[2,256,640]{2,1,0:T(8,128)(2,1)S(1)}, u32[]{:S(2)}, u32[]{:S(2)}) collective-permute-start(bf16[2,256,640]{2,1,0:T(8,128)(2,1)S(1)} %pad_maximum_fusion.1.refs_0_.refs_3_), channel_id=1, source_target_pairs={{0,2},{1,3},{2,0},{3,1},{4,6},{5,7},{6,4},{7,5},{8,10},{9,11},{10,... | collective-permute-start | bytes 1966088 | tf_op jit(solution)/shard_map/ppermute | solution.py:48
  16.9 5.5 %copy-start.8 = (bf16[2,256,384]{2,1,0:T(8,128)(2,1)}, bf16[2,256,384]{2,1,0:T(8,128)(2,1)S(1)}, u32[]{:S(2)}) copy-start(bf16[2,256,384]{2,1,0:T(8,128)(2,1)S(1)} %slice.18) | copy-start | bytes 1179652
  17.0 9.6 %copy-start.10 = (bf16[2,256,384]{2,1,0:T(8,128)(2,1)}, bf16[2,256,384]{2,1,0:T(8,128)(2,1)S(1)}, u32[]{:S(2)}) copy-start(bf16[2,256,384]{2,1,0:T(8,128)(2,1)S(1)} %slice.19) | copy-start | bytes 1179652
  18.5 8.1 %collective-permute-start.10 = (bf16[3,80,640]{2,1,0:T(8,128)(2,1)}, bf16[3,80,640]{2,1,0:T(8,128)(2,1)S(1)}, u32[]{:S(2)}, u32[]{:S(2)}) collective-permute-start(bf16[3,80,640]{2,1,0:T(8,128)(2,1)} %collective-permute-done.7), channel_id=1, source_target_pairs={{1,9},{3,11},{5,13},{7,15},{9,1},{11,3},{13,5},{15,7},{16,24},{18,... | collective-permute-start | bytes 921608 | tf_op jit(solution)/shard_map/ppermute | solution.py:48
  22.4 20.7 %copy-start.4 = (bf16[3,80,640]{2,1,0:T(8,128)(2,1)}, bf16[3,80,640]{2,1,0:T(8,128)(2,1)S(1)}, u32[]{:S(2)}) copy-start(bf16[3,80,640]{2,1,0:T(8,128)(2,1)S(1)} %broadcast_select_fusion.5.refs_6_) | copy-start | bytes 921604
  26.6 37.6 %collective-permute-start.13 = (bf16[4,256,384]{2,1,0:T(8,128)(2,1)}, bf16[4,256,384]{2,1,0:T(8,128)(2,1)}, u32[]{:S(2)}, u32[]{:S(2)}) collective-permute-start(bf16[4,256,384]{2,1,0:T(8,128)(2,1)} %pad_maximum_fusion), channel_id=1, source_target_pairs={{4,12},{5,13},{6,14},{7,15},{12,20},{13,21},{14,22},{15,23},{20,28... | collective-permute-start | bytes 2359304 | tf_op jit(solution)/shard_map/ppermute | solution.py:48
  28.8 12.3 %collective-permute-start.5 = (f32[2,256]{1,0:T(2,128)S(1)}, f32[2,256]{1,0:T(2,128)S(1)}, u32[]{:S(2)}, u32[]{:S(2)}) collective-permute-start(f32[2,256]{1,0:T(2,128)S(1)} %pad_maximum_fusion.5.refs_4_), channel_id=1, source_target_pairs={{0,2},{1,3},{2,0},{3,1},{4,6},{5,7},{6,4},{7,5},{8,10},{9,11},{10,... | collective-permute-start | bytes 6152 | tf_op jit(solution)/shard_map/ppermute | solution.py:48
  31.4 11.7 %collective-permute-start.8 = (bf16[3,80,640]{2,1,0:T(8,128)(2,1)S(1)}, bf16[3,80,640]{2,1,0:T(8,128)(2,1)S(1)}, u32[]{:S(2)}, u32[]{:S(2)}) collective-permute-start(bf16[3,80,640]{2,1,0:T(8,128)(2,1)S(1)} %broadcast_select_fusion.5.refs_6_), channel_id=1, source_target_pairs={{0,4},{1,5},{2,6},{3,7},{4,0},{5,1},{6,2},{7,3},{8,12},{9,13},{10,... | collective-permute-start | bytes 921608 | tf_op jit(solution)/shard_map/ppermute | solution.py:48
  41.1 5.7 %collective-permute-start.11 = (bf16[3,80,640]{2,1,0:T(8,128)(2,1)S(1)}, bf16[3,80,640]{2,1,0:T(8,128)(2,1)S(1)}, u32[]{:S(2)}, u32[]{:S(2)}) collective-permute-start(bf16[3,80,640]{2,1,0:T(8,128)(2,1)S(1)} %broadcast_select_fusion.4.refs_7_), channel_id=1, source_target_pairs={{0,4},{1,5},{2,6},{3,7},{4,0},{5,1},{6,2},{7,3},{8,12},{9,13},{10,... | collective-permute-start | bytes 921608 | tf_op jit(solution)/shard_map/ppermute | solution.py:48
  42.4 0.7 copy-start.6
  49.7 2.4 %copy-start.1 = (f32[3,40,640]{2,1,0:T(8,128)S(1)}, f32[3,40,640]{2,1,0:T(8,128)}, u32[]{:S(2)}) copy-start(f32[3,40,640]{2,1,0:T(8,128)} %refs_5_.1) | copy-start | bytes 921604
  49.7 15.6 %collective-permute-start.12 = (bf16[2,3,80,640]{3,2,1,0:T(8,128)(2,1)}, bf16[2,3,80,640]{3,2,1,0:T(8,128)(2,1)}, u32[]{:S(2)}, u32[]{:S(2)}) collective-permute-start(bf16[2,3,80,640]{3,2,1,0:T(8,128)(2,1)} %shard_map.94), channel_id=1, source_target_pairs={{0,4},{1,5},{2,6},{3,7},{4,0},{5,1},{6,2},{7,3},{8,12},{9,13},{10,... | collective-permute-start | bytes 1843208 | tf_op jit(solution)/shard_map/ppermute | solution.py:48
  51.9 29.4 %collective-permute-start.29 = (bf16[4,256,256]{2,1,0:T(8,128)(2,1)}, bf16[4,256,256]{2,1,0:T(8,128)(2,1)}, u32[]{:S(2)}, u32[]{:S(2)}) collective-permute-start(bf16[4,256,256]{2,1,0:T(8,128)(2,1)} %pad_maximum_fusion.3), channel_id=1, source_target_pairs={{0,4},{1,5},{2,6},{3,7},{4,0},{5,1},{6,2},{7,3},{8,12},{9,13},{10,... | collective-permute-start | bytes 1572872 | tf_op jit(solution)/shard_map/ppermute | solution.py:48
  52.1 33.0 %collective-permute-start.17 = (f32[3,40,640]{2,1,0:T(8,128)S(1)}, f32[3,40,640]{2,1,0:T(8,128)}, u32[]{:S(2)}, u32[]{:S(2)}) collective-permute-start(f32[3,40,640]{2,1,0:T(8,128)S(1)} %copy-done.1), channel_id=1, source_target_pairs={{1,0},{3,2},{5,4},{7,6},{9,8},{11,10},{13,12},{15,14},{16,17},{18,... | collective-permute-start | bytes 921608 | tf_op jit(solution)/shard_map/ppermute | solution.py:48
  60.2 1.0 copy-start.5
  61.1 1.0 copy-start.7
  62.1 2.1 %copy-start.9 = (bf16[2,256,384]{2,1,0:T(8,128)(2,1)S(1)}, bf16[2,256,384]{2,1,0:T(8,128)(2,1)}, u32[]{:S(2)}) copy-start(bf16[2,256,384]{2,1,0:T(8,128)(2,1)} %copy-done.8) | copy-start | bytes 1179652
  62.1 2.1 %copy-start.11 = (bf16[2,256,384]{2,1,0:T(8,128)(2,1)S(1)}, bf16[2,256,384]{2,1,0:T(8,128)(2,1)}, u32[]{:S(2)}) copy-start(bf16[2,256,384]{2,1,0:T(8,128)(2,1)} %copy-done.10) | copy-start | bytes 1179652
  67.3 0.8 copy-start.2
  68.1 17.0 %collective-permute-start.14 = (bf16[3,80,640]{2,1,0:T(8,128)(2,1)}, bf16[3,80,640]{2,1,0:T(8,128)(2,1)}, u32[]{:S(2)}, u32[]{:S(2)}) collective-permute-start(bf16[3,80,640]{2,1,0:T(8,128)(2,1)} %get-tuple-element.27), channel_id=1, source_target_pairs={{1,17},{3,19},{5,21},{7,23},{9,25},{11,27},{13,29},{15,31},{16,0},... | collective-permute-start | bytes 921608 | tf_op jit(solution)/shard_map/ppermute | solution.py:48
  77.8 9.5 %collective-permute-start.15 = (bf16[3,80,640]{2,1,0:T(8,128)(2,1)}, bf16[3,80,640]{2,1,0:T(8,128)(2,1)}, u32[]{:S(2)}, u32[]{:S(2)}) collective-permute-start(bf16[3,80,640]{2,1,0:T(8,128)(2,1)} %get-tuple-element.28), channel_id=1, source_target_pairs={{1,25},{3,27},{5,29},{7,31},{9,17},{11,19},{13,21},{15,23},{16,8},... | collective-permute-start | bytes 921608 | tf_op jit(solution)/shard_map/ppermute | solution.py:48
  80.0 7.4 %collective-permute-start.16 = (bf16[3,80,640]{2,1,0:T(8,128)(2,1)}, bf16[3,80,640]{2,1,0:T(8,128)(2,1)}, u32[]{:S(2)}, u32[]{:S(2)}) collective-permute-start(bf16[3,80,640]{2,1,0:T(8,128)(2,1)} %get-tuple-element.28), channel_id=1, source_target_pairs={{0,8},{2,10},{4,12},{6,14},{8,0},{10,2},{12,4},{14,6},{17,25},{19,... | collective-permute-start | bytes 921608 | tf_op jit(solution)/shard_map/ppermute | solution.py:48
  81.3 30.7 %collective-permute-start.30 = (bf16[4,256,256]{2,1,0:T(8,128)(2,1)}, bf16[4,256,256]{2,1,0:T(8,128)(2,1)}, u32[]{:S(2)}, u32[]{:S(2)}) collective-permute-start(bf16[4,256,256]{2,1,0:T(8,128)(2,1)} %collective-permute-done.29), channel_id=1, source_target_pairs={{0,8},{1,9},{2,10},{3,11},{8,16},{9,17},{10,18},{11,19},{16,24},{1... | collective-permute-start | bytes 1572872 | tf_op jit(solution)/shard_map/ppermute | solution.py:48
  87.4 1.1 copy-start.3
  88.4 2.8 %copy-start.15 = (bf16[256,1280]{1,0:T(8,128)(2,1)S(1)}, bf16[256,1280]{1,0:T(8,128)(2,1)}, u32[]{:S(2)}) copy-start(bf16[256,1280]{1,0:T(8,128)(2,1)} %param.7) | copy-start | bytes 1966084
  89.8 24.6 %copy-start.13 = (bf16[4,256,384]{2,1,0:T(8,128)(2,1)S(1)}, bf16[4,256,384]{2,1,0:T(8,128)(2,1)}, u32[]{:S(2)}) copy-start(bf16[4,256,384]{2,1,0:T(8,128)(2,1)} %broadcast_select_fusion) | copy-start | bytes 2359300
  89.8 20.3 %collective-permute-start.18 = (bf16[3,80,640]{2,1,0:T(8,128)(2,1)S(1)}, bf16[3,80,640]{2,1,0:T(8,128)(2,1)S(1)}, u32[]{:S(2)}, u32[]{:S(2)}) collective-permute-start(bf16[3,80,640]{2,1,0:T(8,128)(2,1)S(1)} %get-tuple-element.29), channel_id=1, source_target_pairs={{0,16},{2,18},{4,20},{6,22},{8,24},{10,26},{12,28},{14,30},{17,1},... | collective-permute-start | bytes 921608 | tf_op jit(solution)/shard_map/ppermute | solution.py:48
  91.3 27.0 %collective-permute-start.28 = (bf16[256,640]{1,0:T(8,128)(2,1)S(1)}, bf16[256,640]{1,0:T(8,128)(2,1)S(1)}, u32[]{:S(2)}, u32[]{:S(2)}) collective-permute-start(bf16[256,640]{1,0:T(8,128)(2,1)S(1)} %get-tuple-element.40), channel_id=1, source_target_pairs={{0,1},{1,0},{2,3},{3,2},{4,5},{5,4},{6,7},{7,6},{8,9},{9,8},{10,11... | collective-permute-start | bytes 983048 | tf_op jit(solution)/shard_map/ppermute | solution.py:48
  98.5 16.1 %collective-permute-start.22 = (bf16[3,80,640]{2,1,0:T(8,128)(2,1)S(1)}, bf16[3,80,640]{2,1,0:T(8,128)(2,1)S(1)}, u32[]{:S(2)}, u32[]{:S(2)}) collective-permute-start(bf16[3,80,640]{2,1,0:T(8,128)(2,1)S(1)} %get-tuple-element.29), channel_id=1, source_target_pairs={{0,8},{2,10},{4,12},{6,14},{8,0},{10,2},{12,4},{14,6},{17,25},{19,... | collective-permute-start | bytes 921608 | tf_op jit(solution)/shard_map/ppermute | solution.py:48
  110.1 7.9 %collective-permute-start.23 = (bf16[3,80,640]{2,1,0:T(8,128)(2,1)S(1)}, bf16[3,80,640]{2,1,0:T(8,128)(2,1)S(1)}, u32[]{:S(2)}, u32[]{:S(2)}) collective-permute-start(bf16[3,80,640]{2,1,0:T(8,128)(2,1)S(1)} %collective-permute-done.18), channel_id=1, source_target_pairs={{1,9},{3,11},{5,13},{7,15},{9,1},{11,3},{13,5},{15,7},{16,24},{18,... | collective-permute-start | bytes 921608 | tf_op jit(solution)/shard_map/ppermute | solution.py:48
  113.1 6.5 %copy-start.17 = (f32[1280]{0:T(1024)S(1)}, f32[1280]{0:T(1024)}, u32[]{:S(2)}) copy-start(f32[1280]{0:T(1024)} %param.13) | copy-start | bytes 15364
  113.1 11.4 %collective-permute-start.31 = (bf16[4,256,256]{2,1,0:T(8,128)(2,1)S(1)}, bf16[4,256,256]{2,1,0:T(8,128)(2,1)S(1)}, u32[]{:S(2)}, u32[]{:S(2)}) collective-permute-start(bf16[4,256,256]{2,1,0:T(8,128)(2,1)S(1)} %broadcast_select_fusion.1.refs_7_), channel_id=1, source_target_pairs={{2,0},{3,1},{6,4},{7,5},{10,8},{11,9},{14,12},{15,13},{18,16},{19,... | collective-permute-start | bytes 1572872 | tf_op jit(solution)/shard_map/ppermute | solution.py:48
  114.4 16.6 %collective-permute-start.32 = (bf16[4,256,384]{2,1,0:T(8,128)(2,1)S(1)}, bf16[4,256,384]{2,1,0:T(8,128)(2,1)S(1)}, u32[]{:S(2)}, u32[]{:S(2)}) collective-permute-start(bf16[4,256,384]{2,1,0:T(8,128)(2,1)S(1)} %copy-done.13), channel_id=1, source_target_pairs={{0,4},{1,5},{2,6},{3,7},{4,0},{5,1},{6,2},{7,3},{8,12},{9,13},{10,... | collective-permute-start | bytes 2359304 | tf_op jit(solution)/shard_map/ppermute | solution.py:48
  114.6 17.9 %collective-permute-start.20 = (bf16[3,80,640]{2,1,0:T(8,128)(2,1)S(1)}, bf16[3,80,640]{2,1,0:T(8,128)(2,1)S(1)}, u32[]{:S(2)}, u32[]{:S(2)}) collective-permute-start(bf16[3,80,640]{2,1,0:T(8,128)(2,1)S(1)} %broadcast_select_fusion.3.refs_2_), channel_id=1, source_target_pairs={{0,2},{1,3},{2,0},{3,1},{4,6},{5,7},{6,4},{7,5},{8,10},{9,11},{10,... | collective-permute-start | bytes 921608 | tf_op jit(solution)/shard_map/ppermute | solution.py:48
  118.0 19.6 %collective-permute-start.25 = (bf16[3,80,640]{2,1,0:T(8,128)(2,1)S(1)}, bf16[3,80,640]{2,1,0:T(8,128)(2,1)S(1)}, u32[]{:S(2)}, u32[]{:S(2)}) collective-permute-start(bf16[3,80,640]{2,1,0:T(8,128)(2,1)S(1)} %broadcast_select_fusion.2.refs_4_), channel_id=1, source_target_pairs={{0,4},{1,5},{2,6},{3,7},{4,0},{5,1},{6,2},{7,3},{8,12},{9,13},{10,... | collective-permute-start | bytes 921608 | tf_op jit(solution)/shard_map/ppermute | solution.py:48
  118.3 21.0 %collective-permute-start.27 = (f32[3,40,640]{2,1,0:T(8,128)S(1)}, f32[3,40,640]{2,1,0:T(8,128)S(1)}, u32[]{:S(2)}, u32[]{:S(2)}) collective-permute-start(f32[3,40,640]{2,1,0:T(8,128)S(1)} %slice_bitcast_fusion), channel_id=1, source_target_pairs={{0,1},{2,3},{4,5},{6,7},{8,9},{10,11},{12,13},{14,15},{17,16},{19,... | collective-permute-start | bytes 921608 | tf_op jit(solution)/shard_map/ppermute | solution.py:48
  128.6 30.7 %collective-permute-start.19 = (bf16[3,80,640]{2,1,0:T(8,128)(2,1)S(1)}, bf16[3,80,640]{2,1,0:T(8,128)(2,1)S(1)}, u32[]{:S(2)}, u32[]{:S(2)}) collective-permute-start(bf16[3,80,640]{2,1,0:T(8,128)(2,1)S(1)} %broadcast_select_fusion.3.refs_2_), channel_id=1, source_target_pairs={{0,4},{1,5},{2,6},{3,7},{4,0},{5,1},{6,2},{7,3},{8,12},{9,13},{10,... | collective-permute-start | bytes 921608 | tf_op jit(solution)/shard_map/ppermute | solution.py:48
  131.0 23.2 %collective-permute-start.33 = (bf16[4,256,384]{2,1,0:T(8,128)(2,1)S(1)}, bf16[4,256,384]{2,1,0:T(8,128)(2,1)S(1)}, u32[]{:S(2)}, u32[]{:S(2)}) collective-permute-start(bf16[4,256,384]{2,1,0:T(8,128)(2,1)S(1)} %collective-permute-done.32.refs_7_), channel_id=1, source_target_pairs={{2,0},{3,1},{6,4},{7,5},{10,8},{11,9},{14,12},{15,13},{18,16},{19,... | collective-permute-start | bytes 2359304 | tf_op jit(solution)/shard_map/ppermute | solution.py:48
  132.5 26.8 %collective-permute-start.24 = (bf16[3,80,640]{2,1,0:T(8,128)(2,1)S(1)}, bf16[3,80,640]{2,1,0:T(8,128)(2,1)S(1)}, u32[]{:S(2)}, u32[]{:S(2)}) collective-permute-start(bf16[3,80,640]{2,1,0:T(8,128)(2,1)S(1)} %broadcast_select_fusion.2.refs_4_), channel_id=1, source_target_pairs={{0,2},{1,3},{2,0},{3,1},{4,6},{5,7},{6,4},{7,5},{8,10},{9,11},{10,... | collective-permute-start | bytes 921608 | tf_op jit(solution)/shard_map/ppermute | solution.py:48
  137.6 21.7 %collective-permute-start.21 = (bf16[3,80,640]{2,1,0:T(8,128)(2,1)S(1)}, bf16[3,80,640]{2,1,0:T(8,128)(2,1)S(1)}, u32[]{:S(2)}, u32[]{:S(2)}) collective-permute-start(bf16[3,80,640]{2,1,0:T(8,128)(2,1)S(1)} %collective-permute-done.20.refs_3_), channel_id=1, source_target_pairs={{0,4},{1,5},{2,6},{3,7},{4,0},{5,1},{6,2},{7,3},{8,12},{9,13},{10,... | collective-permute-start | bytes 921608 | tf_op jit(solution)/shard_map/ppermute | solution.py:48
  139.4 21.9 %collective-permute-start.26 = (bf16[3,80,640]{2,1,0:T(8,128)(2,1)S(1)}, bf16[3,80,640]{2,1,0:T(8,128)(2,1)S(1)}, u32[]{:S(2)}, u32[]{:S(2)}) collective-permute-start(bf16[3,80,640]{2,1,0:T(8,128)(2,1)S(1)} %collective-permute-done.25.refs_5_), channel_id=1, source_target_pairs={{0,2},{1,3},{2,0},{3,1},{4,6},{5,7},{6,4},{7,5},{8,10},{9,11},{10,... | collective-permute-start | bytes 921608 | tf_op jit(solution)/shard_map/ppermute | solution.py:48
  143.2 16.1 %copy-start.12 = (f32[3,40,640]{2,1,0:T(8,128)}, f32[3,40,640]{2,1,0:T(8,128)S(1)}, u32[]{:S(2)}) copy-start(f32[3,40,640]{2,1,0:T(8,128)S(1)} %get-tuple-element.19) | copy-start | bytes 921604
  162.8 2.4 %collective-permute-start.34 = (bf16[256,640]{1,0:T(8,128)(2,1)S(1)}, bf16[256,640]{1,0:T(8,128)(2,1)S(1)}, u32[]{:S(2)}, u32[]{:S(2)}) collective-permute-start(bf16[256,640]{1,0:T(8,128)(2,1)S(1)} %shard_map.99), channel_id=1, source_target_pairs={{0,1},{1,0},{2,3},{3,2},{4,5},{5,4},{6,7},{7,6},{8,9},{9,8},{10,11... | collective-permute-start | bytes 983048 | tf_op jit(solution)/shard_map/ppermute | solution.py:48
